TPU v7x, 32 devices: a whole 2x2x4 slice. The times are simulated.
32 devices in a mesh: seq: 8 (over z, x), wsh: 4 (over y, core).
Axes of the slice: x: 2, y: 2, z: 4, core: 2. Of those that a mesh axis runs over, the one named last changes fastest.
Arguments:
- tokens: bfloat16 [4096, 2048], P(('seq', 'wsh')), may hold values from -6 to 6
- first_layer_values: bfloat16 [4096, 2048], P(('seq', 'wsh')), may hold values from -6 to 6
- teacher: bfloat16 [4096, 2048], P(('seq', 'wsh')), may hold values from -6 to 6
- valid: int32 [4096], P(('seq', 'wsh')), may hold values from 0 to 1, as said below
- destination: int32 [4096], P(('seq', 'wsh')), may hold values from 0 to 4095, as said below
- lengths: int32 [4, 4], P('wsh'), may hold values from 1 to 512, 1024 in all within a row
- receptance_matrix: bfloat16 [2048, 2048], P('wsh'), may hold values from -0.125 to 0.125
- key_matrix: bfloat16 [2048, 2048], P('wsh'), may hold values from -0.125 to 0.125
- value_matrix: bfloat16 [2048, 2048], P('wsh'), may hold values from -0.125 to 0.125
- output_matrix: bfloat16 [2048, 2048], P('wsh'), may hold values from -0.125 to 0.125
- lowrank_down_weight: bfloat16 [2048, 512], P('wsh'), may hold values from -0.125 to 0.125
- lowrank_up_weight: bfloat16 [2048, 512], P('wsh'), may hold values from -0.5 to 0.5
- channel_key_weight: bfloat16 [8192, 2048], P('wsh'), may hold values from -0.125 to 0.125
- channel_value_weight: bfloat16 [8192, 2048], P('wsh'), may hold values from -0.0546875 to 0.0546875
- vectors: float32 [2048, 19], replicated, may hold values from -8 to 1.5
Outputs:
- output: bfloat16 [4096, 2048], P(('seq', 'wsh'))
- grad_tokens: bfloat16 [4096, 2048], P(('seq', 'wsh'))
- grad_first_values: bfloat16 [4096, 2048], P(('seq', 'wsh'))
- grad_receptance: float32 [2048, 2048], P(('seq', 'wsh'))
- grad_key: float32 [2048, 2048], P(('seq', 'wsh'))
- grad_value: float32 [2048, 2048], P(('seq', 'wsh'))
- grad_output_weight: float32 [2048, 2048], P(('seq', 'wsh'))
- grad_lora_down: float32 [2048, 512], P(('seq', 'wsh'))
- grad_lora_up: float32 [2048, 512], P(('seq', 'wsh'))
- grad_ffn_key: float32 [8192, 2048], P(('seq', 'wsh'))
- grad_ffn_value: float32 [8192, 2048], P(('seq', 'wsh'))
- grad_vectors: float32 [2048, 19], P(('seq', 'wsh'))
Inputs may be any that keep to these rules, and one draw needn't show every extreme that they name: `destination`: A permutation of the rows. The rows of a block of 128 go to blocks of the same group, exactly 16 of them to each block of that group. `lengths`: each row sums to 1024; its largest entry is 512. `valid`: the first row of every block of 128 rows is 1.
All inputs are finite; a program needn't handle non-finite values.
Results may differ from a plain program's by a relative error of at most 0.013.
The roundings to bfloat16 on the way count: a program that leaves them out, or rounds other values in their place, can miss the bound.
Values may be sent and summed in bfloat16 or wider, within the bound.
A program may use at most 448 MiB of HBM per device.

v0:
```python
import jax
import jax.numpy as jnp
from jax import lax
from jax.sharding import PartitionSpec as P

LEADER_NUMBER = 32
PER_LEADER_DIMS = 64
RW = 96
RA = 96
RV = 64
RG = 256
BLOCK = 64


HIGH = lax.Precision.HIGHEST


def from_behind(x, axis, by):
    size = lax.axis_size(axis)
    pairs = [(i, i + by) for i in range(size) if 0 <= i + by < size]
    return lax.ppermute(x, axis, pairs)


def layer_norm(values, gain_row, bias_row):
    centered = values - jnp.mean(values, -1, keepdims=True)
    return (
        centered * lax.rsqrt(jnp.mean(centered * centered, -1, keepdims=True) + 1e-05) * gain_row
        + bias_row
    )


def norm_first(values, vectors):
    return layer_norm(values, vectors[:, 0], vectors[:, 1])


def norm_second(values, vectors):
    return layer_norm(values, vectors[:, 16], vectors[:, 17])


def token_mix(standardized_lines, edge_row, vectors, starts):
    previous = jnp.concatenate([edge_row, standardized_lines[:-1]], 0) * (1.0 - starts)[:, None]
    delta_row = previous - standardized_lines
    return tuple(
        (standardized_lines + delta_row * vectors[:, 2 + piece_count] for piece_count in range(6))
    )


def channel_mix(standardized_lines, edge_row, vectors, starts):
    previous = jnp.concatenate([edge_row, standardized_lines[:-1]], 0) * (1.0 - starts)[:, None]
    return standardized_lines + (previous - standardized_lines) * vectors[:, 18]


def shape_front(keys_raw, values_raw, decay_up, rate_up, value_up, first_in, vectors):
    number_lines = keys_raw.shape[0]
    decay_log = -jax.nn.softplus(-(vectors[:, 8] + decay_up)) - 0.5
    learn_rate = jax.nn.sigmoid(vectors[:, 9] + rate_up)
    blended_payload = values_raw + (first_in - values_raw) * jax.nn.sigmoid(
        vectors[:, 10] + value_up
    )
    scaled = (keys_raw * vectors[:, 11]).reshape(number_lines, LEADER_NUMBER, PER_LEADER_DIMS)
    key_dir = (scaled * lax.rsqrt(jnp.sum(scaled * scaled, -1, keepdims=True) + 1e-06)).reshape(
        number_lines, -1
    )
    key_mod = keys_raw * (1.0 + (learn_rate - 1.0) * vectors[:, 12])
    return (decay_log, key_mod, blended_payload, key_dir, learn_rate)


def shape_post(head_out, recept, key_mod, blended_payload, sigmoid_opening, vectors):
    number_lines = head_out.shape[0]
    grouped = head_out.reshape(number_lines, LEADER_NUMBER, PER_LEADER_DIMS)
    centered = grouped - jnp.mean(grouped, -1, keepdims=True)
    standardized_lines = centered * lax.rsqrt(
        jnp.mean(centered * centered, -1, keepdims=True) + PER_LEADER_DIMS * 1e-05
    )
    standardized_lines = (
        standardized_lines.reshape(number_lines, -1) * vectors[:, 14] + vectors[:, 15]
    )
    coefficient_sum = jnp.sum(
        (recept * key_mod * vectors[:, 13]).reshape(number_lines, LEADER_NUMBER, PER_LEADER_DIMS),
        -1,
        keepdims=True,
    )
    extra_reward_share = (
        coefficient_sum * blended_payload.reshape(number_lines, LEADER_NUMBER, PER_LEADER_DIMS)
    ).reshape(number_lines, -1)
    return (standardized_lines + extra_reward_share) * sigmoid_opening


def product(left_side, right_side):
    return jnp.dot(left_side, right_side, preferred_element_type=jnp.float32)


def times_transposed(left_side, right_side):
    return lax.dot_general(
        left_side, right_side, (((1,), (1,)), ((), ())), preferred_element_type=jnp.float32
    )


def trans_times(left_side, right_side):
    return lax.dot_general(
        left_side, right_side, (((0,), (0,)), ((), ())), preferred_element_type=jnp.float32
    )


def pair_dot(form, left_side, right_side):
    return jnp.einsum(form, left_side, right_side, precision=HIGH)


def chain_join(earlier, later_pair):
    return (
        pair_dot("...ij,...jk->...ik", earlier[0], later_pair[0]),
        pair_dot("...ij,...jk->...ik", earlier[1], later_pair[0]) + later_pair[1],
    )


def block_recurrence(pieces, starts):
    number_lines = pieces[0].shape[0]
    head_count = pieces[0].shape[1] // PER_LEADER_DIMS
    blocks = number_lines // BLOCK

    def split_blocks(piece):
        return piece.reshape(blocks, BLOCK, head_count, PER_LEADER_DIMS).transpose(2, 0, 1, 3)

    recept, decay_log, key_mod, blended_payload, key_dir, learn_rate = [
        split_blocks(piece) for piece in pieces
    ]
    block_starts = starts.reshape(blocks, BLOCK)
    segment_ids = jnp.cumsum(starts).reshape(blocks, BLOCK)
    segment_prev = segment_ids[:, 0] - block_starts[:, 0]
    log_step = -jnp.exp(decay_log)
    log_total = jnp.cumsum(log_step, axis=2)
    log_before = log_total - log_step
    growth = jnp.exp(-log_total)
    alpha_hat = -key_dir * jnp.exp(log_before)
    beta_plain = key_dir * learn_rate
    beta_inv = beta_plain * growth
    key_inv = key_mod * growth
    recept_hat = recept * jnp.exp(log_total)
    same_segment = (segment_ids[:, :, None] == segment_ids[:, None, :]).astype(jnp.float32)
    strict_lower = jnp.tril(jnp.ones((BLOCK, BLOCK), jnp.float32), -1) * same_segment
    with_diagonal = jnp.tril(jnp.ones((BLOCK, BLOCK), jnp.float32), 0) * same_segment
    pair_beta = pair_dot("hbik,hbjk->hbij", alpha_hat, beta_inv) * strict_lower
    pair_key = pair_dot("hbik,hbjk->hbij", alpha_hat, key_inv) * strict_lower
    read_beta = pair_dot("hbik,hbjk->hbij", recept_hat, beta_inv) * with_diagonal
    read_key = pair_dot("hbik,hbjk->hbij", recept_hat, key_inv) * with_diagonal
    carry_in = (segment_ids == segment_prev[:, None]).astype(jnp.float32)[:, :, None]
    system = jnp.eye(BLOCK, dtype=jnp.float32) - pair_beta
    solved_state = lax.linalg.triangular_solve(
        system, alpha_hat * carry_in, left_side=True, lower=True, unit_diagonal=True
    )
    solved_free = lax.linalg.triangular_solve(
        system,
        pair_dot("hbij,hbjv->hbiv", pair_key, blended_payload),
        left_side=True,
        lower=True,
        unit_diagonal=True,
    )
    last_same = (segment_ids == segment_ids[:, -1:]).astype(jnp.float32)[:, :, None]
    tail_decay = jnp.exp(log_total[:, :, -1:, :] - log_total) * last_same
    beta_end = beta_plain * tail_decay
    key_end = key_mod * tail_decay
    keep_state = (segment_ids[:, -1] == segment_prev).astype(jnp.float32)[:, None]
    transit_diag = jnp.exp(log_total[:, :, -1, :]) * keep_state
    transit = transit_diag[..., :, None] * jnp.eye(PER_LEADER_DIMS, dtype=jnp.float32) + pair_dot(
        "hbik,hbij->hbkj", solved_state, beta_end
    )
    inject = pair_dot("hbiv,hbik->hbvk", solved_free, beta_end) + pair_dot(
        "hbiv,hbik->hbvk", blended_payload, key_end
    )
    after_block = lax.associative_scan(chain_join, (transit, inject), axis=1)
    entering = jnp.concatenate([jnp.zeros_like(after_block[1][:, :1]), after_block[1][:, :-1]], 1)
    removed = pair_dot("hbik,hbvk->hbiv", solved_state, entering) + solved_free
    outputs = (
        pair_dot("hbik,hbvk->hbiv", recept_hat * carry_in, entering)
        + pair_dot("hbij,hbjv->hbiv", read_beta, removed)
        + pair_dot("hbij,hbjv->hbiv", read_key, blended_payload)
    )
    return outputs.transpose(1, 2, 0, 3).reshape(number_lines, head_count * PER_LEADER_DIMS)


def lowrank_pieces(matrix_operand):
    group_bounds = [0, RW, RW + RA, RW + RA + RV, RW + RA + RV + RG]
    return [
        matrix_operand[:, group_bounds[piece_count] : group_bounds[piece_count + 1]]
        for piece_count in range(4)
    ]


def column_split(left_side, seq_count, wsh_count):
    return left_side.reshape(
        left_side.shape[0], seq_count, wsh_count, left_side.shape[1] // (seq_count * wsh_count)
    )


def row_copies(right_side, wsh_count):
    return jnp.broadcast_to(
        right_side[:, None, None, :], (right_side.shape[0], 1, wsh_count, right_side.shape[1])
    )


def flat_rows(piece):
    return piece.reshape(piece.shape[0], -1)


def local(
    tokens,
    first_layer_values,
    teacher,
    valid,
    destination,
    lengths,
    receptance_matrix,
    key_matrix,
    value_matrix,
    output_matrix,
    lowrank_down_weight,
    lowrank_up_weight,
    channel_key_weight,
    channel_value_weight,
    vectors,
):
    tok_rows = tokens.shape[0]
    seq_count = lax.axis_size("seq")
    wsh_count = lax.axis_size("wsh")
    peer_rows = tok_rows // seq_count
    group_rows = tok_rows * seq_count
    dest_seq = destination // tok_rows // wsh_count
    send_order = jnp.argsort(dest_seq, stable=True)
    restore = jnp.argsort(send_order)
    dest_local = destination % tok_rows

    def arrange(array):
        return array[send_order].reshape((seq_count, peer_rows) + array.shape[1:])

    peer_ids = jnp.arange(seq_count, dtype=jnp.int32)
    is_last = (dest_local == tok_rows - 1) & (dest_seq < seq_count - 1)
    picker = ((dest_seq[None, :] + 1 == peer_ids[:, None]) & is_last[None, :]).astype(jnp.bfloat16)
    edge_send = product(picker, tokens).astype(jnp.bfloat16).reshape(seq_count, 1, -1)
    count_send = jnp.broadcast_to(jnp.sum(valid).reshape(1, 1), (seq_count, 1))
    dealt_rows = (
        lax.all_to_all(arrange(tokens), "seq", split_axis=0, concat_axis=0, tiled=True),
        lax.all_to_all(arrange(first_layer_values), "seq", split_axis=0, concat_axis=0, tiled=True),
        lax.all_to_all(arrange(teacher), "seq", split_axis=0, concat_axis=0, tiled=True),
        lax.all_to_all(arrange(valid), "seq", split_axis=0, concat_axis=0, tiled=True),
        lax.all_to_all(arrange(dest_local), "seq", split_axis=0, concat_axis=0, tiled=True),
        lax.all_to_all(edge_send, "seq", split_axis=0, concat_axis=0, tiled=True),
        lax.all_to_all(count_send, "seq", split_axis=0, concat_axis=0, tiled=True),
    )
    arrived_rows = dealt_rows[4].reshape(tok_rows)
    placing = jnp.argsort(arrived_rows)

    def settle(array):
        return array.reshape((tok_rows,) + array.shape[2:])[placing]

    inputs = settle(dealt_rows[0]).astype(jnp.float32)
    first_in = settle(dealt_rows[1]).astype(jnp.float32)
    target = settle(dealt_rows[2]).astype(jnp.float32)
    mask_rows = settle(dealt_rows[3]).astype(jnp.float32)
    edge_raw = jnp.sum(dealt_rows[5].astype(jnp.float32), 0)
    group_count = jnp.sum(dealt_rows[6]).astype(jnp.int32).reshape(1)
    offsets = jnp.cumsum(lengths[0]) - lengths[0]
    group_places = jnp.arange(group_rows, dtype=jnp.int32)
    group_starts = jnp.any(group_places[:, None] == offsets[None, :], 1).astype(jnp.float32)
    starts = lax.dynamic_slice_in_dim(group_starts, lax.axis_index("seq") * tok_rows, tok_rows)
    gathered = (
        lax.all_gather(receptance_matrix, "wsh", axis=0, tiled=True),
        lax.all_gather(key_matrix, "wsh", axis=0, tiled=True),
        lax.all_gather(value_matrix, "wsh", axis=0, tiled=True),
        lax.all_gather(output_matrix, "wsh", axis=0, tiled=True),
        lax.all_gather(lowrank_down_weight, "wsh", axis=0, tiled=True),
        lax.all_gather(lowrank_up_weight, "wsh", axis=0, tiled=True),
        lax.all_gather(channel_key_weight, "wsh", axis=0, tiled=True),
        lax.all_gather(channel_value_weight, "wsh", axis=0, tiled=True),
        lax.all_gather(group_count, "wsh", axis=0, tiled=True),
    )
    (
        receptance_projection,
        key_projection,
        value_projection,
        output_projection,
        down_factor_full,
        up_factor_full,
        key_full,
        value_full,
        counts_all,
    ) = gathered
    total_valid = jnp.sum(counts_all).astype(jnp.float32)
    down_factor_parts = lowrank_pieces(down_factor_full)
    up_factor_parts = lowrank_pieces(up_factor_full)
    normed_one, norm_one_back = jax.vjp(norm_first, inputs, vectors)
    carried = norm_first(edge_raw, vectors)
    mixed, mix_back = jax.vjp(
        lambda standardized_lines, edge_row, layer_parameters: token_mix(
            standardized_lines, edge_row, layer_parameters, starts
        ),
        normed_one,
        carried,
        vectors,
    )
    mixed_low = [piece.astype(jnp.bfloat16) for piece in mixed]
    recept = product(mixed_low[0], receptance_projection)
    keys_raw = product(mixed_low[2], key_projection)
    values_raw = product(mixed_low[3], value_projection)
    decay_down = product(mixed_low[1], down_factor_parts[0])
    decay_hidden = jnp.tanh(decay_down).astype(jnp.bfloat16)
    decay_up = times_transposed(decay_hidden, up_factor_parts[0])
    rate_hidden = product(mixed_low[4], down_factor_parts[1]).astype(jnp.bfloat16)
    rate_up = times_transposed(rate_hidden, up_factor_parts[1])
    value_hidden = product(mixed_low[3], down_factor_parts[2]).astype(jnp.bfloat16)
    value_up = times_transposed(value_hidden, up_factor_parts[2])
    gate_down = product(mixed_low[5], down_factor_parts[3])
    gate_hidden = jax.nn.sigmoid(gate_down).astype(jnp.bfloat16)
    sigmoid_opening = times_transposed(gate_hidden, up_factor_parts[3])
    fronted, front_back = jax.vjp(
        shape_front, keys_raw, values_raw, decay_up, rate_up, value_up, first_in, vectors
    )
    decay_log, key_mod, blended_payload, key_dir, learn_rate = fronted
    sent_rows = [
        piece.astype(jnp.bfloat16)
        for piece in (recept, decay_log, key_mod, blended_payload, key_dir, learn_rate)
    ]
    to_heads = (
        lax.all_to_all(sent_rows[0], "seq", split_axis=1, concat_axis=0, tiled=True),
        lax.all_to_all(sent_rows[1], "seq", split_axis=1, concat_axis=0, tiled=True),
        lax.all_to_all(sent_rows[2], "seq", split_axis=1, concat_axis=0, tiled=True),
        lax.all_to_all(sent_rows[3], "seq", split_axis=1, concat_axis=0, tiled=True),
        lax.all_to_all(sent_rows[4], "seq", split_axis=1, concat_axis=0, tiled=True),
        lax.all_to_all(sent_rows[5], "seq", split_axis=1, concat_axis=0, tiled=True),
    )
    head_inputs = [piece.astype(jnp.float32) for piece in to_heads]
    head_out, head_back = jax.vjp(
        lambda *pieces: block_recurrence(pieces, group_starts), *head_inputs
    )
    back_tokens = lax.all_to_all(
        head_out.astype(jnp.bfloat16), "seq", split_axis=0, concat_axis=1, tiled=True
    )
    posted, post_back = jax.vjp(
        shape_post,
        back_tokens.astype(jnp.float32),
        recept,
        key_mod,
        blended_payload,
        sigmoid_opening,
        vectors,
    )
    mixed_out = posted.astype(jnp.bfloat16)
    residual = inputs + product(mixed_out, output_projection)
    normed_two, norm_two_back = jax.vjp(norm_second, residual, vectors)
    carried_two = from_behind(normed_two[-1:], "seq", 1)
    channel_in, channel_back = jax.vjp(
        lambda standardized_lines, edge_row, layer_parameters: channel_mix(
            standardized_lines, edge_row, layer_parameters, starts
        ),
        normed_two,
        carried_two,
        vectors,
    )
    channel_low = channel_in.astype(jnp.bfloat16)
    pre_act = times_transposed(channel_low, key_full)
    hidden_rows = jnp.square(jax.nn.relu(pre_act)).astype(jnp.bfloat16)
    result = residual + product(hidden_rows, value_full)
    total_tokens = tok_rows * seq_count * wsh_count
    cotangent = (result - target) * (mask_rows * (total_tokens / total_valid))[:, None]
    cot_low = cotangent.astype(jnp.bfloat16)
    grad_hidden = times_transposed(cot_low, value_full)
    grad_pre = (grad_hidden * 2.0 * jax.nn.relu(pre_act)).astype(jnp.bfloat16)
    grad_channel = product(grad_pre, key_full)
    grad_normed_two, grad_carried_two, grad_vec_channel = channel_back(grad_channel)
    from_after = from_behind(grad_carried_two, "seq", -1)
    grad_normed_two = grad_normed_two.at[-1:].add(from_after)
    grad_residual, grad_vec_two = norm_two_back(grad_normed_two)
    grad_residual = grad_residual + cotangent
    grad_res_low = grad_residual.astype(jnp.bfloat16)
    grad_posted = times_transposed(grad_res_low, output_projection)
    grad_head, grad_recept, grad_key_mod, grad_value_mix, grad_gate, grad_vec_post = post_back(
        grad_posted
    )
    heads_grad = lax.all_to_all(
        grad_head.astype(jnp.bfloat16), "seq", split_axis=1, concat_axis=0, tiled=True
    )
    head_grads = head_back(heads_grad.astype(jnp.float32))
    head_low = [piece.astype(jnp.bfloat16) for piece in head_grads]
    returned = (
        lax.all_to_all(head_low[0], "seq", split_axis=0, concat_axis=1, tiled=True),
        lax.all_to_all(head_low[1], "seq", split_axis=0, concat_axis=1, tiled=True),
        lax.all_to_all(head_low[2], "seq", split_axis=0, concat_axis=1, tiled=True),
        lax.all_to_all(head_low[3], "seq", split_axis=0, concat_axis=1, tiled=True),
        lax.all_to_all(head_low[4], "seq", split_axis=0, concat_axis=1, tiled=True),
        lax.all_to_all(head_low[5], "seq", split_axis=0, concat_axis=1, tiled=True),
    )
    returned = [piece.astype(jnp.float32) for piece in returned]
    grad_recept = grad_recept + returned[0]
    (
        grad_keys_raw,
        grad_values_raw,
        grad_decay_up,
        grad_rate_up,
        grad_value_up,
        grad_first,
        grad_vec_front,
    ) = front_back(
        (
            returned[1],
            grad_key_mod + returned[2],
            grad_value_mix + returned[3],
            returned[4],
            returned[5],
        )
    )
    recept_low = grad_recept.astype(jnp.bfloat16)
    keys_low = grad_keys_raw.astype(jnp.bfloat16)
    values_low = grad_values_raw.astype(jnp.bfloat16)
    grad_mix_recept = times_transposed(recept_low, receptance_projection)
    grad_mix_key = times_transposed(keys_low, key_projection)
    value_mix_gradient = times_transposed(values_low, value_projection)
    decay_up_low = grad_decay_up.astype(jnp.bfloat16)
    rate_up_low = grad_rate_up.astype(jnp.bfloat16)
    value_up_low = grad_value_up.astype(jnp.bfloat16)
    gate_up_low = grad_gate.astype(jnp.bfloat16)
    grad_hid_decay = product(decay_up_low, up_factor_parts[0])
    grad_hid_rate = product(rate_up_low, up_factor_parts[1])
    grad_hid_value = product(value_up_low, up_factor_parts[2])
    grad_hid_gate = product(gate_up_low, up_factor_parts[3])
    gate_sigmoid = jax.nn.sigmoid(gate_down)
    decay_down_low = (grad_hid_decay * (1.0 - jnp.square(jnp.tanh(decay_down)))).astype(
        jnp.bfloat16
    )
    rate_down_low = grad_hid_rate.astype(jnp.bfloat16)
    value_down_lowrank = grad_hid_value.astype(jnp.bfloat16)
    gate_down_low = (grad_hid_gate * gate_sigmoid * (1.0 - gate_sigmoid)).astype(jnp.bfloat16)
    grad_mix_decay = times_transposed(decay_down_low, down_factor_parts[0])
    grad_mix_rate = times_transposed(rate_down_low, down_factor_parts[1])
    value_mix_lowrank_gradient = times_transposed(value_down_lowrank, down_factor_parts[2])
    grad_mix_gate = times_transposed(gate_down_low, down_factor_parts[3])
    grad_normed_one, grad_carried, grad_vec_mix = mix_back(
        (
            grad_mix_recept,
            grad_mix_decay,
            grad_mix_key,
            value_mix_gradient + value_mix_lowrank_gradient,
            grad_mix_rate,
            grad_mix_gate,
        )
    )
    from_after_one = from_behind(grad_carried, "seq", -1)
    grad_normed_one = grad_normed_one.at[-1:].add(from_after_one)
    grad_inputs, grad_vec_one = norm_one_back(grad_normed_one)
    grad_token_rows = grad_residual + grad_inputs
    grad_vectors = (
        grad_vec_one
        + grad_vec_mix
        + grad_vec_front
        + grad_vec_post
        + grad_vec_two
        + grad_vec_channel
    )

    def unsettle(array):
        return array.astype(jnp.bfloat16)[arrived_rows].reshape(
            (seq_count, peer_rows) + array.shape[1:]
        )

    returned_rows = (
        lax.all_to_all(unsettle(result), "seq", split_axis=0, concat_axis=0, tiled=True),
        lax.all_to_all(unsettle(grad_token_rows), "seq", split_axis=0, concat_axis=0, tiled=True),
        lax.all_to_all(unsettle(grad_first), "seq", split_axis=0, concat_axis=0, tiled=True),
    )

    def to_given(array):
        return array.reshape((tok_rows,) + array.shape[2:])[restore]

    down_lows = jnp.concatenate(
        [decay_down_low, rate_down_low, value_down_lowrank, gate_down_low], 1
    )
    up_hiddens = jnp.concatenate([decay_hidden, rate_hidden, value_hidden, gate_hidden], 1)
    left_recept = column_split(mixed_low[0], seq_count, wsh_count)
    left_key = column_split(mixed_low[2], seq_count, wsh_count)
    left_value = column_split(mixed_low[3], seq_count, wsh_count)
    left_out = column_split(mixed_out, seq_count, wsh_count)
    left_decay = column_split(mixed_low[1], seq_count, wsh_count)
    left_rate = column_split(mixed_low[4], seq_count, wsh_count)
    left_gate = column_split(mixed_low[5], seq_count, wsh_count)
    left_up_decay = column_split(decay_up_low, seq_count, wsh_count)
    left_up_rate = column_split(rate_up_low, seq_count, wsh_count)
    left_up_value = column_split(value_up_low, seq_count, wsh_count)
    left_up_gate = column_split(gate_up_low, seq_count, wsh_count)
    left_pre = column_split(grad_pre, seq_count, wsh_count)
    left_hidden = column_split(hidden_rows, seq_count, wsh_count)
    right_recept = row_copies(recept_low, wsh_count)
    right_key = row_copies(keys_low, wsh_count)
    right_value = row_copies(values_low, wsh_count)
    right_out = row_copies(grad_res_low, wsh_count)
    right_channel = row_copies(channel_low, wsh_count)
    right_cot = row_copies(cot_low, wsh_count)
    right_down = row_copies(down_lows, wsh_count)
    right_up = row_copies(up_hiddens, wsh_count)
    moved = (
        lax.all_to_all(left_recept, "wsh", split_axis=2, concat_axis=0, tiled=True),
        lax.all_to_all(left_key, "wsh", split_axis=2, concat_axis=0, tiled=True),
        lax.all_to_all(left_value, "wsh", split_axis=2, concat_axis=0, tiled=True),
        lax.all_to_all(left_out, "wsh", split_axis=2, concat_axis=0, tiled=True),
        lax.all_to_all(left_decay, "wsh", split_axis=2, concat_axis=0, tiled=True),
        lax.all_to_all(left_rate, "wsh", split_axis=2, concat_axis=0, tiled=True),
        lax.all_to_all(left_gate, "wsh", split_axis=2, concat_axis=0, tiled=True),
        lax.all_to_all(left_up_decay, "wsh", split_axis=2, concat_axis=0, tiled=True),
        lax.all_to_all(left_up_rate, "wsh", split_axis=2, concat_axis=0, tiled=True),
        lax.all_to_all(left_up_value, "wsh", split_axis=2, concat_axis=0, tiled=True),
        lax.all_to_all(left_up_gate, "wsh", split_axis=2, concat_axis=0, tiled=True),
        lax.all_to_all(left_pre, "wsh", split_axis=2, concat_axis=0, tiled=True),
        lax.all_to_all(left_hidden, "wsh", split_axis=2, concat_axis=0, tiled=True),
        lax.all_to_all(right_recept, "wsh", split_axis=2, concat_axis=0, tiled=True),
        lax.all_to_all(right_key, "wsh", split_axis=2, concat_axis=0, tiled=True),
        lax.all_to_all(right_value, "wsh", split_axis=2, concat_axis=0, tiled=True),
        lax.all_to_all(right_out, "wsh", split_axis=2, concat_axis=0, tiled=True),
        lax.all_to_all(right_channel, "wsh", split_axis=2, concat_axis=0, tiled=True),
        lax.all_to_all(right_cot, "wsh", split_axis=2, concat_axis=0, tiled=True),
        lax.all_to_all(right_down, "wsh", split_axis=2, concat_axis=0, tiled=True),
        lax.all_to_all(right_up, "wsh", split_axis=2, concat_axis=0, tiled=True),
    )
    lefts = [flat_rows(piece) for piece in moved[:13]]
    rights = [flat_rows(piece) for piece in moved[13:]]
    down_right = lowrank_pieces(rights[6])
    up_right = lowrank_pieces(rights[7])
    part_down = jnp.concatenate(
        [
            trans_times(lefts[4], down_right[0]),
            trans_times(lefts[5], down_right[1]),
            trans_times(lefts[2], down_right[2]),
            trans_times(lefts[6], down_right[3]),
        ],
        1,
    )
    part_up = jnp.concatenate(
        [
            trans_times(lefts[7], up_right[0]),
            trans_times(lefts[8], up_right[1]),
            trans_times(lefts[9], up_right[2]),
            trans_times(lefts[10], up_right[3]),
        ],
        1,
    )
    weight_parts = (
        lax.psum_scatter(
            trans_times(lefts[0], rights[0]).astype(jnp.bfloat16),
            "seq",
            scatter_dimension=0,
            tiled=True,
        ).astype(jnp.float32),
        lax.psum_scatter(
            trans_times(lefts[1], rights[1]).astype(jnp.bfloat16),
            "seq",
            scatter_dimension=0,
            tiled=True,
        ).astype(jnp.float32),
        lax.psum_scatter(
            trans_times(lefts[2], rights[2]).astype(jnp.bfloat16),
            "seq",
            scatter_dimension=0,
            tiled=True,
        ).astype(jnp.float32),
        lax.psum_scatter(
            trans_times(lefts[3], rights[3]).astype(jnp.bfloat16),
            "seq",
            scatter_dimension=0,
            tiled=True,
        ).astype(jnp.float32),
        lax.psum_scatter(
            part_down.astype(jnp.bfloat16), "seq", scatter_dimension=0, tiled=True
        ).astype(jnp.float32),
        lax.psum_scatter(
            part_up.astype(jnp.bfloat16), "seq", scatter_dimension=0, tiled=True
        ).astype(jnp.float32),
        lax.psum_scatter(
            trans_times(lefts[11], rights[4]).astype(jnp.bfloat16),
            "seq",
            scatter_dimension=0,
            tiled=True,
        ).astype(jnp.float32),
        lax.psum_scatter(
            trans_times(lefts[12], rights[5]).astype(jnp.bfloat16),
            "seq",
            scatter_dimension=0,
            tiled=True,
        ).astype(jnp.float32),
    )
    vector_part = lax.psum_scatter(grad_vectors, ("seq", "wsh"), scatter_dimension=0, tiled=True)
    return (
        to_given(returned_rows[0]),
        to_given(returned_rows[1]),
        to_given(returned_rows[2]),
        weight_parts[0],
        weight_parts[1],
        weight_parts[2],
        weight_parts[3],
        weight_parts[4],
        weight_parts[5],
        weight_parts[6],
        weight_parts[7],
        vector_part,
    )


def solution(mesh):
    return jax.shard_map(
        local,
        mesh=mesh,
        in_specs=(
            P(("seq", "wsh"), None),
            P(("seq", "wsh"), None),
            P(("seq", "wsh"), None),
            P(("seq", "wsh")),
            P(("seq", "wsh")),
            P("wsh", None),
            P("wsh", None),
            P("wsh", None),
            P("wsh", None),
            P("wsh", None),
            P("wsh", None),
            P("wsh", None),
            P("wsh", None),
            P("wsh", None),
            P(),
        ),
        out_specs=(
            P(("seq", "wsh"), None),
            P(("seq", "wsh"), None),
            P(("seq", "wsh"), None),
            P(("seq", "wsh"), None),
            P(("seq", "wsh"), None),
            P(("seq", "wsh"), None),
            P(("seq", "wsh"), None),
            P(("seq", "wsh"), None),
            P(("seq", "wsh"), None),
            P(("seq", "wsh"), None),
            P(("seq", "wsh"), None),
            P(("seq", "wsh"), None),
        ),
        check_vma=False,
    )
```

profile of v0, /device:TPU:4, one launch (start us, length us, event | category | flops | bytes accessed | tf_op | source)
XLA Modules:
  0.0 2453.5 jit_solution(15702744446578761407)
XLA Ops:
  101.1 16.0 all-gather.15.cloned.1.call-done
  163.5 13.3 all-gather.9.cloned.1.call-done
  194.5 42.0 %all-gather.17.cloned.1.call-done = bf16[2048,2048]{1,0:T(8,128)(2,1)} async-done(((bf16[512,2048]{1,0:T(8,128)(2,1)}), bf16[2048,2048]{1,0:T(8,128)(2,1)}) %all-gather.17.cloned.1.call-update) | async-done | bytes 8388624 | tf_op jit(solution)/shard_map/all_gather | solution.py:268
  319.1 316.0 %custom-call.10 = f32[4,16,1,64,64]{3,4,2,1,0:T(8,128)} custom-call(f32[4,16,1,64,64]{4,3,2,1,0:T(8,128)} %add_bitcast_fusion), custom_call_target="InvertDiagBlocksLowerTriangular" | custom-call | tf_op jit(solution)/shard_map/jvp()/triangular_solve/custom-call.1 | solution.py:151
  715.2 16.7 pad.442
  861.6 18.5 multiply_convert_fusion
  880.1 17.2 fusion.198
  897.3 18.4 fusion.3
  915.7 17.2 multiply_reduce_fusion.1
  1063.7 16.7 pad.249
  1083.4 16.6 pad.250
  1196.1 16.6 pad.260
  1228.0 17.0 pad.259
  1310.4 13.1 fusion.19
  1392.2 12.2 fusion.168
  1624.8 16.1 all-to-all-done.31
  1646.2 12.0 all_to_all.541
  1666.2 25.8 %all-to-all-done.25 = bf16[128,1,4,2048]{3,0,1,2:T(8,128)(2,1)} async-done(((bf16[128,1,4,2048]{3,0,1,2:T(8,128)(2,1)}), bf16[128,1,4,2048]{3,0,1,2:T(8,128)(2,1)}, u32[]{:S(2)}, u32[]{:S(2)}) %all-to-all-start.25) | async-done | bytes 2097184 | tf_op jit(solution)/shard_map/all_to_all | solution.py:511
  1697.3 12.1 all_to_all.542
  1718.7 21.6 all-to-all-done.27
  1758.7 18.2 all-to-all-done.29
  1786.6 19.6 all-to-all-done.41
  1816.9 22.1 all-to-all-done.42
  1855.4 28.2 %all_to_all.543 = bf16[128,8,4,256]{3,1,0,2:T(8,128)(2,1)S(1)} all-to-all(bf16[128,8,4,256]{3,1,0,2:T(8,128)(2,1)S(1)} %copy.991), channel_id=1, replica_groups=mesh['seq'=8,'wsh'=4] {'wsh'}, dimensions={2} | all-to-all | bytes 4194304 | tf_op jit(solution)/shard_map/all_to_all | solution.py:510
  1893.7 21.8 all-to-all-done.44
  1937.8 16.5 all-to-all-done.23
  1959.9 12.9 all-to-all-done.11
  1983.9 15.3 all-to-all-done.22
  2007.9 61.8 %reduce-scatter.18.cloned.1.call-done = bf16[64,2048]{1,0:T(8,128)(2,1)} async-done(((bf16[512,2048]{1,0:T(8,128)(2,1)}), bf16[64,2048]{1,0:T(8,128)(2,1)}) %reduce-scatter.18.cloned.1.call-update) | async-done | bytes 262160 | tf_op jit(solution)/shard_map/reduce_scatter | solution.py:549
  2071.5 68.7 %reduce-scatter.20.cloned.1.call-done = bf16[64,2048]{1,0:T(8,128)(2,1)} async-done(((bf16[512,2048]{1,0:T(8,128)(2,1)}), bf16[64,2048]{1,0:T(8,128)(2,1)}) %reduce-scatter.20.cloned.1.call-update) | async-done | bytes 262160 | tf_op jit(solution)/shard_map/reduce_scatter | solution.py:555
  2142.0 150.2 %reduce-scatter.24.cloned.1.call-done = bf16[256,2048]{1,0:T(8,128)(2,1)} async-done(((bf16[2048,2048]{1,0:T(8,128)(2,1)}), bf16[256,2048]{1,0:T(8,128)(2,1)}) %reduce-scatter.24.cloned.1.call-update) | async-done | bytes 1048592 | tf_op jit(solution)/shard_map/reduce_scatter | solution.py:573
  2295.0 148.7 %reduce-scatter.26.cloned.1.call-done = bf16[256,2048]{1,0:T(8,128)(2,1)} async-done(((bf16[2048,2048]{1,0:T(8,128)(2,1)}), bf16[256,2048]{1,0:T(8,128)(2,1)}) %reduce-scatter.26.cloned.1.call-update) | async-done | bytes 1048592 | tf_op jit(solution)/shard_map/reduce_scatter | solution.py:579
  (1174 shorter events, 1193.9 us)
Async XLA Ops:
  7.2 78.3 %all-gather.11.cloned.1.call-start = ((), (), s32[]{:S(2)}) async-start(), calls=%async_computation.55 | async-start | bytes 2621440 | tf_op jit(solution)/shard_map/all_gather | solution.py:270
  7.9 80.1 %all-gather.13.cloned.1.call-start = ((), (), s32[]{:S(2)}) async-start(), calls=%async_computation.56 | async-start | bytes 2621440 | tf_op jit(solution)/shard_map/all_gather | solution.py:271
  8.7 108.4 %all-gather.15.cloned.1.call-start = ((), (), s32[]{:S(2)}) async-start(), calls=%async_computation.57 | async-start | bytes 10485760 | tf_op jit(solution)/shard_map/all_gather | solution.py:267
  9.4 167.4 %all-gather.9.cloned.1.call-start = ((), (), s32[]{:S(2)}) async-start(), calls=%async_computation.54 | async-start | bytes 10485760 | tf_op jit(solution)/shard_map/all_gather | solution.py:266
  10.0 226.5 %all-gather.17.cloned.1.call-start = ((), (), s32[]{:S(2)}) async-start(), calls=%async_computation.58 | async-start | bytes 10485760 | tf_op jit(solution)/shard_map/all_gather | solution.py:268
  10.6 835.0 %all-gather.19.cloned.1.call-start = ((), (), s32[]{:S(2)}) async-start(), calls=%async_computation.59 | async-start | bytes 10485760 | tf_op jit(solution)/shard_map/all_gather | solution.py:269
  11.2 850.5 %all-gather.21.cloned.1.call-start = ((), (), s32[]{:S(2)}) async-start(), calls=%async_computation.60 | async-start | bytes 41943040 | tf_op jit(solution)/shard_map/all_gather | solution.py:272
  11.9 868.2 %all-gather.23.cloned.1.call-start = ((), (), s32[]{:S(2)}) async-start(), calls=%async_computation.61 | async-start | bytes 41943040 | tf_op jit(solution)/shard_map/all_gather | solution.py:273
  92.0 41.1 %all-to-all-start.4 = ((bf16[128,8,256]{0,2,1:T(8,128)(2,1)}), bf16[128,8,256]{0,2,1:T(8,128)(2,1)}, u32[]{:S(2)}, u32[]{:S(2)}) async-start(bf16[128,8,256]{0,2,1:T(8,128)(2,1)} %bitcast.16), calls=%async_computation.4 | async-start | bytes 1048576 | tf_op jit(solution)/shard_map/all_to_all | solution.py:324
  153.8 32.3 %all-to-all-start.6 = ((bf16[128,8,256]{0,2,1:T(8,128)(2,1)}), bf16[128,8,256]{0,2,1:T(8,128)(2,1)}, u32[]{:S(2)}, u32[]{:S(2)}) async-start(bf16[128,8,256]{0,2,1:T(8,128)(2,1)} %bitcast.29), calls=%async_computation.6 | async-start | bytes 1048576 | tf_op jit(solution)/shard_map/all_to_all | solution.py:328
  186.1 61.2 %all-to-all-start.3 = ((bf16[128,8,256]{0,2,1:T(8,128)(2,1)}), bf16[128,8,256]{0,2,1:T(8,128)(2,1)}, u32[]{:S(2)}, u32[]{:S(2)}) async-start(bf16[128,8,256]{0,2,1:T(8,128)(2,1)} %bitcast.762), calls=%async_computation.3 | async-start | bytes 1048576 | tf_op jit(solution)/shard_map/all_to_all | solution.py:323
  247.3 33.1 %all-to-all-start.7 = ((bf16[128,8,256]{0,2,1:T(8,128)(2,1)}), bf16[128,8,256]{0,2,1:T(8,128)(2,1)S(1)}, u32[]{:S(2)}, u32[]{:S(2)}) async-start(bf16[128,8,256]{0,2,1:T(8,128)(2,1)} %bitcast.761), calls=%async_computation.7 | async-start | bytes 1048576 | tf_op jit(solution)/shard_map/all_to_all | solution.py:325
  280.4 354.6 %all-to-all-start.9 = ((bf16[128,8,256]{0,2,1:T(8,128)(2,1)}), bf16[128,8,256]{0,2,1:T(8,128)(2,1)}, u32[]{:S(2)}, u32[]{:S(2)}) async-start(bf16[128,8,256]{0,2,1:T(8,128)(2,1)} %bitcast.759), calls=%async_computation.9 | async-start | bytes 1048576 | tf_op jit(solution)/shard_map/all_to_all | solution.py:326
  636.3 130.2 %all-to-all-start.14 = ((s32[8,1,1]{2,1,0:T(1,128)}), s32[8,1,1]{2,1,0:T(1,128)}, u32[]{:S(2)}, u32[]{:S(2)}) async-start(s32[8,1,1]{2,1,0:T(1,128)} %broadcast_in_dim.96), calls=%async_computation.14 | async-start | bytes 8192 | tf_op jit(solution)/shard_map/all_to_all | solution.py:247
  786.9 32.6 %all-to-all-start.10 = ((bf16[8,128,256]{1,2,0:T(8,128)(2,1)}), bf16[8,128,256]{1,2,0:T(8,128)(2,1)}, u32[]{:S(2)}, u32[]{:S(2)}) async-start(bf16[8,128,256]{1,2,0:T(8,128)(2,1)} %copy.871), calls=%async_computation.10 | async-start | bytes 1048576 | tf_op jit(solution)/shard_map/all_to_all | solution.py:334
  819.5 37.3 %all-to-all-start.12 = ((bf16[8,16,2048]{2,1,0:T(8,128)(2,1)}), bf16[8,16,2048]{2,1,0:T(8,128)(2,1)S(1)}, u32[]{:S(2)}, u32[]{:S(2)}) async-start(bf16[8,16,2048]{2,1,0:T(8,128)(2,1)} %bitcast.753), calls=%async_computation.12 | async-start | bytes 1048576 | tf_op jit(solution)/shard_map/all_to_all | solution.py:243
  995.0 295.5 %all-to-all-start.28 = ((bf16[128,8,4,64]{0,3,1,2:T(8,128)(2,1)}), bf16[128,8,4,64]{0,3,1,2:T(8,128)(2,1)}, u32[]{:S(2)}, u32[]{:S(2)}) async-start(bf16[128,8,4,64]{0,3,1,2:T(8,128)(2,1)} %copy.963), calls=%async_computation.30 | async-start | bytes 1048576 | tf_op jit(solution)/shard_map/all_to_all | solution.py:500
  1497.4 45.5 %all-to-all-start.37 = ((bf16[128,1,4,512]{3,0,1,2:T(8,128)(2,1)}), bf16[128,1,4,512]{3,0,1,2:T(8,128)(2,1)}, u32[]{:S(2)}, u32[]{:S(2)}) async-start(bf16[128,1,4,512]{3,0,1,2:T(8,128)(2,1)} %broadcast_in_dim.114), calls=%async_computation.41 | async-start | bytes 1048576 | tf_op jit(solution)/shard_map/all_to_all | solution.py:518
  1573.2 405.8 %reduce-scatter.32.cloned.1.call-start = ((), (), s32[]{:S(2)}) async-start(), calls=%async_computation.70 | async-start | bytes 1081344
  1599.1 401.8 %reduce-scatter.28.cloned.1.call-start = ((), (), s32[]{:S(2)}) async-start(), calls=%async_computation.68 | async-start | bytes 589824
  1608.4 32.5 %all-to-all-start.31 = ((bf16[128,1,4,2048]{3,0,1,2:T(8,128)(2,1)}), bf16[128,1,4,2048]{3,0,1,2:T(8,128)(2,1)}, u32[]{:S(2)}, u32[]{:S(2)}) async-start(bf16[128,1,4,2048]{3,0,1,2:T(8,128)(2,1)} %broadcast_in_dim.112), calls=%async_computation.34 | async-start | bytes 4194304 | tf_op jit(solution)/shard_map/all_to_all | solution.py:514
  1614.9 387.7 %reduce-scatter.30.cloned.1.call-start = ((), (), s32[]{:S(2)}) async-start(), calls=%async_computation.69 | async-start | bytes 589824
  1624.4 380.0 %reduce-scatter.22.cloned.1.call-start = ((), (), s32[]{:S(2)}) async-start(), calls=%async_computation.65 | async-start | bytes 2359296 | tf_op jit(solution)/shard_map/reduce_scatter | solution.py:561
  1659.7 32.3 %all-to-all-start.25 = ((bf16[128,1,4,2048]{3,0,1,2:T(8,128)(2,1)}), bf16[128,1,4,2048]{3,0,1,2:T(8,128)(2,1)}, u32[]{:S(2)}, u32[]{:S(2)}) async-start(bf16[128,1,4,2048]{3,0,1,2:T(8,128)(2,1)} %broadcast_in_dim.109), calls=%async_computation.25 | async-start | bytes 4194304 | tf_op jit(solution)/shard_map/all_to_all | solution.py:511
  1665.8 340.3 %reduce-scatter.16.cloned.1.call-start = ((), (), s32[]{:S(2)}) async-start(), calls=%async_computation.62 | async-start | bytes 2359296 | tf_op jit(solution)/shard_map/reduce_scatter | solution.py:543
  1716.2 353.5 %reduce-scatter.18.cloned.1.call-start = ((), (), s32[]{:S(2)}) async-start(), calls=%async_computation.63 | async-start | bytes 2359296 | tf_op jit(solution)/shard_map/reduce_scatter | solution.py:549
  1746.6 30.3 %all-to-all-start.29 = ((bf16[128,1,4,2048]{3,0,1,2:T(8,128)(2,1)}), bf16[128,1,4,2048]{3,0,1,2:T(8,128)(2,1)}, u32[]{:S(2)}, u32[]{:S(2)}) async-start(bf16[128,1,4,2048]{3,0,1,2:T(8,128)(2,1)} %broadcast_in_dim.111), calls=%async_computation.31 | async-start | bytes 4194304 | tf_op jit(solution)/shard_map/all_to_all | solution.py:513
  1782.2 358.0 %reduce-scatter.20.cloned.1.call-start = ((), (), s32[]{:S(2)}) async-start(), calls=%async_computation.64 | async-start | bytes 2359296 | tf_op jit(solution)/shard_map/reduce_scatter | solution.py:555
  1808.9 30.2 %all-to-all-start.42 = ((bf16[128,1,4,2048]{3,0,1,2:T(8,128)(2,1)}), bf16[128,1,4,2048]{3,0,1,2:T(8,128)(2,1)}, u32[]{:S(2)}, u32[]{:S(2)}) async-start(bf16[128,1,4,2048]{3,0,1,2:T(8,128)(2,1)} %broadcast_in_dim.115), calls=%async_computation.46 | async-start | bytes 4194304 | tf_op jit(solution)/shard_map/all_to_all | solution.py:515
  1814.9 477.3 %reduce-scatter.24.cloned.1.call-start = ((), (), s32[]{:S(2)}) async-start(), calls=%async_computation.66 | async-start | bytes 9437184 | tf_op jit(solution)/shard_map/reduce_scatter | solution.py:573
  1885.3 30.2 %all-to-all-start.44 = ((bf16[128,1,4,2048]{3,0,1,2:T(8,128)(2,1)}), bf16[128,1,4,2048]{3,0,1,2:T(8,128)(2,1)}, u32[]{:S(2)}, u32[]{:S(2)}) async-start(bf16[128,1,4,2048]{3,0,1,2:T(8,128)(2,1)} %broadcast_in_dim.116), calls=%async_computation.49 | async-start | bytes 4194304 | tf_op jit(solution)/shard_map/all_to_all | solution.py:516
  1891.4 552.3 %reduce-scatter.26.cloned.1.call-start = ((), (), s32[]{:S(2)}) async-start(), calls=%async_computation.67 | async-start | bytes 9437184 | tf_op jit(solution)/shard_map/reduce_scatter | solution.py:579
  (319 other events, 7741.5 us)
Sparse Core Ops, SparseCore 0:
  9.6 22.6 all-gather.10
  33.8 22.6 all-gather.12
  58.1 58.9 all-gather.14
  118.5 58.2 all-gather.8
  178.2 58.2 all-gather.16
  237.9 58.2 all-gather.18
  297.8 201.7 all-gather.20
  501.1 201.4 all-gather.22
  1576.3 131.8 reduce-scatter.31
  1711.7 63.2 reduce-scatter.27
  1778.3 60.8 reduce-scatter.29
  1843.0 66.8 reduce-scatter.21
  1914.4 85.0 reduce-scatter.15
  2003.9 65.7 reduce-scatter.17
  2073.5 66.6 reduce-scatter.19
  2144.1 148.0 reduce-scatter.23
  2295.7 148.0 reduce-scatter.25
where the time goes:
time: 2480 us; the launch traced here: 2450 us
  waiting for transfers between devices  758 us (31%)
  local copies, waits for them, and re-layouts  481 us (19%)
  other arithmetic  475 us (19%)
  matrix products  431 us (17%)
  starting transfers between devices  231 us (9%)
  blocking collectives  57.4 us (2%)
    another operation x4, other arithmetic, block_recurrence(): lax.linalg.triangular_solve(system, pair_dot('hbij,hbjv->hbiv', pair_key,...  317 us
    dot_general x65, matrix products, pair_dot(): return jnp.einsum(form, left_side, right_side, precision=HIGH)  207 us
    pad x24, local copies, waits for them, and re-layouts, block_recurrence(): after_block = lax.associative_scan(chain_join, (transit, inject), axis=1)  173 us
    reduce_scatter x1, waiting for transfers between devices, local(): lax.psum_scatter(trans_times(lefts[11], rights[4]).astype(jnp.bfloat16),...  150 us
    reduce_scatter x1, waiting for transfers between devices, local(): lax.psum_scatter(trans_times(lefts[12], rights[5]).astype(jnp.bfloat16),...  149 us
    dot_general x14, matrix products, times_transposed(): lax.dot_general(left_side, right_side, (((1,), (1,)), ((), ())), preferre...  74.3 us
    dot_general x15, matrix products, product(): return jnp.dot(left_side, right_side, preferred_element_type=jnp.float32)  72 us
    reduce_scatter x1, waiting for transfers between devices, local(): lax.psum_scatter(trans_times(lefts[2], rights[2]).astype(jnp.bfloat16), '...  68.7 us
  transfers between devices with their start and end apart: 62, of which 31 were waited for; matrix products, arithmetic and copies ran while one was open for 52% of the time, Pallas kernels for 0%

commit v1 on v0

v1 whole, which is shorter than its diff:
```python
import functools

import jax
import jax.numpy as jnp
from jax import lax
from jax.experimental import pallas as pl
from jax.experimental.pallas import tpu as pltpu
from jax.sharding import PartitionSpec as P

HEAD = 64
BLOCK = 64
RANKS = (96, 96, 64, 256)
PADDED = (128, 128, 128, 256)
OFFSETS = (0, 128, 256, 384)
WIDE = 640
EXTRA = 128
DIGIT = 64

F32 = jnp.float32
BF16 = jnp.bfloat16

NN = (((1,), (0,)), ((), ()))
NT = (((1,), (1,)), ((), ()))
TN = (((0,), (0,)), ((), ()))


def dot(a, b, dims=NN):
    return lax.dot_general(a, b, dims, preferred_element_type=F32)


def halves(x):
    high = x.astype(BF16)
    return high, (x - high.astype(F32)).astype(BF16)


def dot3(a, b, dims=NN):
    a_high, a_low = halves(a)
    b_high, b_low = halves(b)
    return dot(a_high, b_high, dims) + (dot(a_high, b_low, dims) + dot(a_low, b_high, dims))


def sum_left(mask, x):
    high, low = halves(x)
    low_two = (x - high.astype(F32) - low.astype(F32)).astype(BF16)
    return dot(mask, high) + (dot(mask, low) + dot(mask, low_two))


def head_sum(x, ones):
    high, low = halves(x)
    return dot(high, ones) + dot(low, ones)


def low(x):
    return x.astype(BF16).astype(F32)


def iotas(rows, columns):
    return (
        lax.broadcasted_iota(jnp.int32, (rows, columns), 0),
        lax.broadcasted_iota(jnp.int32, (rows, columns), 1),
    )


def head_ones(width):
    i, j = iotas(width, width)
    return jnp.where((i >> 6) == (j >> 6), 1.0, 0.0).astype(BF16)


def front(keys, values, hidden, up, first, vec, ones):
    z = vec[0:1] + dot(hidden[:, 0:128], up[0:128])
    decay_log = -(jnp.maximum(-z, 0.0) + jnp.log1p(jnp.exp(-jnp.abs(z)))) - 0.5
    rate = jax.nn.sigmoid(vec[1:2] + dot(hidden[:, 128:256], up[128:256]))
    blend = jax.nn.sigmoid(vec[2:3] + dot(hidden[:, 256:384], up[256:384]))
    gate = dot(hidden[:, 384:640], up[384:640])
    mixed_value = values + (first - values) * blend
    scaled = keys * vec[3:4]
    scale = lax.rsqrt(head_sum(scaled * scaled, ones) + 1e-06)
    key_dir = scaled * scale
    key_mod = keys * (1.0 + (rate - 1.0) * vec[4:5])
    return z, decay_log, rate, blend, gate, mixed_value, scale, key_dir, key_mod


def block_masks(segments):
    i, j = iotas(BLOCK, BLOCK)
    across = jnp.broadcast_to(segments[0:1], (BLOCK, BLOCK))
    down = across.T
    before = jnp.broadcast_to(segments[1:2], (BLOCK, BLOCK))
    last = jnp.broadcast_to(segments[2:3], (BLOCK, BLOCK))
    same = across == down
    strict = jnp.where(same & (i > j), 1.0, 0.0)
    closed = jnp.where(same & (i >= j), 1.0, 0.0)
    carry = jnp.where(down == before, 1.0, 0.0)
    tail = jnp.where(down == last, 1.0, 0.0)
    keep = jnp.where(segments[2:3] == segments[1:2], 1.0, 0.0)
    quad = jnp.concatenate(
        [jnp.concatenate([strict, strict], 1), jnp.concatenate([closed, closed], 1)], 0
    )
    return quad, carry, tail, keep


def tile_heads(x, heads):
    return jnp.concatenate([x] * heads, 1) if heads > 1 else x


def join(pieces, axis):
    return jnp.concatenate(pieces, axis) if len(pieces) > 1 else pieces[0]


def decayed(decay_low, key_low, dir_low, rate_low, recept_low, carry, tail):
    i, j = iotas(BLOCK, BLOCK)
    lower = jnp.where(i >= j, 1.0, 0.0).astype(BF16)
    log_step = -jnp.exp(decay_low)
    total = sum_left(lower, log_step)
    before = jnp.exp(total - log_step)
    grown = jnp.exp(total)
    shrunk = jnp.exp(-total)
    end = total[BLOCK - 1 : BLOCK]
    tail_decay = jnp.exp(end - total) * tail
    alpha = -dir_low * before
    beta_plain = dir_low * rate_low
    beta = beta_plain * shrunk
    key = key_low * shrunk
    recept = recept_low * grown
    return dict(
        log_step=log_step, before=before, grown=grown, shrunk=shrunk, end=jnp.exp(end), tail=tail_decay,
        alpha=alpha, beta_plain=beta_plain, beta=beta, key=key, recept=recept,
        beta_end=beta_plain * tail_decay, key_end=key_low * tail_decay,
        alpha_in=alpha * carry, recept_in=recept * carry,
    )


def unit_inverse(lower_part):
    i, j = iotas(BLOCK, BLOCK)

    def within(size):
        return (i // size) == (j // size)

    small = jnp.where(within(8), lower_part, 0.0)
    two = dot3(small, small)
    four = dot3(two, two)
    inverse = jnp.where(i == j, 1.0, 0.0) + small
    inverse = inverse + dot3(inverse, two)
    inverse = inverse + dot3(inverse, four)
    for size in (16, 32, 64):
        off = jnp.where(within(size) & ~within(size // 2), lower_part, 0.0)
        inverse = inverse + dot3(inverse, dot3(off, inverse))
    return inverse


def post_norm(head_low, ones):
    centered = head_low - head_sum(head_low, ones) * (1.0 / HEAD)
    spread = lax.rsqrt(head_sum(centered * centered, ones) * (1.0 / HEAD) + HEAD * 1e-05)
    return centered * spread, spread


def forward_kernel(
    count, recept_ref, keys_ref, values_ref, hidden_ref, first_ref, up_ref, vec_ref, segment_ref,
    mixed_ref, head_ref, state_ref, inverse_ref, removed_ref, state,
):
    width = recept_ref.shape[1]
    heads = width // HEAD

    @pl.when(pl.program_id(0) == 0)
    def _():
        state[...] = jnp.zeros_like(state)

    ones = head_ones(width)
    vec = vec_ref[...]
    up = up_ref[...]
    for block in range(count):
        rows = slice(block * BLOCK, (block + 1) * BLOCK)
        recept, keys, values = recept_ref[rows], keys_ref[rows], values_ref[rows]
        _, decay_log, rate, _, gate, mixed_value, _, key_dir, key_mod = front(
            keys, values, hidden_ref[rows], up, first_ref[rows].astype(F32), vec, ones
        )
        quad, carry, tail, keep = block_masks(segment_ref[block * 8 : block * 8 + 8])
        parts = decayed(
            low(decay_log), low(key_mod), low(key_dir), low(rate), low(recept),
            tile_heads(carry, heads), tile_heads(tail, heads),
        )
        value_low = low(mixed_value)
        entering = state[...]
        state_ref[rows] = entering
        leaving, outs, inverses, removals = [], [], [], []
        for head in range(heads):
            cols = slice(head * HEAD, (head + 1) * HEAD)
            own = value_low[:, cols]
            now = entering[:, cols]
            pairs = quad * dot3(
                jnp.concatenate([parts["alpha"][:, cols], parts["recept"][:, cols]], 0),
                jnp.concatenate([parts["beta"][:, cols], parts["key"][:, cols]], 0),
                NT,
            )
            inverse = unit_inverse(pairs[:BLOCK, :BLOCK])
            inward = dot3(
                jnp.concatenate([parts["alpha_in"][:, cols], parts["recept_in"][:, cols]], 0), now, NT
            )
            by_value = dot3(pairs[:, BLOCK:], own)
            removed = dot3(inverse, inward[:BLOCK] + by_value[:BLOCK])
            outs.append(inward[BLOCK:] + by_value[BLOCK:] + dot3(pairs[BLOCK:, :BLOCK], removed))
            leaving.append(
                now * (parts["end"][:, cols] * keep)
                + dot3(
                    jnp.concatenate([removed, own], 0),
                    jnp.concatenate([parts["beta_end"][:, cols], parts["key_end"][:, cols]], 0),
                    TN,
                )
            )
            inverses.append(inverse)
            removals.append(removed)
        state[...] = join(leaving, 1)
        inverse_ref[rows] = join(inverses, 1)
        removed_ref[rows] = join(removals, 1)
        head_low = join(outs, 1).astype(BF16)
        head_ref[rows] = head_low
        normed, _ = post_norm(head_low.astype(F32), ones)
        bonus = head_sum(recept * key_mod * vec[5:6], ones) * mixed_value
        mixed_ref[rows] = ((normed * vec[6:7] + vec[7:8] + bonus) * gate).astype(BF16)


def backward_kernel(
    count, grad_ref, recept_ref, keys_ref, values_ref, hidden_ref, first_ref, up_ref, vec_ref, segment_ref,
    head_ref, state_ref, inverse_ref, removed_ref,
    recept_out, keys_out, values_out, ups_out, first_out, vec_out, state,
):
    width = recept_ref.shape[1]
    heads = width // HEAD

    @pl.when(pl.program_id(0) == 0)
    def _():
        state[...] = jnp.zeros_like(state)
        vec_out[...] = jnp.zeros_like(vec_out)

    ones = head_ones(width)
    vec = vec_ref[...]
    up = up_ref[...]
    i, j = iotas(BLOCK, BLOCK)
    upper = jnp.where(i <= j, 1.0, 0.0).astype(BF16)
    for block in range(count - 1, -1, -1):
        rows = slice(block * BLOCK, (block + 1) * BLOCK)
        recept, keys, values = recept_ref[rows], keys_ref[rows], values_ref[rows]
        first = first_ref[rows].astype(F32)
        z, decay_log, rate, blend, gate, mixed_value, scale, key_dir, key_mod = front(
            keys, values, hidden_ref[rows], up, first, vec, ones
        )
        quad, carry, tail, keep = block_masks(segment_ref[block * 8 : block * 8 + 8])
        carry_wide = tile_heads(carry, heads)
        rate_low, dir_low = low(rate), low(key_dir)
        parts = decayed(
            low(decay_log), low(key_mod), dir_low, rate_low, low(recept), carry_wide, tile_heads(tail, heads)
        )
        value_low = low(mixed_value)

        grad = grad_ref[rows].astype(F32)
        normed, spread = post_norm(head_ref[rows].astype(F32), ones)
        product = recept * key_mod
        coefficient = head_sum(product * vec[5:6], ones)
        grad_gate = grad * (normed * vec[6:7] + vec[7:8] + coefficient * mixed_value)
        opened = grad * gate
        grad_normed = opened * vec[6:7]
        grad_head = spread * (
            grad_normed
            - head_sum(grad_normed, ones) * (1.0 / HEAD)
            - normed * (head_sum(grad_normed * normed, ones) * (1.0 / HEAD))
        )
        grad_coefficient = head_sum(opened * mixed_value, ones)
        grad_mixed_value = opened * coefficient
        weighted = grad_coefficient * vec[5:6]
        grad_recept = weighted * key_mod
        grad_key_mod = weighted * recept
        head_grad = low(grad_head)

        entering, removed_all, inverse_all = state_ref[rows], removed_ref[rows], inverse_ref[rows]
        after = state[...]
        leaving, g_alpha, g_recept, g_beta, g_key, g_beta_end, g_key_end, g_value, g_end = (
            [], [], [], [], [], [], [], [], [],
        )
        for head in range(heads):
            cols = slice(head * HEAD, (head + 1) * HEAD)
            own, now, later = value_low[:, cols], entering[:, cols], after[:, cols]
            removed, inverse, out_grad = removed_all[:, cols], inverse_all[:, cols], head_grad[:, cols]
            left = jnp.concatenate([parts["alpha"][:, cols], parts["recept"][:, cols]], 0)
            right = jnp.concatenate([parts["beta"][:, cols], parts["key"][:, cols]], 0)
            ends = jnp.concatenate([parts["beta_end"][:, cols], parts["key_end"][:, cols]], 0)
            pairs = quad * dot3(left, right, NT)
            from_end = dot3(ends, later, NT)
            grad_removed = dot3(pairs[BLOCK:, :BLOCK], out_grad, TN) + from_end[:BLOCK]
            grad_inner = dot3(inverse, grad_removed, TN)
            both = jnp.concatenate([grad_inner, out_grad], 0)
            sources = jnp.concatenate([removed, own], 0)
            grad_pairs = quad * dot3(both, sources, NT)
            carry_two = jnp.concatenate([carry, carry], 0)
            grad_left = dot3(grad_pairs, right) + carry_two * dot3(both, now)
            grad_right = dot3(grad_pairs, left, TN)
            grad_ends = dot3(sources, later)
            g_value.append(dot3(pairs[:, BLOCK:], both, TN) + from_end[BLOCK:])
            kept = later * (parts["end"][:, cols] * keep)
            leaving.append(kept + dot3(both, carry_two * left, TN))
            g_end.append(jnp.sum(now * kept, 0, keepdims=True))
            g_alpha.append(grad_left[:BLOCK])
            g_recept.append(grad_left[BLOCK:])
            g_beta.append(grad_right[:BLOCK])
            g_key.append(grad_right[BLOCK:])
            g_beta_end.append(grad_ends[:BLOCK])
            g_key_end.append(grad_ends[BLOCK:])
        state[...] = join(leaving, 1)
        d_alpha, d_recept, d_beta, d_key = join(g_alpha, 1), join(g_recept, 1), join(g_beta, 1), join(g_key, 1)
        d_beta_end, d_key_end = join(g_beta_end, 1), join(g_key_end, 1)
        ended = parts["beta_end"] * d_beta_end + parts["key_end"] * d_key_end
        alphas = parts["alpha"] * d_alpha
        d_total = parts["recept"] * d_recept - parts["beta"] * d_beta - parts["key"] * d_key - ended + alphas
        d_step = sum_left(upper, d_total) + (jnp.sum(ended, 0, keepdims=True) + join(g_end, 1)) - alphas
        d_beta_plain = d_beta * parts["shrunk"] + d_beta_end * parts["tail"]
        copy_recept = low(d_recept * parts["grown"])
        copy_decay = low(d_step * parts["log_step"])
        copy_key = low(d_key * parts["shrunk"] + d_key_end * parts["tail"])
        copy_value = low(join(g_value, 1))
        copy_dir = low(d_beta_plain * rate_low - d_alpha * parts["before"])
        copy_rate = low(d_beta_plain * dir_low)

        grad_recept = grad_recept + copy_recept
        grad_key_mod = grad_key_mod + copy_key
        grad_mixed_value = grad_mixed_value + copy_value
        grad_z = copy_decay * jax.nn.sigmoid(-z)
        factor = 1.0 + (rate - 1.0) * vec[4:5]
        keyed = grad_key_mod * keys
        grad_rate = copy_rate + keyed * vec[4:5]
        grad_scaled = scale * (copy_dir - key_dir * head_sum(copy_dir * key_dir, ones))
        grad_keys = grad_key_mod * factor + grad_scaled * vec[3:4]
        grad_rate_up = grad_rate * rate * (1.0 - rate)
        grad_blend = grad_mixed_value * (first - values)
        grad_value_up = grad_blend * blend * (1.0 - blend)
        recept_out[rows] = grad_recept.astype(BF16)
        keys_out[rows] = grad_keys.astype(BF16)
        values_out[rows] = (grad_mixed_value * (1.0 - blend)).astype(BF16)
        first_out[rows] = (grad_mixed_value * blend).astype(BF16)
        ups_out[0, rows] = grad_z.astype(BF16)
        ups_out[1, rows] = grad_rate_up.astype(BF16)
        ups_out[2, rows] = grad_value_up.astype(BF16)
        ups_out[3, rows] = grad_gate.astype(BF16)

        def total(x):
            return jnp.sum(x, 0, keepdims=True)

        vec_out[...] += jnp.concatenate(
            [
                total(grad_z), total(grad_rate_up), total(grad_value_up), total(grad_scaled * keys),
                total(keyed * (rate - 1.0)), total(grad_coefficient * product),
                total(opened * normed), total(opened),
            ],
            0,
        )


def per_step(rows):
    return 2 if (rows // BLOCK) % 2 == 0 else 1


def run_forward(recept, keys, values, hidden, first, up, vec, segments):
    rows, width = recept.shape
    count = per_step(rows)
    step = count * BLOCK

    def spec(columns):
        return pl.BlockSpec((step, columns), lambda i: (i, 0))

    def whole(array):
        return pl.BlockSpec(array.shape, lambda i: (0, 0))

    return pl.pallas_call(
        functools.partial(forward_kernel, count),
        grid=(rows // step,),
        in_specs=[
            spec(width), spec(width), spec(width), spec(WIDE), spec(width), whole(up), whole(vec),
            pl.BlockSpec((count * 8, BLOCK), lambda i: (i, 0)),
        ],
        out_specs=[spec(width)] * 5,
        out_shape=[jax.ShapeDtypeStruct((rows, width), d) for d in (BF16, BF16, F32, F32, F32)],
        scratch_shapes=[pltpu.VMEM((BLOCK, width), F32)],
        compiler_params=pltpu.CompilerParams(vmem_limit_bytes=48 << 20),
        name="mix_forward",
    )(recept, keys, values, hidden, first, up, vec, segments)


def run_backward(grad, recept, keys, values, hidden, first, up, vec, segments, saved):
    rows, width = recept.shape
    count = per_step(rows)
    step = count * BLOCK
    last = rows // step - 1

    def spec(columns):
        return pl.BlockSpec((step, columns), lambda i: (last - i, 0))

    def whole(array):
        return pl.BlockSpec(array.shape, lambda i: (0, 0))

    return pl.pallas_call(
        functools.partial(backward_kernel, count),
        grid=(rows // step,),
        in_specs=[
            spec(width), spec(width), spec(width), spec(width), spec(WIDE), spec(width), whole(up), whole(vec),
            pl.BlockSpec((count * 8, BLOCK), lambda i: (last - i, 0)),
            spec(width), spec(width), spec(width), spec(width),
        ],
        out_specs=[
            spec(width), spec(width), spec(width),
            pl.BlockSpec((4, step, width), lambda i: (0, last - i, 0)),
            spec(width), pl.BlockSpec((8, width), lambda i: (0, 0)),
        ],
        out_shape=[
            jax.ShapeDtypeStruct((rows, width), BF16), jax.ShapeDtypeStruct((rows, width), BF16),
            jax.ShapeDtypeStruct((rows, width), BF16), jax.ShapeDtypeStruct((4, rows, width), BF16),
            jax.ShapeDtypeStruct((rows, width), BF16), jax.ShapeDtypeStruct((8, width), F32),
        ],
        scratch_shapes=[pltpu.VMEM((BLOCK, width), F32)],
        compiler_params=pltpu.CompilerParams(vmem_limit_bytes=48 << 20),
        name="mix_backward",
    )(grad, recept, keys, values, hidden, first, up, vec, segments, *saved)


def norm_stats(values):
    centered = values - jnp.mean(values, -1, keepdims=True)
    scale = lax.rsqrt(jnp.mean(centered * centered, -1, keepdims=True) + 1e-05)
    return centered * scale, scale


def norm_back(grad, standard, scale, gain):
    scaled = grad * gain
    return scale * (
        scaled
        - jnp.mean(scaled, -1, keepdims=True)
        - standard * jnp.mean(scaled * standard, -1, keepdims=True)
    )


def pad_ranks(matrix):
    pieces, start = [], 0
    for rank, padded in zip(RANKS, PADDED):
        pieces.append(jnp.pad(matrix[:, start : start + rank], ((0, 0), (0, padded - rank))))
        start += rank
    return jnp.concatenate(pieces, 1)


def unpad_ranks(matrix):
    return jnp.concatenate([matrix[..., o : o + r] for o, r in zip(OFFSETS, RANKS)], -1)


def from_behind(x, axis, by):
    size = lax.axis_size(axis)
    pairs = [(i, i + by) for i in range(size) if 0 <= i + by < size]
    return lax.ppermute(x, axis, pairs)


def exchange(x, axis):
    return lax.all_to_all(x, axis, split_axis=0, concat_axis=0, tiled=True)


def local(
    tokens, first_layer_values, teacher, valid, destination, lengths,
    receptance_matrix, key_matrix, value_matrix, output_matrix,
    lowrank_down_weight, lowrank_up_weight, channel_key_weight, channel_value_weight, vectors,
):
    rows, width = tokens.shape
    seqs, parts = lax.axis_size("seq"), lax.axis_size("wsh")
    me = lax.axis_index("seq")
    group = rows * seqs
    own_width = width // seqs
    shard = width // parts
    piece = shard // seqs
    column = me * own_width

    dest_seq = destination // rows // parts
    position = dest_seq * rows + destination % rows
    digits = jnp.stack([position // DIGIT, position % DIGIT, valid], 1).astype(BF16)
    tail = jnp.pad(digits, ((0, 0), (0, EXTRA - 3)))
    given = lax.all_gather(jnp.concatenate([tokens, tail], 1), "seq", axis=0, tiled=True)
    info = given[:, width : width + 3].astype(F32)
    places = (info[:, 0] * DIGIT + info[:, 1]).astype(jnp.int32)
    numbers = jnp.arange(group, dtype=jnp.int32)
    permute = (numbers[:, None] == places[None, :]).astype(BF16)
    total_valid = jnp.sum(lax.all_gather(jnp.sum(info[:, 2]).reshape(1), "wsh", axis=0, tiled=True))

    index = jnp.arange(rows, dtype=jnp.int32)
    same_dest = (dest_seq[:, None] == dest_seq[None, :]) & (index[None, :] < index[:, None])
    slot = dest_seq * (rows // seqs) + jnp.sum(same_dest.astype(jnp.int32), 1)
    arrange = (index[:, None] == slot[None, :]).astype(BF16)
    mine = (places // rows) == me
    arrival = jnp.cumsum(mine.astype(jnp.int32)) - 1
    own_rows = ((index[:, None] + me * rows) == places[None, :]).astype(BF16)
    settle = dot(own_rows, (mine[:, None] & (arrival[:, None] == index[None, :])).astype(BF16)).astype(BF16)

    def deal(array):
        moved = exchange(dot(arrange, array).astype(BF16).reshape(seqs, rows // seqs, width), "seq")
        return dot(settle, moved.reshape(rows, width))

    def undeal(array):
        back = dot(settle, array.astype(BF16), TN).astype(BF16)
        moved = exchange(back.reshape(seqs, rows // seqs, width), "seq")
        return dot(arrange, moved.reshape(rows, width), TN).astype(BF16)

    target = deal(teacher)
    first_given = exchange(
        first_layer_values.reshape(rows, seqs, own_width).transpose(1, 0, 2), "seq"
    ).reshape(group, own_width)
    first = dot(permute, first_given).astype(BF16)

    offsets = jnp.cumsum(lengths[0]) - lengths[0]
    starts = jnp.any(numbers[:, None] == offsets[None, :], 1).astype(F32)
    segment_ids = jnp.cumsum(starts).reshape(-1, BLOCK)
    before = segment_ids[:, :1] - starts.reshape(-1, BLOCK)[:, :1]
    segments = jnp.stack(
        [segment_ids, jnp.broadcast_to(before, segment_ids.shape), jnp.broadcast_to(segment_ids[:, -1:], segment_ids.shape)]
        + [jnp.zeros_like(segment_ids)] * 5,
        1,
    ).reshape(-1, BLOCK)
    flowing = (1.0 - starts)[:, None]

    def own_columns(matrix):
        return lax.dynamic_slice_in_dim(matrix, column, own_width, 1)

    weights = lax.all_gather(
        jnp.concatenate(
            [own_columns(receptance_matrix), own_columns(key_matrix), own_columns(value_matrix), pad_ranks(lowrank_down_weight)], 1
        ),
        "wsh", axis=0, tiled=True,
    )
    w_recept, w_key = weights[:, :own_width], weights[:, own_width : 2 * own_width]
    w_value, down = weights[:, 2 * own_width : 3 * own_width], weights[:, 3 * own_width :]
    up_piece = lax.dynamic_slice_in_dim(lowrank_up_weight, column % shard, own_width, 0)
    ups = lax.all_gather(up_piece, "wsh", axis=0, tiled=False)
    up = pad_ranks(lax.dynamic_index_in_dim(ups, column // shard, 0, keepdims=False))
    w_out = lax.all_gather(output_matrix, "wsh", axis=0, tiled=True)
    vec = lax.dynamic_slice_in_dim(vectors, column, own_width, 0)[:, 8:16].T

    balanced = dot(permute, given[:, :width])
    standard, scale_one = norm_stats(balanced)
    normed = standard * vectors[:, 0] + vectors[:, 1]
    previous = jnp.concatenate([jnp.zeros_like(normed[:1]), normed[:-1]], 0) * flowing
    delta = previous - normed
    mixed = [(normed + delta * vectors[:, 2 + c]).astype(BF16) for c in range(6)]
    recept = dot(mixed[0], w_recept)
    keys = dot(mixed[2], w_key)
    values = dot(mixed[3], w_value)
    downs = [dot(mixed[c], down[:, o : o + n]) for c, o, n in zip((1, 4, 3, 5), OFFSETS, PADDED)]
    decay_tanh, gate_sigmoid = jnp.tanh(downs[0]), jax.nn.sigmoid(downs[3])
    hidden = jnp.concatenate(
        [decay_tanh.astype(BF16), downs[1].astype(BF16), downs[2].astype(BF16), gate_sigmoid.astype(BF16)], 1
    )
    inputs = (recept, keys, values, hidden, first, up.T, vec, segments)
    mixed_out, *saved = run_forward(*inputs)

    mixed_rows = exchange(mixed_out.reshape(seqs, rows, own_width), "seq").transpose(1, 0, 2).reshape(rows, width)
    own = lax.dynamic_slice_in_dim(balanced, me * rows, rows, 0)
    own_starts = lax.dynamic_slice_in_dim(starts, me * rows, rows, 0)
    own_flowing = (1.0 - own_starts)[:, None]
    own_valid = dot(own_rows, given[:, width : width + EXTRA])[:, 2]
    residual = own + dot(mixed_rows, w_out)
    standard_two, scale_two = norm_stats(residual)
    normed_two = standard_two * vectors[:, 16] + vectors[:, 17]
    carried_two = from_behind(normed_two[-1:], "seq", 1)
    delta_two = jnp.concatenate([carried_two, normed_two[:-1]], 0) * own_flowing - normed_two
    channel = lax.all_gather(
        (normed_two + delta_two * vectors[:, 18]).astype(BF16), "wsh", axis=0, tiled=True
    )
    active = jax.nn.relu(dot(channel, channel_key_weight, NT))
    hidden_rows = jnp.square(active).astype(BF16)
    result = residual + lax.psum_scatter(
        dot(hidden_rows, channel_value_weight), "wsh", scatter_dimension=0, tiled=True
    )
    total_tokens = group * parts
    cotangent = (result - target) * (own_valid * (total_tokens / total_valid))[:, None]
    cot = lax.all_gather(cotangent.astype(BF16), "wsh", axis=0, tiled=True)

    grad_pre = (dot(cot, channel_value_weight, NT) * 2.0 * active).astype(BF16)
    grad_channel = lax.psum_scatter(dot(grad_pre, channel_key_weight), "wsh", scatter_dimension=0, tiled=True)
    blocks = [(s * parts + w, w * seqs + s) for s in range(seqs) for w in range(parts)]

    def ffn_grad(left, right):
        part = lax.psum_scatter(dot(left, right, TN).astype(BF16), "seq", scatter_dimension=0, tiled=True)
        return lax.ppermute(part, ("seq", "wsh"), blocks).astype(F32)

    grad_ffn_value = ffn_grad(hidden_rows, cot)
    grad_ffn_key = ffn_grad(grad_pre, channel)
    grad_vec_mix_two = jnp.sum(grad_channel * delta_two, 0)
    shifted = grad_channel * vectors[:, 18] * own_flowing
    behind = from_behind(shifted[:1], "seq", -1)
    grad_normed_two = grad_channel * (1.0 - vectors[:, 18]) + jnp.concatenate([shifted[1:], behind], 0)
    grad_residual = cotangent + norm_back(grad_normed_two, standard_two, scale_two, vectors[:, 16])
    grad_low = grad_residual.astype(BF16)

    grad_posted = dot(grad_low, w_out, NT).astype(BF16)
    grad_heads = exchange(grad_posted.reshape(rows, seqs, own_width).transpose(1, 0, 2), "seq").reshape(group, own_width)
    recept_low, keys_low, values_low, ups_low, grad_first, grad_vec_heads = run_backward(grad_heads, *inputs, saved)
    grad_low_all = lax.all_gather(grad_low, "seq", axis=0, tiled=True)
    hid = [dot(ups_low[k], up[:, o : o + n]) for k, (o, n) in enumerate(zip(OFFSETS, PADDED))]
    down_lows = [
        (hid[0] * (1.0 - jnp.square(decay_tanh))).astype(BF16),
        hid[1].astype(BF16),
        hid[2].astype(BF16),
        (hid[3] * gate_sigmoid * (1.0 - gate_sigmoid)).astype(BF16),
    ]
    down_cols = [down[:, o : o + n] for o, n in zip(OFFSETS, PADDED)]
    grad_mix = [
        dot(recept_low, w_recept, NT),
        dot(down_lows[0], down_cols[0], NT),
        dot(keys_low, w_key, NT),
        dot(values_low, w_value, NT) + dot(down_lows[2], down_cols[2], NT),
        dot(down_lows[1], down_cols[1], NT),
        dot(down_lows[3], down_cols[3], NT),
    ]
    grad_vec_mix = [jnp.sum(g * delta, 0) for g in grad_mix]
    kept = sum(g * (1.0 - vectors[:, 2 + c]) for c, g in enumerate(grad_mix))
    sent = sum(g * vectors[:, 2 + c] for c, g in enumerate(grad_mix)) * flowing
    grad_normed = kept + jnp.concatenate([sent[1:], jnp.zeros_like(sent[:1])], 0)
    grad_vec_one = [jnp.sum(grad_normed * standard, 0), jnp.sum(grad_normed, 0)]
    grad_balanced = norm_back(grad_normed, standard, scale_one, vectors[:, 0])
    mine_rows = lax.dynamic_slice_in_dim(grad_balanced, me * rows, rows, 0) + grad_residual
    grad_balanced = lax.dynamic_update_slice_in_dim(grad_balanced, mine_rows, me * rows, 0)
    grad_given = dot(permute, grad_balanced.astype(BF16), TN).astype(BF16)
    grad_tokens = lax.psum_scatter(grad_given, "seq", scatter_dimension=0, tiled=True)
    first_back = exchange(dot(permute, grad_first, TN).astype(BF16).reshape(seqs, rows, own_width), "seq")
    grad_first_rows = first_back.transpose(1, 0, 2).reshape(rows, width)

    wide = jnp.concatenate(
        [dot(mixed[0], recept_low, TN), dot(mixed[2], keys_low, TN), dot(mixed[3], values_low, TN)]
        + [dot(mixed[c], l, TN)[:, :r] for c, l, r in zip((1, 4, 3, 5), down_lows, RANKS)],
        1,
    ).astype(BF16)
    ordered = wide.reshape(seqs, parts, piece, -1).transpose(1, 0, 2, 3).reshape(parts * seqs * piece, -1)
    wide_part = lax.psum_scatter(ordered, "wsh", scatter_dimension=0, tiled=True)
    wide_all = exchange(wide_part.reshape(seqs, piece, -1), "seq").astype(F32)

    def square(number):
        taken = wide_all[:, :, number * own_width : (number + 1) * own_width]
        return taken.transpose(1, 0, 2).reshape(piece, width)

    grad_down = jnp.sum(wide_all[:, :, 3 * own_width :], 0)
    tall = jnp.concatenate(
        [dot(mixed_out, grad_low_all, TN)]
        + [dot(ups_low[k], hidden[:, o : o + r], TN) for k, (o, r) in enumerate(zip(OFFSETS, RANKS))],
        1,
    ).astype(BF16)
    tall_part = lax.psum_scatter(tall, "wsh", scatter_dimension=0, tiled=True).astype(F32)

    heads_part = lax.dynamic_update_slice_in_dim(jnp.zeros((width, 8), F32), grad_vec_heads.T, column, 0)
    grad_vectors = jnp.concatenate(
        [
            jnp.stack(grad_vec_one + grad_vec_mix, 1),
            heads_part,
            jnp.stack([jnp.sum(grad_normed_two * standard_two, 0), jnp.sum(grad_normed_two, 0), grad_vec_mix_two], 1),
        ],
        1,
    )
    vec_part = jnp.sum(exchange(grad_vectors.reshape(seqs, parts * piece, -1), "seq"), 0)
    vec_part = jnp.sum(exchange(vec_part.reshape(parts, piece, -1), "wsh"), 0)
    return (
        undeal(result), grad_tokens, grad_first_rows,
        square(0), square(1), square(2),
        tall_part[:, :width], grad_down, tall_part[:, width:],
        grad_ffn_key, grad_ffn_value, vec_part,
    )


def solution(mesh):
    both, shard = P(("seq", "wsh"), None), P("wsh", None)
    flat = P(("seq", "wsh"))
    return jax.shard_map(
        local,
        mesh=mesh,
        in_specs=(both, both, both, flat, flat) + (shard,) * 9 + (P(),),
        out_specs=(both,) * 12,
        check_vma=False,
    )
```

time: 2480 us -> 1260 us (0.51)
  local copies, waits for them, and re-layouts: 481 us -> 67.7 us
  other arithmetic: 475 us -> 119 us
  matrix products: 431 us -> 172 us
  waiting for transfers between devices: 758 us -> 549 us
  Pallas kernels: 0 us -> 207 us
  starting transfers between devices: 231 us -> 45.5 us
    another operation x10, other arithmetic: 325 us -> 2.82 us  [the longest x3 1.89 us: local(): jnp.stack([position // DIGIT, position % DIGIT, valid], 1).astype(BF16)]
    dot_general x110 -> x48, matrix products: 408 us -> 172 us  [dot(): return lax.dot_general(a, b, dims, preferred_element_type=F32)]
    pallas_call x0 -> x2, Pallas kernels: none -> 207 us  [the longest x1 129 us: run_forward(): pl.pallas_call(functools.partial(forward_kernel, count), grid=(rows // st...]
    all_to_all x42 -> x7, waiting for transfers between devices: 248 us -> 46.4 us  [exchange(): return lax.all_to_all(x, axis, split_axis=0, concat_axis=0, tiled=True)]
    all_to_all x42 -> x7, starting transfers between devices: 223 us -> 32.4 us  [exchange(): return lax.all_to_all(x, axis, split_axis=0, concat_axis=0, tiled=True)]
    pad x24 -> x2, local copies, waits for them, and re-layouts: 173 us -> 0.01 us  [pad_ranks(): jnp.pad(matrix[:, start:start + rank], ((0, 0), (0, padded - rank)))]
    convert_element_type x47 -> x1, local copies, waits for them, and re-layouts: 64.4 us -> 0.08 us  [local(): starts = jnp.any(numbers[:, None] == offsets[None, :], 1).astype(F32)]
    reduce_scatter x6 -> x7, waiting for transfers between devices: 429 us -> 368 us  [the longest x2 211 us: ffn_grad(): lax.psum_scatter(dot(left, right, TN).astype(BF16), 'seq', scatter_dimens...]
  transfers between devices with their start and end apart: 62 -> 25, of which waited for: 31 -> 19; matrix products, arithmetic and copies ran while one was open for 52% -> 23% of each run, Pallas kernels for 0% -> 17%
where the time goes in v1:
time: 1260 us; the launch traced here: 1250 us
  waiting for transfers between devices  549 us (44%)
  Pallas kernels  207 us (16%)
  matrix products  172 us (14%)
  other arithmetic  119 us (9%)
  blocking collectives  74.9 us (6%)
  local copies, waits for them, and re-layouts  67.7 us (5%)
  starting transfers between devices  45.5 us (4%)
  between operations  16.8 us (1%)
    reduce_scatter x2, waiting for transfers between devices, ffn_grad(): lax.psum_scatter(dot(left, right, TN).astype(BF16), 'seq', scatter_dimens...  211 us
    dot_general x48, matrix products, dot(): return lax.dot_general(a, b, dims, preferred_element_type=F32)  172 us
    pallas_call x1, Pallas kernels, run_forward(): pl.pallas_call(functools.partial(forward_kernel, count), grid=(rows // st...  129 us
    reduce_scatter x1, waiting for transfers between devices, local(): lax.psum_scatter(grad_given, 'seq', scatter_dimension=0, tiled=True)  85.4 us
    pallas_call x1, Pallas kernels, run_backward(): pl.pallas_call(functools.partial(backward_kernel, count), grid=(rows // s...  77.7 us
    all_to_all x2, blocking collectives, exchange(): return lax.all_to_all(x, axis, split_axis=0, concat_axis=0, tiled=True)  67.9 us
    all_gather x1, waiting for transfers between devices, local(): lax.all_gather(jnp.concatenate([tokens, tail], 1), 'seq', axis=0, tiled=T...  61.6 us
    all_to_all x7, waiting for transfers between devices, exchange(): return lax.all_to_all(x, axis, split_axis=0, concat_axis=0, tiled=True)  46.4 us
  transfers between devices with their start and end apart: 25, of which 19 were waited for; matrix products, arithmetic and copies ran while one was open for 23% of the time, Pallas kernels for 17%

profile of v1, /device:TPU:4, one launch (start us, length us, event | category | flops | bytes accessed | tf_op | source)
XLA Modules:
  0.0 1251.2 jit_solution(8882148554491906615)
XLA Ops:
  31.8 11.5 all-to-all-done
  46.2 61.6 %all-gather.9.cloned.1.call-done = bf16[1024,2176]{1,0:T(8,128)(2,1)} async-done(((bf16[128,2176]{1,0:T(8,128)(2,1)}), bf16[1024,2176]{1,0:T(8,128)(2,1)}) %all-gather.9.cloned.1.call-update) | async-done | bytes 4456464 | tf_op jit(solution)/shard_map/all_gather | solution.py:476
  121.6 13.7 %add_convert_fusion.2 = (bf16[1024,2048]{1,0:T(8,128)(2,1)}, f32[1024,2048]{1,0:T(8,128)S(1)}) fusion(f32[2048]{0:T(1024)S(1)} %bitcast.266, f32[1024]{0:T(1024)S(1)} %convert_subtract_fusion, f32[1023,2048]{1,0:T(8,128)} %bitcast.200, f32[2048]{0:T(1024)S(1)} %bitcast.246, f32[2048]{0:T(1024)S(1)} %bitcast.236, f32[1024]{0:T(1024)S(1)} %add_rsqrt_fusion, ...), kind=kLoop, calls=%fused_computation.22 | loop fusion | flops 18874368 | bytes 29388800 | tf_op jit(solution)/shard_map/convert_element_type | solution.py:540
  138.5 10.4 add_convert_fusion.1
  170.5 128.8 %mix_forward.1 = (bf16[1024,256]{1,0:T(8,128)(2,1)S(1)}, bf16[1024,256]{1,0:T(8,128)(2,1)S(1)}, f32[1024,256]{1,0:T(8,128)S(1)}, f32[1024,256]{1,0:T(8,128)S(1)}, f32[1024,256]{1,0:T(8,128)S(1)}) custom-call(f32[1024,256]{1,0:T(8,128)S(1)} %fusion.42.recept_ref, f32[1024,256]{1,0:T(8,128)} %fusion.38.keys_ref, f32[1024,256]{1,0:T(8,128)} %fusion.34.values_ref, ...), custom_call_target="tpu_custom_call" | custom-call | tf_op jit(solution)/shard_map/mix_forward/pallas_call | solution.py:370
  309.3 14.9 %all-to-all-done.1 = bf16[8,128,256]{1,2,0:T(8,128)(2,1)} async-done(((bf16[8,128,256]{1,2,0:T(8,128)(2,1)}), bf16[8,128,256]{1,2,0:T(8,128)(2,1)}, u32[]{:S(2)}, u32[]{:S(2)}) %all-to-all-start.1) | async-done | bytes 524320 | tf_op jit(solution)/shard_map/all_to_all | solution.py:455
  336.2 21.5 %all-gather.15.cloned.1.call-done = bf16[512,2048]{1,0:T(8,128)(2,1)} async-done(((bf16[128,2048]{1,0:T(8,128)(2,1)}), bf16[512,2048]{1,0:T(8,128)(2,1)}) %all-gather.15.cloned.1.call-update) | async-done | bytes 2097168 | tf_op jit(solution)/shard_map/all_gather | solution.py:562
  357.7 7.8 fusion.122
  367.5 9.5 fusion.47
  386.9 7.0 all-reduce.7
  399.0 22.8 %reduce-scatter.8.cloned.1.call-done = f32[128,2048]{1,0:T(8,128)} async-done(((f32[512,2048]{1,0:T(8,128)}), f32[128,2048]{1,0:T(8,128)}) %reduce-scatter.8.cloned.1.call-update) | async-done | bytes 1048592 | tf_op jit(solution)/shard_map/reduce_scatter | solution.py:567
  424.8 22.6 %all-gather.17.cloned.1.call-done = bf16[512,2048]{1,0:T(8,128)(2,1)} async-done(((bf16[128,2048]{1,0:T(8,128)(2,1)}), bf16[512,2048]{1,0:T(8,128)(2,1)}) %all-gather.17.cloned.1.call-update) | async-done | bytes 2097168 | tf_op jit(solution)/shard_map/all_gather | solution.py:572
  447.4 9.7 multiply_convert_fusion
  458.5 9.6 fusion.123
  468.4 44.4 %reduce-scatter.10.cloned.1.call-done = f32[128,2048]{1,0:T(8,128)} async-done(((f32[512,2048]{1,0:T(8,128)}), f32[128,2048]{1,0:T(8,128)}) %reduce-scatter.10.cloned.1.call-update) | async-done | bytes 1048592 | tf_op jit(solution)/shard_map/reduce_scatter | solution.py:575
  524.4 6.5 convolution_convert_fusion.7
  531.0 33.5 %all_to_all.45 = bf16[8,128,256]{2,1,0:T(8,128)(2,1)S(1)} all-to-all(bf16[8,128,256]{2,1,0:T(8,128)(2,1)S(1)} %bitcast.212), channel_id=1, replica_groups=mesh['seq'=8,'wsh'=4] {'seq'}, dimensions={0} | all-to-all | bytes 1048576 | tf_op jit(solution)/shard_map/all_to_all | solution.py:455
  564.5 77.7 %mix_backward.1 = (bf16[1024,256]{1,0:T(8,128)(2,1)S(1)}, bf16[1024,256]{1,0:T(8,128)(2,1)S(1)}, bf16[1024,256]{1,0:T(8,128)(2,1)S(1)}, bf16[4,1024,256]{2,1,0:T...) custom-call(bf16[1024,256]{1,0:T(8,128)(2,1)S(1)} %bitcast.196, f32[1024,256]{1,0:T(8,128)S(1)} %fusion.42.recept_ref, ...), custom_call_target="tpu_custom_call" | custom-call | tf_op jit(solution)/shard_map/mix_backward/pallas_call | solution.py:397
  677.1 8.7 concatenate.90
  686.0 10.9 convolution_convert_fusion
  698.6 8.4 convolution_convert_fusion.1
  729.7 7.2 broadcast_multiply_fusion
  741.7 7.3 broadcast_multiply_fusion.1
  749.0 23.4 %fusion.1 = f32[1023,2048]{1,0:T(8,128)} fusion(f32[1024,2048]{1,0:T(8,128)} %fusion.30, f32[1024,2048]{1,0:T(8,128)} %fusion.67, f32[1024,2048]{1,0:T(8,128)} %convolution_add_fusion, f32[1024,2048]{1,0:T(8,128)} %fusion.36, f32[1024,2048]{1,0:T(8,128)} %get-tuple-element.97, f32[1024,2048]{1,0:T(8,128)} %get-tuple-element.99, f32[1023]{0:T(1024)S(1)} %slice.331, ...), kind=kLoop, calls=%fused_computation.2 | loop fusion | flops 20951040 | bytes 58699772 | tf_op jit(solution)/shard_map/mul | solution.py:613
  772.5 31.3 %multiply_reduce_fusion = (f32[2048]{0:T(1024)S(1)}, f32[2048]{0:T(1024)S(1)}, f32[2048]{0:T(1024)S(1)}, f32[2048]{0:T(1024)S(1)}, f32[2048]{0:T(1024)S(1)}, /*i...) fusion(f32[1024,2048]{1,0:T(8,128)} %fusion.30, ...), kind=kLoop, calls=%fused_computation.10 | loop fusion | flops 69187584 | bytes 84017152 | tf_op jit(solution)/shard_map/reduce_sum | solution.py:611
  810.8 7.7 subtract_multiply_fusion
  832.1 6.7 all-to-all-done.7
  843.2 12.0 all-to-all-done.2
  861.4 34.3 %all_to_all.46 = bf16[8,128,256]{2,1,0:T(8,128)(2,1)S(1)} all-to-all(bf16[8,128,256]{2,1,0:T(8,128)(2,1)S(1)} %bitcast.229), channel_id=1, replica_groups=mesh['seq'=8,'wsh'=4] {'seq'}, dimensions={0} | all-to-all | bytes 1048576 | tf_op jit(solution)/shard_map/all_to_all | solution.py:455
  905.8 208.8 %reduce-scatter.18.cloned.1.call-done = bf16[256,2048]{1,0:T(8,128)(2,1)} async-done(((bf16[2048,2048]{1,0:T(8,128)(2,1)}), bf16[256,2048]{1,0:T(8,128)(2,1)}) %reduce-scatter.18.cloned.1.call-update) | async-done | bytes 1048592 | tf_op jit(solution)/shard_map/reduce_scatter | solution.py:579
  1123.3 21.6 %collective-permute-done.2 = bf16[256,2048]{1,0:T(8,128)(2,1)} collective-permute-done((bf16[256,2048]{1,0:T(8,128)(2,1)}, bf16[256,2048]{1,0:T(8,128)(2,1)}, u32[]{:S(2)}, u32[]{:S(2)}) %collective-permute-start.2) | collective-permute-done | bytes 1048608 | tf_op jit(solution)/shard_map/ppermute | solution.py:580
  1158.7 85.4 %reduce-scatter.12.cloned.1.call-done = bf16[128,2048]{1,0:T(8,128)(2,1)} async-done(((bf16[1024,2048]{1,0:T(8,128)(2,1)}), bf16[128,2048]{1,0:T(8,128)(2,1)}) %reduce-scatter.12.cloned.1.call-update) | async-done | bytes 524304 | tf_op jit(solution)/shard_map/reduce_scatter | solution.py:620
  (441 shorter events, 246.7 us)
Async XLA Ops:
  7.2 370.0 %copy-start = (bf16[128,2048]{1,0:T(8,128)(2,1)S(1)}, bf16[128,2048]{1,0:T(8,128)(2,1)}, u32[]{:S(2)}) copy-start(bf16[128,2048]{1,0:T(8,128)(2,1)} %param.17) | copy-start | bytes 1572868
  7.2 36.3 %all-gather.21.cloned.1.call-start = ((), (), s32[]{:S(2)}) async-start(), calls=%async_computation.29 | async-start | bytes 1310720 | tf_op jit(solution)/shard_map/all_gather | solution.py:530
  9.1 98.7 %all-gather.9.cloned.1.call-start = ((), (), s32[]{:S(2)}) async-start(), calls=%async_computation.16 | async-start | bytes 5013504 | tf_op jit(solution)/shard_map/all_gather | solution.py:476
  13.0 137.3 %all-gather.11.cloned.1.call-start = ((), (), s32[]{:S(2)}) async-start(), calls=%async_computation.17 | async-start | bytes 7208960 | tf_op jit(solution)/shard_map/all_gather | solution.py:521
  21.3 303.0 %all-gather.13.cloned.1.call-start = ((), (), s32[]{:S(2)}) async-start(), calls=%async_computation.18 | async-start | bytes 10485760 | tf_op jit(solution)/shard_map/all_gather | solution.py:532
  22.9 20.4 %all-to-all-start = ((bf16[8,128,256]{1,2,0:T(8,128)(2,1)}), bf16[8,128,256]{1,2,0:T(8,128)(2,1)S(1)}, u32[]{:S(2)}, u32[]{:S(2)}) async-start(bf16[8,128,256]{1,2,0:T(8,128)(2,1)} %bitcast.14), calls=%async_computation | async-start | bytes 1048576 | tf_op jit(solution)/shard_map/all_to_all | solution.py:455
  31.8 103.5 %copy-start.75 = (f32[2048,1]{0,1:T(1,128)}, f32[2048,1]{0,1:T(1,128)S(1)}, u32[]{:S(2)}) copy-start(f32[2048,1]{0,1:T(1,128)S(1)} %get-tuple-element.79) | copy-start | bytes 24580
  303.6 20.7 %all-to-all-start.1 = ((bf16[8,128,256]{1,2,0:T(8,128)(2,1)}), bf16[8,128,256]{1,2,0:T(8,128)(2,1)}, u32[]{:S(2)}, u32[]{:S(2)}) async-start(bf16[8,128,256]{1,2,0:T(8,128)(2,1)} %copy.162), calls=%async_computation.1 | async-start | bytes 1048576 | tf_op jit(solution)/shard_map/all_to_all | solution.py:455
  309.3 48.4 %all-gather.15.cloned.1.call-start = ((), (), s32[]{:S(2)}) async-start(), calls=%async_computation.19 | async-start | bytes 2621440 | tf_op jit(solution)/shard_map/all_gather | solution.py:562
  330.0 4.7 collective-permute-start
  336.2 85.6 %reduce-scatter.8.cloned.1.call-start = ((), (), s32[]{:S(2)}) async-start(), calls=%async_computation.20 | async-start | bytes 5242880 | tf_op jit(solution)/shard_map/reduce_scatter | solution.py:567
  378.3 20.6 %all-to-all-start.3 = ((bf16[8,16,2048]{2,1,0:T(8,128)(2,1)}), bf16[8,16,2048]{2,1,0:T(8,128)(2,1)S(1)}, u32[]{:S(2)}, u32[]{:S(2)}) async-start(bf16[8,16,2048]{2,1,0:T(8,128)(2,1)} %bitcast.31), calls=%async_computation.4 | async-start | bytes 1048576 | tf_op jit(solution)/shard_map/all_to_all | solution.py:455
  384.1 63.4 %all-gather.17.cloned.1.call-start = ((), (), s32[]{:S(2)}) async-start(), calls=%async_computation.21 | async-start | bytes 2621440 | tf_op jit(solution)/shard_map/all_gather | solution.py:572
  424.7 88.1 %reduce-scatter.10.cloned.1.call-start = ((), (), s32[]{:S(2)}) async-start(), calls=%async_computation.22 | async-start | bytes 5242880 | tf_op jit(solution)/shard_map/reduce_scatter | solution.py:575
  468.2 337.1 %all-gather.19.cloned.1.call-start = ((), (), s32[]{:S(2)}) async-start(), calls=%async_computation.25 | async-start | bytes 4718592 | tf_op jit(solution)/shard_map/all_gather | solution.py:594
  516.0 5.5 collective-permute-start.1
  524.3 371.4 %reduce-scatter.14.cloned.1.call-start = ((), (), s32[]{:S(2)}) async-start(), calls=%async_computation.24 | async-start | bytes 6553600 | tf_op jit(solution)/shard_map/reduce_scatter | solution.py:630
  530.9 111.4 %copy-start.42 = (bf16[1,256,512]{1,2,0:T(8,128)(2,1)S(1)}, bf16[1,256,512]{1,2,0:T(8,128)(2,1)}, u32[]{:S(2)}) copy-start(bf16[1,256,512]{1,2,0:T(8,128)(2,1)} %copy-done.41) | copy-start | bytes 786436
  530.9 111.4 %copy-start.51 = (f32[1024,128]{1,0:T(8,128)S(1)}, f32[1024,128]{1,0:T(8,128)}, u32[]{:S(2)}) copy-start(f32[1024,128]{1,0:T(8,128)} %get-tuple-element.92) | copy-start | bytes 1572868
  530.9 111.4 %copy-start.96 = (pred[128]{0:T(512)(128)(4,1)S(1)}, pred[128]{0:T(512)(128)(4,1)}, u32[]{:S(2)}) copy-start(pred[128]{0:T(512)(128)(4,1)} %constant.157.clone.1) | copy-start | bytes 388
  531.0 113.4 %copy-start.32 = (bf16[1024,2048]{1,0:T(8,128)(2,1)S(1)}, bf16[1024,2048]{1,0:T(8,128)(2,1)}, u32[]{:S(2)}) copy-start(bf16[1024,2048]{1,0:T(8,128)(2,1)} %get-tuple-element.54) | copy-start | bytes 12582916
  685.8 215.9 %reduce-scatter.20.cloned.1.call-start = ((), (), s32[]{:S(2)}) async-start(), calls=%async_computation.28 | async-start | bytes 9437184 | tf_op jit(solution)/shard_map/reduce_scatter | solution.py:579
  697.0 417.7 %reduce-scatter.18.cloned.1.call-start = ((), (), s32[]{:S(2)}) async-start(), calls=%async_computation.27 | async-start | bytes 9437184 | tf_op jit(solution)/shard_map/reduce_scatter | solution.py:579
  707.1 444.7 %reduce-scatter.16.cloned.1.call-start = ((), (), s32[]{:S(2)}) async-start(), calls=%async_computation.26 | async-start | bytes 1638400 | tf_op jit(solution)/shard_map/reduce_scatter | solution.py:643
  810.8 433.4 %reduce-scatter.12.cloned.1.call-start = ((), (), s32[]{:S(2)}) async-start(), calls=%async_computation.23 | async-start | bytes 4718592 | tf_op jit(solution)/shard_map/reduce_scatter | solution.py:620
  827.2 11.7 all-to-all-start.7
  831.0 286.8 %copy-start.98 = (s32[128]{0:T(128)S(1)}, s32[128]{0:T(128)}, u32[]{:S(2)}) copy-start(s32[128]{0:T(128)} %copy-done.97) | copy-start | bytes 1540
  838.9 16.4 %all-to-all-start.2 = ((bf16[8,16,2048]{2,1,0:T(8,128)(2,1)}), bf16[8,16,2048]{2,1,0:T(8,128)(2,1)S(1)}, u32[]{:S(2)}, u32[]{:S(2)}) async-start(bf16[8,16,2048]{2,1,0:T(8,128)(2,1)} %bitcast.29), calls=%async_computation.3 | async-start | bytes 1048576 | tf_op jit(solution)/shard_map/all_to_all | solution.py:455
  855.2 6.2 all-to-all-start.8
  895.7 259.4 %all-to-all-start.6 = ((bf16[8,64,1280]{2,1,0:T(8,128)(2,1)}), bf16[8,64,1280]{2,1,0:T(8,128)(2,1)S(1)}, u32[]{:S(2)}, u32[]{:S(2)}) async-start(bf16[8,64,1280]{2,1,0:T(8,128)(2,1)} %bitcast.219), calls=%async_computation.10 | async-start | bytes 2621440 | tf_op jit(solution)/shard_map/all_to_all | solution.py:455
  901.7 220.0 %collective-permute-start.3 = (bf16[256,2048]{1,0:T(8,128)(2,1)}, bf16[256,2048]{1,0:T(8,128)(2,1)S(1)}, u32[]{:S(2)}, u32[]{:S(2)}) collective-permute-start(bf16[256,2048]{1,0:T(8,128)(2,1)} %reduce-scatter.20.cloned.1.call-done), channel_id=1, source_target_pairs={{0,0},{1,8},{2,16},{3,24},{4,1},{5,9},{6,17},{7,25},{8,2},{9,10},{... | collective-permute-start | bytes 3145736 | tf_op jit(solution)/shard_map/ppermute | solution.py:580
  1114.7 30.2 %collective-permute-start.2 = (bf16[256,2048]{1,0:T(8,128)(2,1)}, bf16[256,2048]{1,0:T(8,128)(2,1)}, u32[]{:S(2)}, u32[]{:S(2)}) collective-permute-start(bf16[256,2048]{1,0:T(8,128)(2,1)} %reduce-scatter.18.cloned.1.call-done), channel_id=1, source_target_pairs={{0,0},{1,8},{2,16},{3,24},{4,1},{5,9},{6,17},{7,25},{8,2},{9,10},{... | collective-permute-start | bytes 3145736 | tf_op jit(solution)/shard_map/ppermute | solution.py:580
  (100 other events, 1831.6 us)
Sparse Core Ops, SparseCore 0:
  10.2 16.7 all-gather.20
  29.7 77.9 all-gather.8
  109.9 40.4 all-gather.10
  151.8 58.8 all-gather.12
  336.3 21.3 all-gather.14
  377.1 44.5 reduce-scatter.7
  424.9 22.5 all-gather.16
  468.3 44.4 reduce-scatter.9
  524.4 85.7 all-gather.18
  685.9 48.3 reduce-scatter.13
  738.4 163.3 reduce-scatter.19
  905.2 209.4 reduce-scatter.17
  1117.4 34.3 reduce-scatter.15
  1155.8 88.3 reduce-scatter.11

commit v2 on v1

--- a/solution.py
+++ b/solution.py
@@ -129,22 +129,26 @@
     )
 
 
-def unit_inverse(lower_part):
+def unit_inverses(lowers):
     i, j = iotas(BLOCK, BLOCK)
+    eye = jnp.where(i == j, 1.0, 0.0)
 
     def within(size):
         return (i // size) == (j // size)
 
-    small = jnp.where(within(8), lower_part, 0.0)
-    two = dot3(small, small)
-    four = dot3(two, two)
-    inverse = jnp.where(i == j, 1.0, 0.0) + small
-    inverse = inverse + dot3(inverse, two)
-    inverse = inverse + dot3(inverse, four)
-    for size in (16, 32, 64):
-        off = jnp.where(within(size) & ~within(size // 2), lower_part, 0.0)
-        inverse = inverse + dot3(inverse, dot3(off, inverse))
-    return inverse
+    smalls = [jnp.where(within(4), x, 0.0) for x in lowers]
+    low_smalls = [x.astype(BF16) for x in smalls]
+    twos = [dot(x, x) for x in low_smalls]
+    inverses = [eye + x for x in smalls]
+    inverses = [x + dot(x.astype(BF16), y.astype(BF16)) for x, y in zip(inverses, twos)]
+    for size in (8, 16, 32, 64):
+        mask = within(size) & ~within(size // 2)
+        offs = [jnp.where(mask, x, 0.0).astype(BF16) for x in lowers]
+        lows = [x.astype(BF16) for x in inverses]
+        inner = [dot(x, y).astype(BF16) for x, y in zip(offs, lows)]
+        inverses = [x + dot(y, z) for x, y, z in zip(inverses, lows, inner)]
+    errors = [eye - x + dot3(y, x) for x, y in zip(inverses, lowers)]
+    return [x + dot(x.astype(BF16), y.astype(BF16)) for x, y in zip(inverses, errors)]
 
 
 def post_norm(head_low, ones):
@@ -167,6 +171,8 @@
     ones = head_ones(width)
     vec = vec_ref[...]
     up = up_ref[...]
+    columns = [slice(head * HEAD, (head + 1) * HEAD) for head in range(heads)]
+    done = []
     for block in range(count):
         rows = slice(block * BLOCK, (block + 1) * BLOCK)
         recept, keys, values = recept_ref[rows], keys_ref[rows], values_ref[rows]
@@ -178,38 +184,33 @@
             low(decay_log), low(key_mod), low(key_dir), low(rate), low(recept),
             tile_heads(carry, heads), tile_heads(tail, heads),
         )
+        lefts = [jnp.concatenate([parts["alpha"][:, c], parts["recept"][:, c]], 0) for c in columns]
+        rights = [jnp.concatenate([parts["beta"][:, c], parts["key"][:, c]], 0) for c in columns]
+        pairs = [quad * dot3(x, y, NT) for x, y in zip(lefts, rights)]
+        done.append((rows, recept, key_mod, gate, mixed_value, keep, parts, pairs))
+    inverses = unit_inverses([x[:BLOCK, :BLOCK] for item in done for x in item[-1]])
+    for block, (rows, recept, key_mod, gate, mixed_value, keep, parts, pairs) in enumerate(done):
+        mine = inverses[block * heads : (block + 1) * heads]
         value_low = low(mixed_value)
+        owns = [value_low[:, c] for c in columns]
+        by_values = [dot3(x[:, BLOCK:], y) for x, y in zip(pairs, owns)]
+        ends = [jnp.concatenate([parts["beta_end"][:, c], parts["key_end"][:, c]], 0) for c in columns]
+        inners = [jnp.concatenate([parts["alpha_in"][:, c], parts["recept_in"][:, c]], 0) for c in columns]
         entering = state[...]
         state_ref[rows] = entering
-        leaving, outs, inverses, removals = [], [], [], []
-        for head in range(heads):
-            cols = slice(head * HEAD, (head + 1) * HEAD)
-            own = value_low[:, cols]
-            now = entering[:, cols]
-            pairs = quad * dot3(
-                jnp.concatenate([parts["alpha"][:, cols], parts["recept"][:, cols]], 0),
-                jnp.concatenate([parts["beta"][:, cols], parts["key"][:, cols]], 0),
-                NT,
-            )
-            inverse = unit_inverse(pairs[:BLOCK, :BLOCK])
-            inward = dot3(
-                jnp.concatenate([parts["alpha_in"][:, cols], parts["recept_in"][:, cols]], 0), now, NT
-            )
-            by_value = dot3(pairs[:, BLOCK:], own)
-            removed = dot3(inverse, inward[:BLOCK] + by_value[:BLOCK])
-            outs.append(inward[BLOCK:] + by_value[BLOCK:] + dot3(pairs[BLOCK:, :BLOCK], removed))
-            leaving.append(
-                now * (parts["end"][:, cols] * keep)
-                + dot3(
-                    jnp.concatenate([removed, own], 0),
-                    jnp.concatenate([parts["beta_end"][:, cols], parts["key_end"][:, cols]], 0),
-                    TN,
-                )
-            )
-            inverses.append(inverse)
-            removals.append(removed)
+        nows = [entering[:, c] for c in columns]
+        inwards = [dot3(x, y, NT) for x, y in zip(inners, nows)]
+        removals = [dot3(x, y[:BLOCK] + z[:BLOCK]) for x, y, z in zip(mine, inwards, by_values)]
+        outs = [
+            y[BLOCK:] + z[BLOCK:] + dot3(x[BLOCK:, :BLOCK], r)
+            for x, y, z, r in zip(pairs, inwards, by_values, removals)
+        ]
+        leaving = [
+            x * (parts["end"][:, c] * keep) + dot3(jnp.concatenate([r, v], 0), e, TN)
+            for x, c, r, v, e in zip(nows, columns, removals, owns, ends)
+        ]
         state[...] = join(leaving, 1)
-        inverse_ref[rows] = join(inverses, 1)
+        inverse_ref[rows] = join(mine, 1)
         removed_ref[rows] = join(removals, 1)
         head_low = join(outs, 1).astype(BF16)
         head_ref[rows] = head_low
@@ -236,7 +237,10 @@
     up = up_ref[...]
     i, j = iotas(BLOCK, BLOCK)
     upper = jnp.where(i <= j, 1.0, 0.0).astype(BF16)
-    for block in range(count - 1, -1, -1):
+    columns = [slice(head * HEAD, (head + 1) * HEAD) for head in range(heads)]
+    order = range(count - 1, -1, -1)
+    kept = {}
+    for block in order:
         rows = slice(block * BLOCK, (block + 1) * BLOCK)
         recept, keys, values = recept_ref[rows], keys_ref[rows], values_ref[rows]
         first = first_ref[rows].astype(F32)
@@ -244,10 +248,10 @@
             keys, values, hidden_ref[rows], up, first, vec, ones
         )
         quad, carry, tail, keep = block_masks(segment_ref[block * 8 : block * 8 + 8])
-        carry_wide = tile_heads(carry, heads)
         rate_low, dir_low = low(rate), low(key_dir)
         parts = decayed(
-            low(decay_log), low(key_mod), dir_low, rate_low, low(recept), carry_wide, tile_heads(tail, heads)
+            low(decay_log), low(key_mod), dir_low, rate_low, low(recept),
+            tile_heads(carry, heads), tile_heads(tail, heads),
         )
         value_low = low(mixed_value)
 
@@ -264,72 +268,78 @@
             - normed * (head_sum(grad_normed * normed, ones) * (1.0 / HEAD))
         )
         grad_coefficient = head_sum(opened * mixed_value, ones)
-        grad_mixed_value = opened * coefficient
         weighted = grad_coefficient * vec[5:6]
-        grad_recept = weighted * key_mod
-        grad_key_mod = weighted * recept
         head_grad = low(grad_head)
 
-        entering, removed_all, inverse_all = state_ref[rows], removed_ref[rows], inverse_ref[rows]
-        after = state[...]
-        leaving, g_alpha, g_recept, g_beta, g_key, g_beta_end, g_key_end, g_value, g_end = (
-            [], [], [], [], [], [], [], [], [],
+        lefts = [jnp.concatenate([parts["alpha"][:, c], parts["recept"][:, c]], 0) for c in columns]
+        rights = [jnp.concatenate([parts["beta"][:, c], parts["key"][:, c]], 0) for c in columns]
+        ends = [jnp.concatenate([parts["beta_end"][:, c], parts["key_end"][:, c]], 0) for c in columns]
+        inners = [jnp.concatenate([parts["alpha_in"][:, c], parts["recept_in"][:, c]], 0) for c in columns]
+        pairs = [quad * dot3(x, y, NT) for x, y in zip(lefts, rights)]
+        out_grads = [head_grad[:, c] for c in columns]
+        through = [dot3(x[BLOCK:, :BLOCK], y, TN) for x, y in zip(pairs, out_grads)]
+        kept[block] = dict(
+            rows=rows, recept=recept, keys=keys, values=values, first=first, z=z, rate=rate, blend=blend,
+            mixed_value=mixed_value, scale=scale, key_dir=key_dir, key_mod=key_mod, quad=quad, carry=carry, keep=keep,
+            rate_low=rate_low, dir_low=dir_low, parts=parts, value_low=value_low, normed=normed, product=product,
+            grad_gate=grad_gate, opened=opened, grad_coefficient=grad_coefficient,
+            grad_mixed_value=opened * coefficient, grad_recept=weighted * key_mod, grad_key_mod=weighted * recept,
+            lefts=lefts, rights=rights, ends=ends, inners=inners, pairs=pairs, out_grads=out_grads, through=through,
         )
-        for head in range(heads):
-            cols = slice(head * HEAD, (head + 1) * HEAD)
-            own, now, later = value_low[:, cols], entering[:, cols], after[:, cols]
-            removed, inverse, out_grad = removed_all[:, cols], inverse_all[:, cols], head_grad[:, cols]
-            left = jnp.concatenate([parts["alpha"][:, cols], parts["recept"][:, cols]], 0)
-            right = jnp.concatenate([parts["beta"][:, cols], parts["key"][:, cols]], 0)
-            ends = jnp.concatenate([parts["beta_end"][:, cols], parts["key_end"][:, cols]], 0)
-            pairs = quad * dot3(left, right, NT)
-            from_end = dot3(ends, later, NT)
-            grad_removed = dot3(pairs[BLOCK:, :BLOCK], out_grad, TN) + from_end[:BLOCK]
-            grad_inner = dot3(inverse, grad_removed, TN)
-            both = jnp.concatenate([grad_inner, out_grad], 0)
-            sources = jnp.concatenate([removed, own], 0)
-            grad_pairs = quad * dot3(both, sources, NT)
-            carry_two = jnp.concatenate([carry, carry], 0)
-            grad_left = dot3(grad_pairs, right) + carry_two * dot3(both, now)
-            grad_right = dot3(grad_pairs, left, TN)
-            grad_ends = dot3(sources, later)
-            g_value.append(dot3(pairs[:, BLOCK:], both, TN) + from_end[BLOCK:])
-            kept = later * (parts["end"][:, cols] * keep)
-            leaving.append(kept + dot3(both, carry_two * left, TN))
-            g_end.append(jnp.sum(now * kept, 0, keepdims=True))
-            g_alpha.append(grad_left[:BLOCK])
-            g_recept.append(grad_left[BLOCK:])
-            g_beta.append(grad_right[:BLOCK])
-            g_key.append(grad_right[BLOCK:])
-            g_beta_end.append(grad_ends[:BLOCK])
-            g_key_end.append(grad_ends[BLOCK:])
-        state[...] = join(leaving, 1)
-        d_alpha, d_recept, d_beta, d_key = join(g_alpha, 1), join(g_recept, 1), join(g_beta, 1), join(g_key, 1)
-        d_beta_end, d_key_end = join(g_beta_end, 1), join(g_key_end, 1)
+    for block in order:
+        k = kept[block]
+        after, entering, inverse_all = state[...], state_ref[k["rows"]], inverse_ref[k["rows"]]
+        laters, nows = [after[:, c] for c in columns], [entering[:, c] for c in columns]
+        from_ends = [dot3(x, y, NT) for x, y in zip(k["ends"], laters)]
+        inner_grads = [
+            dot3(inverse_all[:, c], x + y[:BLOCK], TN) for c, x, y in zip(columns, k["through"], from_ends)
+        ]
+        boths = [jnp.concatenate([x, y], 0) for x, y in zip(inner_grads, k["out_grads"])]
+        stays = [x * (k["parts"]["end"][:, c] * k["keep"]) for x, c in zip(laters, columns)]
+        state[...] = join([x + dot3(y, z, TN) for x, y, z in zip(stays, boths, k["inners"])], 1)
+        k.update(
+            laters=laters, nows=nows, from_ends=from_ends, boths=boths,
+            end_sum=join([jnp.sum(x * y, 0, keepdims=True) for x, y in zip(nows, stays)], 1),
+        )
+    vec_total = jnp.zeros_like(vec)
+    for block in order:
+        k = kept[block]
+        rows, parts, quad = k["rows"], k["parts"], k["quad"]
+        removed_all = removed_ref[rows]
+        carry_two = jnp.concatenate([k["carry"], k["carry"]], 0)
+        sources = [jnp.concatenate([removed_all[:, c], k["value_low"][:, c]], 0) for c in columns]
+        grad_pairs = [quad * dot3(x, y, NT) for x, y in zip(k["boths"], sources)]
+        grad_values = [
+            dot3(x[:, BLOCK:], y, TN) + z[BLOCK:] for x, y, z in zip(k["pairs"], k["boths"], k["from_ends"])
+        ]
+        grad_ends = [dot3(x, y) for x, y in zip(sources, k["laters"])]
+        to_state = [carry_two * dot3(x, y) for x, y in zip(k["boths"], k["nows"])]
+        grad_lefts = [dot3(x, y) + z for x, y, z in zip(grad_pairs, k["rights"], to_state)]
+        grad_rights = [dot3(x, y, TN) for x, y in zip(grad_pairs, k["lefts"])]
+        d_alpha, d_recept = join([x[:BLOCK] for x in grad_lefts], 1), join([x[BLOCK:] for x in grad_lefts], 1)
+        d_beta, d_key = join([x[:BLOCK] for x in grad_rights], 1), join([x[BLOCK:] for x in grad_rights], 1)
+        d_beta_end, d_key_end = join([x[:BLOCK] for x in grad_ends], 1), join([x[BLOCK:] for x in grad_ends], 1)
         ended = parts["beta_end"] * d_beta_end + parts["key_end"] * d_key_end
         alphas = parts["alpha"] * d_alpha
         d_total = parts["recept"] * d_recept - parts["beta"] * d_beta - parts["key"] * d_key - ended + alphas
-        d_step = sum_left(upper, d_total) + (jnp.sum(ended, 0, keepdims=True) + join(g_end, 1)) - alphas
+        d_step = sum_left(upper, d_total) + (jnp.sum(ended, 0, keepdims=True) + k["end_sum"]) - alphas
         d_beta_plain = d_beta * parts["shrunk"] + d_beta_end * parts["tail"]
-        copy_recept = low(d_recept * parts["grown"])
         copy_decay = low(d_step * parts["log_step"])
-        copy_key = low(d_key * parts["shrunk"] + d_key_end * parts["tail"])
-        copy_value = low(join(g_value, 1))
-        copy_dir = low(d_beta_plain * rate_low - d_alpha * parts["before"])
-        copy_rate = low(d_beta_plain * dir_low)
-
-        grad_recept = grad_recept + copy_recept
-        grad_key_mod = grad_key_mod + copy_key
-        grad_mixed_value = grad_mixed_value + copy_value
-        grad_z = copy_decay * jax.nn.sigmoid(-z)
+        copy_dir = low(d_beta_plain * k["rate_low"] - d_alpha * parts["before"])
+        copy_rate = low(d_beta_plain * k["dir_low"])
+
+        keys, values, rate, blend = k["keys"], k["values"], k["rate"], k["blend"]
+        grad_recept = k["grad_recept"] + low(d_recept * parts["grown"])
+        grad_key_mod = k["grad_key_mod"] + low(d_key * parts["shrunk"] + d_key_end * parts["tail"])
+        grad_mixed_value = k["grad_mixed_value"] + low(join(grad_values, 1))
+        grad_z = copy_decay * jax.nn.sigmoid(-k["z"])
         factor = 1.0 + (rate - 1.0) * vec[4:5]
         keyed = grad_key_mod * keys
         grad_rate = copy_rate + keyed * vec[4:5]
-        grad_scaled = scale * (copy_dir - key_dir * head_sum(copy_dir * key_dir, ones))
+        grad_scaled = k["scale"] * (copy_dir - k["key_dir"] * head_sum(copy_dir * k["key_dir"], ones))
         grad_keys = grad_key_mod * factor + grad_scaled * vec[3:4]
         grad_rate_up = grad_rate * rate * (1.0 - rate)
-        grad_blend = grad_mixed_value * (first - values)
-        grad_value_up = grad_blend * blend * (1.0 - blend)
+        grad_value_up = grad_mixed_value * (k["first"] - values) * blend * (1.0 - blend)
         recept_out[rows] = grad_recept.astype(BF16)
         keys_out[rows] = grad_keys.astype(BF16)
         values_out[rows] = (grad_mixed_value * (1.0 - blend)).astype(BF16)
@@ -337,28 +347,29 @@
         ups_out[0, rows] = grad_z.astype(BF16)
         ups_out[1, rows] = grad_rate_up.astype(BF16)
         ups_out[2, rows] = grad_value_up.astype(BF16)
-        ups_out[3, rows] = grad_gate.astype(BF16)
+        ups_out[3, rows] = k["grad_gate"].astype(BF16)
 
         def total(x):
             return jnp.sum(x, 0, keepdims=True)
 
-        vec_out[...] += jnp.concatenate(
+        vec_total = vec_total + jnp.concatenate(
             [
                 total(grad_z), total(grad_rate_up), total(grad_value_up), total(grad_scaled * keys),
-                total(keyed * (rate - 1.0)), total(grad_coefficient * product),
-                total(opened * normed), total(opened),
+                total(keyed * (rate - 1.0)), total(k["grad_coefficient"] * k["product"]),
+                total(k["opened"] * k["normed"]), total(k["opened"]),
             ],
             0,
         )
-
-
-def per_step(rows):
-    return 2 if (rows // BLOCK) % 2 == 0 else 1
+    vec_out[...] += vec_total
+
+
+def per_step(rows, most):
+    return most if (rows // BLOCK) % most == 0 else 1
 
 
 def run_forward(recept, keys, values, hidden, first, up, vec, segments):
     rows, width = recept.shape
-    count = per_step(rows)
+    count = per_step(rows, 4)
     step = count * BLOCK
 
     def spec(columns):
@@ -384,7 +395,7 @@
 
 def run_backward(grad, recept, keys, values, hidden, first, up, vec, segments, saved):
     rows, width = recept.shape
-    count = per_step(rows)
+    count = per_step(rows, 2)
     step = count * BLOCK
     last = rows // step - 1
 
@@ -418,6 +429,179 @@
     )(grad, recept, keys, values, hidden, first, up, vec, segments, *saved)
 
 
+def mix_norm(block_ref, stats_ref, vec_ref):
+    stats = stats_ref[...]
+    flowing = stats[:, 2:3]
+    standard = (block_ref[...].astype(F32) - stats[:, 0:1]) * stats[:, 1:2]
+    normed = standard * vec_ref[0:1] + vec_ref[1:2]
+    delta = pltpu.roll(normed, 1, 0) * flowing - normed
+    return standard, normed, delta, flowing
+
+
+def project_kernel(
+    width, number_ref, block_ref, stats_ref, vec_ref, weight_ref,
+    recept_ref, keys_ref, values_ref, downs_ref, hidden_ref,
+):
+    base = 3 * width
+    _, normed, delta, _ = mix_norm(block_ref, stats_ref, vec_ref)
+    weight = weight_ref[...]
+    uses = (
+        ((recept_ref, 0, width, 0),),
+        ((downs_ref, base + OFFSETS[0], PADDED[0], OFFSETS[0]),),
+        ((keys_ref, width, width, 0),),
+        ((values_ref, 2 * width, width, 0), (downs_ref, base + OFFSETS[2], PADDED[2], OFFSETS[2])),
+        ((downs_ref, base + OFFSETS[1], PADDED[1], OFFSETS[1]),),
+        ((downs_ref, base + OFFSETS[3], PADDED[3], OFFSETS[3]),),
+    )
+
+    @pl.when(pl.program_id(0) == 0)
+    def _():
+        for ref in (recept_ref, keys_ref, values_ref, downs_ref):
+            ref[...] = jnp.zeros_like(ref)
+
+    for c, targets in enumerate(uses):
+        mixed = (normed + delta * vec_ref[2 + c : 3 + c]).astype(BF16)
+        for ref, start, size, at in targets:
+            ref[:, at : at + size] += dot(mixed, weight[:, start : start + size])
+
+    @pl.when(pl.program_id(0) == pl.num_programs(0) - 1)
+    def _():
+        hidden_ref[:, 0:128] = jnp.tanh(downs_ref[:, 0:128]).astype(BF16)
+        hidden_ref[:, 128:384] = downs_ref[:, 128:384].astype(BF16)
+        hidden_ref[:, 384:640] = jax.nn.sigmoid(downs_ref[:, 384:640]).astype(BF16)
+
+
+def unproject_kernel(
+    width, parts, piece, number_ref, block_ref, stats_ref, vec_ref, weight_ref,
+    recept_ref, keys_ref, values_ref, ups_ref, hidden_ref, downs_ref, up_ref,
+    grad_ref, sums_ref, vec_out, wide_ref, up_out, down_lows,
+):
+    rows = block_ref.shape[0]
+    base = 3 * width
+
+    @pl.when(pl.program_id(0) == 0)
+    def _():
+        sums_ref[...] = jnp.zeros_like(sums_ref)
+        for k, (at, size) in enumerate(zip(OFFSETS, PADDED)):
+            cols = slice(at, at + size)
+            grad = dot(ups_ref[k], up_ref[cols], NT)
+            if k == 0:
+                grad = grad * (1.0 - jnp.square(jnp.tanh(downs_ref[:, cols])))
+            if k == 3:
+                opening = jax.nn.sigmoid(downs_ref[:, cols])
+                grad = grad * opening * (1.0 - opening)
+            down_lows[:, cols] = grad.astype(BF16)
+            up_out[:, cols] = dot(ups_ref[k], hidden_ref[:, cols], TN).astype(BF16)
+
+    standard, normed, delta, flowing = mix_norm(block_ref, stats_ref, vec_ref)
+    weight = weight_ref[...]
+
+    def down(k):
+        return (down_lows[:, OFFSETS[k] : OFFSETS[k] + PADDED[k]], base + OFFSETS[k], PADDED[k])
+
+    uses = (
+        ((recept_ref[...], 0, width),),
+        (down(0),),
+        ((keys_ref[...], width, width),),
+        ((values_ref[...], 2 * width, width), down(2)),
+        (down(1),),
+        (down(3),),
+    )
+    kept, sent, vec_rows = None, None, []
+    per_seq = parts * piece
+    for c, sources in enumerate(uses):
+        share = vec_ref[2 + c : 3 + c]
+        mixed = (normed + delta * share).astype(BF16)
+        grad = None
+        for source, start, size in sources:
+            part = dot(source, weight[:, start : start + size], NT)
+            grad = part if grad is None else grad + part
+            product = dot(mixed, source, TN).astype(BF16)
+            for number in range(product.shape[0] // per_seq):
+                for w in range(parts):
+                    at = number * per_seq + w * piece
+                    wide_ref[w, number, :, start : start + size] = product[at : at + piece]
+        vec_rows.append(jnp.sum(grad * delta, 0, keepdims=True))
+        moved = grad * share
+        kept = grad - moved if kept is None else kept + (grad - moved)
+        sent = moved if sent is None else sent + moved
+    grad = kept + pltpu.roll(sent * flowing, rows - 1, 0)
+    vec_out[...] = jnp.concatenate(
+        [jnp.sum(grad * standard, 0, keepdims=True), jnp.sum(grad, 0, keepdims=True)] + vec_rows, 0
+    )
+    scaled = grad * vec_ref[0:1]
+    sums_ref[:, 0:1] += jnp.sum(scaled, 1, keepdims=True)
+    sums_ref[:, 1:2] += jnp.sum(scaled * standard, 1, keepdims=True)
+    grad_ref[...] = scaled
+
+
+def mix_specs(rows, width, own_width, parts):
+    block = 256 if rows <= 1024 else 128
+    per_shard = width // parts // block
+
+    def columns(height):
+        return pl.BlockSpec((height, block), lambda j, n: (0, j))
+
+    def whole(shape):
+        return pl.BlockSpec(shape, lambda j, n: (0,) * len(shape))
+
+    def weights(array):
+        size = array.shape[1] if rows > 1024 else 3 * own_width + WIDE
+        return pl.BlockSpec((block, size), lambda j, n: (((j // per_shard) ^ n[0]) * per_shard + j % per_shard, 0))
+
+    return block, columns, whole, weights
+
+
+def run_project(number, balanced, stats, vec, weights, own_width, parts):
+    rows, width = balanced.shape
+    block, columns, whole, weight_spec = mix_specs(rows, width, own_width, parts)
+    shapes = [(rows, own_width)] * 3 + [(rows, WIDE)] * 2
+    return pl.pallas_call(
+        functools.partial(project_kernel, own_width),
+        grid_spec=pltpu.PrefetchScalarGridSpec(
+            num_scalar_prefetch=1,
+            grid=(width // block,),
+            in_specs=[columns(rows), whole(stats.shape), columns(8), weight_spec(weights)],
+            out_specs=[whole(s) for s in shapes],
+        ),
+        out_shape=[jax.ShapeDtypeStruct(s, d) for s, d in zip(shapes, (F32, F32, F32, F32, BF16))],
+        compiler_params=pltpu.CompilerParams(vmem_limit_bytes=60 << 20),
+        name="mix_project",
+    )(number, balanced, stats, vec, weights)
+
+
+def run_unproject(number, balanced, stats, vec, weights, lows, ups, hidden, downs, up, parts):
+    rows, width = balanced.shape
+    own_width = lows[0].shape[1]
+    seqs = width // own_width
+    piece = own_width // parts
+    block, columns, whole, weight_spec = mix_specs(rows, width, own_width, parts)
+    taken = block // own_width
+    total = 3 * own_width + WIDE
+    return pl.pallas_call(
+        functools.partial(unproject_kernel, own_width, parts, piece),
+        grid_spec=pltpu.PrefetchScalarGridSpec(
+            num_scalar_prefetch=1,
+            grid=(width // block,),
+            in_specs=[columns(rows), whole(stats.shape), columns(8), weight_spec(weights)]
+            + [whole(a.shape) for a in (*lows, ups, hidden, downs, up)],
+            out_specs=[
+                columns(rows), whole((rows, 2)), columns(8),
+                pl.BlockSpec((parts, taken, piece, total), lambda j, n: (0, j, 0, 0)),
+                whole((own_width, WIDE)),
+            ],
+            scratch_shapes=[pltpu.VMEM((rows, WIDE), BF16)],
+        ),
+        out_shape=[
+            jax.ShapeDtypeStruct((rows, width), F32), jax.ShapeDtypeStruct((rows, 2), F32),
+            jax.ShapeDtypeStruct((8, width), F32), jax.ShapeDtypeStruct((parts, seqs, piece, total), BF16),
+            jax.ShapeDtypeStruct((own_width, WIDE), BF16),
+        ],
+        compiler_params=pltpu.CompilerParams(vmem_limit_bytes=60 << 20),
+        name="mix_unproject",
+    )(number, balanced, stats, vec, weights, *lows, ups, hidden, downs, up)
+
+
 def norm_stats(values):
     centered = values - jnp.mean(values, -1, keepdims=True)
     scale = lax.rsqrt(jnp.mean(centered * centered, -1, keepdims=True) + 1e-05)
@@ -453,6 +637,49 @@
 
 def exchange(x, axis):
     return lax.all_to_all(x, axis, split_axis=0, concat_axis=0, tiled=True)
+
+
+def swap(x, by):
+    size = lax.axis_size("wsh")
+    return lax.ppermute(x, "wsh", [(i, i ^ by) for i in range(size)])
+
+
+def gather_near(x):
+    if lax.axis_size("wsh") != 4:
+        return lax.all_gather(x, "wsh", axis=0, tiled=True)
+    across = swap(x, 2)
+    beside = swap(x, 1)
+    return jnp.concatenate([x, beside, across, swap(across, 1)], 0)
+
+
+def scalar_sum(x):
+    if lax.axis_size("wsh") != 4:
+        return jnp.sum(lax.all_gather(x.reshape(1), "wsh", axis=0, tiled=True))
+    x = jnp.full((8, 128), x)
+    x = x + swap(x, 1)
+    return (x + swap(x, 2))[0, 0]
+
+
+def near_sum(x):
+    if lax.axis_size("wsh") != 4:
+        return lax.psum_scatter(x, "wsh", scatter_dimension=0, tiled=True)
+    rows = x.shape[0] // 4
+    beside = swap(jnp.concatenate([x[rows : 2 * rows], x[3 * rows :]], 0), 1)
+    far = x[2 * rows : 3 * rows] + beside[rows:]
+    return x[:rows] + beside[:rows] + swap(far.astype(BF16), 2).astype(F32)
+
+
+def block_sum(x):
+    if lax.axis_size("wsh") != 4:
+        return lax.psum_scatter(x, "wsh", scatter_dimension=0, tiled=False).astype(F32)
+    number = lax.axis_index("wsh")
+
+    def block(by):
+        return lax.dynamic_index_in_dim(x, number ^ by, 0, keepdims=False)
+
+    beside = swap(jnp.stack([block(1), block(3)]), 1).astype(F32)
+    far = block(2).astype(F32) + beside[1]
+    return block(0).astype(F32) + beside[0] + swap(far.astype(BF16), 2).astype(F32)
 
 
 def local(
@@ -478,7 +705,7 @@
     places = (info[:, 0] * DIGIT + info[:, 1]).astype(jnp.int32)
     numbers = jnp.arange(group, dtype=jnp.int32)
     permute = (numbers[:, None] == places[None, :]).astype(BF16)
-    total_valid = jnp.sum(lax.all_gather(jnp.sum(info[:, 2]).reshape(1), "wsh", axis=0, tiled=True))
+    total_valid = scalar_sum(jnp.sum(info[:, 2]))
 
     index = jnp.arange(rows, dtype=jnp.int32)
     same_dest = (dest_seq[:, None] == dest_seq[None, :]) & (index[None, :] < index[:, None])
@@ -518,39 +745,40 @@
     def own_columns(matrix):
         return lax.dynamic_slice_in_dim(matrix, column, own_width, 1)
 
-    weights = lax.all_gather(
+    near = parts == 4
+    number = lax.axis_index("wsh") if near else 0
+    up_piece = lax.dynamic_slice_in_dim(lowrank_up_weight, column % shard, own_width, 0)
+    total = 3 * own_width + WIDE
+    weights = gather_near(
         jnp.concatenate(
-            [own_columns(receptance_matrix), own_columns(key_matrix), own_columns(value_matrix), pad_ranks(lowrank_down_weight)], 1
-        ),
-        "wsh", axis=0, tiled=True,
-    )
-    w_recept, w_key = weights[:, :own_width], weights[:, own_width : 2 * own_width]
-    w_value, down = weights[:, 2 * own_width : 3 * own_width], weights[:, 3 * own_width :]
-    up_piece = lax.dynamic_slice_in_dim(lowrank_up_weight, column % shard, own_width, 0)
-    ups = lax.all_gather(up_piece, "wsh", axis=0, tiled=False)
-    up = pad_ranks(lax.dynamic_index_in_dim(ups, column // shard, 0, keepdims=False))
+            [
+                own_columns(receptance_matrix), own_columns(key_matrix), own_columns(value_matrix),
+                pad_ranks(lowrank_down_weight), up_piece.reshape(shard, -1),
+            ],
+            1,
+        )
+    )
+    up = pad_ranks(
+        lax.dynamic_slice(
+            weights, (((column // shard) ^ number) * shard, total), (shard, weights.shape[1] - total)
+        ).reshape(own_width, -1)
+    ).T
+    number = jnp.full((1,), number, jnp.int32)
     w_out = lax.all_gather(output_matrix, "wsh", axis=0, tiled=True)
     vec = lax.dynamic_slice_in_dim(vectors, column, own_width, 0)[:, 8:16].T
 
-    balanced = dot(permute, given[:, :width])
-    standard, scale_one = norm_stats(balanced)
-    normed = standard * vectors[:, 0] + vectors[:, 1]
-    previous = jnp.concatenate([jnp.zeros_like(normed[:1]), normed[:-1]], 0) * flowing
-    delta = previous - normed
-    mixed = [(normed + delta * vectors[:, 2 + c]).astype(BF16) for c in range(6)]
-    recept = dot(mixed[0], w_recept)
-    keys = dot(mixed[2], w_key)
-    values = dot(mixed[3], w_value)
-    downs = [dot(mixed[c], down[:, o : o + n]) for c, o, n in zip((1, 4, 3, 5), OFFSETS, PADDED)]
-    decay_tanh, gate_sigmoid = jnp.tanh(downs[0]), jax.nn.sigmoid(downs[3])
-    hidden = jnp.concatenate(
-        [decay_tanh.astype(BF16), downs[1].astype(BF16), downs[2].astype(BF16), gate_sigmoid.astype(BF16)], 1
-    )
-    inputs = (recept, keys, values, hidden, first, up.T, vec, segments)
+    balanced = dot(permute, given[:, :width]).astype(BF16)
+    wide_rows = balanced.astype(F32)
+    mean = jnp.mean(wide_rows, -1, keepdims=True)
+    scale_one = lax.rsqrt(jnp.mean(jnp.square(wide_rows - mean), -1, keepdims=True) + 1e-05)
+    stats = jnp.concatenate([mean, scale_one, flowing, flowing], 1)
+    mix_vec = vectors[:, :8].T
+    recept, keys, values, downs, hidden = run_project(number, balanced, stats, mix_vec, weights, own_width, parts)
+    inputs = (recept, keys, values, hidden, first, up, vec, segments)
     mixed_out, *saved = run_forward(*inputs)
 
     mixed_rows = exchange(mixed_out.reshape(seqs, rows, own_width), "seq").transpose(1, 0, 2).reshape(rows, width)
-    own = lax.dynamic_slice_in_dim(balanced, me * rows, rows, 0)
+    own = lax.dynamic_slice_in_dim(balanced, me * rows, rows, 0).astype(F32)
     own_starts = lax.dynamic_slice_in_dim(starts, me * rows, rows, 0)
     own_flowing = (1.0 - own_starts)[:, None]
     own_valid = dot(own_rows, given[:, width : width + EXTRA])[:, 2]
@@ -559,28 +787,26 @@
     normed_two = standard_two * vectors[:, 16] + vectors[:, 17]
     carried_two = from_behind(normed_two[-1:], "seq", 1)
     delta_two = jnp.concatenate([carried_two, normed_two[:-1]], 0) * own_flowing - normed_two
-    channel = lax.all_gather(
-        (normed_two + delta_two * vectors[:, 18]).astype(BF16), "wsh", axis=0, tiled=True
-    )
+    channel = gather_near((normed_two + delta_two * vectors[:, 18]).astype(BF16))
     active = jax.nn.relu(dot(channel, channel_key_weight, NT))
     hidden_rows = jnp.square(active).astype(BF16)
-    result = residual + lax.psum_scatter(
-        dot(hidden_rows, channel_value_weight), "wsh", scatter_dimension=0, tiled=True
-    )
+    result = residual + near_sum(dot(hidden_rows, channel_value_weight))
     total_tokens = group * parts
     cotangent = (result - target) * (own_valid * (total_tokens / total_valid))[:, None]
-    cot = lax.all_gather(cotangent.astype(BF16), "wsh", axis=0, tiled=True)
-
+    cot = gather_near(cotangent.astype(BF16))
+
+    blocks = [(s * parts + w, w * seqs + s) for s in range(seqs) for w in range(parts)]
+
+    def ffn_grad(part):
+        part = lax.psum_scatter(part, "seq", scatter_dimension=0, tiled=True)
+        return lax.ppermute(part, ("seq", "wsh"), blocks).astype(F32)
+
+    value_part, cot = lax.optimization_barrier((dot(hidden_rows, cot, TN).astype(BF16), cot))
+    grad_ffn_value = ffn_grad(value_part)
     grad_pre = (dot(cot, channel_value_weight, NT) * 2.0 * active).astype(BF16)
-    grad_channel = lax.psum_scatter(dot(grad_pre, channel_key_weight), "wsh", scatter_dimension=0, tiled=True)
-    blocks = [(s * parts + w, w * seqs + s) for s in range(seqs) for w in range(parts)]
-
-    def ffn_grad(left, right):
-        part = lax.psum_scatter(dot(left, right, TN).astype(BF16), "seq", scatter_dimension=0, tiled=True)
-        return lax.ppermute(part, ("seq", "wsh"), blocks).astype(F32)
-
-    grad_ffn_value = ffn_grad(hidden_rows, cot)
-    grad_ffn_key = ffn_grad(grad_pre, channel)
+    channel_part = dot(grad_pre, channel_key_weight)
+    key_part, grad_channel = lax.optimization_barrier((dot(grad_pre, channel, TN).astype(BF16), near_sum(channel_part)))
+    grad_ffn_key = ffn_grad(key_part)
     grad_vec_mix_two = jnp.sum(grad_channel * delta_two, 0)
     shifted = grad_channel * vectors[:, 18] * own_flowing
     behind = from_behind(shifted[:1], "seq", -1)
@@ -588,64 +814,40 @@
     grad_residual = cotangent + norm_back(grad_normed_two, standard_two, scale_two, vectors[:, 16])
     grad_low = grad_residual.astype(BF16)
 
+    lefts = exchange(mixed_rows.reshape(rows, seqs, parts, piece).transpose(2, 0, 1, 3), "wsh")
+    if near:
+        lefts = jnp.stack([lax.dynamic_index_in_dim(lefts, number[0] ^ k, 0, keepdims=False) for k in range(4)])
+    out_part = dot(lefts.reshape(rows * parts, -1), gather_near(grad_low), TN).astype(BF16)
+    grad_out = lax.psum_scatter(out_part, "seq", scatter_dimension=0, tiled=True).astype(F32)
+
     grad_posted = dot(grad_low, w_out, NT).astype(BF16)
     grad_heads = exchange(grad_posted.reshape(rows, seqs, own_width).transpose(1, 0, 2), "seq").reshape(group, own_width)
     recept_low, keys_low, values_low, ups_low, grad_first, grad_vec_heads = run_backward(grad_heads, *inputs, saved)
-    grad_low_all = lax.all_gather(grad_low, "seq", axis=0, tiled=True)
-    hid = [dot(ups_low[k], up[:, o : o + n]) for k, (o, n) in enumerate(zip(OFFSETS, PADDED))]
-    down_lows = [
-        (hid[0] * (1.0 - jnp.square(decay_tanh))).astype(BF16),
-        hid[1].astype(BF16),
-        hid[2].astype(BF16),
-        (hid[3] * gate_sigmoid * (1.0 - gate_sigmoid)).astype(BF16),
-    ]
-    down_cols = [down[:, o : o + n] for o, n in zip(OFFSETS, PADDED)]
-    grad_mix = [
-        dot(recept_low, w_recept, NT),
-        dot(down_lows[0], down_cols[0], NT),
-        dot(keys_low, w_key, NT),
-        dot(values_low, w_value, NT) + dot(down_lows[2], down_cols[2], NT),
-        dot(down_lows[1], down_cols[1], NT),
-        dot(down_lows[3], down_cols[3], NT),
-    ]
-    grad_vec_mix = [jnp.sum(g * delta, 0) for g in grad_mix]
-    kept = sum(g * (1.0 - vectors[:, 2 + c]) for c, g in enumerate(grad_mix))
-    sent = sum(g * vectors[:, 2 + c] for c, g in enumerate(grad_mix)) * flowing
-    grad_normed = kept + jnp.concatenate([sent[1:], jnp.zeros_like(sent[:1])], 0)
-    grad_vec_one = [jnp.sum(grad_normed * standard, 0), jnp.sum(grad_normed, 0)]
-    grad_balanced = norm_back(grad_normed, standard, scale_one, vectors[:, 0])
+    scaled_grad, sums, vec_mix, wide, up_grad = run_unproject(
+        number, balanced, stats, mix_vec, weights, (recept_low, keys_low, values_low), ups_low, hidden, downs, up, parts
+    )
+    standard = (balanced.astype(F32) - mean) * scale_one
+    grad_balanced = scale_one * (scaled_grad - sums[:, :1] * (1.0 / width) - standard * (sums[:, 1:] * (1.0 / width)))
     mine_rows = lax.dynamic_slice_in_dim(grad_balanced, me * rows, rows, 0) + grad_residual
     grad_balanced = lax.dynamic_update_slice_in_dim(grad_balanced, mine_rows, me * rows, 0)
     grad_given = dot(permute, grad_balanced.astype(BF16), TN).astype(BF16)
-    grad_tokens = lax.psum_scatter(grad_given, "seq", scatter_dimension=0, tiled=True)
+    grad_tokens = jnp.sum(exchange(grad_given.reshape(seqs, rows, width), "seq").astype(F32), 0).astype(BF16)
     first_back = exchange(dot(permute, grad_first, TN).astype(BF16).reshape(seqs, rows, own_width), "seq")
     grad_first_rows = first_back.transpose(1, 0, 2).reshape(rows, width)
 
-    wide = jnp.concatenate(
-        [dot(mixed[0], recept_low, TN), dot(mixed[2], keys_low, TN), dot(mixed[3], values_low, TN)]
-        + [dot(mixed[c], l, TN)[:, :r] for c, l, r in zip((1, 4, 3, 5), down_lows, RANKS)],
-        1,
-    ).astype(BF16)
-    ordered = wide.reshape(seqs, parts, piece, -1).transpose(1, 0, 2, 3).reshape(parts * seqs * piece, -1)
-    wide_part = lax.psum_scatter(ordered, "wsh", scatter_dimension=0, tiled=True)
-    wide_all = exchange(wide_part.reshape(seqs, piece, -1), "seq").astype(F32)
-
-    def square(number):
-        taken = wide_all[:, :, number * own_width : (number + 1) * own_width]
+    wide_all = exchange(block_sum(wide).astype(BF16), "seq").astype(F32)
+
+    def square(at):
+        taken = wide_all[:, :, at * own_width : (at + 1) * own_width]
         return taken.transpose(1, 0, 2).reshape(piece, width)
 
-    grad_down = jnp.sum(wide_all[:, :, 3 * own_width :], 0)
-    tall = jnp.concatenate(
-        [dot(mixed_out, grad_low_all, TN)]
-        + [dot(ups_low[k], hidden[:, o : o + r], TN) for k, (o, r) in enumerate(zip(OFFSETS, RANKS))],
-        1,
-    ).astype(BF16)
-    tall_part = lax.psum_scatter(tall, "wsh", scatter_dimension=0, tiled=True).astype(F32)
+    grad_down = unpad_ranks(jnp.sum(wide_all[:, :, 3 * own_width :], 0))
+    up_part = unpad_ranks(block_sum(up_grad.reshape(parts, piece, WIDE)))
 
     heads_part = lax.dynamic_update_slice_in_dim(jnp.zeros((width, 8), F32), grad_vec_heads.T, column, 0)
     grad_vectors = jnp.concatenate(
         [
-            jnp.stack(grad_vec_one + grad_vec_mix, 1),
+            vec_mix.T,
             heads_part,
             jnp.stack([jnp.sum(grad_normed_two * standard_two, 0), jnp.sum(grad_normed_two, 0), grad_vec_mix_two], 1),
         ],
@@ -656,7 +858,7 @@
     return (
         undeal(result), grad_tokens, grad_first_rows,
         square(0), square(1), square(2),
-        tall_part[:, :width], grad_down, tall_part[:, width:],
+        grad_out, grad_down, up_part,
         grad_ffn_key, grad_ffn_value, vec_part,
     )
 

time: 1260 us -> 876 us (0.70)
  waiting for transfers between devices: 549 us -> 417 us
  matrix products: 172 us -> 79 us
  blocking collectives: 74.9 us -> 0 us
  Pallas kernels: 207 us -> 142 us
  other arithmetic: 119 us -> 81.5 us
  starting transfers between devices: 45.5 us -> 80.2 us
  local copies, waits for them, and re-layouts: 67.7 us -> 44.6 us
    reduce_scatter x7 -> x3, waiting for transfers between devices: 368 us -> 183 us  [the longest x1 145 us: local(): lax.psum_scatter(out_part, 'seq', scatter_dimension=0, tiled=True)]
    dot_general x48 -> x19, matrix products: 172 us -> 79 us  [dot(): return lax.dot_general(a, b, dims, preferred_element_type=F32)]
    pallas_call x1, Pallas kernels: 129 us -> 36.6 us  [run_forward(): pl.pallas_call(functools.partial(forward_kernel, count), grid=(rows // st...]
    ppermute x0 -> x22, waiting for transfers between devices: none -> 88.6 us  [swap(): return lax.ppermute(x, 'wsh', [(i, i ^ by) for i in range(size)])]
    all_to_all x2 -> x0, blocking collectives: 67.9 us -> none  [exchange(): return lax.all_to_all(x, axis, split_axis=0, concat_axis=0, tiled=True)]
    all_to_all x7 -> x11, waiting for transfers between devices: 46.4 us -> 106 us  [exchange(): return lax.all_to_all(x, axis, split_axis=0, concat_axis=0, tiled=True)]
    pallas_call x0 -> x2, Pallas kernels: none -> 58.6 us  [the longest x1 39 us: run_unproject(): pl.pallas_call(functools.partial(unproject_kernel, own_width, parts, piec...]
    all_gather x5 -> x0, waiting for transfers between devices: 45.6 us -> none  [the longest x1 22.6 us: local(): cot = lax.all_gather(cotangent.astype(BF16), 'wsh', axis=0, tiled=True)]
  transfers between devices with their start and end apart: 25 -> 42, of which waited for: 19 -> 23; matrix products, arithmetic and copies ran while one was open for 23% -> 18% of each run, Pallas kernels for 17% -> 17%
where the time goes in v2:
time: 876 us; the launch traced here: 860 us
  waiting for transfers between devices  417 us (48%)
  Pallas kernels  142 us (16%)
  other arithmetic  81.5 us (9%)
  starting transfers between devices  80.2 us (9%)
  matrix products  79 us (9%)
  local copies, waits for them, and re-layouts  44.6 us (5%)
  between operations  16.1 us (2%)
    reduce_scatter x1, waiting for transfers between devices, local(): lax.psum_scatter(out_part, 'seq', scatter_dimension=0, tiled=True)  145 us
    all_to_all x11, waiting for transfers between devices, exchange(): return lax.all_to_all(x, axis, split_axis=0, concat_axis=0, tiled=True)  106 us
    ppermute x22, waiting for transfers between devices, swap(): return lax.ppermute(x, 'wsh', [(i, i ^ by) for i in range(size)])  88.6 us
    dot_general x19, matrix products, dot(): return lax.dot_general(a, b, dims, preferred_element_type=F32)  79 us
    all_to_all x11, starting transfers between devices, exchange(): return lax.all_to_all(x, axis, split_axis=0, concat_axis=0, tiled=True)  49.7 us
    pallas_call x1, Pallas kernels, run_backward(): pl.pallas_call(functools.partial(backward_kernel, count), grid=(rows // s...  47.2 us
    pallas_call x1, Pallas kernels, run_unproject(): pl.pallas_call(functools.partial(unproject_kernel, own_width, parts, piec...  39 us
    reduce_scatter x2, waiting for transfers between devices, ffn_grad(): part = lax.psum_scatter(part, 'seq', scatter_dimension=0, tiled=True)  38 us
  transfers between devices with their start and end apart: 42, of which 23 were waited for; matrix products, arithmetic and copies ran while one was open for 18% of the time, Pallas kernels for 17%

profile of v2, /device:TPU:4, one launch (start us, length us, event | category | flops | bytes accessed | tf_op | source)
XLA Modules:
  0.0 860.3 jit_solution(4510344411115012184)
XLA Ops:
  18.8 6.2 all-to-all-start
  25.2 30.5 %collective-permute-done.1 = bf16[512,1664]{1,0:T(8,128)(2,1)} collective-permute-done((bf16[512,1664]{1,0:T(8,128)(2,1)S(1)}, bf16[512,1664]{1,0:T(8,128)(2,1)}, u32[]{:S(2)}, u32[]{:S(2)}) %collective-permute-start.1) | collective-permute-done | bytes 1703968 | tf_op jit(solution)/shard_map/ppermute | solution.py:644
  60.3 5.8 pad_maximum_fusion.weight_ref
  67.9 32.7 %all-gather.3.cloned.1.call-done = bf16[1024,2176]{1,0:T(8,128)(2,1)} async-done(((bf16[128,2176]{1,0:T(8,128)(2,1)}), bf16[1024,2176]{1,0:T(8,128)(2,1)}) %all-gather.3.cloned.1.call-update) | async-done | bytes 4456464 | tf_op jit(solution)/shard_map/all_gather | solution.py:703
  101.9 8.3 convert_reduce_fusion
  115.7 19.7 %mix_project.1 = (f32[1024,256]{1,0:T(8,128)}, f32[1024,256]{1,0:T(8,128)}, f32[1024,256]{1,0:T(8,128)}, f32[1024,640]{1,0:T(8,128)}, bf16[1024,640]{1,0:T(8,128)(2,1)}) custom-call(s32[1]{0:T(128)} %bitcast.4.number_ref, bf16[1024,2048]{1,0:T(8,128)(2,1)} %get-tuple-element.103.block_ref, f32[1024,4]{1,0:T(8,128)} %copy.107.stats_ref, ...), custom_call_target="tpu_custom_call" | custom-call | tf_op jit(solution)/shard_map/mix_project/pallas_call | solution.py:559
  136.6 36.6 %mix_forward.1 = (bf16[1024,256]{1,0:T(8,128)(2,1)S(1)}, bf16[1024,256]{1,0:T(8,128)(2,1)S(1)}, f32[1024,256]{1,0:T(8,128)S(1)}, f32[1024,256]{1,0:T(8,128)S(1)}, f32[1024,256]{1,0:T(8,128)S(1)}) custom-call(f32[1024,256]{1,0:T(8,128)S(1)} %copy-done.3, f32[1024,256]{1,0:T(8,128)} %get-tuple-element.38.keys_ref, f32[1024,256]{1,0:T(8,128)} %get-tuple-element.39.values_ref, ...), custom_call_target="tpu_custom_call" | custom-call | tf_op jit(solution)/shard_map/mix_forward/pallas_call | solution.py:381
  184.9 11.8 %all-to-all-done.1 = bf16[8,128,256]{1,2,0:T(8,128)(2,1)} async-done(((bf16[8,128,256]{1,2,0:T(8,128)(2,1)}), bf16[8,128,256]{1,2,0:T(8,128)(2,1)}, u32[]{:S(2)}, u32[]{:S(2)}) %all-to-all-start.1) | async-done | bytes 524320 | tf_op jit(solution)/shard_map/all_to_all | solution.py:639
  208.0 10.7 %collective-permute-done.5 = bf16[128,2048]{1,0:T(8,128)(2,1)S(1)} collective-permute-done((bf16[128,2048]{1,0:T(8,128)(2,1)S(1)}, bf16[128,2048]{1,0:T(8,128)(2,1)S(1)}, u32[]{:S(2)}, u32[]{:S(2)}) %collective-permute-start.5) | collective-permute-done | bytes 524320 | tf_op jit(solution)/shard_map/ppermute | solution.py:644
  220.6 7.1 fusion.63
  263.8 7.4 collective-permute-done.8
  278.3 11.4 %collective-permute-done.12 = bf16[128,2048]{1,0:T(8,128)(2,1)S(1)} collective-permute-done((bf16[128,2048]{1,0:T(8,128)(2,1)S(1)}, bf16[128,2048]{1,0:T(8,128)(2,1)S(1)}, u32[]{:S(2)}, u32[]{:S(2)}) %collective-permute-start.12) | collective-permute-done | bytes 524320 | tf_op jit(solution)/shard_map/ppermute | solution.py:644
  293.2 6.9 convolution_convert_fusion.1
  300.3 9.7 %multiply_convert_fusion = bf16[512,2048]{1,0:T(8,128)(2,1)S(1)} fusion(f32[512,2048]{1,0:T(8,128)} %copy-done.74, bf16[512,2048]{1,0:T(8,128)(2,1)} %pad_maximum_fusion.4, bf16[2048,2048]{1,0:T(8,128)(2,1)} %param.28), kind=kOutput, calls=%fused_computation.15 | convolution fusion | flops 4299161600 | bytes 16777216 | tf_op jit(solution)/shard_map/dot_general | solution.py:28
  310.0 7.0 fusion.112
  324.9 6.9 convolution_convert_fusion
  331.8 5.6 collective-permute-done.15
  356.2 6.5 all-to-all-start.4
  362.7 27.7 %all-to-all-done.4 = bf16[8,128,256]{2,1,0:T(8,128)(2,1)S(1)} async-done(((bf16[8,128,256]{2,1,0:T(8,128)(2,1)}), bf16[8,128,256]{2,1,0:T(8,128)(2,1)S(1)}, u32[]{:S(2)}, u32[]{:S(2)}) %all-to-all-start.4) | async-done | bytes 524320 | tf_op jit(solution)/shard_map/all_to_all | solution.py:639
  391.6 47.2 %mix_backward.1 = (bf16[1024,256]{1,0:T(8,128)(2,1)S(1)}, bf16[1024,256]{1,0:T(8,128)(2,1)S(1)}, bf16[1024,256]{1,0:T(8,128)(2,1)S(1)}, bf16[4,1024,256]{2,1,0:T...) custom-call(bf16[1024,256]{1,0:T(8,128)(2,1)S(1)} %bitcast.146, f32[1024,256]{1,0:T(8,128)S(1)} %copy-done.3, ...), custom_call_target="tpu_custom_call" | custom-call | tf_op jit(solution)/shard_map/mix_backward/pallas_call | solution.py:408
  441.9 39.0 %mix_unproject.1 = (f32[1024,2048]{1,0:T(8,128)}, f32[1024,2]{1,0:T(8,128)}, f32[8,2048]{1,0:T(8,128)}, bf16[4,8,64,1408]{3,2,1,0:T(8,128)(2,1)}, bf16[256,640]{1,0:T(8,128)(2,1)}) custom-call(s32[1]{0:T(128)} %bitcast.4.number_ref, bf16[1024,2048]{1,0:T(8,128)(2,1)} %get-tuple-element.103.block_ref, f32[1024,4]{1,0:T(8,128)} %copy.107.stats_ref, ...), custom_call_target="tpu_custom_call" | custom-call | tf_op jit(solution)/shard_map/mix_unproject/pallas_call | solution.py:581
  507.8 7.8 all-to-all-done.9
  519.9 27.6 %all-to-all-done.2 = bf16[8,16,2048]{2,1,0:T(8,128)(2,1)S(1)} async-done(((bf16[8,16,2048]{2,1,0:T(8,128)(2,1)}), bf16[8,16,2048]{2,1,0:T(8,128)(2,1)S(1)}, u32[]{:S(2)}, u32[]{:S(2)}) %all-to-all-start.2) | async-done | bytes 524320 | tf_op jit(solution)/shard_map/all_to_all | solution.py:639
  561.8 10.3 %all-to-all-done.6 = bf16[8,128,256]{2,1,0:T(8,128)(2,1)S(1)} async-done(((bf16[8,128,256]{2,1,0:T(8,128)(2,1)}), bf16[8,128,256]{2,1,0:T(8,128)(2,1)S(1)}, u32[]{:S(2)}, u32[]{:S(2)}) %all-to-all-start.6) | async-done | bytes 524320 | tf_op jit(solution)/shard_map/all_to_all | solution.py:639
  576.3 6.2 fusion.5
  582.8 6.3 fusion.12
  589.0 21.1 %all-to-all-done.7 = bf16[8,64,1408]{2,1,0:T(8,128)(2,1)S(1)} async-done(((bf16[8,64,1408]{2,1,0:T(8,128)(2,1)}), bf16[8,64,1408]{2,1,0:T(8,128)(2,1)S(1)}, u32[]{:S(2)}, u32[]{:S(2)}) %all-to-all-start.7) | async-done | bytes 1441824 | tf_op jit(solution)/shard_map/all_to_all | solution.py:639
  616.8 10.9 %collective-permute-done.20 = bf16[128,2048]{1,0:T(8,128)(2,1)S(1)} collective-permute-done((bf16[128,2048]{1,0:T(8,128)(2,1)S(1)}, bf16[128,2048]{1,0:T(8,128)(2,1)S(1)}, u32[]{:S(2)}, u32[]{:S(2)}) %collective-permute-start.20) | collective-permute-done | bytes 524320 | tf_op jit(solution)/shard_map/ppermute | solution.py:644
  638.5 5.6 collective-permute-start.25
  644.1 37.9 %reduce-scatter.6.cloned.1.call-done = bf16[256,2048]{1,0:T(8,128)(2,1)} async-done(((bf16[2048,2048]{1,0:T(8,128)(2,1)}), bf16[256,2048]{1,0:T(8,128)(2,1)}) %reduce-scatter.6.cloned.1.call-update) | async-done | bytes 1048592 | tf_op jit(solution)/shard_map/reduce_scatter | solution.py:801
  682.0 8.0 collective-permute-start.24
  694.3 145.4 %reduce-scatter.4.cloned.1.call-done = bf16[64,2048]{1,0:T(8,128)(2,1)} async-done(((bf16[512,2048]{1,0:T(8,128)(2,1)}), bf16[64,2048]{1,0:T(8,128)(2,1)}) %reduce-scatter.4.cloned.1.call-update) | async-done | bytes 262160 | tf_op jit(solution)/shard_map/reduce_scatter | solution.py:821
  (394 shorter events, 212.4 us)
Async XLA Ops:
  7.2 93.3 %all-gather.3.cloned.1.call-start = ((), (), s32[]{:S(2)}) async-start(), calls=%async_computation.14 | async-start | bytes 5013504 | tf_op jit(solution)/shard_map/all_gather | solution.py:703
  11.3 185.4 %all-gather.5.cloned.1.call-start = ((), (), s32[]{:S(2)}) async-start(), calls=%async_computation.15 | async-start | bytes 10485760 | tf_op jit(solution)/shard_map/all_gather | solution.py:767
  16.6 39.1 %collective-permute-start.1 = (bf16[512,1664]{1,0:T(8,128)(2,1)S(1)}, bf16[512,1664]{1,0:T(8,128)(2,1)}, u32[]{:S(2)}, u32[]{:S(2)}) collective-permute-start(bf16[512,1664]{1,0:T(8,128)(2,1)S(1)} %constant_dynamic-update-slice_fusion), channel_id=1, source_target_pairs={{0,2},{1,3},{2,0},{3,1},{4,6},{5,7},{6,4},{7,5},{8,10},{9,11},{10,... | collective-permute-start | bytes 5111816 | tf_op jit(solution)/shard_map/ppermute | solution.py:644
  16.6 43.6 %collective-permute-start = (bf16[512,1664]{1,0:T(8,128)(2,1)S(1)}, bf16[512,1664]{1,0:T(8,128)(2,1)}, u32[]{:S(2)}, u32[]{:S(2)}) collective-permute-start(bf16[512,1664]{1,0:T(8,128)(2,1)S(1)} %constant_dynamic-update-slice_fusion), channel_id=1, source_target_pairs={{0,1},{1,0},{2,3},{3,2},{4,5},{5,4},{6,7},{7,6},{8,9},{9,8},{10,11... | collective-permute-start | bytes 5111816 | tf_op jit(solution)/shard_map/ppermute | solution.py:644
  18.8 41.3 %all-to-all-start = ((bf16[8,128,256]{1,2,0:T(8,128)(2,1)}), bf16[8,128,256]{1,2,0:T(8,128)(2,1)S(1)}, u32[]{:S(2)}, u32[]{:S(2)}) async-start(bf16[8,128,256]{1,2,0:T(8,128)(2,1)} %bitcast.11), calls=%async_computation | async-start | bytes 1048576 | tf_op jit(solution)/shard_map/all_to_all | solution.py:639
  179.2 17.5 %all-to-all-start.1 = ((bf16[8,128,256]{1,2,0:T(8,128)(2,1)}), bf16[8,128,256]{1,2,0:T(8,128)(2,1)}, u32[]{:S(2)}, u32[]{:S(2)}) async-start(bf16[8,128,256]{1,2,0:T(8,128)(2,1)} %copy.115), calls=%async_computation.1 | async-start | bytes 1048576 | tf_op jit(solution)/shard_map/all_to_all | solution.py:639
  207.6 11.1 %collective-permute-start.5 = (bf16[128,2048]{1,0:T(8,128)(2,1)S(1)}, bf16[128,2048]{1,0:T(8,128)(2,1)S(1)}, u32[]{:S(2)}, u32[]{:S(2)}) collective-permute-start(bf16[128,2048]{1,0:T(8,128)(2,1)S(1)} %add_convert_fusion), channel_id=1, source_target_pairs={{0,2},{1,3},{2,0},{3,1},{4,6},{5,7},{6,4},{7,5},{8,10},{9,11},{10,... | collective-permute-start | bytes 1572872 | tf_op jit(solution)/shard_map/ppermute | solution.py:644
  208.0 10.7 %collective-permute-start.4 = (bf16[128,2048]{1,0:T(8,128)(2,1)S(1)}, bf16[128,2048]{1,0:T(8,128)(2,1)S(1)}, u32[]{:S(2)}, u32[]{:S(2)}) collective-permute-start(bf16[128,2048]{1,0:T(8,128)(2,1)S(1)} %add_convert_fusion), channel_id=1, source_target_pairs={{0,1},{1,0},{2,3},{3,2},{4,5},{5,4},{6,7},{7,6},{8,9},{9,8},{10,11... | collective-permute-start | bytes 1572872 | tf_op jit(solution)/shard_map/ppermute | solution.py:644
  235.0 20.4 %collective-permute-start.7 = (f32[256,2048]{1,0:T(8,128)}, f32[256,2048]{1,0:T(8,128)}, u32[]{:S(2)}, u32[]{:S(2)}) collective-permute-start(f32[256,2048]{1,0:T(8,128)} %pad_maximum_fusion.3), channel_id=1, source_target_pairs={{0,1},{1,0},{2,3},{3,2},{4,5},{5,4},{6,7},{7,6},{8,9},{9,8},{10,11... | collective-permute-start | bytes 6291464 | tf_op jit(solution)/shard_map/ppermute | solution.py:644
  236.9 37.0 %all-to-all-start.3 = ((bf16[8,16,2048]{2,1,0:T(8,128)(2,1)}), bf16[8,16,2048]{2,1,0:T(8,128)(2,1)S(1)}, u32[]{:S(2)}, u32[]{:S(2)}) async-start(bf16[8,16,2048]{2,1,0:T(8,128)(2,1)} %bitcast.158), calls=%async_computation.3 | async-start | bytes 1048576 | tf_op jit(solution)/shard_map/all_to_all | solution.py:639
  242.3 396.2 %reduce-scatter.8.cloned.1.call-start = ((), (), s32[]{:S(2)}) async-start(), calls=%async_computation.18 | async-start | bytes 9437184 | tf_op jit(solution)/shard_map/reduce_scatter | solution.py:801
  257.1 14.1 %collective-permute-start.8 = (bf16[128,2048]{1,0:T(8,128)(2,1)S(1)}, bf16[128,2048]{1,0:T(8,128)(2,1)S(1)}, u32[]{:S(2)}, u32[]{:S(2)}) collective-permute-start(bf16[128,2048]{1,0:T(8,128)(2,1)S(1)} %fusion.40), channel_id=1, source_target_pairs={{0,2},{1,3},{2,0},{3,1},{4,6},{5,7},{6,4},{7,5},{8,10},{9,11},{10,... | collective-permute-start | bytes 1572872 | tf_op jit(solution)/shard_map/ppermute | solution.py:644
  276.6 13.2 %collective-permute-start.12 = (bf16[128,2048]{1,0:T(8,128)(2,1)S(1)}, bf16[128,2048]{1,0:T(8,128)(2,1)S(1)}, u32[]{:S(2)}, u32[]{:S(2)}) collective-permute-start(bf16[128,2048]{1,0:T(8,128)(2,1)S(1)} %get-tuple-element.106), channel_id=1, source_target_pairs={{0,2},{1,3},{2,0},{3,1},{4,6},{5,7},{6,4},{7,5},{8,10},{9,11},{10,... | collective-permute-start | bytes 1572872 | tf_op jit(solution)/shard_map/ppermute | solution.py:644
  278.3 11.4 %collective-permute-start.11 = (bf16[128,2048]{1,0:T(8,128)(2,1)S(1)}, bf16[128,2048]{1,0:T(8,128)(2,1)S(1)}, u32[]{:S(2)}, u32[]{:S(2)}) collective-permute-start(bf16[128,2048]{1,0:T(8,128)(2,1)S(1)} %get-tuple-element.106), channel_id=1, source_target_pairs={{0,1},{1,0},{2,3},{3,2},{4,5},{5,4},{6,7},{7,6},{8,9},{9,8},{10,11... | collective-permute-start | bytes 1572872 | tf_op jit(solution)/shard_map/ppermute | solution.py:644
  300.0 382.0 %reduce-scatter.6.cloned.1.call-start = ((), (), s32[]{:S(2)}) async-start(), calls=%async_computation.17 | async-start | bytes 9437184 | tf_op jit(solution)/shard_map/reduce_scatter | solution.py:801
  323.2 14.2 %collective-permute-start.15 = (bf16[128,2048]{1,0:T(8,128)(2,1)}, bf16[128,2048]{1,0:T(8,128)(2,1)S(1)}, u32[]{:S(2)}, u32[]{:S(2)}) collective-permute-start(bf16[128,2048]{1,0:T(8,128)(2,1)} %fusion.38), channel_id=1, source_target_pairs={{0,2},{1,3},{2,0},{3,1},{4,6},{5,7},{6,4},{7,5},{8,10},{9,11},{10,... | collective-permute-start | bytes 1572872 | tf_op jit(solution)/shard_map/ppermute | solution.py:644
  344.1 5.7 collective-permute-start.16
  356.2 34.2 %all-to-all-start.4 = ((bf16[8,128,256]{2,1,0:T(8,128)(2,1)}), bf16[8,128,256]{2,1,0:T(8,128)(2,1)S(1)}, u32[]{:S(2)}, u32[]{:S(2)}) async-start(bf16[8,128,256]{2,1,0:T(8,128)(2,1)} %bitcast.159), calls=%async_computation.4 | async-start | bytes 1048576 | tf_op jit(solution)/shard_map/all_to_all | solution.py:639
  483.2 9.0 %collective-permute-start.17 = (bf16[2,8,64,1408]{3,2,1,0:T(8,128)(2,1)S(1)}, bf16[2,8,64,1408]{3,2,1,0:T(8,128)(2,1)}, u32[]{:S(2)}, u32[]{:S(2)}) collective-permute-start(bf16[2,8,64,1408]{3,2,1,0:T(8,128)(2,1)S(1)} %pad_maximum_fusion.1), channel_id=1, source_target_pairs={{0,1},{1,0},{2,3},{3,2},{4,5},{5,4},{6,7},{7,6},{8,9},{9,8},{10,11... | collective-permute-start | bytes 8650760 | tf_op jit(solution)/shard_map/ppermute | solution.py:644
  485.2 12.1 %all-to-all-start.8 = ((bf16[4,128,8,64]{1,3,2,0:T(8,128)(2,1)}), bf16[4,128,8,64]{1,3,2,0:T(8,128)(2,1)S(1)}, u32[]{:S(2)}, u32[]{:S(2)}) async-start(bf16[4,128,8,64]{1,3,2,0:T(8,128)(2,1)} %copy.122), calls=%async_computation.8 | async-start | bytes 1048576 | tf_op jit(solution)/shard_map/all_to_all | solution.py:639
  498.0 17.6 %all-to-all-start.9 = ((f32[8,256,19]{1,2,0:T(8,128)}), f32[8,256,19]{1,2,0:T(8,128)S(1)}, u32[]{:S(2)}, u32[]{:S(2)}) async-start(f32[8,256,19]{1,2,0:T(8,128)} %concatenate.75), calls=%async_computation.12 | async-start | bytes 393216 | tf_op jit(solution)/shard_map/all_to_all | solution.py:639
  505.5 51.8 %collective-permute-start.18 = (bf16[8,64,1408]{2,1,0:T(8,128)(2,1)}, bf16[8,64,1408]{2,1,0:T(8,128)(2,1)}, u32[]{:S(2)}, u32[]{:S(2)}) collective-permute-start(bf16[8,64,1408]{2,1,0:T(8,128)(2,1)} %fusion.34), channel_id=1, source_target_pairs={{0,2},{1,3},{2,0},{3,1},{4,6},{5,7},{6,4},{7,5},{8,10},{9,11},{10,... | collective-permute-start | bytes 4325384 | tf_op jit(solution)/shard_map/ppermute | solution.py:644
  515.6 31.9 %all-to-all-start.2 = ((bf16[8,16,2048]{2,1,0:T(8,128)(2,1)}), bf16[8,16,2048]{2,1,0:T(8,128)(2,1)S(1)}, u32[]{:S(2)}, u32[]{:S(2)}) async-start(bf16[8,16,2048]{2,1,0:T(8,128)(2,1)} %bitcast.24), calls=%async_computation.2 | async-start | bytes 1048576 | tf_op jit(solution)/shard_map/all_to_all | solution.py:639
  547.5 6.0 all-to-all-start.10
  553.6 18.5 %all-to-all-start.6 = ((bf16[8,128,256]{2,1,0:T(8,128)(2,1)}), bf16[8,128,256]{2,1,0:T(8,128)(2,1)S(1)}, u32[]{:S(2)}, u32[]{:S(2)}) async-start(bf16[8,128,256]{2,1,0:T(8,128)(2,1)} %bitcast.33), calls=%async_computation.6 | async-start | bytes 1048576 | tf_op jit(solution)/shard_map/all_to_all | solution.py:639
  572.1 38.1 %all-to-all-start.7 = ((bf16[8,64,1408]{2,1,0:T(8,128)(2,1)}), bf16[8,64,1408]{2,1,0:T(8,128)(2,1)S(1)}, u32[]{:S(2)}, u32[]{:S(2)}) async-start(bf16[8,64,1408]{2,1,0:T(8,128)(2,1)} %fusion.21), calls=%async_computation.7 | async-start | bytes 2883584 | tf_op jit(solution)/shard_map/all_to_all | solution.py:639
  610.2 235.1 %all-to-all-start.5 = ((bf16[8,128,2048]{2,1,0:T(8,128)(2,1)}), bf16[8,128,2048]{2,1,0:T(8,128)(2,1)}, u32[]{:S(2)}, u32[]{:S(2)}) async-start(bf16[8,128,2048]{2,1,0:T(8,128)(2,1)} %bitcast.154), calls=%async_computation.5 | async-start | bytes 8388608 | tf_op jit(solution)/shard_map/all_to_all | solution.py:639
  614.9 224.9 %reduce-scatter.4.cloned.1.call-start = ((), (), s32[]{:S(2)}) async-start(), calls=%async_computation.16 | async-start | bytes 2359296 | tf_op jit(solution)/shard_map/reduce_scatter | solution.py:821
  614.9 12.8 %collective-permute-start.20 = (bf16[128,2048]{1,0:T(8,128)(2,1)S(1)}, bf16[128,2048]{1,0:T(8,128)(2,1)S(1)}, u32[]{:S(2)}, u32[]{:S(2)}) collective-permute-start(bf16[128,2048]{1,0:T(8,128)(2,1)S(1)} %copy-done.27), channel_id=1, source_target_pairs={{0,2},{1,3},{2,0},{3,1},{4,6},{5,7},{6,4},{7,5},{8,10},{9,11},{10,... | collective-permute-start | bytes 1572872 | tf_op jit(solution)/shard_map/ppermute | solution.py:644
  616.8 11.5 %collective-permute-start.19 = (bf16[128,2048]{1,0:T(8,128)(2,1)S(1)}, bf16[128,2048]{1,0:T(8,128)(2,1)S(1)}, u32[]{:S(2)}, u32[]{:S(2)}) collective-permute-start(bf16[128,2048]{1,0:T(8,128)(2,1)S(1)} %copy-done.27), channel_id=1, source_target_pairs={{0,1},{1,0},{2,3},{3,2},{4,5},{5,4},{6,7},{7,6},{8,9},{9,8},{10,11... | collective-permute-start | bytes 1572872 | tf_op jit(solution)/shard_map/ppermute | solution.py:644
  638.5 210.7 %collective-permute-start.25 = (bf16[256,2048]{1,0:T(8,128)(2,1)}, bf16[256,2048]{1,0:T(8,128)(2,1)S(1)}, u32[]{:S(2)}, u32[]{:S(2)}) collective-permute-start(bf16[256,2048]{1,0:T(8,128)(2,1)} %reduce-scatter.8.cloned.1.call-done), channel_id=1, source_target_pairs={{0,0},{1,8},{2,16},{3,24},{4,1},{5,9},{6,17},{7,25},{8,2},{9,10},{... | collective-permute-start | bytes 3145736 | tf_op jit(solution)/shard_map/ppermute | solution.py:802
  682.0 168.7 %collective-permute-start.24 = (bf16[256,2048]{1,0:T(8,128)(2,1)}, bf16[256,2048]{1,0:T(8,128)(2,1)}, u32[]{:S(2)}, u32[]{:S(2)}) collective-permute-start(bf16[256,2048]{1,0:T(8,128)(2,1)} %reduce-scatter.6.cloned.1.call-done), channel_id=1, source_target_pairs={{0,0},{1,8},{2,16},{3,24},{4,1},{5,9},{6,17},{7,25},{8,2},{9,10},{... | collective-permute-start | bytes 3145736 | tf_op jit(solution)/shard_map/ppermute | solution.py:802
  (90 other events, 1403.3 us)
Sparse Core Ops, SparseCore 0:
  11.4 89.1 all-gather.2
  102.1 55.3 all-gather.4
  300.2 162.6 reduce-scatter.7
  466.7 215.2 reduce-scatter.5
  686.0 153.6 reduce-scatter.3

commit v3 on v2

--- a/solution.py
+++ b/solution.py
@@ -363,6 +363,10 @@
     vec_out[...] += vec_total
 
 
+def kernel_cost(rows, width, passes):
+    return pl.CostEstimate(flops=2 * rows * width * width, bytes_accessed=4 * rows * width * passes, transcendentals=0)
+
+
 def per_step(rows, most):
     return most if (rows // BLOCK) % most == 0 else 1
 
@@ -389,6 +393,7 @@
         out_shape=[jax.ShapeDtypeStruct((rows, width), d) for d in (BF16, BF16, F32, F32, F32)],
         scratch_shapes=[pltpu.VMEM((BLOCK, width), F32)],
         compiler_params=pltpu.CompilerParams(vmem_limit_bytes=48 << 20),
+        cost_estimate=kernel_cost(rows, width, 110),
         name="mix_forward",
     )(recept, keys, values, hidden, first, up, vec, segments)
 
@@ -425,6 +430,7 @@
         ],
         scratch_shapes=[pltpu.VMEM((BLOCK, width), F32)],
         compiler_params=pltpu.CompilerParams(vmem_limit_bytes=48 << 20),
+        cost_estimate=kernel_cost(rows, width, 150),
         name="mix_backward",
     )(grad, recept, keys, values, hidden, first, up, vec, segments, *saved)
 
@@ -566,6 +572,7 @@
         ),
         out_shape=[jax.ShapeDtypeStruct(s, d) for s, d in zip(shapes, (F32, F32, F32, F32, BF16))],
         compiler_params=pltpu.CompilerParams(vmem_limit_bytes=60 << 20),
+        cost_estimate=kernel_cost(rows, own_width, 60),
         name="mix_project",
     )(number, balanced, stats, vec, weights)
 
@@ -598,6 +605,7 @@
             jax.ShapeDtypeStruct((own_width, WIDE), BF16),
         ],
         compiler_params=pltpu.CompilerParams(vmem_limit_bytes=60 << 20),
+        cost_estimate=kernel_cost(rows, own_width, 120),
         name="mix_unproject",
     )(number, balanced, stats, vec, weights, *lows, ups, hidden, downs, up)
 
@@ -650,6 +658,19 @@
     across = swap(x, 2)
     beside = swap(x, 1)
     return jnp.concatenate([x, beside, across, swap(across, 1)], 0)
+
+
+def beside(x):
+    return lax.ppermute(x, "seq", [(i, i ^ 1) for i in range(lax.axis_size("seq"))])
+
+
+def own_half(x, me):
+    half = x.shape[1] // 2
+    side = me % 2
+    return (
+        lax.dynamic_slice_in_dim(x, side * half, half, 1),
+        beside(lax.dynamic_slice_in_dim(x, (1 - side) * half, half, 1)),
+    )
 
 
 def scalar_sum(x):
@@ -725,7 +746,6 @@
         moved = exchange(back.reshape(seqs, rows // seqs, width), "seq")
         return dot(arrange, moved.reshape(rows, width), TN).astype(BF16)
 
-    target = deal(teacher)
     first_given = exchange(
         first_layer_values.reshape(rows, seqs, own_width).transpose(1, 0, 2), "seq"
     ).reshape(group, own_width)
@@ -774,6 +794,8 @@
     stats = jnp.concatenate([mean, scale_one, flowing, flowing], 1)
     mix_vec = vectors[:, :8].T
     recept, keys, values, downs, hidden = run_project(number, balanced, stats, mix_vec, weights, own_width, parts)
+    teacher_late, recept = lax.optimization_barrier((teacher, recept))
+    target = deal(teacher_late)
     inputs = (recept, keys, values, hidden, first, up, vec, segments)
     mixed_out, *saved = run_forward(*inputs)
 
@@ -795,18 +817,21 @@
     cotangent = (result - target) * (own_valid * (total_tokens / total_valid))[:, None]
     cot = gather_near(cotangent.astype(BF16))
 
-    blocks = [(s * parts + w, w * seqs + s) for s in range(seqs) for w in range(parts)]
-
-    def ffn_grad(part):
-        part = lax.psum_scatter(part, "seq", scatter_dimension=0, tiled=True)
-        return lax.ppermute(part, ("seq", "wsh"), blocks).astype(F32)
-
-    value_part, cot = lax.optimization_barrier((dot(hidden_rows, cot, TN).astype(BF16), cot))
-    grad_ffn_value = ffn_grad(value_part)
+    paired = near and seqs == 8
+    channel_other = beside(channel) if paired else None
+    lefts_hidden = own_half(hidden_rows, me) if paired else (hidden_rows,)
+
+    def token_product(left, right, right_other=None):
+        if not paired:
+            return dot(left[0], right, TN).astype(BF16)
+        other = beside(right) if right_other is None else right_other
+        return (dot(left[0], right, TN) + dot(left[1], other, TN)).astype(BF16)
+
+    value_part = token_product(lefts_hidden, cot)
     grad_pre = (dot(cot, channel_value_weight, NT) * 2.0 * active).astype(BF16)
     channel_part = dot(grad_pre, channel_key_weight)
-    key_part, grad_channel = lax.optimization_barrier((dot(grad_pre, channel, TN).astype(BF16), near_sum(channel_part)))
-    grad_ffn_key = ffn_grad(key_part)
+    grad_channel = near_sum(channel_part)
+    key_part = token_product(own_half(grad_pre, me) if paired else (grad_pre,), channel, channel_other)
     grad_vec_mix_two = jnp.sum(grad_channel * delta_two, 0)
     shifted = grad_channel * vectors[:, 18] * own_flowing
     behind = from_behind(shifted[:1], "seq", -1)
@@ -818,7 +843,38 @@
     if near:
         lefts = jnp.stack([lax.dynamic_index_in_dim(lefts, number[0] ^ k, 0, keepdims=False) for k in range(4)])
     out_part = dot(lefts.reshape(rows * parts, -1), gather_near(grad_low), TN).astype(BF16)
-    grad_out = lax.psum_scatter(out_part, "seq", scatter_dimension=0, tiled=True).astype(F32)
+    if paired:
+        halves_out = out_part.reshape(seqs // 2, 2, piece, width)
+        x_side = me % 2
+        out_mine = lax.dynamic_index_in_dim(halves_out, x_side, 1, keepdims=False).astype(F32)
+        out_other = beside(lax.dynamic_index_in_dim(halves_out, 1 - x_side, 1, keepdims=False))
+        out_half = (out_mine + out_other.astype(F32)).astype(BF16)
+        lines = [[0, 2, 4, 6], [1, 3, 5, 7]]
+        turned = [
+            ((z * 2 + x) * 4 + w, (w * 2 + x) * 4 + z) for z in range(4) for x in range(2) for w in range(4)
+        ]
+
+        def along(part):
+            return lax.psum_scatter(part, "seq", scatter_dimension=0, tiled=True, axis_index_groups=lines)
+
+        def turn(part):
+            return lax.ppermute(part, ("seq", "wsh"), turned).astype(F32)
+
+        grad_ffn_value = turn(along(value_part))
+        both_parts = along(
+            jnp.concatenate([key_part.reshape(4, -1, width), out_half], 1).reshape(-1, width)
+        )
+        grad_ffn_key = turn(both_parts[:-piece])
+        grad_out = both_parts[-piece:].astype(F32)
+    else:
+        moves = [(s * parts + w, w * seqs + s) for s in range(seqs) for w in range(parts)]
+
+        def ffn_grad(part):
+            part = lax.psum_scatter(part, "seq", scatter_dimension=0, tiled=True)
+            return lax.ppermute(part, ("seq", "wsh"), moves).astype(F32)
+
+        grad_ffn_value, grad_ffn_key = ffn_grad(value_part), ffn_grad(key_part)
+        grad_out = lax.psum_scatter(out_part, "seq", scatter_dimension=0, tiled=True).astype(F32)
 
     grad_posted = dot(grad_low, w_out, NT).astype(BF16)
     grad_heads = exchange(grad_posted.reshape(rows, seqs, own_width).transpose(1, 0, 2), "seq").reshape(group, own_width)

time: 876 us -> 971 us (1.11)
  starting transfers between devices: 80.2 us -> 117 us
  matrix products: 79 us -> 99.8 us
  local copies, waits for them, and re-layouts: 44.6 us -> 58.7 us
  waiting for transfers between devices: 417 us -> 431 us
  other arithmetic: 81.5 us -> 94.1 us
    reduce_scatter x3 -> x2, waiting for transfers between devices: 183 us -> 0.04 us  [along(): lax.psum_scatter(part, 'seq', scatter_dimension=0, tiled=True, axis_index...]
    ppermute x2 -> x7, waiting for transfers between devices: 0.01 us -> 148 us  [the longest x2 81.4 us: turn(): return lax.ppermute(part, ('seq', 'wsh'), turned).astype(F32)]
    all_to_all x11, waiting for transfers between devices: 106 us -> 175 us  [exchange(): return lax.all_to_all(x, axis, split_axis=0, concat_axis=0, tiled=True)]
    ppermute x2 -> x7, starting transfers between devices: 13.6 us -> 42 us  [the longest x2 34.9 us: turn(): return lax.ppermute(part, ('seq', 'wsh'), turned).astype(F32)]
    dot_general x19 -> x21, matrix products: 79 us -> 99.8 us  [dot(): return lax.dot_general(a, b, dims, preferred_element_type=F32)]
    ppermute x22, waiting for transfers between devices: 88.6 us -> 74.7 us  [swap(): return lax.ppermute(x, 'wsh', [(i, i ^ by) for i in range(size)])]
    unnamed x175 -> x201, local copies, waits for them, and re-layouts: 18.2 us -> 24.6 us
  transfers between devices with their start and end apart: 42 -> 46, of which waited for: 23 -> 21; matrix products, arithmetic and copies ran while one was open for 18% -> 18% of each run, Pallas kernels for 17% -> 15%
where the time goes in v3:
time: 971 us; the launch traced here: 960 us
  waiting for transfers between devices  431 us (44%)
  Pallas kernels  142 us (15%)
  starting transfers between devices  117 us (12%)
  matrix products  99.8 us (10%)
  other arithmetic  94.1 us (10%)
  local copies, waits for them, and re-layouts  58.7 us (6%)
  between operations  16.6 us (2%)
    all_to_all x11, waiting for transfers between devices, exchange(): return lax.all_to_all(x, axis, split_axis=0, concat_axis=0, tiled=True)  175 us
    dot_general x21, matrix products, dot(): return lax.dot_general(a, b, dims, preferred_element_type=F32)  99.8 us
    ppermute x2, waiting for transfers between devices, turn(): return lax.ppermute(part, ('seq', 'wsh'), turned).astype(F32)  81.4 us
    ppermute x22, waiting for transfers between devices, swap(): return lax.ppermute(x, 'wsh', [(i, i ^ by) for i in range(size)])  74.7 us
    ppermute x5, waiting for transfers between devices, beside(): lax.ppermute(x, 'seq', [(i, i ^ 1) for i in range(lax.axis_size('seq'))])  66.4 us
    all_to_all x11, starting transfers between devices, exchange(): return lax.all_to_all(x, axis, split_axis=0, concat_axis=0, tiled=True)  57.5 us
    pallas_call x1, Pallas kernels, run_backward(): pl.pallas_call(functools.partial(backward_kernel, count), grid=(rows // s...  47.1 us
    pallas_call x1, Pallas kernels, run_unproject(): pl.pallas_call(functools.partial(unproject_kernel, own_width, parts, piec...  38.9 us
  transfers between devices with their start and end apart: 46, of which 21 were waited for; matrix products, arithmetic and copies ran while one was open for 18% of the time, Pallas kernels for 15%

profile of v3, /device:TPU:4, one launch (start us, length us, event | category | flops | bytes accessed | tf_op | source)
XLA Modules:
  0.0 959.6 jit_solution(14524733344794611629)
XLA Ops:
  18.8 6.2 all-to-all-start
  25.2 30.5 %collective-permute-done.1 = bf16[512,1664]{1,0:T(8,128)(2,1)} collective-permute-done((bf16[512,1664]{1,0:T(8,128)(2,1)S(1)}, bf16[512,1664]{1,0:T(8,128)(2,1)}, u32[]{:S(2)}, u32[]{:S(2)}) %collective-permute-start.1) | collective-permute-done | bytes 1703968 | tf_op jit(solution)/shard_map/ppermute | solution.py:652
  67.9 32.7 %all-gather.3.cloned.1.call-done = bf16[1024,2176]{1,0:T(8,128)(2,1)} async-done(((bf16[128,2176]{1,0:T(8,128)(2,1)}), bf16[1024,2176]{1,0:T(8,128)(2,1)}) %all-gather.3.cloned.1.call-update) | async-done | bytes 4456464 | tf_op jit(solution)/shard_map/all_gather | solution.py:724
  101.9 8.3 convert_reduce_fusion
  115.7 19.7 %mix_project.1 = (f32[1024,256]{1,0:T(8,128)}, f32[1024,256]{1,0:T(8,128)}, f32[1024,256]{1,0:T(8,128)}, f32[1024,640]{1,0:T(8,128)}, bf16[1024,640]{1,0:T(8,128)(2,1)}) custom-call(s32[1]{0:T(128)} %bitcast.4.number_ref, bf16[1024,2048]{1,0:T(8,128)(2,1)} %get-tuple-element.99.block_ref, f32[1024,4]{1,0:T(8,128)} %copy.112.stats_ref, ...), custom_call_target="tpu_custom_call" | custom-call | flops 134217728 | bytes 62914560 | tf_op jit(solution)/shard_map/mix_project/pallas_call | solution.py:565
  136.6 36.3 %mix_forward.1 = (bf16[1024,256]{1,0:T(8,128)(2,1)S(1)}, bf16[1024,256]{1,0:T(8,128)(2,1)S(1)}, f32[1024,256]{1,0:T(8,128)S(1)}, f32[1024,256]{1,0:T(8,128)S(1)}, f32[1024,256]{1,0:T(8,128)S(1)}) custom-call(f32[1024,256]{1,0:T(8,128)S(1)} %copy-done.3, f32[1024,256]{1,0:T(8,128)} %get-tuple-element.37.keys_ref, f32[1024,256]{1,0:T(8,128)} %get-tuple-element.38.values_ref, ...), custom_call_target="tpu_custom_call" | custom-call | flops 134217728 | bytes 115343360 | tf_op jit(solution)/shard_map/mix_forward/pallas_call | solution.py:385
  184.6 11.8 %all-to-all-done.1 = bf16[8,128,256]{1,2,0:T(8,128)(2,1)} async-done(((bf16[8,128,256]{1,2,0:T(8,128)(2,1)}), bf16[8,128,256]{1,2,0:T(8,128)(2,1)}, u32[]{:S(2)}, u32[]{:S(2)}) %all-to-all-start.1) | async-done | bytes 524320 | tf_op jit(solution)/shard_map/all_to_all | solution.py:647
  207.7 10.7 %collective-permute-done.5 = bf16[128,2048]{1,0:T(8,128)(2,1)S(1)} collective-permute-done((bf16[128,2048]{1,0:T(8,128)(2,1)S(1)}, bf16[128,2048]{1,0:T(8,128)(2,1)S(1)}, u32[]{:S(2)}, u32[]{:S(2)}) %collective-permute-start.5) | collective-permute-done | bytes 524320 | tf_op jit(solution)/shard_map/ppermute | solution.py:652
  220.3 11.3 %multiply_convert_fusion.1 = (bf16[512,2048]{1,0:T(8,128)(2,1)S(1)}, f32[512,2048]{1,0:T(8,128)}) fusion(bf16[2048,2048]{1,0:T(8,128)(2,1)} %param.27, bf16[128,2048]{1,0:T(8,128)(2,1)S(1)} %collective-permute-done.6, bf16[128,2048]{1,0:T(8,128)(2,1)S(1)} %collective-permute-done.5, bf16[128,2048]{1,0:T(8,128)(2,1)S(1)} %collective-permute-done.4, ...), kind=kOutput, calls=%fused_computation.17 | convolution fusion | flops 4306501632 | bytes 16777216 | tf_op jit(solution)/shard_map/dot_general | solution.py:28
  267.6 7.4 collective-permute-done.8
  282.0 11.4 %collective-permute-done.12 = bf16[128,2048]{1,0:T(8,128)(2,1)S(1)} collective-permute-done((bf16[128,2048]{1,0:T(8,128)(2,1)S(1)}, bf16[128,2048]{1,0:T(8,128)(2,1)S(1)}, u32[]{:S(2)}, u32[]{:S(2)}) %collective-permute-start.12) | collective-permute-done | bytes 524320 | tf_op jit(solution)/shard_map/ppermute | solution.py:652
  295.4 10.6 %multiply_convert_fusion = bf16[512,2048]{1,0:T(8,128)(2,1)S(1)} fusion(f32[512,2048]{1,0:T(8,128)} %get-tuple-element.103, bf16[2048,2048]{1,0:T(8,128)(2,1)} %param.28, bf16[128,2048]{1,0:T(8,128)(2,1)S(1)} %collective-permute-done.13, bf16[128,2048]{1,0:T(8,128)(2,1)S(1)} %collective-permute-done.12, bf16[128,2048]{1,0:T(8,128)(2,1)S(1)} %collective-permute-done.11, ...), kind=kOutput, calls=%fused_computation.16 | convolution fusion | flops 4307550208 | bytes 16777216 | tf_op jit(solution)/shard_map/dot_general | solution.py:28
  306.0 7.6 fusion.114
  327.9 61.1 %collective-permute-done.28 = bf16[512,1024]{1,0:T(8,128)(2,1)} collective-permute-done((bf16[512,1024]{1,0:T(8,128)(2,1)}, bf16[512,1024]{1,0:T(8,128)(2,1)}, u32[]{:S(2)}, u32[]{:S(2)}) %collective-permute-start.28) | collective-permute-done | bytes 1048608 | tf_op jit(solution)/shard_map/ppermute | solution.py:664
  410.2 6.4 convolution_convert_fusion.1
  417.5 8.4 all-to-all-start.4
  431.1 23.5 %all-to-all-done.4 = bf16[8,128,256]{2,1,0:T(8,128)(2,1)S(1)} async-done(((bf16[8,128,256]{2,1,0:T(8,128)(2,1)}), bf16[8,128,256]{2,1,0:T(8,128)(2,1)S(1)}, u32[]{:S(2)}, u32[]{:S(2)}) %all-to-all-start.4) | async-done | bytes 524320 | tf_op jit(solution)/shard_map/all_to_all | solution.py:647
  455.7 47.1 %mix_backward.1 = (bf16[1024,256]{1,0:T(8,128)(2,1)S(1)}, bf16[1024,256]{1,0:T(8,128)(2,1)S(1)}, bf16[1024,256]{1,0:T(8,128)(2,1)S(1)}, bf16[4,1024,256]{2,1,0:T...) custom-call(bf16[1024,256]{1,0:T(8,128)(2,1)S(1)} %bitcast.159, f32[1024,256]{1,0:T(8,128)S(1)} %copy-done.3, ...), custom_call_target="tpu_custom_call" | custom-call | flops 134217728 | bytes 157286400 | tf_op jit(solution)/shard_map/mix_backward/pallas_call | solution.py:413
  506.0 38.9 %mix_unproject.1 = (f32[1024,2048]{1,0:T(8,128)}, f32[1024,2]{1,0:T(8,128)}, f32[8,2048]{1,0:T(8,128)}, bf16[4,8,64,1408]{3,2,1,0:T(8,128)(2,1)}, bf16[256,640]{1,0:T(8,128)(2,1)}) custom-call(s32[1]{0:T(128)} %bitcast.4.number_ref, bf16[1024,2048]{1,0:T(8,128)(2,1)} %get-tuple-element.99.block_ref, f32[1024,4]{1,0:T(8,128)} %copy.112.stats_ref, ...), custom_call_target="tpu_custom_call" | custom-call | flops 134217728 | bytes 125829120 | tf_op jit(solution)/shard_map/mix_unproject/pallas_call | solution.py:588
  552.2 6.0 all-to-all-start.8
  558.4 7.3 all-to-all-done.8
  569.0 7.8 collective-permute-done.22
  576.8 7.6 fusion.115
  611.2 8.6 add_convert_fusion.1
  640.1 5.9 all-to-all-start.6
  650.3 27.2 %all-to-all-done.6 = bf16[8,128,256]{2,1,0:T(8,128)(2,1)S(1)} async-done(((bf16[8,128,256]{2,1,0:T(8,128)(2,1)}), bf16[8,128,256]{2,1,0:T(8,128)(2,1)S(1)}, u32[]{:S(2)}, u32[]{:S(2)}) %all-to-all-start.6) | async-done | bytes 524320 | tf_op jit(solution)/shard_map/all_to_all | solution.py:647
  688.0 6.2 fusion.12
  694.3 58.6 %all-to-all-done.7 = bf16[8,64,1408]{2,1,0:T(8,128)(2,1)S(1)} async-done(((bf16[8,64,1408]{2,1,0:T(8,128)(2,1)}), bf16[8,64,1408]{2,1,0:T(8,128)(2,1)S(1)}, u32[]{:S(2)}, u32[]{:S(2)}) %all-to-all-start.7) | async-done | bytes 1441824 | tf_op jit(solution)/shard_map/all_to_all | solution.py:647
  781.2 29.0 %collective-permute-start.27 = (bf16[256,2048]{1,0:T(8,128)(2,1)}, bf16[256,2048]{1,0:T(8,128)(2,1)}, u32[]{:S(2)}, u32[]{:S(2)}) collective-permute-start(bf16[256,2048]{1,0:T(8,128)(2,1)} %slice.321), channel_id=1, source_target_pairs={{0,0},{1,8},{2,16},{3,24},{4,4},{5,12},{6,20},{7,28},{8,1},{9,9},{... | collective-permute-start | bytes 3145736 | tf_op jit(solution)/shard_map/ppermute | solution.py:861
  813.7 46.2 %all-to-all-done.5 = bf16[8,128,2048]{2,1,0:T(8,128)(2,1)} async-done(((bf16[8,128,2048]{2,1,0:T(8,128)(2,1)}), bf16[8,128,2048]{2,1,0:T(8,128)(2,1)}, u32[]{:S(2)}, u32[]{:S(2)}) %all-to-all-start.5) | async-done | bytes 4194336 | tf_op jit(solution)/shard_map/all_to_all | solution.py:647
  863.8 65.7 %collective-permute-done.30 = bf16[256,2048]{1,0:T(8,128)(2,1)} collective-permute-done((bf16[256,2048]{1,0:T(8,128)(2,1)}, bf16[256,2048]{1,0:T(8,128)(2,1)}, u32[]{:S(2)}, u32[]{:S(2)}) %collective-permute-start.30) | collective-permute-done | bytes 1048608 | tf_op jit(solution)/shard_map/ppermute | solution.py:861
  934.1 15.7 %collective-permute-done.27 = bf16[256,2048]{1,0:T(8,128)(2,1)} collective-permute-done((bf16[256,2048]{1,0:T(8,128)(2,1)}, bf16[256,2048]{1,0:T(8,128)(2,1)}, u32[]{:S(2)}, u32[]{:S(2)}) %collective-permute-start.27) | collective-permute-done | bytes 1048608 | tf_op jit(solution)/shard_map/ppermute | solution.py:861
  (437 shorter events, 261.0 us)
Async XLA Ops:
  7.2 93.3 %all-gather.3.cloned.1.call-start = ((), (), s32[]{:S(2)}) async-start(), calls=%async_computation.13 | async-start | bytes 5013504 | tf_op jit(solution)/shard_map/all_gather | solution.py:724
  11.3 185.1 %all-gather.5.cloned.1.call-start = ((), (), s32[]{:S(2)}) async-start(), calls=%async_computation.14 | async-start | bytes 10485760 | tf_op jit(solution)/shard_map/all_gather | solution.py:787
  16.6 39.1 %collective-permute-start.1 = (bf16[512,1664]{1,0:T(8,128)(2,1)S(1)}, bf16[512,1664]{1,0:T(8,128)(2,1)}, u32[]{:S(2)}, u32[]{:S(2)}) collective-permute-start(bf16[512,1664]{1,0:T(8,128)(2,1)S(1)} %constant_dynamic-update-slice_fusion), channel_id=1, source_target_pairs={{0,2},{1,3},{2,0},{3,1},{4,6},{5,7},{6,4},{7,5},{8,10},{9,11},{10,... | collective-permute-start | bytes 5111816 | tf_op jit(solution)/shard_map/ppermute | solution.py:652
  16.6 43.6 %collective-permute-start = (bf16[512,1664]{1,0:T(8,128)(2,1)S(1)}, bf16[512,1664]{1,0:T(8,128)(2,1)}, u32[]{:S(2)}, u32[]{:S(2)}) collective-permute-start(bf16[512,1664]{1,0:T(8,128)(2,1)S(1)} %constant_dynamic-update-slice_fusion), channel_id=1, source_target_pairs={{0,1},{1,0},{2,3},{3,2},{4,5},{5,4},{6,7},{7,6},{8,9},{9,8},{10,11... | collective-permute-start | bytes 5111816 | tf_op jit(solution)/shard_map/ppermute | solution.py:652
  18.8 41.3 %all-to-all-start = ((bf16[8,128,256]{1,2,0:T(8,128)(2,1)}), bf16[8,128,256]{1,2,0:T(8,128)(2,1)S(1)}, u32[]{:S(2)}, u32[]{:S(2)}) async-start(bf16[8,128,256]{1,2,0:T(8,128)(2,1)} %bitcast.11), calls=%async_computation | async-start | bytes 1048576 | tf_op jit(solution)/shard_map/all_to_all | solution.py:647
  178.9 17.5 %all-to-all-start.1 = ((bf16[8,128,256]{1,2,0:T(8,128)(2,1)}), bf16[8,128,256]{1,2,0:T(8,128)(2,1)}, u32[]{:S(2)}, u32[]{:S(2)}) async-start(bf16[8,128,256]{1,2,0:T(8,128)(2,1)} %copy.120), calls=%async_computation.1 | async-start | bytes 1048576 | tf_op jit(solution)/shard_map/all_to_all | solution.py:647
  238.8 20.4 %collective-permute-start.7 = (f32[256,2048]{1,0:T(8,128)}, f32[256,2048]{1,0:T(8,128)}, u32[]{:S(2)}, u32[]{:S(2)}) collective-permute-start(f32[256,2048]{1,0:T(8,128)} %pad_maximum_fusion.4), channel_id=1, source_target_pairs={{0,1},{1,0},{2,3},{3,2},{4,5},{5,4},{6,7},{7,6},{8,9},{9,8},{10,11... | collective-permute-start | bytes 6291464 | tf_op jit(solution)/shard_map/ppermute | solution.py:652
  241.4 36.4 %all-to-all-start.3 = ((bf16[8,16,2048]{2,1,0:T(8,128)(2,1)}), bf16[8,16,2048]{2,1,0:T(8,128)(2,1)S(1)}, u32[]{:S(2)}, u32[]{:S(2)}) async-start(bf16[8,16,2048]{2,1,0:T(8,128)(2,1)} %bitcast.173), calls=%async_computation.3 | async-start | bytes 1048576 | tf_op jit(solution)/shard_map/all_to_all | solution.py:647
  246.7 521.0 %reduce-scatter.5.cloned.1.call-start = ((), (), s32[]{:S(2)}) async-start(), calls=%async_computation.16 | async-start | bytes 5242880 | tf_op jit(solution)/shard_map/reduce_scatter | solution.py:858
  260.9 14.1 %collective-permute-start.8 = (bf16[128,2048]{1,0:T(8,128)(2,1)S(1)}, bf16[128,2048]{1,0:T(8,128)(2,1)S(1)}, u32[]{:S(2)}, u32[]{:S(2)}) collective-permute-start(bf16[128,2048]{1,0:T(8,128)(2,1)S(1)} %fusion.41), channel_id=1, source_target_pairs={{0,2},{1,3},{2,0},{3,1},{4,6},{5,7},{6,4},{7,5},{8,10},{9,11},{10,... | collective-permute-start | bytes 1572872 | tf_op jit(solution)/shard_map/ppermute | solution.py:652
  280.3 13.2 %collective-permute-start.12 = (bf16[128,2048]{1,0:T(8,128)(2,1)S(1)}, bf16[128,2048]{1,0:T(8,128)(2,1)S(1)}, u32[]{:S(2)}, u32[]{:S(2)}) collective-permute-start(bf16[128,2048]{1,0:T(8,128)(2,1)S(1)} %get-tuple-element.104), channel_id=1, source_target_pairs={{0,2},{1,3},{2,0},{3,1},{4,6},{5,7},{6,4},{7,5},{8,10},{9,11},{10,... | collective-permute-start | bytes 1572872 | tf_op jit(solution)/shard_map/ppermute | solution.py:652
  318.0 71.0 %collective-permute-start.29 = (bf16[512,2048]{1,0:T(8,128)(2,1)}, bf16[512,2048]{1,0:T(8,128)(2,1)}, u32[]{:S(2)}, u32[]{:S(2)}) collective-permute-start(bf16[512,2048]{1,0:T(8,128)(2,1)} %pad_maximum_fusion.5), channel_id=1, source_target_pairs={{0,4},{4,0},{8,12},{12,8},{16,20},{20,16},{24,28},{28,24},{1,5},{5... | collective-permute-start | bytes 6291464 | tf_op jit(solution)/shard_map/ppermute | solution.py:664
  322.4 66.6 %collective-permute-start.28 = (bf16[512,1024]{1,0:T(8,128)(2,1)}, bf16[512,1024]{1,0:T(8,128)(2,1)}, u32[]{:S(2)}, u32[]{:S(2)}) collective-permute-start(bf16[512,1024]{1,0:T(8,128)(2,1)} %constant_dynamic-slice_fusion), channel_id=1, source_target_pairs={{0,4},{4,0},{8,12},{12,8},{16,20},{20,16},{24,28},{28,24},{1,5},{5... | collective-permute-start | bytes 3145736 | tf_op jit(solution)/shard_map/ppermute | solution.py:664
  324.9 68.5 %collective-permute-start.15 = (bf16[128,2048]{1,0:T(8,128)(2,1)}, bf16[128,2048]{1,0:T(8,128)(2,1)}, u32[]{:S(2)}, u32[]{:S(2)}) collective-permute-start(bf16[128,2048]{1,0:T(8,128)(2,1)} %fusion.39), channel_id=1, source_target_pairs={{0,2},{1,3},{2,0},{3,1},{4,6},{5,7},{6,4},{7,5},{8,10},{9,11},{10,... | collective-permute-start | bytes 1572872 | tf_op jit(solution)/shard_map/ppermute | solution.py:652
  417.5 37.1 %all-to-all-start.4 = ((bf16[8,128,256]{2,1,0:T(8,128)(2,1)}), bf16[8,128,256]{2,1,0:T(8,128)(2,1)S(1)}, u32[]{:S(2)}, u32[]{:S(2)}) async-start(bf16[8,128,256]{2,1,0:T(8,128)(2,1)} %bitcast.174), calls=%async_computation.4 | async-start | bytes 1048576 | tf_op jit(solution)/shard_map/all_to_all | solution.py:647
  429.1 147.7 %collective-permute-start.20 = (bf16[512,2048]{1,0:T(8,128)(2,1)}, bf16[512,2048]{1,0:T(8,128)(2,1)}, u32[]{:S(2)}, u32[]{:S(2)}) collective-permute-start(bf16[512,2048]{1,0:T(8,128)(2,1)} %pad_maximum_fusion.3), channel_id=1, source_target_pairs={{0,4},{4,0},{8,12},{12,8},{16,20},{20,16},{24,28},{28,24},{1,5},{5... | collective-permute-start | bytes 6291464 | tf_op jit(solution)/shard_map/ppermute | solution.py:664
  548.8 48.4 %collective-permute-start.17 = (bf16[2,8,64,1408]{3,2,1,0:T(8,128)(2,1)}, bf16[2,8,64,1408]{3,2,1,0:T(8,128)(2,1)}, u32[]{:S(2)}, u32[]{:S(2)}) collective-permute-start(bf16[2,8,64,1408]{3,2,1,0:T(8,128)(2,1)} %pad_maximum_fusion.2), channel_id=1, source_target_pairs={{0,1},{1,0},{2,3},{3,2},{4,5},{5,4},{6,7},{7,6},{8,9},{9,8},{10,11... | collective-permute-start | bytes 8650760 | tf_op jit(solution)/shard_map/ppermute | solution.py:652
  549.3 27.5 %collective-permute-start.19 = (bf16[512,1024]{1,0:T(8,128)(2,1)S(1)}, bf16[512,1024]{1,0:T(8,128)(2,1)}, u32[]{:S(2)}, u32[]{:S(2)}) collective-permute-start(bf16[512,1024]{1,0:T(8,128)(2,1)S(1)} %constant_dynamic-slice_fusion.7), channel_id=1, source_target_pairs={{0,4},{4,0},{8,12},{12,8},{16,20},{20,16},{24,28},{28,24},{1,5},{5... | collective-permute-start | bytes 3145736 | tf_op jit(solution)/shard_map/ppermute | solution.py:664
  552.2 13.4 %all-to-all-start.8 = ((bf16[4,128,8,64]{1,3,2,0:T(8,128)(2,1)}), bf16[4,128,8,64]{1,3,2,0:T(8,128)(2,1)S(1)}, u32[]{:S(2)}, u32[]{:S(2)}) async-start(bf16[4,128,8,64]{1,3,2,0:T(8,128)(2,1)} %copy.127), calls=%async_computation.8 | async-start | bytes 1048576 | tf_op jit(solution)/shard_map/all_to_all | solution.py:647
  558.3 18.5 %collective-permute-start.22 = (bf16[128,2048]{1,0:T(8,128)(2,1)S(1)}, bf16[128,2048]{1,0:T(8,128)(2,1)}, u32[]{:S(2)}, u32[]{:S(2)}) collective-permute-start(bf16[128,2048]{1,0:T(8,128)(2,1)S(1)} %copy-done.31), channel_id=1, source_target_pairs={{0,2},{1,3},{2,0},{3,1},{4,6},{5,7},{6,4},{7,5},{8,10},{9,11},{10,... | collective-permute-start | bytes 1572872 | tf_op jit(solution)/shard_map/ppermute | solution.py:652
  568.9 20.9 %collective-permute-start.21 = (bf16[128,2048]{1,0:T(8,128)(2,1)S(1)}, bf16[128,2048]{1,0:T(8,128)(2,1)S(1)}, u32[]{:S(2)}, u32[]{:S(2)}) collective-permute-start(bf16[128,2048]{1,0:T(8,128)(2,1)S(1)} %copy-done.31), channel_id=1, source_target_pairs={{0,1},{1,0},{2,3},{3,2},{4,5},{5,4},{6,7},{7,6},{8,9},{9,8},{10,11... | collective-permute-start | bytes 1572872 | tf_op jit(solution)/shard_map/ppermute | solution.py:652
  576.8 13.1 %collective-permute-start.23 = (bf16[128,2048]{1,0:T(8,128)(2,1)}, bf16[128,2048]{1,0:T(8,128)(2,1)S(1)}, u32[]{:S(2)}, u32[]{:S(2)}) collective-permute-start(bf16[128,2048]{1,0:T(8,128)(2,1)} %collective-permute-done.22), channel_id=1, source_target_pairs={{0,1},{1,0},{2,3},{3,2},{4,5},{5,4},{6,7},{7,6},{8,9},{9,8},{10,11... | collective-permute-start | bytes 1572872 | tf_op jit(solution)/shard_map/ppermute | solution.py:652
  586.4 20.2 %all-to-all-start.9 = ((f32[8,256,19]{1,2,0:T(8,128)}), f32[8,256,19]{1,2,0:T(8,128)S(1)}, u32[]{:S(2)}, u32[]{:S(2)}) async-start(f32[8,256,19]{1,2,0:T(8,128)} %concatenate.79), calls=%async_computation.11 | async-start | bytes 393216 | tf_op jit(solution)/shard_map/all_to_all | solution.py:647
  595.2 30.6 %collective-permute-start.24 = (bf16[4,64,2048]{2,1,0:T(8,128)(2,1)}, bf16[4,64,2048]{2,1,0:T(8,128)(2,1)}, u32[]{:S(2)}, u32[]{:S(2)}) collective-permute-start(bf16[4,64,2048]{2,1,0:T(8,128)(2,1)} %dynamic-slice_bitcast_fusion), channel_id=1, source_target_pairs={{0,4},{4,0},{8,12},{12,8},{16,20},{20,16},{24,28},{28,24},{1,5},{5... | collective-permute-start | bytes 3145736 | tf_op jit(solution)/shard_map/ppermute | solution.py:664
  604.9 41.1 %collective-permute-start.18 = (bf16[8,64,1408]{2,1,0:T(8,128)(2,1)}, bf16[8,64,1408]{2,1,0:T(8,128)(2,1)}, u32[]{:S(2)}, u32[]{:S(2)}) collective-permute-start(bf16[8,64,1408]{2,1,0:T(8,128)(2,1)} %fusion.35), channel_id=1, source_target_pairs={{0,2},{1,3},{2,0},{3,1},{4,6},{5,7},{6,4},{7,5},{8,10},{9,11},{10,... | collective-permute-start | bytes 4325384 | tf_op jit(solution)/shard_map/ppermute | solution.py:652
  606.6 26.4 %all-to-all-start.2 = ((bf16[8,16,2048]{2,1,0:T(8,128)(2,1)}), bf16[8,16,2048]{2,1,0:T(8,128)(2,1)S(1)}, u32[]{:S(2)}, u32[]{:S(2)}) async-start(bf16[8,16,2048]{2,1,0:T(8,128)(2,1)} %bitcast.24), calls=%async_computation.2 | async-start | bytes 1048576 | tf_op jit(solution)/shard_map/all_to_all | solution.py:647
  611.1 167.8 %reduce-scatter.3.cloned.1.call-start = ((), (), s32[]{:S(2)}) async-start(), calls=%async_computation.15 | async-start | bytes 6553600 | tf_op jit(solution)/shard_map/reduce_scatter | solution.py:858
  640.1 37.4 %all-to-all-start.6 = ((bf16[8,128,256]{2,1,0:T(8,128)(2,1)}), bf16[8,128,256]{2,1,0:T(8,128)(2,1)S(1)}, u32[]{:S(2)}, u32[]{:S(2)}) async-start(bf16[8,128,256]{2,1,0:T(8,128)(2,1)} %bitcast.33), calls=%async_computation.6 | async-start | bytes 1048576 | tf_op jit(solution)/shard_map/all_to_all | solution.py:647
  677.6 75.3 %all-to-all-start.7 = ((bf16[8,64,1408]{2,1,0:T(8,128)(2,1)}), bf16[8,64,1408]{2,1,0:T(8,128)(2,1)S(1)}, u32[]{:S(2)}, u32[]{:S(2)}) async-start(bf16[8,64,1408]{2,1,0:T(8,128)(2,1)} %fusion.21), calls=%async_computation.7 | async-start | bytes 2883584 | tf_op jit(solution)/shard_map/all_to_all | solution.py:647
  754.0 105.9 %all-to-all-start.5 = ((bf16[8,128,2048]{2,1,0:T(8,128)(2,1)}), bf16[8,128,2048]{2,1,0:T(8,128)(2,1)}, u32[]{:S(2)}, u32[]{:S(2)}) async-start(bf16[8,128,2048]{2,1,0:T(8,128)(2,1)} %bitcast.166), calls=%async_computation.5 | async-start | bytes 8388608 | tf_op jit(solution)/shard_map/all_to_all | solution.py:647
  767.7 161.8 %collective-permute-start.30 = (bf16[256,2048]{1,0:T(8,128)(2,1)}, bf16[256,2048]{1,0:T(8,128)(2,1)}, u32[]{:S(2)}, u32[]{:S(2)}) collective-permute-start(bf16[256,2048]{1,0:T(8,128)(2,1)} %reduce-scatter.5.cloned.1.call-done), channel_id=1, source_target_pairs={{0,0},{1,8},{2,16},{3,24},{4,4},{5,12},{6,20},{7,28},{8,1},{9,9},{... | collective-permute-start | bytes 3145736 | tf_op jit(solution)/shard_map/ppermute | solution.py:861
  781.2 168.6 %collective-permute-start.27 = (bf16[256,2048]{1,0:T(8,128)(2,1)}, bf16[256,2048]{1,0:T(8,128)(2,1)}, u32[]{:S(2)}, u32[]{:S(2)}) collective-permute-start(bf16[256,2048]{1,0:T(8,128)(2,1)} %slice.321), channel_id=1, source_target_pairs={{0,0},{1,8},{2,16},{3,24},{4,4},{5,12},{6,20},{7,28},{8,1},{9,9},{... | collective-permute-start | bytes 3145736 | tf_op jit(solution)/shard_map/ppermute | solution.py:861
  (109 other events, 2111.4 us)
Sparse Core Ops, SparseCore 0:
  11.4 89.1 all-gather.2
  102.1 55.2 all-gather.4
  404.9 88.2 reduce-scatter.4
  633.1 129.1 reduce-scatter.2

commit v4 on v3

--- a/solution.py
+++ b/solution.py
@@ -479,8 +479,8 @@
 
 def unproject_kernel(
     width, parts, piece, number_ref, block_ref, stats_ref, vec_ref, weight_ref,
-    recept_ref, keys_ref, values_ref, ups_ref, hidden_ref, downs_ref, up_ref,
-    grad_ref, sums_ref, vec_out, wide_ref, up_out, down_lows,
+    other_ref, recept_ref, keys_ref, values_ref, ups_ref, hidden_ref, downs_ref, up_ref,
+    grad_ref, sums_ref, wide_ref, up_out, down_lows,
 ):
     rows = block_ref.shape[0]
     base = 3 * width
@@ -532,9 +532,14 @@
         kept = grad - moved if kept is None else kept + (grad - moved)
         sent = moved if sent is None else sent + moved
     grad = kept + pltpu.roll(sent * flowing, rows - 1, 0)
-    vec_out[...] = jnp.concatenate(
+    vec_rows = jnp.concatenate(
         [jnp.sum(grad * standard, 0, keepdims=True), jnp.sum(grad, 0, keepdims=True)] + vec_rows, 0
     )
+    spare = jnp.concatenate([vec_rows.T, other_ref[...]], 1).astype(BF16)
+    for number in range(spare.shape[0] // per_seq):
+        for w in range(parts):
+            at = number * per_seq + w * piece
+            wide_ref[w, number, :, base + RANKS[0] : base + PADDED[0]] = spare[at : at + piece]
     scaled = grad * vec_ref[0:1]
     sums_ref[:, 0:1] += jnp.sum(scaled, 1, keepdims=True)
     sums_ref[:, 1:2] += jnp.sum(scaled * standard, 1, keepdims=True)
@@ -577,7 +582,7 @@
     )(number, balanced, stats, vec, weights)
 
 
-def run_unproject(number, balanced, stats, vec, weights, lows, ups, hidden, downs, up, parts):
+def run_unproject(number, balanced, stats, vec, weights, others, lows, ups, hidden, downs, up, parts):
     rows, width = balanced.shape
     own_width = lows[0].shape[1]
     seqs = width // own_width
@@ -590,10 +595,13 @@
         grid_spec=pltpu.PrefetchScalarGridSpec(
             num_scalar_prefetch=1,
             grid=(width // block,),
-            in_specs=[columns(rows), whole(stats.shape), columns(8), weight_spec(weights)]
+            in_specs=[
+                columns(rows), whole(stats.shape), columns(8), weight_spec(weights),
+                pl.BlockSpec((block, others.shape[1]), lambda j, n: (j, 0)),
+            ]
             + [whole(a.shape) for a in (*lows, ups, hidden, downs, up)],
             out_specs=[
-                columns(rows), whole((rows, 2)), columns(8),
+                columns(rows), whole((rows, 2)),
                 pl.BlockSpec((parts, taken, piece, total), lambda j, n: (0, j, 0, 0)),
                 whole((own_width, WIDE)),
             ],
@@ -601,13 +609,13 @@
         ),
         out_shape=[
             jax.ShapeDtypeStruct((rows, width), F32), jax.ShapeDtypeStruct((rows, 2), F32),
-            jax.ShapeDtypeStruct((8, width), F32), jax.ShapeDtypeStruct((parts, seqs, piece, total), BF16),
+            jax.ShapeDtypeStruct((parts, seqs, piece, total), BF16),
             jax.ShapeDtypeStruct((own_width, WIDE), BF16),
         ],
         compiler_params=pltpu.CompilerParams(vmem_limit_bytes=60 << 20),
         cost_estimate=kernel_cost(rows, own_width, 120),
         name="mix_unproject",
-    )(number, balanced, stats, vec, weights, *lows, ups, hidden, downs, up)
+    )(number, balanced, stats, vec, weights, others, *lows, ups, hidden, downs, up)
 
 
 def norm_stats(values):
@@ -637,6 +645,412 @@
     return jnp.concatenate([matrix[..., o : o + r] for o, r in zip(OFFSETS, RANKS)], -1)
 
 
+MESH_ID = pl.DeviceIdType.MESH
+
+
+def places():
+    s, w = lax.axis_index("seq"), lax.axis_index("wsh")
+    side = s % 2
+    return s, w, side, s // 2, (s + 1 - 2 * side, w), (s, w + 1 - 2 * (w % 2)), (s, w + 2 - 4 * (w // 2))
+
+
+def greet(neighbours, number):
+    barrier = pltpu.get_barrier_semaphore()
+    for there, device in neighbours:
+        if there is None:
+            pl.semaphore_signal(barrier, inc=1, device_id=device, device_id_type=MESH_ID)
+        else:
+
+            @pl.when(there)
+            def _(device=device):
+                pl.semaphore_signal(barrier, inc=1, device_id=device, device_id_type=MESH_ID)
+
+    pl.semaphore_wait(barrier, number)
+
+
+def send(source, target, send_sem, recv_sem, device):
+    return pltpu.make_async_remote_copy(
+        src_ref=source, dst_ref=target, send_sem=send_sem, recv_sem=recv_sem, device_id=device, device_id_type=MESH_ID
+    )
+
+
+def line_ends(z):
+    return jnp.where(z > 0, 1, 0) + jnp.where(z < 3, 1, 0)
+
+
+def gather_kernel(own_ref, out_ref, copy_sem, right_send, right_recv, left_send, left_recv, x_send, x_recv):
+    s, w, side, z, x_device, _, _ = places()
+    up, down = (s + 2, w), (s - 2, w)
+    copy = pltpu.make_async_copy(own_ref, out_ref.at[s], copy_sem)
+    copy.start()
+    greet(((None, x_device), (z < 3, up), (z > 0, down)), 1 + line_ends(z))
+
+    def to_right(j, source, number):
+        return send(source, out_ref.at[number], right_send.at[j], right_recv.at[j], up)
+
+    def to_left(j, source, number):
+        return send(source, out_ref.at[number], left_send.at[j], left_recv.at[j], down)
+
+    def to_x(at, source, number):
+        return send(source, out_ref.at[number], x_send.at[at], x_recv.at[at], x_device)
+
+    @pl.when(z < 3)
+    def _():
+        to_right(0, own_ref, s).start()
+
+    @pl.when(z > 0)
+    def _():
+        to_left(0, own_ref, s).start()
+
+    to_x(z, own_ref, s).start()
+    for j in (1, 2, 3):
+        lower, upper = s - 2 * j, s + 2 * j
+
+        @pl.when(z >= j)
+        def _(j=j, lower=lower):
+            block = out_ref.at[lower]
+            to_right(j - 1, block, lower).wait_recv()
+
+            @pl.when(z < 3)
+            def _():
+                to_right(j, block, lower).start()
+
+            to_x(z - j, block, lower).start()
+
+        @pl.when(z + j <= 3)
+        def _(j=j, upper=upper):
+            block = out_ref.at[upper]
+            to_left(j - 1, block, upper).wait_recv()
+
+            @pl.when(z > 0)
+            def _():
+                to_left(j, block, upper).start()
+
+            to_x(z + j, block, upper).start()
+
+    for number in range(4):
+        done = to_x(number, own_ref, s)
+        done.wait_send()
+        done.wait_recv()
+    for j in range(3):
+
+        @pl.when((z >= j) & (z < 3))
+        def _(j=j):
+            to_right(j, own_ref, s).wait_send()
+
+        @pl.when((z + j <= 3) & (z > 0))
+        def _(j=j):
+            to_left(j, own_ref, s).wait_send()
+
+    copy.wait()
+
+
+def gather_seq(own):
+    seqs = lax.axis_size("seq")
+    if seqs != 8 or lax.axis_size("wsh") != 4:
+        return lax.all_gather(own, "seq", axis=0, tiled=False)
+    sems = [pltpu.SemaphoreType.DMA((3,))] * 4 + [pltpu.SemaphoreType.DMA((4,))] * 2
+    return pl.pallas_call(
+        gather_kernel,
+        in_specs=[pl.BlockSpec(memory_space=pl.ANY)],
+        out_specs=pl.BlockSpec(memory_space=pl.ANY),
+        out_shape=jax.ShapeDtypeStruct((seqs,) + own.shape, own.dtype),
+        scratch_shapes=[pltpu.SemaphoreType.DMA] + sems,
+        compiler_params=pltpu.CompilerParams(collective_id=1, has_side_effects=True),
+        cost_estimate=pl.CostEstimate(flops=0, bytes_accessed=100 << 20, transcendentals=0),
+        name="gather_seq",
+    )(own)
+
+
+def reduce_kernel(
+    splits, x_ref, out_ref, x_buf, right_buf, left_buf, right_out, left_out,
+    x_send, x_recv, right_send, right_recv, left_send, left_recv,
+):
+    s, w, side, z, x_device, _, _ = places()
+    up, down = (s + 2, w), (s - 2, w)
+    size = x_ref.shape[2] // splits
+    columns = [slice(c * size, (c + 1) * size) for c in range(splits)]
+    greet(((None, x_device), (z < 3, up), (z > 0, down)), 1 + line_ends(z))
+
+    def to_x(target, c):
+        return send(
+            x_ref.at[target * 2 + 1 - side, :, columns[c]], x_buf.at[target, :, columns[c]],
+            x_send.at[target, c], x_recv.at[target, c], x_device,
+        )
+
+    def start_x(target):
+        for c in range(splits):
+            to_x(target, c).start()
+
+    def to_right(k, c):
+        return send(
+            right_out.at[k - 1, :, columns[c]], right_buf.at[k - 1, :, columns[c]],
+            right_send.at[k - 1, c], right_recv.at[k - 1, c], up,
+        )
+
+    def to_left(k, c):
+        return send(
+            left_out.at[k - 1, :, columns[c]], left_buf.at[k - 1, :, columns[c]],
+            left_send.at[k - 1, c], left_recv.at[k - 1, c], down,
+        )
+
+    def pair(target, c):
+        to_x(target, c).wait_recv()
+        return x_ref[target * 2 + side, :, columns[c]].astype(F32) + x_buf[target, :, columns[c]].astype(F32)
+
+    for k in (3, 2, 1):
+
+        @pl.when(z + k <= 3)
+        def _(k=k):
+            start_x(z + k)
+
+        @pl.when(z >= k)
+        def _(k=k):
+            start_x(z - k)
+
+    start_x(z)
+    for k in (3, 2, 1):
+        for c in range(splits):
+
+            @pl.when(z + k <= 3)
+            def _(k=k, c=c):
+                right_out[k - 1, :, columns[c]] = pair(z + k, c).astype(BF16)
+                if k < 3:
+
+                    @pl.when(z > 0)
+                    def _():
+                        to_right(k + 1, c).wait_recv()
+                        right_out[k - 1, :, columns[c]] = (
+                            right_out[k - 1, :, columns[c]].astype(F32) + right_buf[k, :, columns[c]].astype(F32)
+                        ).astype(BF16)
+
+                to_right(k, c).start()
+
+            @pl.when(z >= k)
+            def _(k=k, c=c):
+                left_out[k - 1, :, columns[c]] = pair(z - k, c).astype(BF16)
+                if k < 3:
+
+                    @pl.when(z < 3)
+                    def _():
+                        to_left(k + 1, c).wait_recv()
+                        left_out[k - 1, :, columns[c]] = (
+                            left_out[k - 1, :, columns[c]].astype(F32) + left_buf[k, :, columns[c]].astype(F32)
+                        ).astype(BF16)
+
+                to_left(k, c).start()
+
+    for c in range(splits):
+        out_ref[:, columns[c]] = pair(z, c)
+
+        @pl.when(z > 0)
+        def _(c=c):
+            to_right(1, c).wait_recv()
+            out_ref[:, columns[c]] += right_buf[0, :, columns[c]].astype(F32)
+
+        @pl.when(z < 3)
+        def _(c=c):
+            to_left(1, c).wait_recv()
+            out_ref[:, columns[c]] += left_buf[0, :, columns[c]].astype(F32)
+
+    for c in range(splits):
+        for target in range(4):
+            to_x(target, c).wait_send()
+        for k in (3, 2, 1):
+
+            @pl.when(z + k <= 3)
+            def _(k=k, c=c):
+                to_right(k, c).wait_send()
+
+            @pl.when(z >= k)
+            def _(k=k, c=c):
+                to_left(k, c).wait_send()
+
+
+def reduce_seq(x):
+    seqs, rows, width = x.shape
+    if seqs != 8 or lax.axis_size("wsh") != 4:
+        return jnp.sum(exchange(x, "seq").astype(F32), 0)
+    splits = 2
+    return pl.pallas_call(
+        functools.partial(reduce_kernel, splits),
+        in_specs=[pl.BlockSpec(memory_space=pltpu.VMEM)],
+        out_specs=pl.BlockSpec(memory_space=pltpu.VMEM),
+        out_shape=jax.ShapeDtypeStruct((rows, width), F32),
+        scratch_shapes=[pltpu.VMEM((4, rows, width), BF16)]
+        + [pltpu.VMEM((3, rows, width), BF16)] * 4
+        + [pltpu.SemaphoreType.DMA((4, splits))] * 2
+        + [pltpu.SemaphoreType.DMA((3, splits))] * 4,
+        compiler_params=pltpu.CompilerParams(collective_id=2, has_side_effects=True, vmem_limit_bytes=40 << 20),
+        cost_estimate=pl.CostEstimate(flops=0, bytes_accessed=120 << 20, transcendentals=0),
+        name="reduce_seq",
+    )(x)
+
+
+def channel_kernel(
+    forward, x_ref, first_hbm, second_hbm, active_hbm,
+    sum_ref, all_hbm, mine_hbm, other_hbm, extra_hbm,
+    first, second, rows_all, middle, active, part, core_buf, far_out, far_buf,
+    load_sem, store_sem, core_send, core_recv, y_send, y_recv, x_send, x_recv, r_send, r_recv, f_send, f_recv,
+):
+    s, w, side, z, x_device, core_device, y_device = places()
+    rows, width = x_ref.shape
+    units = first.shape[0]
+    half = units // 2
+    loads = [
+        pltpu.make_async_copy(first_hbm, first, load_sem.at[0]),
+        pltpu.make_async_copy(second_hbm, second, load_sem.at[1]),
+    ]
+    if not forward:
+        loads.append(pltpu.make_async_copy(active_hbm, active, load_sem.at[2]))
+    for load in loads:
+        load.start()
+    rows_all[0:rows] = x_ref[...]
+    greet(((None, x_device), (None, core_device), (None, y_device)), 3)
+
+    def block(number):
+        return rows_all.at[pl.ds(number * rows, rows)]
+
+    to_core = [
+        send(block(0), block(1), core_send.at[0], core_recv.at[0], core_device),
+        send(block(2), block(3), core_send.at[1], core_recv.at[1], core_device),
+    ]
+    to_y = send(block(0), block(2), y_send, y_recv, y_device)
+    if forward:
+        to_x = [
+            send(
+                middle.at[1 - side, pl.ds(2 * n * rows, 2 * rows)], other_hbm.at[pl.ds(2 * n * rows, 2 * rows)],
+                x_send.at[n], x_recv.at[n], x_device,
+            )
+            for n in range(2)
+        ]
+    else:
+        to_x = [
+            send(block(n), other_hbm.at[pl.ds(n * rows, rows)], x_send.at[n], x_recv.at[n], x_device) for n in range(4)
+        ]
+    sums_core = [
+        send(part.at[pl.ds((2 * n + 1) * rows, rows)], core_buf.at[n], r_send.at[n], r_recv.at[n], core_device)
+        for n in range(2)
+    ]
+    far = send(far_out, far_buf, f_send, f_recv, y_device)
+    stores = [
+        pltpu.make_async_copy(rows_all, all_hbm, store_sem.at[0]),
+        pltpu.make_async_copy(middle.at[side], mine_hbm, store_sem.at[1]),
+        pltpu.make_async_copy(active if forward else middle.at[1 - side], extra_hbm, store_sem.at[2]),
+    ]
+
+    def pass_on(number):
+        if not forward:
+            to_x[number].start()
+
+    to_y.start()
+    to_core[0].start()
+    pass_on(0)
+    tile = min(512, half)
+
+    def multiply(number):
+        two = pl.ds(2 * number * rows, 2 * rows)
+
+        def up(t, carry):
+            for side_units in range(2):
+                at = pl.multiple_of(t * tile, tile)
+                unit = pl.multiple_of(side_units * half + at, tile)
+                raw = dot(rows_all[two, :], first[pl.ds(unit, tile), :], NT)
+                if forward:
+                    raw = jnp.maximum(raw, 0.0)
+                    active[two, pl.ds(unit, tile)] = raw
+                    mid = raw * raw
+                else:
+                    mid = raw * 2.0 * active[two, pl.ds(unit, tile)]
+                middle[side_units, two, pl.ds(at, tile)] = mid.astype(BF16)
+            return carry
+
+        lax.fori_loop(0, half // tile, up, 0)
+        if forward:
+            to_x[number].start()
+        if number == 0:
+            loads[1].wait()
+
+        def down(t, carry):
+            at = pl.multiple_of(t * tile, tile)
+            part[two, pl.ds(at, tile)] = dot(middle[0, two, :], second[0:half, pl.ds(at, tile)]) + dot(
+                middle[1, two, :], second[half:units, pl.ds(at, tile)]
+            )
+            return carry
+
+        lax.fori_loop(0, width // tile, down, 0)
+        sums_core[number].start()
+
+    loads[0].wait()
+    if not forward:
+        loads[2].wait()
+    to_core[0].wait_recv()
+    pass_on(1)
+    multiply(0)
+    to_y.wait_recv()
+    to_core[1].start()
+    pass_on(2)
+    to_core[1].wait_recv()
+    pass_on(3)
+    stores[0].start()
+    multiply(1)
+    for store in stores[1:]:
+        store.start()
+    sums_core[1].wait_recv()
+    far_out[...] = (part[2 * rows : 3 * rows] + core_buf[1]).astype(BF16)
+    far.start()
+    sums_core[0].wait_recv()
+    sum_ref[...] = part[0:rows] + core_buf[0]
+    far.wait_recv()
+    sum_ref[...] += far_buf[...].astype(F32)
+    for copy in to_x:
+        copy.wait_recv()
+    for copy in to_x + to_core + sums_core + [to_y, far]:
+        copy.wait_send()
+    for store in stores:
+        store.wait()
+
+
+def channel_stage(x, first, second, active):
+    rows, width = x.shape
+    units = first.shape[0]
+    forward = active is None
+    given = (x, first, second) if forward else (x, first, second, active)
+    everything = pl.BlockSpec(memory_space=pl.ANY)
+    shapes = [
+        ((rows, width), F32), ((4 * rows, width), BF16), ((4 * rows, units // 2), BF16),
+        ((4 * rows, units // 2 if forward else width), BF16),
+        ((4 * rows, units), F32) if forward else ((4 * rows, units // 2), BF16),
+    ]
+
+    def body(*refs):
+        refs = list(refs)
+        if forward:
+            refs.insert(3, None)
+        channel_kernel(forward, *refs)
+
+    dma = pltpu.SemaphoreType.DMA
+    return pl.pallas_call(
+        body,
+        in_specs=[pl.BlockSpec(memory_space=pltpu.VMEM)] + [everything] * (len(given) - 1),
+        out_specs=[pl.BlockSpec(memory_space=pltpu.VMEM)] + [everything] * (len(shapes) - 1),
+        out_shape=[jax.ShapeDtypeStruct(s, d) for s, d in shapes],
+        scratch_shapes=[
+            pltpu.VMEM((units, width), BF16), pltpu.VMEM((units, width), BF16), pltpu.VMEM((4 * rows, width), BF16),
+            pltpu.VMEM((2, 4 * rows, units // 2), BF16), pltpu.VMEM((4 * rows, units), F32),
+            pltpu.VMEM((4 * rows, width), F32), pltpu.VMEM((2, rows, width), F32),
+            pltpu.VMEM((rows, width), BF16), pltpu.VMEM((rows, width), BF16),
+            dma((3,)), dma((3,)), dma((2,)), dma((2,)), dma, dma, dma((4,)), dma((4,)), dma((2,)), dma((2,)),
+            dma, dma,
+        ],
+        compiler_params=pltpu.CompilerParams(
+            collective_id=3 if forward else 4, has_side_effects=True, vmem_limit_bytes=60 << 20
+        ),
+        cost_estimate=pl.CostEstimate(flops=0, bytes_accessed=100 << 20, transcendentals=0),
+        name="channel_forward" if forward else "channel_backward",
+    )(*given)
+
+
 def from_behind(x, axis, by):
     size = lax.axis_size(axis)
     pairs = [(i, i + by) for i in range(size) if 0 <= i + by < size]
@@ -662,15 +1076,6 @@
 
 def beside(x):
     return lax.ppermute(x, "seq", [(i, i ^ 1) for i in range(lax.axis_size("seq"))])
-
-
-def own_half(x, me):
-    half = x.shape[1] // 2
-    side = me % 2
-    return (
-        lax.dynamic_slice_in_dim(x, side * half, half, 1),
-        beside(lax.dynamic_slice_in_dim(x, (1 - side) * half, half, 1)),
-    )
 
 
 def scalar_sum(x):
@@ -693,14 +1098,18 @@
 def block_sum(x):
     if lax.axis_size("wsh") != 4:
         return lax.psum_scatter(x, "wsh", scatter_dimension=0, tiled=False).astype(F32)
+    kept, far = block_halves(x)
+    return kept + swap(far, 2).astype(F32)
+
+
+def block_halves(x):
     number = lax.axis_index("wsh")
 
     def block(by):
         return lax.dynamic_index_in_dim(x, number ^ by, 0, keepdims=False)
 
     beside = swap(jnp.stack([block(1), block(3)]), 1).astype(F32)
-    far = block(2).astype(F32) + beside[1]
-    return block(0).astype(F32) + beside[0] + swap(far.astype(BF16), 2).astype(F32)
+    return block(0).astype(F32) + beside[0], (block(2).astype(F32) + beside[1]).astype(BF16)
 
 
 def local(
@@ -721,7 +1130,8 @@
     position = dest_seq * rows + destination % rows
     digits = jnp.stack([position // DIGIT, position % DIGIT, valid], 1).astype(BF16)
     tail = jnp.pad(digits, ((0, 0), (0, EXTRA - 3)))
-    given = lax.all_gather(jnp.concatenate([tokens, tail], 1), "seq", axis=0, tiled=True)
+    given = gather_seq(jnp.concatenate([tokens, tail], 1)).reshape(group, -1)
+    first_values, given = lax.optimization_barrier((first_layer_values, given))
     info = given[:, width : width + 3].astype(F32)
     places = (info[:, 0] * DIGIT + info[:, 1]).astype(jnp.int32)
     numbers = jnp.arange(group, dtype=jnp.int32)
@@ -737,17 +1147,8 @@
     own_rows = ((index[:, None] + me * rows) == places[None, :]).astype(BF16)
     settle = dot(own_rows, (mine[:, None] & (arrival[:, None] == index[None, :])).astype(BF16)).astype(BF16)
 
-    def deal(array):
-        moved = exchange(dot(arrange, array).astype(BF16).reshape(seqs, rows // seqs, width), "seq")
-        return dot(settle, moved.reshape(rows, width))
-
-    def undeal(array):
-        back = dot(settle, array.astype(BF16), TN).astype(BF16)
-        moved = exchange(back.reshape(seqs, rows // seqs, width), "seq")
-        return dot(arrange, moved.reshape(rows, width), TN).astype(BF16)
-
     first_given = exchange(
-        first_layer_values.reshape(rows, seqs, own_width).transpose(1, 0, 2), "seq"
+        first_values.reshape(rows, seqs, own_width).transpose(1, 0, 2), "seq"
     ).reshape(group, own_width)
     first = dot(permute, first_given).astype(BF16)
 
@@ -795,9 +1196,11 @@
     mix_vec = vectors[:, :8].T
     recept, keys, values, downs, hidden = run_project(number, balanced, stats, mix_vec, weights, own_width, parts)
     teacher_late, recept = lax.optimization_barrier((teacher, recept))
-    target = deal(teacher_late)
+    teacher_rows = exchange(dot(arrange, teacher_late).astype(BF16).reshape(seqs, rows // seqs, width), "seq")
     inputs = (recept, keys, values, hidden, first, up, vec, segments)
     mixed_out, *saved = run_forward(*inputs)
+    teacher_rows, mixed_out = lax.optimization_barrier((teacher_rows, mixed_out))
+    target = dot(settle, teacher_rows.reshape(rows, width))
 
     mixed_rows = exchange(mixed_out.reshape(seqs, rows, own_width), "seq").transpose(1, 0, 2).reshape(rows, width)
     own = lax.dynamic_slice_in_dim(balanced, me * rows, rows, 0).astype(F32)
@@ -809,29 +1212,31 @@
     normed_two = standard_two * vectors[:, 16] + vectors[:, 17]
     carried_two = from_behind(normed_two[-1:], "seq", 1)
     delta_two = jnp.concatenate([carried_two, normed_two[:-1]], 0) * own_flowing - normed_two
-    channel = gather_near((normed_two + delta_two * vectors[:, 18]).astype(BF16))
-    active = jax.nn.relu(dot(channel, channel_key_weight, NT))
-    hidden_rows = jnp.square(active).astype(BF16)
-    result = residual + near_sum(dot(hidden_rows, channel_value_weight))
+    channel_in = (normed_two + delta_two * vectors[:, 18]).astype(BF16)
+    paired = near and seqs == 8
+    if paired:
+        summed, channel, hidden_mine, hidden_other, active = channel_stage(
+            channel_in, channel_key_weight, channel_value_weight, None
+        )
+    else:
+        channel = gather_near(channel_in)
+        active = jax.nn.relu(dot(channel, channel_key_weight, NT))
+        hidden_rows = jnp.square(active).astype(BF16)
+        summed = near_sum(dot(hidden_rows, channel_value_weight))
+    result = residual + summed
     total_tokens = group * parts
     cotangent = (result - target) * (own_valid * (total_tokens / total_valid))[:, None]
-    cot = gather_near(cotangent.astype(BF16))
-
-    paired = near and seqs == 8
-    channel_other = beside(channel) if paired else None
-    lefts_hidden = own_half(hidden_rows, me) if paired else (hidden_rows,)
-
-    def token_product(left, right, right_other=None):
-        if not paired:
-            return dot(left[0], right, TN).astype(BF16)
-        other = beside(right) if right_other is None else right_other
-        return (dot(left[0], right, TN) + dot(left[1], other, TN)).astype(BF16)
-
-    value_part = token_product(lefts_hidden, cot)
-    grad_pre = (dot(cot, channel_value_weight, NT) * 2.0 * active).astype(BF16)
-    channel_part = dot(grad_pre, channel_key_weight)
-    grad_channel = near_sum(channel_part)
-    key_part = token_product(own_half(grad_pre, me) if paired else (grad_pre,), channel, channel_other)
+    cot_low = cotangent.astype(BF16)
+
+    if paired:
+        grad_channel, cot, pre_mine, cot_other, pre_spare = channel_stage(
+            cot_low, channel_value_weight, channel_key_weight, active
+        )
+        channel_other, pre_other = beside(channel), beside(pre_spare)
+    else:
+        cot = gather_near(cot_low)
+        grad_pre = (dot(cot, channel_value_weight, NT) * 2.0 * active).astype(BF16)
+        grad_channel = near_sum(dot(grad_pre, channel_key_weight))
     grad_vec_mix_two = jnp.sum(grad_channel * delta_two, 0)
     shifted = grad_channel * vectors[:, 18] * own_flowing
     behind = from_behind(shifted[:1], "seq", -1)
@@ -839,16 +1244,51 @@
     grad_residual = cotangent + norm_back(grad_normed_two, standard_two, scale_two, vectors[:, 16])
     grad_low = grad_residual.astype(BF16)
 
-    lefts = exchange(mixed_rows.reshape(rows, seqs, parts, piece).transpose(2, 0, 1, 3), "wsh")
+    grad_posted = dot(grad_low, w_out, NT).astype(BF16)
+    if paired:
+        hidden_mine, grad_posted = lax.optimization_barrier((hidden_mine, grad_posted))
+        value_part = (dot(hidden_mine, cot, TN) + dot(hidden_other, cot_other, TN)).astype(BF16)
+    else:
+        value_part = dot(hidden_rows, cot, TN).astype(BF16)
+    grad_heads = exchange(grad_posted.reshape(rows, seqs, own_width).transpose(1, 0, 2), "seq").reshape(group, own_width)
+    grad_heads, value_part, mixed_late = lax.optimization_barrier((grad_heads, value_part, mixed_rows))
+    lefts = exchange(mixed_late.reshape(rows, seqs, parts, piece).transpose(2, 0, 1, 3), "wsh")
+    near_grad = gather_near(grad_low)
+    recept_low, keys_low, values_low, ups_low, grad_first, grad_vec_heads = run_backward(grad_heads, *inputs, saved)
+    if paired:
+        channel_other, pre_other, lefts, near_grad, recept_low = lax.optimization_barrier(
+            (channel_other, pre_other, lefts, near_grad, recept_low)
+        )
+        key_part = (dot(pre_mine, channel, TN) + dot(pre_other, channel_other, TN)).astype(BF16)
+    else:
+        lefts, near_grad, recept_low = lax.optimization_barrier((lefts, near_grad, recept_low))
+        key_part = dot(grad_pre, channel, TN).astype(BF16)
     if near:
         lefts = jnp.stack([lax.dynamic_index_in_dim(lefts, number[0] ^ k, 0, keepdims=False) for k in range(4)])
-    out_part = dot(lefts.reshape(rows * parts, -1), gather_near(grad_low), TN).astype(BF16)
+    out_part = dot(lefts.reshape(rows * parts, -1), near_grad, TN).astype(BF16)
+
+    result_back = dot(settle, result.astype(BF16), TN).astype(BF16).reshape(seqs, rows // seqs, width)
+    first_back = dot(permute, grad_first, TN).astype(BF16).reshape(seqs, rows // seqs, width)
+    moved = exchange(jnp.concatenate([result_back, first_back], 1), "seq")
+    recept_low, key_part, out_part = lax.optimization_barrier((recept_low, key_part, out_part))
+    heads_part = lax.dynamic_update_slice_in_dim(jnp.zeros((width, 8), F32), grad_vec_heads.T, column, 0)
+    vec_two = jnp.stack(
+        [jnp.sum(grad_normed_two * standard_two, 0), jnp.sum(grad_normed_two, 0), grad_vec_mix_two], 1
+    )
+    others = jnp.concatenate([heads_part, jnp.pad(vec_two, ((0, 0), (0, 13)))], 1)
+    scaled_grad, sums, wide, up_grad = run_unproject(
+        number, balanced, stats, mix_vec, weights, others, (recept_low, keys_low, values_low), ups_low, hidden, downs, up, parts
+    )
+    moved, sums = lax.optimization_barrier((moved, sums))
+    output = dot(arrange, moved[:, : rows // seqs].reshape(rows, width), TN).astype(BF16)
+    grad_first_rows = moved[:, rows // seqs :].reshape(seqs, rows, own_width).transpose(1, 0, 2).reshape(rows, width)
+
     if paired:
         halves_out = out_part.reshape(seqs // 2, 2, piece, width)
         x_side = me % 2
         out_mine = lax.dynamic_index_in_dim(halves_out, x_side, 1, keepdims=False).astype(F32)
         out_other = beside(lax.dynamic_index_in_dim(halves_out, 1 - x_side, 1, keepdims=False))
-        out_half = (out_mine + out_other.astype(F32)).astype(BF16)
+        out_half = (out_mine + out_other.astype(F32)).astype(BF16).reshape(-1, width)
         lines = [[0, 2, 4, 6], [1, 3, 5, 7]]
         turned = [
             ((z * 2 + x) * 4 + w, (w * 2 + x) * 4 + z) for z in range(4) for x in range(2) for w in range(4)
@@ -860,12 +1300,8 @@
         def turn(part):
             return lax.ppermute(part, ("seq", "wsh"), turned).astype(F32)
 
-        grad_ffn_value = turn(along(value_part))
-        both_parts = along(
-            jnp.concatenate([key_part.reshape(4, -1, width), out_half], 1).reshape(-1, width)
-        )
-        grad_ffn_key = turn(both_parts[:-piece])
-        grad_out = both_parts[-piece:].astype(F32)
+        grad_ffn_value, grad_ffn_key = turn(along(value_part)), turn(along(key_part))
+        grad_out = along(out_half).astype(F32)
     else:
         moves = [(s * parts + w, w * seqs + s) for s in range(seqs) for w in range(parts)]
 
@@ -876,46 +1312,35 @@
         grad_ffn_value, grad_ffn_key = ffn_grad(value_part), ffn_grad(key_part)
         grad_out = lax.psum_scatter(out_part, "seq", scatter_dimension=0, tiled=True).astype(F32)
 
-    grad_posted = dot(grad_low, w_out, NT).astype(BF16)
-    grad_heads = exchange(grad_posted.reshape(rows, seqs, own_width).transpose(1, 0, 2), "seq").reshape(group, own_width)
-    recept_low, keys_low, values_low, ups_low, grad_first, grad_vec_heads = run_backward(grad_heads, *inputs, saved)
-    scaled_grad, sums, vec_mix, wide, up_grad = run_unproject(
-        number, balanced, stats, mix_vec, weights, (recept_low, keys_low, values_low), ups_low, hidden, downs, up, parts
-    )
     standard = (balanced.astype(F32) - mean) * scale_one
     grad_balanced = scale_one * (scaled_grad - sums[:, :1] * (1.0 / width) - standard * (sums[:, 1:] * (1.0 / width)))
     mine_rows = lax.dynamic_slice_in_dim(grad_balanced, me * rows, rows, 0) + grad_residual
     grad_balanced = lax.dynamic_update_slice_in_dim(grad_balanced, mine_rows, me * rows, 0)
-    grad_given = dot(permute, grad_balanced.astype(BF16), TN).astype(BF16)
-    grad_tokens = jnp.sum(exchange(grad_given.reshape(seqs, rows, width), "seq").astype(F32), 0).astype(BF16)
-    first_back = exchange(dot(permute, grad_first, TN).astype(BF16).reshape(seqs, rows, own_width), "seq")
-    grad_first_rows = first_back.transpose(1, 0, 2).reshape(rows, width)
-
-    wide_all = exchange(block_sum(wide).astype(BF16), "seq").astype(F32)
+    grad_given = dot(permute, grad_balanced.astype(BF16), TN).astype(BF16).reshape(seqs, rows, width)
+    if near:
+        kept_part, far = block_halves(wide)
+        grad_given, far = lax.optimization_barrier((grad_given, far))
+        wide_part = kept_part + swap(far, 2).astype(F32)
+    else:
+        wide_part = block_sum(wide)
+    grad_tokens = reduce_seq(grad_given).astype(BF16)
+    wide_part, grad_tokens = lax.optimization_barrier((wide_part, grad_tokens))
+    wide_all = exchange(wide_part.astype(BF16), "seq").astype(F32)
 
     def square(at):
         taken = wide_all[:, :, at * own_width : (at + 1) * own_width]
         return taken.transpose(1, 0, 2).reshape(piece, width)
 
-    grad_down = unpad_ranks(jnp.sum(wide_all[:, :, 3 * own_width :], 0))
+    narrow = jnp.sum(wide_all[:, :, 3 * own_width :], 0)
+    grad_down = unpad_ranks(narrow)
+    grad_vectors = narrow[:, RANKS[0] : RANKS[0] + vectors.shape[1]]
     up_part = unpad_ranks(block_sum(up_grad.reshape(parts, piece, WIDE)))
 
-    heads_part = lax.dynamic_update_slice_in_dim(jnp.zeros((width, 8), F32), grad_vec_heads.T, column, 0)
-    grad_vectors = jnp.concatenate(
-        [
-            vec_mix.T,
-            heads_part,
-            jnp.stack([jnp.sum(grad_normed_two * standard_two, 0), jnp.sum(grad_normed_two, 0), grad_vec_mix_two], 1),
-        ],
-        1,
-    )
-    vec_part = jnp.sum(exchange(grad_vectors.reshape(seqs, parts * piece, -1), "seq"), 0)
-    vec_part = jnp.sum(exchange(vec_part.reshape(parts, piece, -1), "wsh"), 0)
     return (
-        undeal(result), grad_tokens, grad_first_rows,
+        output, grad_tokens, grad_first_rows,
         square(0), square(1), square(2),
         grad_out, grad_down, up_part,
-        grad_ffn_key, grad_ffn_value, vec_part,
+        grad_ffn_key, grad_ffn_value, grad_vectors,
     )
 
 

time: 971 us -> 763 us (0.79)
  waiting for transfers between devices: 431 us -> 148 us
  Pallas kernels: 142 us -> 353 us
  starting transfers between devices: 117 us -> 59.5 us
  matrix products: 99.8 us -> 65.4 us
  other arithmetic: 94.1 us -> 59.9 us
    pallas_call x0 -> x4, Pallas kernels: none -> 209 us  [the longest x2 88.8 us: channel_stage(): pl.pallas_call(body, in_specs=[pl.BlockSpec(memory_space=pltpu.VMEM)] + [...]
    all_to_all x11 -> x7, waiting for transfers between devices: 175 us -> 15.7 us  [exchange(): return lax.all_to_all(x, axis, split_axis=0, concat_axis=0, tiled=True)]
    ppermute x5 -> x3, waiting for transfers between devices: 66.4 us -> 0.01 us  [beside(): lax.ppermute(x, 'seq', [(i, i ^ 1) for i in range(lax.axis_size('seq'))])]
    ppermute x22 -> x12, waiting for transfers between devices: 74.7 us -> 15.3 us  [swap(): return lax.ppermute(x, 'wsh', [(i, i ^ by) for i in range(size)])]
    dot_general x21 -> x17, matrix products: 99.8 us -> 65.4 us  [dot(): return lax.dot_general(a, b, dims, preferred_element_type=F32)]
    all_gather x1 -> x0, waiting for transfers between devices: 32.7 us -> none  [local(): lax.all_gather(jnp.concatenate([tokens, tail], 1), 'seq', axis=0, tiled=T...]
    reduce_scatter x2 -> x3, waiting for transfers between devices: 0.04 us -> 28.2 us  [along(): lax.psum_scatter(part, 'seq', scatter_dimension=0, tiled=True, axis_index...]
    ppermute x2, starting transfers between devices: 34.9 us -> 7.63 us  [turn(): return lax.ppermute(part, ('seq', 'wsh'), turned).astype(F32)]
  transfers between devices with their start and end apart: 46 -> 30, of which waited for: 21 -> 12; matrix products, arithmetic and copies ran while one was open for 18% -> 19% of each run, Pallas kernels for 15% -> 35%
where the time goes in v4:
time: 763 us; the launch traced here: 752 us
  Pallas kernels  353 us (46%)
  waiting for transfers between devices  148 us (19%)
  matrix products  65.4 us (9%)
  other arithmetic  59.9 us (8%)
  starting transfers between devices  59.5 us (8%)
  local copies, waits for them, and re-layouts  50.7 us (7%)
  between operations  16.2 us (2%)
    pallas_call x2, Pallas kernels, channel_stage(): pl.pallas_call(body, in_specs=[pl.BlockSpec(memory_space=pltpu.VMEM)] + [...  88.8 us
    ppermute x2, waiting for transfers between devices, turn(): return lax.ppermute(part, ('seq', 'wsh'), turned).astype(F32)  83.6 us
    dot_general x17, matrix products, dot(): return lax.dot_general(a, b, dims, preferred_element_type=F32)  65.4 us
    pallas_call x1, Pallas kernels, reduce_seq(): pl.pallas_call(functools.partial(reduce_kernel, splits), in_specs=[pl.Blo...  63.2 us
    pallas_call x1, Pallas kernels, gather_seq(): pl.pallas_call(gather_kernel, in_specs=[pl.BlockSpec(memory_space=pl.ANY)...  57.4 us
    pallas_call x1, Pallas kernels, run_backward(): pl.pallas_call(functools.partial(backward_kernel, count), grid=(rows // s...  47.4 us
    pallas_call x1, Pallas kernels, run_unproject(): pl.pallas_call(functools.partial(unproject_kernel, own_width, parts, piec...  40.3 us
    pallas_call x1, Pallas kernels, run_forward(): pl.pallas_call(functools.partial(forward_kernel, count), grid=(rows // st...  36.2 us
  transfers between devices with their start and end apart: 30, of which 12 were waited for; matrix products, arithmetic and copies ran while one was open for 19% of the time, Pallas kernels for 35%

profile of v4, /device:TPU:4, one launch (start us, length us, event | category | flops | bytes accessed | tf_op | source)
XLA Modules:
  0.0 752.4 jit_solution(715053481528043831)
XLA Ops:
  18.7 57.4 %gather_seq.1 = bf16[8,128,2176]{2,1,0:T(8,128)(2,1)} custom-call(bf16[128,2176]{1,0:T(8,128)(2,1)} %fusion.39.own_ref), custom_call_target="tpu_custom_call" | custom-call | bytes 104857600 | tf_op jit(solution)/shard_map/gather_seq/pallas_call | solution.py:753
  80.7 6.6 copy.131
  90.7 8.3 %convert_reduce_fusion = (f32[1024]{0:T(1024)S(1)}, bf16[1024,2048]{1,0:T(8,128)(2,1)}) fusion(bf16[1024,2176]{1,0:T(8,128)(2,1)} %bitcast.132, s32[1024]{0:T(1024)S(1)} %bitcast.174), kind=kOutput, calls=%fused_computation.1 | convolution fusion | flops 4302306304 | bytes 8396800 | tf_op jit(solution)/shard_map/dot_general | solution.py:28
  110.3 5.8 pad_maximum_fusion.weight_ref
  116.1 19.7 %mix_project.1 = (f32[1024,256]{1,0:T(8,128)}, f32[1024,256]{1,0:T(8,128)}, f32[1024,256]{1,0:T(8,128)}, f32[1024,640]{1,0:T(8,128)}, bf16[1024,640]{1,0:T(8,128)(2,1)}) custom-call(s32[1]{0:T(128)} %bitcast.7.number_ref, bf16[1024,2048]{1,0:T(8,128)(2,1)} %get-tuple-element.235.block_ref, f32[1024,4]{1,0:T(8,128)} %copy.132.stats_ref, ...), custom_call_target="tpu_custom_call" | custom-call | flops 134217728 | bytes 62914560 | tf_op jit(solution)/shard_map/mix_project/pallas_call | solution.py:570
  137.0 6.2 all-to-all-start
  148.2 36.2 %mix_forward.1 = (bf16[1024,256]{1,0:T(8,128)(2,1)S(1)}, bf16[1024,256]{1,0:T(8,128)(2,1)S(1)}, f32[1024,256]{1,0:T(8,128)S(1)}, f32[1024,256]{1,0:T(8,128)S(1)}, f32[1024,256]{1,0:T(8,128)S(1)}) custom-call(f32[1024,256]{1,0:T(8,128)S(1)} %copy-done.4, f32[1024,256]{1,0:T(8,128)} %get-tuple-element.71.keys_ref, f32[1024,256]{1,0:T(8,128)} %get-tuple-element.72.values_ref, ...), custom_call_target="tpu_custom_call" | custom-call | flops 134217728 | bytes 115343360 | tf_op jit(solution)/shard_map/mix_forward/pallas_call | solution.py:385
  188.4 6.0 all-to-all-start.2
  204.4 4.2 all-to-all-done.2
  208.6 4.8 fusion.82
  220.5 37.4 %channel_forward.1 = (f32[128,2048]{1,0:T(8,128)}, bf16[512,2048]{1,0:T(8,128)(2,1)}, bf16[512,1024]{1,0:T(8,128)(2,1)}, bf16[512,1024]{1,0:T(8,128)(2,1)}, f32[512,2048]{1,0:T(8,128)}) custom-call(bf16[128,2048]{1,0:T(8,128)(2,1)} %add_convert_fusion.2.refs_0_, bf16[2048,2048]{1,0:T(8,128)(2,1)} %refs_2_.3, bf16[2048,2048]{1,0:T(8,128)(2,1)} %refs_1_.3), custom_call_target="tpu_custom_call" | custom-call | bytes 104857600 | tf_op jit(solution)/shard_map/channel_forward/pallas_call | solution.py:1033
  260.9 51.3 %channel_backward.1 = (f32[128,2048]{1,0:T(8,128)}, bf16[512,2048]{1,0:T(8,128)(2,1)}, bf16[512,1024]{1,0:T(8,128)(2,1)}, bf16[512,2048]{1,0:T(8,128)(2,1)}, bf16[512,1024]{1,0:T(8,128)(2,1)}) custom-call(bf16[128,2048]{1,0:T(8,128)(2,1)} %get-tuple-element.238.refs_0_, bf16[2048,2048]{1,0:T(8,128)(2,1)} %refs_1_.3, bf16[2048,2048]{1,0:T(8,128)(2,1)} %refs_2_.3, ...), custom_call_target="tpu_custom_call" | custom-call | bytes 104857600 | tf_op jit(solution)/shard_map/channel_backward/pallas_call | solution.py:1033
  317.1 4.1 collective-permute-done.6
  323.9 6.4 convolution_convert_fusion.1
  335.2 4.5 fusion.88
  339.7 4.7 add_convert_fusion.1
  352.3 9.6 %collective-permute-done.10 = bf16[128,2048]{1,0:T(8,128)(2,1)} collective-permute-done((bf16[128,2048]{1,0:T(8,128)(2,1)}, bf16[128,2048]{1,0:T(8,128)(2,1)}, u32[]{:S(2)}, u32[]{:S(2)}) %collective-permute-start.10) | collective-permute-done | bytes 524320 | tf_op jit(solution)/shard_map/ppermute | solution.py:1066
  362.7 5.8 all-to-all-start.5
  368.6 7.7 %fusion.89 = f32[1024,2048]{1,0:T(8,128)} fusion(bf16[512,1024]{1,0:T(8,128)(2,1)} %get-tuple-element.99, bf16[512,2048]{1,0:T(8,128)(2,1)} %get-tuple-element.94), kind=kOutput, calls=%fused_computation.215 | convolution fusion | flops 2147483648 | bytes 11534336 | tf_op jit(solution)/shard_map/dot_general | solution.py:28
  376.3 47.4 %mix_backward.1 = (bf16[1024,256]{1,0:T(8,128)(2,1)S(1)}, bf16[1024,256]{1,0:T(8,128)(2,1)S(1)}, bf16[1024,256]{1,0:T(8,128)(2,1)S(1)}, bf16[4,1024,256]{2,1,0:T...) custom-call(bf16[1024,256]{1,0:T(8,128)(2,1)S(1)} %bitcast.127, f32[1024,256]{1,0:T(8,128)S(1)} %copy-done.4, ...), custom_call_target="tpu_custom_call" | custom-call | flops 134217728 | bytes 157286400 | tf_op jit(solution)/shard_map/mix_backward/pallas_call | solution.py:413
  431.8 8.7 %add_convert_fusion = bf16[1024,2048]{1,0:T(8,128)(2,1)} fusion(f32[1024,2048]{1,0:T(8,128)} %fusion.89, bf16[512,1024]{1,0:T(8,128)(2,1)} %collective-permute-done.8, bf16[512,2048]{1,0:T(8,128)(2,1)} %collective-permute-done.7), kind=kOutput, calls=%fused_computation.8 | convolution fusion | flops 2151677952 | bytes 15728640 | tf_op jit(solution)/shard_map/dot_general | solution.py:28
  445.1 4.1 all-to-all-start.4
  450.6 40.3 %mix_unproject.1 = (f32[1024,2048]{1,0:T(8,128)}, f32[1024,2]{1,0:T(8,128)}, bf16[4,8,64,1408]{3,2,1,0:T(8,128)(2,1)}, bf16[256,640]{1,0:T(8,128)(2,1)}) custom-call(s32[1]{0:T(128)} %bitcast.7.number_ref, bf16[1024,2048]{1,0:T(8,128)(2,1)} %get-tuple-element.235.block_ref, f32[1024,4]{1,0:T(8,128)} %copy.132.stats_ref, ...), custom_call_target="tpu_custom_call" | custom-call | flops 134217728 | bytes 125829120 | tf_op jit(solution)/shard_map/mix_unproject/pallas_call | solution.py:593
  494.9 9.1 %all-to-all-done.4 = bf16[8,32,2048]{2,1,0:T(8,128)(2,1)S(1)} async-done(((bf16[8,32,2048]{2,1,0:T(8,128)(2,1)}), bf16[8,32,2048]{2,1,0:T(8,128)(2,1)S(1)}, u32[]{:S(2)}, u32[]{:S(2)}) %all-to-all-start.4) | async-done | bytes 1048608 | tf_op jit(solution)/shard_map/all_to_all | solution.py:1061
  504.5 5.9 fusion.5
  510.6 6.3 fusion.15
  528.5 63.2 %reduce_seq.1 = f32[128,2048]{1,0:T(8,128)S(1)} custom-call(bf16[8,128,2048]{2,1,0:T(8,128)(2,1)S(1)} %bitcast.126), custom_call_target="tpu_custom_call" | custom-call | bytes 125829120 | tf_op jit(solution)/shard_map/reduce_seq/pallas_call | solution.py:875
  595.6 5.8 all-to-all-start.6
  611.4 5.7 collective-permute-start.18
  621.4 28.2 %reduce-scatter.4.cloned.1.call-done = bf16[64,2048]{1,0:T(8,128)(2,1)} async-done(((bf16[256,2048]{1,0:T(8,128)(2,1)}), bf16[64,2048]{1,0:T(8,128)(2,1)}) %reduce-scatter.4.cloned.1.call-update) | async-done | bytes 262160 | tf_op jit(solution)/shard_map/reduce_scatter | solution.py:1298
  656.2 66.0 %collective-permute-done.18 = bf16[256,2048]{1,0:T(8,128)(2,1)} collective-permute-done((bf16[256,2048]{1,0:T(8,128)(2,1)}, bf16[256,2048]{1,0:T(8,128)(2,1)}, u32[]{:S(2)}, u32[]{:S(2)}) %collective-permute-start.18) | collective-permute-done | bytes 1048608 | tf_op jit(solution)/shard_map/ppermute | solution.py:1301
  725.1 17.6 %collective-permute-done.17 = bf16[256,2048]{1,0:T(8,128)(2,1)} collective-permute-done((bf16[256,2048]{1,0:T(8,128)(2,1)}, bf16[256,2048]{1,0:T(8,128)(2,1)}, u32[]{:S(2)}, u32[]{:S(2)}) %collective-permute-start.17) | collective-permute-done | bytes 1048608 | tf_op jit(solution)/shard_map/ppermute | solution.py:1301
  (317 shorter events, 141.2 us)
Async XLA Ops:
  7.2 128.7 %copy-start = (bf16[128,2048]{1,0:T(8,128)(2,1)S(1)}, bf16[128,2048]{1,0:T(8,128)(2,1)}, u32[]{:S(2)}) copy-start(bf16[128,2048]{1,0:T(8,128)(2,1)} %param.17) | copy-start | bytes 1572868
  7.2 201.3 %all-gather.2.cloned.1.call-start = ((), (), s32[]{:S(2)}) async-start(), calls=%async_computation.10 | async-start | bytes 10485760 | tf_op jit(solution)/shard_map/all_gather | solution.py:1188
  17.5 87.9 %collective-permute-start.1 = (bf16[512,1664]{1,0:T(8,128)(2,1)S(1)}, bf16[512,1664]{1,0:T(8,128)(2,1)}, u32[]{:S(2)}, u32[]{:S(2)}) collective-permute-start(bf16[512,1664]{1,0:T(8,128)(2,1)S(1)} %constant_dynamic-update-slice_fusion), channel_id=1, source_target_pairs={{0,2},{1,3},{2,0},{3,1},{4,6},{5,7},{6,4},{7,5},{8,10},{9,11},{10,... | collective-permute-start | bytes 5111816 | tf_op jit(solution)/shard_map/ppermute | solution.py:1066
  17.6 92.7 %collective-permute-start = (bf16[512,1664]{1,0:T(8,128)(2,1)S(1)}, bf16[512,1664]{1,0:T(8,128)(2,1)}, u32[]{:S(2)}, u32[]{:S(2)}) collective-permute-start(bf16[512,1664]{1,0:T(8,128)(2,1)S(1)} %constant_dynamic-update-slice_fusion), channel_id=1, source_target_pairs={{0,1},{1,0},{2,3},{3,2},{4,5},{5,4},{6,7},{7,6},{8,9},{9,8},{10,11... | collective-permute-start | bytes 5111816 | tf_op jit(solution)/shard_map/ppermute | solution.py:1066
  77.1 59.8 %all-to-all-start.1 = ((bf16[8,128,256]{1,2,0:T(8,128)(2,1)}), bf16[8,128,256]{1,2,0:T(8,128)(2,1)S(1)}, u32[]{:S(2)}, u32[]{:S(2)}) async-start(bf16[8,128,256]{1,2,0:T(8,128)(2,1)} %bitcast.15), calls=%async_computation.1 | async-start | bytes 1048576 | tf_op jit(solution)/shard_map/all_to_all | solution.py:1061
  89.8 107.1 %collective-permute-start.4 = (f32[8,128]{1,0:T(8,128)}, f32[8,128]{1,0:T(8,128)}, u32[]{:S(2)}, u32[]{:S(2)}) collective-permute-start(f32[8,128]{1,0:T(8,128)} %broadcast_in_dim.7), channel_id=1, source_target_pairs={{0,1},{1,0},{2,3},{3,2},{4,5},{5,4},{6,7},{7,6},{8,9},{9,8},{10,11... | collective-permute-start | bytes 12296 | tf_op jit(solution)/shard_map/ppermute | solution.py:1066
  105.9 4.4 collective-permute-start.2
  137.0 50.4 %all-to-all-start = ((bf16[8,16,2048]{2,1,0:T(8,128)(2,1)}), bf16[8,16,2048]{2,1,0:T(8,128)(2,1)S(1)}, u32[]{:S(2)}, u32[]{:S(2)}) async-start(bf16[8,16,2048]{2,1,0:T(8,128)(2,1)} %bitcast.13), calls=%async_computation | async-start | bytes 1048576 | tf_op jit(solution)/shard_map/all_to_all | solution.py:1061
  148.2 228.1 %copy-start.2 = (bf16[640,256]{1,0:T(8,128)(2,1)}, bf16[640,256]{1,0:T(8,128)(2,1)S(1)}, u32[]{:S(2)}) copy-start(bf16[640,256]{1,0:T(8,128)(2,1)S(1)} %fusion.48.up_ref) | copy-start | bytes 983044
  188.4 20.2 %all-to-all-start.2 = ((bf16[8,128,256]{1,2,0:T(8,128)(2,1)}), bf16[8,128,256]{1,2,0:T(8,128)(2,1)S(1)}, u32[]{:S(2)}, u32[]{:S(2)}) async-start(bf16[8,128,256]{1,2,0:T(8,128)(2,1)} %copy.140), calls=%async_computation.2 | async-start | bytes 1048576 | tf_op jit(solution)/shard_map/all_to_all | solution.py:1061
  198.3 3.6 collective-permute-start.5
  214.0 5.0 collective-permute-start.3
  315.7 5.5 collective-permute-start.6
  331.2 15.4 %all-to-all-start.3 = ((bf16[8,128,256]{2,1,0:T(8,128)(2,1)}), bf16[8,128,256]{2,1,0:T(8,128)(2,1)S(1)}, u32[]{:S(2)}, u32[]{:S(2)}) async-start(bf16[8,128,256]{2,1,0:T(8,128)(2,1)} %bitcast.143), calls=%async_computation.3 | async-start | bytes 1048576 | tf_op jit(solution)/shard_map/all_to_all | solution.py:1061
  335.0 276.4 %reduce-scatter.8.cloned.1.call-start = ((), (), s32[]{:S(2)}) async-start(), calls=%async_computation.13 | async-start | bytes 5242880 | tf_op jit(solution)/shard_map/reduce_scatter | solution.py:1298
  346.6 81.0 %collective-permute-start.7 = (bf16[512,2048]{1,0:T(8,128)(2,1)}, bf16[512,2048]{1,0:T(8,128)(2,1)}, u32[]{:S(2)}, u32[]{:S(2)}) collective-permute-start(bf16[512,2048]{1,0:T(8,128)(2,1)} %get-tuple-element.94), channel_id=1, source_target_pairs={{0,4},{4,0},{8,12},{12,8},{16,20},{20,16},{24,28},{28,24},{1,5},{5... | collective-permute-start | bytes 6291464 | tf_op jit(solution)/shard_map/ppermute | solution.py:1078
  348.2 13.7 %collective-permute-start.10 = (bf16[128,2048]{1,0:T(8,128)(2,1)}, bf16[128,2048]{1,0:T(8,128)(2,1)}, u32[]{:S(2)}, u32[]{:S(2)}) collective-permute-start(bf16[128,2048]{1,0:T(8,128)(2,1)} %copy-done.18), channel_id=1, source_target_pairs={{0,2},{1,3},{2,0},{3,1},{4,6},{5,7},{6,4},{7,5},{8,10},{9,11},{10,... | collective-permute-start | bytes 1572872 | tf_op jit(solution)/shard_map/ppermute | solution.py:1066
  351.7 75.8 %collective-permute-start.8 = (bf16[512,1024]{1,0:T(8,128)(2,1)}, bf16[512,1024]{1,0:T(8,128)(2,1)}, u32[]{:S(2)}, u32[]{:S(2)}) collective-permute-start(bf16[512,1024]{1,0:T(8,128)(2,1)} %get-tuple-element.95), channel_id=1, source_target_pairs={{0,4},{4,0},{8,12},{12,8},{16,20},{20,16},{24,28},{28,24},{1,5},{5... | collective-permute-start | bytes 3145736 | tf_op jit(solution)/shard_map/ppermute | solution.py:1078
  352.3 73.7 %collective-permute-start.9 = (bf16[128,2048]{1,0:T(8,128)(2,1)}, bf16[128,2048]{1,0:T(8,128)(2,1)}, u32[]{:S(2)}, u32[]{:S(2)}) collective-permute-start(bf16[128,2048]{1,0:T(8,128)(2,1)} %copy-done.18), channel_id=1, source_target_pairs={{0,1},{1,0},{2,3},{3,2},{4,5},{5,4},{6,7},{7,6},{8,9},{9,8},{10,11... | collective-permute-start | bytes 1572872 | tf_op jit(solution)/shard_map/ppermute | solution.py:1066
  361.9 64.1 %collective-permute-start.11 = (bf16[128,2048]{1,0:T(8,128)(2,1)}, bf16[128,2048]{1,0:T(8,128)(2,1)}, u32[]{:S(2)}, u32[]{:S(2)}) collective-permute-start(bf16[128,2048]{1,0:T(8,128)(2,1)} %collective-permute-done.10), channel_id=1, source_target_pairs={{0,1},{1,0},{2,3},{3,2},{4,5},{5,4},{6,7},{7,6},{8,9},{9,8},{10,11... | collective-permute-start | bytes 1572872 | tf_op jit(solution)/shard_map/ppermute | solution.py:1066
  362.7 64.8 %all-to-all-start.5 = ((bf16[4,128,8,64]{1,3,2,0:T(8,128)(2,1)}), bf16[4,128,8,64]{1,3,2,0:T(8,128)(2,1)}, u32[]{:S(2)}, u32[]{:S(2)}) async-start(bf16[4,128,8,64]{1,3,2,0:T(8,128)(2,1)} %copy.142), calls=%async_computation.5 | async-start | bytes 1048576 | tf_op jit(solution)/shard_map/all_to_all | solution.py:1061
  368.6 248.6 %reduce-scatter.6.cloned.1.call-start = ((), (), s32[]{:S(2)}) async-start(), calls=%async_computation.12 | async-start | bytes 5242880 | tf_op jit(solution)/shard_map/reduce_scatter | solution.py:1298
  445.1 58.9 %all-to-all-start.4 = ((bf16[8,32,2048]{2,1,0:T(8,128)(2,1)}), bf16[8,32,2048]{2,1,0:T(8,128)(2,1)S(1)}, u32[]{:S(2)}, u32[]{:S(2)}) async-start(bf16[8,32,2048]{2,1,0:T(8,128)(2,1)} %pad_maximum_fusion.3), calls=%async_computation.4 | async-start | bytes 2097152 | tf_op jit(solution)/shard_map/all_to_all | solution.py:1061
  494.8 22.1 %collective-permute-start.12 = (bf16[2,8,64,1408]{3,2,1,0:T(8,128)(2,1)}, bf16[2,8,64,1408]{3,2,1,0:T(8,128)(2,1)}, u32[]{:S(2)}, u32[]{:S(2)}) collective-permute-start(bf16[2,8,64,1408]{3,2,1,0:T(8,128)(2,1)} %pad_maximum_fusion.1), channel_id=1, source_target_pairs={{0,1},{1,0},{2,3},{3,2},{4,5},{5,4},{6,7},{7,6},{8,9},{9,8},{10,11... | collective-permute-start | bytes 8650760 | tf_op jit(solution)/shard_map/ppermute | solution.py:1066
  523.2 69.4 %collective-permute-start.13 = (bf16[8,64,1408]{2,1,0:T(8,128)(2,1)}, bf16[8,64,1408]{2,1,0:T(8,128)(2,1)S(1)}, u32[]{:S(2)}, u32[]{:S(2)}) collective-permute-start(bf16[8,64,1408]{2,1,0:T(8,128)(2,1)} %fusion.27), channel_id=1, source_target_pairs={{0,2},{1,3},{2,0},{3,1},{4,6},{5,7},{6,4},{7,5},{8,10},{9,11},{10,... | collective-permute-start | bytes 4325384 | tf_op jit(solution)/shard_map/ppermute | solution.py:1066
  524.8 76.6 %collective-permute-start.14 = (bf16[4,64,2048]{2,1,0:T(8,128)(2,1)S(1)}, bf16[4,64,2048]{2,1,0:T(8,128)(2,1)}, u32[]{:S(2)}, u32[]{:S(2)}) collective-permute-start(bf16[4,64,2048]{2,1,0:T(8,128)(2,1)S(1)} %dynamic-slice_bitcast_fusion), channel_id=1, source_target_pairs={{0,4},{4,0},{8,12},{12,8},{16,20},{20,16},{24,28},{28,24},{1,5},{5... | collective-permute-start | bytes 3145736 | tf_op jit(solution)/shard_map/ppermute | solution.py:1078
  595.6 56.1 %all-to-all-start.6 = ((bf16[8,64,1408]{2,1,0:T(8,128)(2,1)}), bf16[8,64,1408]{2,1,0:T(8,128)(2,1)S(1)}, u32[]{:S(2)}, u32[]{:S(2)}) async-start(bf16[8,64,1408]{2,1,0:T(8,128)(2,1)} %fusion.20), calls=%async_computation.6 | async-start | bytes 2883584 | tf_op jit(solution)/shard_map/all_to_all | solution.py:1061
  601.3 48.3 %reduce-scatter.4.cloned.1.call-start = ((), (), s32[]{:S(2)}) async-start(), calls=%async_computation.11 | async-start | bytes 1310720 | tf_op jit(solution)/shard_map/reduce_scatter | solution.py:1298
  604.5 1.5 collective-permute-start.15
  606.0 4.6 collective-permute-start.16
  611.4 110.9 %collective-permute-start.18 = (bf16[256,2048]{1,0:T(8,128)(2,1)}, bf16[256,2048]{1,0:T(8,128)(2,1)}, u32[]{:S(2)}, u32[]{:S(2)}) collective-permute-start(bf16[256,2048]{1,0:T(8,128)(2,1)} %reduce-scatter.8.cloned.1.call-done), channel_id=1, source_target_pairs={{0,0},{1,8},{2,16},{3,24},{4,4},{5,12},{6,20},{7,28},{8,1},{9,9},{... | collective-permute-start | bytes 3145736 | tf_op jit(solution)/shard_map/ppermute | solution.py:1301
  617.1 125.5 %collective-permute-start.17 = (bf16[256,2048]{1,0:T(8,128)(2,1)}, bf16[256,2048]{1,0:T(8,128)(2,1)}, u32[]{:S(2)}, u32[]{:S(2)}) collective-permute-start(bf16[256,2048]{1,0:T(8,128)(2,1)} %reduce-scatter.6.cloned.1.call-done), channel_id=1, source_target_pairs={{0,0},{1,8},{2,16},{3,24},{4,4},{5,12},{6,20},{7,28},{8,1},{9,9},{... | collective-permute-start | bytes 3145736 | tf_op jit(solution)/shard_map/ppermute | solution.py:1301
  (55 other events, 686.8 us)
Sparse Core Ops, SparseCore 0:
  9.6 93.5 all-gather.1
  346.7 77.9 reduce-scatter.7
  440.7 92.8 reduce-scatter.5
  604.5 45.0 reduce-scatter.3

commit v5 on v4

--- a/solution.py
+++ b/solution.py
@@ -445,7 +445,7 @@
 
 
 def project_kernel(
-    width, number_ref, block_ref, stats_ref, vec_ref, weight_ref,
+    width, block_ref, stats_ref, vec_ref, weight_ref,
     recept_ref, keys_ref, values_ref, downs_ref, hidden_ref,
 ):
     base = 3 * width
@@ -478,7 +478,7 @@
 
 
 def unproject_kernel(
-    width, parts, piece, number_ref, block_ref, stats_ref, vec_ref, weight_ref,
+    width, parts, piece, block_ref, stats_ref, vec_ref, weight_ref,
     other_ref, recept_ref, keys_ref, values_ref, ups_ref, hidden_ref, downs_ref, up_ref,
     grad_ref, sums_ref, wide_ref, up_out, down_lows,
 ):
@@ -548,29 +548,28 @@
 
 def mix_specs(rows, width, own_width, parts):
     block = 256 if rows <= 1024 else 128
-    per_shard = width // parts // block
 
     def columns(height):
-        return pl.BlockSpec((height, block), lambda j, n: (0, j))
+        return pl.BlockSpec((height, block), lambda j: (0, j))
 
     def whole(shape):
-        return pl.BlockSpec(shape, lambda j, n: (0,) * len(shape))
+        return pl.BlockSpec(shape, lambda j: (0,) * len(shape))
 
     def weights(array):
         size = array.shape[1] if rows > 1024 else 3 * own_width + WIDE
-        return pl.BlockSpec((block, size), lambda j, n: (((j // per_shard) ^ n[0]) * per_shard + j % per_shard, 0))
+        return pl.BlockSpec((block, size), lambda j: (j, 0))
 
     return block, columns, whole, weights
 
 
-def run_project(number, balanced, stats, vec, weights, own_width, parts):
+def run_project(balanced, stats, vec, weights, own_width, parts):
     rows, width = balanced.shape
     block, columns, whole, weight_spec = mix_specs(rows, width, own_width, parts)
     shapes = [(rows, own_width)] * 3 + [(rows, WIDE)] * 2
     return pl.pallas_call(
         functools.partial(project_kernel, own_width),
         grid_spec=pltpu.PrefetchScalarGridSpec(
-            num_scalar_prefetch=1,
+            num_scalar_prefetch=0,
             grid=(width // block,),
             in_specs=[columns(rows), whole(stats.shape), columns(8), weight_spec(weights)],
             out_specs=[whole(s) for s in shapes],
@@ -579,10 +578,10 @@
         compiler_params=pltpu.CompilerParams(vmem_limit_bytes=60 << 20),
         cost_estimate=kernel_cost(rows, own_width, 60),
         name="mix_project",
-    )(number, balanced, stats, vec, weights)
-
-
-def run_unproject(number, balanced, stats, vec, weights, others, lows, ups, hidden, downs, up, parts):
+    )(balanced, stats, vec, weights)
+
+
+def run_unproject(balanced, stats, vec, weights, others, lows, ups, hidden, downs, up, parts):
     rows, width = balanced.shape
     own_width = lows[0].shape[1]
     seqs = width // own_width
@@ -593,16 +592,16 @@
     return pl.pallas_call(
         functools.partial(unproject_kernel, own_width, parts, piece),
         grid_spec=pltpu.PrefetchScalarGridSpec(
-            num_scalar_prefetch=1,
+            num_scalar_prefetch=0,
             grid=(width // block,),
             in_specs=[
                 columns(rows), whole(stats.shape), columns(8), weight_spec(weights),
-                pl.BlockSpec((block, others.shape[1]), lambda j, n: (j, 0)),
+                pl.BlockSpec((block, others.shape[1]), lambda j: (j, 0)),
             ]
             + [whole(a.shape) for a in (*lows, ups, hidden, downs, up)],
             out_specs=[
                 columns(rows), whole((rows, 2)),
-                pl.BlockSpec((parts, taken, piece, total), lambda j, n: (0, j, 0, 0)),
+                pl.BlockSpec((parts, taken, piece, total), lambda j: (0, j, 0, 0)),
                 whole((own_width, WIDE)),
             ],
             scratch_shapes=[pltpu.VMEM((rows, WIDE), BF16)],
@@ -615,7 +614,7 @@
         compiler_params=pltpu.CompilerParams(vmem_limit_bytes=60 << 20),
         cost_estimate=kernel_cost(rows, own_width, 120),
         name="mix_unproject",
-    )(number, balanced, stats, vec, weights, others, *lows, ups, hidden, downs, up)
+    )(balanced, stats, vec, weights, others, *lows, ups, hidden, downs, up)
 
 
 def norm_stats(values):
@@ -678,88 +677,117 @@
     return jnp.where(z > 0, 1, 0) + jnp.where(z < 3, 1, 0)
 
 
-def gather_kernel(own_ref, out_ref, copy_sem, right_send, right_recv, left_send, left_recv, x_send, x_recv):
-    s, w, side, z, x_device, _, _ = places()
+def gather_kernel(
+    own_ref, tail_ref, weight_ref, out_ref, tails_ref, weights_ref,
+    copy_sem, right_send, right_recv, left_send, left_recv, x_send, x_recv, c_send, c_recv, y_send, y_recv,
+):
+    s, w, side, z, x_device, core_device, y_device = places()
     up, down = (s + 2, w), (s - 2, w)
-    copy = pltpu.make_async_copy(own_ref, out_ref.at[s], copy_sem)
-    copy.start()
-    greet(((None, x_device), (z < 3, up), (z > 0, down)), 1 + line_ends(z))
-
-    def to_right(j, source, number):
-        return send(source, out_ref.at[number], right_send.at[j], right_recv.at[j], up)
-
-    def to_left(j, source, number):
-        return send(source, out_ref.at[number], left_send.at[j], left_recv.at[j], down)
-
-    def to_x(at, source, number):
-        return send(source, out_ref.at[number], x_send.at[at], x_recv.at[at], x_device)
-
-    @pl.when(z < 3)
-    def _():
-        to_right(0, own_ref, s).start()
-
-    @pl.when(z > 0)
-    def _():
-        to_left(0, own_ref, s).start()
-
-    to_x(z, own_ref, s).start()
+    across = w + 2 - 4 * (w // 2)
+    kinds = ((own_ref, out_ref), (tail_ref, tails_ref))
+    copies = [pltpu.make_async_copy(own, out.at[s], copy_sem.at[k]) for k, (own, out) in enumerate(kinds)]
+    copies.append(pltpu.make_async_copy(weight_ref, weights_ref.at[w], copy_sem.at[2]))
+    for copy in copies:
+        copy.start()
+    greet(((None, x_device), (None, core_device), (None, y_device), (z < 3, up), (z > 0, down)), 3 + line_ends(z))
+
+    weight_y = send(weight_ref, weights_ref.at[w], y_send, y_recv, y_device)
+    weight_core = send(weight_ref, weights_ref.at[w], c_send.at[0], c_recv.at[0], core_device)
+    weight_on = send(weights_ref.at[across], weights_ref.at[across], c_send.at[1], c_recv.at[1], core_device)
+    weight_y.start()
+    weight_core.start()
+
+    def to_right(j, k, source, number):
+        return send(source, kinds[k][1].at[number], right_send.at[j, k], right_recv.at[j, k], up)
+
+    def to_left(j, k, source, number):
+        return send(source, kinds[k][1].at[number], left_send.at[j, k], left_recv.at[j, k], down)
+
+    def to_x(at, k, source, number):
+        return send(source, kinds[k][1].at[number], x_send.at[at, k], x_recv.at[at, k], x_device)
+
+    for k, (own, _) in enumerate(kinds):
+
+        @pl.when(z < 3)
+        def _(k=k, own=own):
+            to_right(0, k, own, s).start()
+
+        @pl.when(z > 0)
+        def _(k=k, own=own):
+            to_left(0, k, own, s).start()
+
+        to_x(z, k, own, s).start()
     for j in (1, 2, 3):
         lower, upper = s - 2 * j, s + 2 * j
-
-        @pl.when(z >= j)
-        def _(j=j, lower=lower):
-            block = out_ref.at[lower]
-            to_right(j - 1, block, lower).wait_recv()
-
-            @pl.when(z < 3)
-            def _():
-                to_right(j, block, lower).start()
-
-            to_x(z - j, block, lower).start()
-
-        @pl.when(z + j <= 3)
-        def _(j=j, upper=upper):
-            block = out_ref.at[upper]
-            to_left(j - 1, block, upper).wait_recv()
-
-            @pl.when(z > 0)
-            def _():
-                to_left(j, block, upper).start()
-
-            to_x(z + j, block, upper).start()
-
-    for number in range(4):
-        done = to_x(number, own_ref, s)
-        done.wait_send()
-        done.wait_recv()
-    for j in range(3):
-
-        @pl.when((z >= j) & (z < 3))
-        def _(j=j):
-            to_right(j, own_ref, s).wait_send()
-
-        @pl.when((z + j <= 3) & (z > 0))
-        def _(j=j):
-            to_left(j, own_ref, s).wait_send()
-
-    copy.wait()
-
-
-def gather_seq(own):
-    seqs = lax.axis_size("seq")
-    if seqs != 8 or lax.axis_size("wsh") != 4:
-        return lax.all_gather(own, "seq", axis=0, tiled=False)
-    sems = [pltpu.SemaphoreType.DMA((3,))] * 4 + [pltpu.SemaphoreType.DMA((4,))] * 2
+        for k, (_, out) in enumerate(kinds):
+
+            @pl.when(z >= j)
+            def _(j=j, k=k, out=out, lower=lower):
+                block = out.at[lower]
+                to_right(j - 1, k, block, lower).wait_recv()
+
+                @pl.when(z < 3)
+                def _():
+                    to_right(j, k, block, lower).start()
+
+                to_x(z - j, k, block, lower).start()
+
+            @pl.when(z + j <= 3)
+            def _(j=j, k=k, out=out, upper=upper):
+                block = out.at[upper]
+                to_left(j - 1, k, block, upper).wait_recv()
+
+                @pl.when(z > 0)
+                def _():
+                    to_left(j, k, block, upper).start()
+
+                to_x(z + j, k, block, upper).start()
+
+    weight_y.wait_recv()
+    weight_on.start()
+    for k, (own, _) in enumerate(kinds):
+        for number in range(4):
+            done = to_x(number, k, own, s)
+            done.wait_send()
+            done.wait_recv()
+        for j in range(3):
+
+            @pl.when((z >= j) & (z < 3))
+            def _(j=j, k=k, own=own):
+                to_right(j, k, own, s).wait_send()
+
+            @pl.when((z + j <= 3) & (z > 0))
+            def _(j=j, k=k, own=own):
+                to_left(j, k, own, s).wait_send()
+
+    weight_core.wait_recv()
+    weight_on.wait_recv()
+    for copy in (weight_y, weight_core, weight_on):
+        copy.wait_send()
+    for copy in copies:
+        copy.wait()
+
+
+def gather_first(own, tail, weight):
+    seqs, parts = lax.axis_size("seq"), lax.axis_size("wsh")
+    if seqs != 8 or parts != 4:
+        return (
+            lax.all_gather(own, "seq", axis=0, tiled=False),
+            lax.all_gather(tail, "seq", axis=0, tiled=False),
+            lax.all_gather(weight, "wsh", axis=0, tiled=False),
+        )
+    dma = pltpu.SemaphoreType.DMA
+    given = ((seqs, own), (seqs, tail), (parts, weight))
     return pl.pallas_call(
         gather_kernel,
-        in_specs=[pl.BlockSpec(memory_space=pl.ANY)],
-        out_specs=pl.BlockSpec(memory_space=pl.ANY),
-        out_shape=jax.ShapeDtypeStruct((seqs,) + own.shape, own.dtype),
-        scratch_shapes=[pltpu.SemaphoreType.DMA] + sems,
+        in_specs=[pl.BlockSpec(memory_space=pl.ANY)] * 3,
+        out_specs=[pl.BlockSpec(memory_space=pl.ANY)] * 3,
+        out_shape=[jax.ShapeDtypeStruct((n,) + x.shape, x.dtype) for n, x in given],
+        scratch_shapes=[dma((3,))] + [dma((3, 2))] * 4 + [dma((4, 2))] * 2 + [dma((2,))] * 2 + [dma] * 2,
         compiler_params=pltpu.CompilerParams(collective_id=1, has_side_effects=True),
         cost_estimate=pl.CostEstimate(flops=0, bytes_accessed=100 << 20, transcendentals=0),
-        name="gather_seq",
-    )(own)
+        name="gather_first",
+    )(own, tail, weight)
 
 
 def reduce_kernel(
@@ -882,7 +910,7 @@
         + [pltpu.SemaphoreType.DMA((4, splits))] * 2
         + [pltpu.SemaphoreType.DMA((3, splits))] * 4,
         compiler_params=pltpu.CompilerParams(collective_id=2, has_side_effects=True, vmem_limit_bytes=40 << 20),
-        cost_estimate=pl.CostEstimate(flops=0, bytes_accessed=120 << 20, transcendentals=0),
+        cost_estimate=pl.CostEstimate(flops=0, bytes_accessed=1 << 20, transcendentals=0),
         name="reduce_seq",
     )(x)
 
@@ -1069,8 +1097,10 @@
 def gather_near(x):
     if lax.axis_size("wsh") != 4:
         return lax.all_gather(x, "wsh", axis=0, tiled=True)
-    across = swap(x, 2)
-    beside = swap(x, 1)
+    return gathered_near(x, swap(x, 1), swap(x, 2))
+
+
+def gathered_near(x, beside, across):
     return jnp.concatenate([x, beside, across, swap(across, 1)], 0)
 
 
@@ -1126,13 +1156,27 @@
     piece = shard // seqs
     column = me * own_width
 
+    def own_columns(matrix):
+        return lax.dynamic_slice_in_dim(matrix, column, own_width, 1)
+
+    near = parts == 4
+    up_piece = lax.dynamic_slice_in_dim(lowrank_up_weight, column % shard, own_width, 0)
+    total = 3 * own_width + WIDE
+    own_weights = jnp.concatenate(
+        [
+            own_columns(receptance_matrix), own_columns(key_matrix), own_columns(value_matrix),
+            pad_ranks(lowrank_down_weight), up_piece.reshape(shard, -1),
+        ],
+        1,
+    )
+
     dest_seq = destination // rows // parts
     position = dest_seq * rows + destination % rows
     digits = jnp.stack([position // DIGIT, position % DIGIT, valid], 1).astype(BF16)
     tail = jnp.pad(digits, ((0, 0), (0, EXTRA - 3)))
-    given = gather_seq(jnp.concatenate([tokens, tail], 1)).reshape(group, -1)
-    first_values, given = lax.optimization_barrier((first_layer_values, given))
-    info = given[:, width : width + 3].astype(F32)
+    given, tails, weights = gather_first(tokens, tail, own_weights)
+    given, tails, weights = given.reshape(group, width), tails.reshape(group, EXTRA), weights.reshape(width, -1)
+    info = tails[:, :3].astype(F32)
     places = (info[:, 0] * DIGIT + info[:, 1]).astype(jnp.int32)
     numbers = jnp.arange(group, dtype=jnp.int32)
     permute = (numbers[:, None] == places[None, :]).astype(BF16)
@@ -1146,11 +1190,6 @@
     arrival = jnp.cumsum(mine.astype(jnp.int32)) - 1
     own_rows = ((index[:, None] + me * rows) == places[None, :]).astype(BF16)
     settle = dot(own_rows, (mine[:, None] & (arrival[:, None] == index[None, :])).astype(BF16)).astype(BF16)
-
-    first_given = exchange(
-        first_values.reshape(rows, seqs, own_width).transpose(1, 0, 2), "seq"
-    ).reshape(group, own_width)
-    first = dot(permute, first_given).astype(BF16)
 
     offsets = jnp.cumsum(lengths[0]) - lengths[0]
     starts = jnp.any(numbers[:, None] == offsets[None, :], 1).astype(F32)
@@ -1163,39 +1202,28 @@
     ).reshape(-1, BLOCK)
     flowing = (1.0 - starts)[:, None]
 
-    def own_columns(matrix):
-        return lax.dynamic_slice_in_dim(matrix, column, own_width, 1)
-
-    near = parts == 4
-    number = lax.axis_index("wsh") if near else 0
-    up_piece = lax.dynamic_slice_in_dim(lowrank_up_weight, column % shard, own_width, 0)
-    total = 3 * own_width + WIDE
-    weights = gather_near(
-        jnp.concatenate(
-            [
-                own_columns(receptance_matrix), own_columns(key_matrix), own_columns(value_matrix),
-                pad_ranks(lowrank_down_weight), up_piece.reshape(shard, -1),
-            ],
-            1,
-        )
-    )
     up = pad_ranks(
         lax.dynamic_slice(
-            weights, (((column // shard) ^ number) * shard, total), (shard, weights.shape[1] - total)
+            weights, (column // shard * shard, total), (shard, weights.shape[1] - total)
         ).reshape(own_width, -1)
     ).T
-    number = jnp.full((1,), number, jnp.int32)
-    w_out = lax.all_gather(output_matrix, "wsh", axis=0, tiled=True)
     vec = lax.dynamic_slice_in_dim(vectors, column, own_width, 0)[:, 8:16].T
 
-    balanced = dot(permute, given[:, :width]).astype(BF16)
+    output_late, given = lax.optimization_barrier((output_matrix, given))
+    w_out = lax.all_gather(output_late, "wsh", axis=0, tiled=True)
+    balanced = dot(permute, given).astype(BF16)
     wide_rows = balanced.astype(F32)
     mean = jnp.mean(wide_rows, -1, keepdims=True)
     scale_one = lax.rsqrt(jnp.mean(jnp.square(wide_rows - mean), -1, keepdims=True) + 1e-05)
     stats = jnp.concatenate([mean, scale_one, flowing, flowing], 1)
     mix_vec = vectors[:, :8].T
-    recept, keys, values, downs, hidden = run_project(number, balanced, stats, mix_vec, weights, own_width, parts)
-    teacher_late, recept = lax.optimization_barrier((teacher, recept))
+    first_values, stats = lax.optimization_barrier((first_layer_values, stats))
+    first_given = exchange(
+        first_values.reshape(rows, seqs, own_width).transpose(1, 0, 2), "seq"
+    ).reshape(group, own_width)
+    recept, keys, values, downs, hidden = run_project(balanced, stats, mix_vec, weights, own_width, parts)
+    teacher_late, recept, first_given = lax.optimization_barrier((teacher, recept, first_given))
+    first = dot(permute, first_given).astype(BF16)
     teacher_rows = exchange(dot(arrange, teacher_late).astype(BF16).reshape(seqs, rows // seqs, width), "seq")
     inputs = (recept, keys, values, hidden, first, up, vec, segments)
     mixed_out, *saved = run_forward(*inputs)
@@ -1206,7 +1234,7 @@
     own = lax.dynamic_slice_in_dim(balanced, me * rows, rows, 0).astype(F32)
     own_starts = lax.dynamic_slice_in_dim(starts, me * rows, rows, 0)
     own_flowing = (1.0 - own_starts)[:, None]
-    own_valid = dot(own_rows, given[:, width : width + EXTRA])[:, 2]
+    own_valid = dot(own_rows, tails)[:, 2]
     residual = own + dot(mixed_rows, w_out)
     standard_two, scale_two = norm_stats(residual)
     normed_two = standard_two * vectors[:, 16] + vectors[:, 17]
@@ -1253,7 +1281,7 @@
     grad_heads = exchange(grad_posted.reshape(rows, seqs, own_width).transpose(1, 0, 2), "seq").reshape(group, own_width)
     grad_heads, value_part, mixed_late = lax.optimization_barrier((grad_heads, value_part, mixed_rows))
     lefts = exchange(mixed_late.reshape(rows, seqs, parts, piece).transpose(2, 0, 1, 3), "wsh")
-    near_grad = gather_near(grad_low)
+    near_grad = (swap(grad_low, 1), swap(grad_low, 2)) if near else gather_near(grad_low)
     recept_low, keys_low, values_low, ups_low, grad_first, grad_vec_heads = run_backward(grad_heads, *inputs, saved)
     if paired:
         channel_other, pre_other, lefts, near_grad, recept_low = lax.optimization_barrier(
@@ -1264,53 +1292,61 @@
         lefts, near_grad, recept_low = lax.optimization_barrier((lefts, near_grad, recept_low))
         key_part = dot(grad_pre, channel, TN).astype(BF16)
     if near:
-        lefts = jnp.stack([lax.dynamic_index_in_dim(lefts, number[0] ^ k, 0, keepdims=False) for k in range(4)])
+        near_grad = gathered_near(grad_low, *near_grad)
+        lefts = jnp.stack([lax.dynamic_index_in_dim(lefts, lax.axis_index("wsh") ^ k, 0, keepdims=False) for k in range(4)])
     out_part = dot(lefts.reshape(rows * parts, -1), near_grad, TN).astype(BF16)
 
     result_back = dot(settle, result.astype(BF16), TN).astype(BF16).reshape(seqs, rows // seqs, width)
     first_back = dot(permute, grad_first, TN).astype(BF16).reshape(seqs, rows // seqs, width)
     moved = exchange(jnp.concatenate([result_back, first_back], 1), "seq")
     recept_low, key_part, out_part = lax.optimization_barrier((recept_low, key_part, out_part))
+    if paired:
+        lines = [[0, 2, 4, 6], [1, 3, 5, 7]]
+        turned = [
+            ((z * 2 + x) * 4 + w, (w * 2 + x) * 4 + z) for z in range(4) for x in range(2) for w in range(4)
+        ]
+
+        def along(part):
+            return lax.psum_scatter(part, "seq", scatter_dimension=0, tiled=True, axis_index_groups=lines)
+
+        def turn(part):
+            return lax.ppermute(part, ("seq", "wsh"), turned)
+
+        halves_out = out_part.reshape(seqs // 2, 2, piece, width)
+        x_side = me % 2
+        out_mine = lax.dynamic_index_in_dim(halves_out, x_side, 1, keepdims=False).astype(F32)
+        out_other = beside(lax.dynamic_index_in_dim(halves_out, 1 - x_side, 1, keepdims=False))
+        value_turned, key_sum = turn(along(value_part)), along(key_part)
+    else:
+        moves = [(s * parts + w, w * seqs + s) for s in range(seqs) for w in range(parts)]
+
+        def ffn_grad(part):
+            part = lax.psum_scatter(part, "seq", scatter_dimension=0, tiled=True)
+            return lax.ppermute(part, ("seq", "wsh"), moves).astype(F32)
+
+        grad_ffn_value, grad_ffn_key = ffn_grad(value_part), ffn_grad(key_part)
+        grad_out = lax.psum_scatter(out_part, "seq", scatter_dimension=0, tiled=True)
+
     heads_part = lax.dynamic_update_slice_in_dim(jnp.zeros((width, 8), F32), grad_vec_heads.T, column, 0)
     vec_two = jnp.stack(
         [jnp.sum(grad_normed_two * standard_two, 0), jnp.sum(grad_normed_two, 0), grad_vec_mix_two], 1
     )
     others = jnp.concatenate([heads_part, jnp.pad(vec_two, ((0, 0), (0, 13)))], 1)
     scaled_grad, sums, wide, up_grad = run_unproject(
-        number, balanced, stats, mix_vec, weights, others, (recept_low, keys_low, values_low), ups_low, hidden, downs, up, parts
+        balanced, stats, mix_vec, weights, others, (recept_low, keys_low, values_low), ups_low, hidden, downs, up, parts
     )
-    moved, sums = lax.optimization_barrier((moved, sums))
+    if paired:
+        moved, value_turned, out_other, scaled_grad, sums, wide, up_grad = lax.optimization_barrier(
+            (moved, value_turned, out_other, scaled_grad, sums, wide, up_grad)
+        )
+        out_half = (out_mine + out_other.astype(F32)).astype(BF16).reshape(-1, width)
+        out_half, sums = lax.optimization_barrier((out_half, sums))
+        grad_out = along(out_half)
+        grad_ffn_value, grad_ffn_key = value_turned.astype(F32), turn(key_sum).astype(F32)
+    else:
+        moved, scaled_grad, sums, wide = lax.optimization_barrier((moved, scaled_grad, sums, wide))
     output = dot(arrange, moved[:, : rows // seqs].reshape(rows, width), TN).astype(BF16)
     grad_first_rows = moved[:, rows // seqs :].reshape(seqs, rows, own_width).transpose(1, 0, 2).reshape(rows, width)
-
-    if paired:
-        halves_out = out_part.reshape(seqs // 2, 2, piece, width)
-        x_side = me % 2
-        out_mine = lax.dynamic_index_in_dim(halves_out, x_side, 1, keepdims=False).astype(F32)
-        out_other = beside(lax.dynamic_index_in_dim(halves_out, 1 - x_side, 1, keepdims=False))
-        out_half = (out_mine + out_other.astype(F32)).astype(BF16).reshape(-1, width)
-        lines = [[0, 2, 4, 6], [1, 3, 5, 7]]
-        turned = [
-            ((z * 2 + x) * 4 + w, (w * 2 + x) * 4 + z) for z in range(4) for x in range(2) for w in range(4)
-        ]
-
-        def along(part):
-            return lax.psum_scatter(part, "seq", scatter_dimension=0, tiled=True, axis_index_groups=lines)
-
-        def turn(part):
-            return lax.ppermute(part, ("seq", "wsh"), turned).astype(F32)
-
-        grad_ffn_value, grad_ffn_key = turn(along(value_part)), turn(along(key_part))
-        grad_out = along(out_half).astype(F32)
-    else:
-        moves = [(s * parts + w, w * seqs + s) for s in range(seqs) for w in range(parts)]
-
-        def ffn_grad(part):
-            part = lax.psum_scatter(part, "seq", scatter_dimension=0, tiled=True)
-            return lax.ppermute(part, ("seq", "wsh"), moves).astype(F32)
-
-        grad_ffn_value, grad_ffn_key = ffn_grad(value_part), ffn_grad(key_part)
-        grad_out = lax.psum_scatter(out_part, "seq", scatter_dimension=0, tiled=True).astype(F32)
 
     standard = (balanced.astype(F32) - mean) * scale_one
     grad_balanced = scale_one * (scaled_grad - sums[:, :1] * (1.0 / width) - standard * (sums[:, 1:] * (1.0 / width)))
@@ -1324,7 +1360,7 @@
     else:
         wide_part = block_sum(wide)
     grad_tokens = reduce_seq(grad_given).astype(BF16)
-    wide_part, grad_tokens = lax.optimization_barrier((wide_part, grad_tokens))
+    wide_part, grad_tokens, grad_out = lax.optimization_barrier((wide_part, grad_tokens, grad_out))
     wide_all = exchange(wide_part.astype(BF16), "seq").astype(F32)
 
     def square(at):
@@ -1339,7 +1375,7 @@
     return (
         output, grad_tokens, grad_first_rows,
         square(0), square(1), square(2),
-        grad_out, grad_down, up_part,
+        grad_out.astype(F32), grad_down, up_part,
         grad_ffn_key, grad_ffn_value, grad_vectors,
     )
 

time: 763 us -> 716 us (0.938)
  waiting for transfers between devices: 148 us -> 115 us
  other arithmetic: 59.9 us -> 35.4 us
  Pallas kernels: 353 us -> 368 us
  starting transfers between devices: 59.5 us -> 68.6 us
  matrix products: 65.4 us -> 57.7 us
    ppermute x2, waiting for transfers between devices: 83.6 us -> 42.2 us  [turn(): return lax.ppermute(part, ('seq', 'wsh'), turned)]
    reduce_scatter x3, waiting for transfers between devices: 28.2 us -> 51.9 us  [along(): lax.psum_scatter(part, 'seq', scatter_dimension=0, tiled=True, axis_index...]
    pallas_call x1, Pallas kernels: 57.4 us -> 70 us  [gather_first(): pl.pallas_call(gather_kernel, in_specs=[pl.BlockSpec(memory_space=pl.ANY)...]
    ppermute x12 -> x9, waiting for transfers between devices: 15.3 us -> 4.01 us  [swap(): return lax.ppermute(x, 'wsh', [(i, i ^ by) for i in range(size)])]
    concatenate x3 -> x0, other arithmetic: 8.16 us -> none  [the longest x2 7.31 us: gather_near(): return jnp.concatenate([x, beside, across, swap(across, 1)], 0)]
    dot_general x17, matrix products: 65.4 us -> 57.7 us  [dot(): return lax.dot_general(a, b, dims, preferred_element_type=F32)]
    unnamed x127 -> x112, local copies, waits for them, and re-layouts: 16.8 us -> 22 us
  transfers between devices with their start and end apart: 30 -> 27, of which waited for: 12 -> 9; matrix products, arithmetic and copies ran while one was open for 19% -> 12% of each run, Pallas kernels for 35% -> 30%
where the time goes in v5:
time: 716 us; the launch traced here: 706 us
  Pallas kernels  368 us (51%)
  waiting for transfers between devices  115 us (16%)
  starting transfers between devices  68.6 us (10%)
  matrix products  57.7 us (8%)
  local copies, waits for them, and re-layouts  44.8 us (6%)
  other arithmetic  35.4 us (5%)
  between operations  16.3 us (2%)
    pallas_call x2, Pallas kernels, channel_stage(): pl.pallas_call(body, in_specs=[pl.BlockSpec(memory_space=pltpu.VMEM)] + [...  89.3 us
    pallas_call x1, Pallas kernels, gather_first(): pl.pallas_call(gather_kernel, in_specs=[pl.BlockSpec(memory_space=pl.ANY)...  70 us
    pallas_call x1, Pallas kernels, reduce_seq(): pl.pallas_call(functools.partial(reduce_kernel, splits), in_specs=[pl.Blo...  66.1 us
    dot_general x17, matrix products, dot(): return lax.dot_general(a, b, dims, preferred_element_type=F32)  57.7 us
    reduce_scatter x3, waiting for transfers between devices, along(): lax.psum_scatter(part, 'seq', scatter_dimension=0, tiled=True, axis_index...  51.9 us
    pallas_call x1, Pallas kernels, run_backward(): pl.pallas_call(functools.partial(backward_kernel, count), grid=(rows // s...  47.3 us
    all_to_all x7, starting transfers between devices, exchange(): return lax.all_to_all(x, axis, split_axis=0, concat_axis=0, tiled=True)  42.7 us
    ppermute x2, waiting for transfers between devices, turn(): return lax.ppermute(part, ('seq', 'wsh'), turned)  42.2 us
  transfers between devices with their start and end apart: 27, of which 9 were waited for; matrix products, arithmetic and copies ran while one was open for 12% of the time, Pallas kernels for 30%

profile of v5, /device:TPU:4, one launch (start us, length us, event | category | flops | bytes accessed | tf_op | source)
XLA Modules:
  0.0 706.4 jit_solution(5934598566625254174)
XLA Ops:
  18.3 70.0 %gather_first.1 = (bf16[8,128,2048]{2,1,0:T(8,128)(2,1)}, bf16[8,128,128]{2,1,0:T(8,128)(2,1)}, bf16[4,512,1664]{2,1,0:T(8,128)(2,1)}) custom-call(bf16[128,2048]{1,0:T(8,128)(2,1)} %own_ref.1, bf16[128,128]{1,0:T(8,128)(2,1)} %pad.30.tail_ref, bf16[512,1664]{1,0:T(8,128)(2,1)} %copy-done.28), custom_call_target="tpu_custom_call" | custom-call | bytes 104857600 | tf_op jit(solution)/shard_map/gather_first/pallas_call | solution.py:781
  89.9 7.0 convert_reduce_fusion
  101.3 5.9 all-to-all-start
  113.8 19.4 %mix_project.1 = (f32[1024,256]{1,0:T(8,128)}, f32[1024,256]{1,0:T(8,128)}, f32[1024,256]{1,0:T(8,128)}, f32[1024,640]{1,0:T(8,128)}, bf16[1024,640]{1,0:T(8,128)(2,1)}) custom-call(bf16[1024,2048]{1,0:T(8,128)(2,1)} %copy-done.18, f32[1024,4]{1,0:T(8,128)} %copy.132.stats_ref, f32[8,2048]{1,0:T(8,128)} %slice_bitcast_fusion.3.vec_ref, ...), custom_call_target="tpu_custom_call" | custom-call | flops 134217728 | bytes 62914560 | tf_op jit(solution)/shard_map/mix_project/pallas_call | solution.py:569
  134.9 6.2 all-to-all-start.1
  142.1 36.2 %mix_forward.1 = (bf16[1024,256]{1,0:T(8,128)(2,1)S(1)}, bf16[1024,256]{1,0:T(8,128)(2,1)S(1)}, f32[1024,256]{1,0:T(8,128)S(1)}, f32[1024,256]{1,0:T(8,128)S(1)}, f32[1024,256]{1,0:T(8,128)S(1)}) custom-call(f32[1024,256]{1,0:T(8,128)S(1)} %copy-done.3, f32[1024,256]{1,0:T(8,128)} %get-tuple-element.91.keys_ref, f32[1024,256]{1,0:T(8,128)} %get-tuple-element.92.values_ref, ...), custom_call_target="tpu_custom_call" | custom-call | flops 134217728 | bytes 115343360 | tf_op jit(solution)/shard_map/mix_forward/pallas_call | solution.py:385
  183.1 6.0 all-to-all-start.2
  195.9 7.7 %all-to-all-done.2 = bf16[8,128,256]{1,2,0:T(8,128)(2,1)S(1)} async-done(((bf16[8,128,256]{1,2,0:T(8,128)(2,1)}), bf16[8,128,256]{1,2,0:T(8,128)(2,1)S(1)}, u32[]{:S(2)}, u32[]{:S(2)}) %all-to-all-start.2) | async-done | bytes 524320 | tf_op jit(solution)/shard_map/all_to_all | solution.py:1089
  203.7 5.0 fusion.85
  215.4 37.4 %channel_forward.1 = (f32[128,2048]{1,0:T(8,128)}, bf16[512,2048]{1,0:T(8,128)(2,1)}, bf16[512,1024]{1,0:T(8,128)(2,1)}, bf16[512,1024]{1,0:T(8,128)(2,1)}, f32[512,2048]{1,0:T(8,128)}) custom-call(bf16[128,2048]{1,0:T(8,128)(2,1)} %add_convert_fusion.2.refs_0_, bf16[2048,2048]{1,0:T(8,128)(2,1)} %refs_2_.3, bf16[2048,2048]{1,0:T(8,128)(2,1)} %refs_1_.3), custom_call_target="tpu_custom_call" | custom-call | bytes 104857600 | tf_op jit(solution)/shard_map/channel_forward/pallas_call | solution.py:1061
  255.5 51.9 %channel_backward.1 = (f32[128,2048]{1,0:T(8,128)}, bf16[512,2048]{1,0:T(8,128)(2,1)}, bf16[512,1024]{1,0:T(8,128)(2,1)}, bf16[512,2048]{1,0:T(8,128)(2,1)}, bf16[512,1024]{1,0:T(8,128)(2,1)}) custom-call(bf16[128,2048]{1,0:T(8,128)(2,1)} %get-tuple-element.268.refs_0_, bf16[2048,2048]{1,0:T(8,128)(2,1)} %refs_1_.3, bf16[2048,2048]{1,0:T(8,128)(2,1)} %refs_2_.3, ...), custom_call_target="tpu_custom_call" | custom-call | bytes 104857600 | tf_op jit(solution)/shard_map/channel_backward/pallas_call | solution.py:1061
  311.5 4.1 collective-permute-done.3
  317.9 3.9 convolution_convert_fusion.1
  322.6 3.8 all-to-all-start.3
  326.7 4.5 fusion.91
  331.2 4.7 add_convert_fusion.1
  335.9 3.9 all-to-all-done.3
  342.0 7.5 %fusion.92 = f32[1024,2048]{1,0:T(8,128)} fusion(bf16[512,1024]{1,0:T(8,128)(2,1)S(1)} %copy-done.42, bf16[512,2048]{1,0:T(8,128)(2,1)} %get-tuple-element.115), kind=kOutput, calls=%fused_computation.216 | convolution fusion | flops 2147483648 | bytes 11534336 | tf_op jit(solution)/shard_map/dot_general | solution.py:28
  351.5 6.3 all-to-all-start.5
  360.0 47.3 %mix_backward.1 = (bf16[1024,256]{1,0:T(8,128)(2,1)S(1)}, bf16[1024,256]{1,0:T(8,128)(2,1)S(1)}, bf16[1024,256]{1,0:T(8,128)(2,1)S(1)}, bf16[4,1024,256]{2,1,0:T...) custom-call(bf16[1024,256]{1,0:T(8,128)(2,1)S(1)} %bitcast.129, f32[1024,256]{1,0:T(8,128)S(1)} %copy-done.3, ...), custom_call_target="tpu_custom_call" | custom-call | flops 134217728 | bytes 157286400 | tf_op jit(solution)/shard_map/mix_backward/pallas_call | solution.py:413
  412.2 4.0 all-to-all-start.4
  416.4 8.7 %add_convert_fusion = bf16[1024,2048]{1,0:T(8,128)(2,1)} fusion(f32[1024,2048]{1,0:T(8,128)} %fusion.92, bf16[512,1024]{1,0:T(8,128)(2,1)} %collective-permute-done.6, bf16[512,2048]{1,0:T(8,128)(2,1)} %collective-permute-done.5), kind=kOutput, calls=%fused_computation.8 | convolution fusion | flops 2151677952 | bytes 15728640 | tf_op jit(solution)/shard_map/dot_general | solution.py:28
  433.7 4.0 collective-permute-start.4
  439.1 40.0 %mix_unproject.1 = (f32[1024,2048]{1,0:T(8,128)}, f32[1024,2]{1,0:T(8,128)}, bf16[4,8,64,1408]{3,2,1,0:T(8,128)(2,1)}, bf16[256,640]{1,0:T(8,128)(2,1)}) custom-call(bf16[1024,2048]{1,0:T(8,128)(2,1)} %copy-done.18, f32[1024,4]{1,0:T(8,128)} %copy.132.stats_ref, f32[8,2048]{1,0:T(8,128)} %slice_bitcast_fusion.3.vec_ref, bf16[2048,1664]{1,0:T(8,128)(2,1)} %bitcast.137, ...), custom_call_target="tpu_custom_call" | custom-call | flops 134217728 | bytes 125829120 | tf_op jit(solution)/shard_map/mix_unproject/pallas_call | solution.py:592
  479.1 8.0 %collective-permute-done.4 = bf16[256,2048]{1,0:T(8,128)(2,1)S(1)} collective-permute-done((bf16[256,2048]{1,0:T(8,128)(2,1)}, bf16[256,2048]{1,0:T(8,128)(2,1)S(1)}, u32[]{:S(2)}, u32[]{:S(2)}) %collective-permute-start.4) | collective-permute-done | bytes 1048608 | tf_op jit(solution)/shard_map/ppermute | solution.py:1313
  499.7 4.9 fusion.12
  505.6 66.1 %reduce_seq.1 = f32[128,2048]{1,0:T(8,128)S(1)} custom-call(bf16[8,128,2048]{2,1,0:T(8,128)(2,1)S(1)} %bitcast.128), custom_call_target="tpu_custom_call" | custom-call | bytes 1048576 | tf_op jit(solution)/shard_map/reduce_seq/pallas_call | solution.py:903
  574.2 10.5 %all-to-all-start.6 = ((bf16[8,64,1408]{2,1,0:T(8,128)(2,1)}), bf16[8,64,1408]{2,1,0:T(8,128)(2,1)S(1)}, u32[]{:S(2)}, u32[]{:S(2)}) async-start(bf16[8,64,1408]{2,1,0:T(8,128)(2,1)} %fusion.17), calls=%async_computation.8 | async-start | bytes 2883584 | tf_op jit(solution)/shard_map/all_to_all | solution.py:1089
  587.7 51.9 %reduce-scatter.8.cloned.1.call-done = bf16[256,2048]{1,0:T(8,128)(2,1)} async-done(((bf16[1024,2048]{1,0:T(8,128)(2,1)}), bf16[256,2048]{1,0:T(8,128)(2,1)}) %reduce-scatter.8.cloned.1.call-update) | async-done | bytes 1048592 | tf_op jit(solution)/shard_map/reduce_scatter | solution.py:1310
  639.5 4.5 collective-permute-start.15
  645.0 5.2 collective-permute-start.14
  657.0 34.2 %collective-permute-done.15 = bf16[256,2048]{1,0:T(8,128)(2,1)} collective-permute-done((bf16[256,2048]{1,0:T(8,128)(2,1)}, bf16[256,2048]{1,0:T(8,128)(2,1)}, u32[]{:S(2)}, u32[]{:S(2)}) %collective-permute-start.15) | collective-permute-done | bytes 1048608 | tf_op jit(solution)/shard_map/ppermute | solution.py:1313
  (295 shorter events, 109.2 us)
Async XLA Ops:
  7.2 126.6 %copy-start = (bf16[128,2048]{1,0:T(8,128)(2,1)S(1)}, bf16[128,2048]{1,0:T(8,128)(2,1)}, u32[]{:S(2)}) copy-start(bf16[128,2048]{1,0:T(8,128)(2,1)} %param.17) | copy-start | bytes 1572868
  7.2 196.5 %all-gather.2.cloned.1.call-start = ((), (), s32[]{:S(2)}) async-start(), calls=%async_computation.10 | async-start | bytes 10485760 | tf_op jit(solution)/shard_map/all_gather | solution.py:1213
  15.6 72.8 %copy-start.44 = (s32[1,4]{1,0:T(1,128)S(1)}, s32[1,4]{1,0:T(1,128)}, u32[]{:S(2)}) copy-start(s32[1,4]{1,0:T(1,128)} %param.20) | copy-start | bytes 52
  101.3 32.2 %all-to-all-start = ((bf16[8,128,256]{1,2,0:T(8,128)(2,1)}), bf16[8,128,256]{1,2,0:T(8,128)(2,1)S(1)}, u32[]{:S(2)}, u32[]{:S(2)}) async-start(bf16[8,128,256]{1,2,0:T(8,128)(2,1)} %bitcast.15), calls=%async_computation | async-start | bytes 1048576 | tf_op jit(solution)/shard_map/all_to_all | solution.py:1089
  108.5 81.3 %collective-permute-start.1 = (f32[8,128]{1,0:T(8,128)S(1)}, f32[8,128]{1,0:T(8,128)S(1)}, u32[]{:S(2)}, u32[]{:S(2)}) collective-permute-start(f32[8,128]{1,0:T(8,128)S(1)} %broadcast_in_dim.4), channel_id=1, source_target_pairs={{0,1},{1,0},{2,3},{3,2},{4,5},{5,4},{6,7},{7,6},{8,9},{9,8},{10,11... | collective-permute-start | bytes 12296 | tf_op jit(solution)/shard_map/ppermute | solution.py:1094
  134.9 47.2 %all-to-all-start.1 = ((bf16[8,16,2048]{2,1,0:T(8,128)(2,1)}), bf16[8,16,2048]{2,1,0:T(8,128)(2,1)S(1)}, u32[]{:S(2)}, u32[]{:S(2)}) async-start(bf16[8,16,2048]{2,1,0:T(8,128)(2,1)} %bitcast.17), calls=%async_computation.1 | async-start | bytes 1048576 | tf_op jit(solution)/shard_map/all_to_all | solution.py:1089
  141.3 216.6 %copy-start.2 = (bf16[640,256]{1,0:T(8,128)(2,1)}, bf16[640,256]{1,0:T(8,128)(2,1)S(1)}, u32[]{:S(2)}) copy-start(bf16[640,256]{1,0:T(8,128)(2,1)S(1)} %fusion.50.up_ref) | copy-start | bytes 983044
  183.1 20.6 %all-to-all-start.2 = ((bf16[8,128,256]{1,2,0:T(8,128)(2,1)}), bf16[8,128,256]{1,2,0:T(8,128)(2,1)S(1)}, u32[]{:S(2)}, u32[]{:S(2)}) async-start(bf16[8,128,256]{1,2,0:T(8,128)(2,1)} %copy.140), calls=%async_computation.2 | async-start | bytes 1048576 | tf_op jit(solution)/shard_map/all_to_all | solution.py:1089
  190.4 3.7 collective-permute-start.2
  209.3 4.7 collective-permute-start
  215.4 37.4 %copy-start.16 = (f32[128,2048]{1,0:T(8,128)S(1)}, f32[128,2048]{1,0:T(8,128)}, u32[]{:S(2)}) copy-start(f32[128,2048]{1,0:T(8,128)} %copy-done.15) | copy-start | bytes 3145732
  310.0 5.5 collective-permute-start.3
  322.6 17.2 %all-to-all-start.3 = ((bf16[8,128,256]{2,1,0:T(8,128)(2,1)}), bf16[8,128,256]{2,1,0:T(8,128)(2,1)S(1)}, u32[]{:S(2)}, u32[]{:S(2)}) async-start(bf16[8,128,256]{2,1,0:T(8,128)(2,1)} %bitcast.125), calls=%async_computation.3 | async-start | bytes 1048576 | tf_op jit(solution)/shard_map/all_to_all | solution.py:1089
  326.5 107.2 %reduce-scatter.4.cloned.1.call-start = ((), (), s32[]{:S(2)}) async-start(), calls=%async_computation.11 | async-start | bytes 5242880 | tf_op jit(solution)/shard_map/reduce_scatter | solution.py:1310
  339.9 76.4 %collective-permute-start.5 = (bf16[512,2048]{1,0:T(8,128)(2,1)}, bf16[512,2048]{1,0:T(8,128)(2,1)}, u32[]{:S(2)}, u32[]{:S(2)}) collective-permute-start(bf16[512,2048]{1,0:T(8,128)(2,1)} %get-tuple-element.115), channel_id=1, source_target_pairs={{0,4},{4,0},{8,12},{12,8},{16,20},{20,16},{24,28},{28,24},{1,5},{5... | collective-permute-start | bytes 6291464 | tf_op jit(solution)/shard_map/ppermute | solution.py:1108
  341.4 74.8 %collective-permute-start.6 = (bf16[512,1024]{1,0:T(8,128)(2,1)}, bf16[512,1024]{1,0:T(8,128)(2,1)}, u32[]{:S(2)}, u32[]{:S(2)}) collective-permute-start(bf16[512,1024]{1,0:T(8,128)(2,1)} %get-tuple-element.116), channel_id=1, source_target_pairs={{0,4},{4,0},{8,12},{12,8},{16,20},{20,16},{24,28},{28,24},{1,5},{5... | collective-permute-start | bytes 3145736 | tf_op jit(solution)/shard_map/ppermute | solution.py:1108
  349.5 66.8 %collective-permute-start.7 = (bf16[128,2048]{1,0:T(8,128)(2,1)}, bf16[128,2048]{1,0:T(8,128)(2,1)}, u32[]{:S(2)}, u32[]{:S(2)}) collective-permute-start(bf16[128,2048]{1,0:T(8,128)(2,1)} %get-tuple-element.232), channel_id=1, source_target_pairs={{0,1},{1,0},{2,3},{3,2},{4,5},{5,4},{6,7},{7,6},{8,9},{9,8},{10,11... | collective-permute-start | bytes 1572872 | tf_op jit(solution)/shard_map/ppermute | solution.py:1094
  349.5 66.8 %collective-permute-start.8 = (bf16[128,2048]{1,0:T(8,128)(2,1)}, bf16[128,2048]{1,0:T(8,128)(2,1)}, u32[]{:S(2)}, u32[]{:S(2)}) collective-permute-start(bf16[128,2048]{1,0:T(8,128)(2,1)} %get-tuple-element.232), channel_id=1, source_target_pairs={{0,2},{1,3},{2,0},{3,1},{4,6},{5,7},{6,4},{7,5},{8,10},{9,11},{10,... | collective-permute-start | bytes 1572872 | tf_op jit(solution)/shard_map/ppermute | solution.py:1094
  351.5 60.7 %all-to-all-start.5 = ((bf16[4,128,8,64]{1,3,2,0:T(8,128)(2,1)}), bf16[4,128,8,64]{1,3,2,0:T(8,128)(2,1)}, u32[]{:S(2)}, u32[]{:S(2)}) async-start(bf16[4,128,8,64]{1,3,2,0:T(8,128)(2,1)} %copy.142), calls=%async_computation.6 | async-start | bytes 1048576 | tf_op jit(solution)/shard_map/all_to_all | solution.py:1089
  412.2 66.8 %all-to-all-start.4 = ((bf16[8,32,2048]{2,1,0:T(8,128)(2,1)}), bf16[8,32,2048]{2,1,0:T(8,128)(2,1)S(1)}, u32[]{:S(2)}, u32[]{:S(2)}) async-start(bf16[8,32,2048]{2,1,0:T(8,128)(2,1)} %pad_maximum_fusion.1), calls=%async_computation.4 | async-start | bytes 2097152 | tf_op jit(solution)/shard_map/all_to_all | solution.py:1089
  416.2 158.0 %reduce-scatter.6.cloned.1.call-start = ((), (), s32[]{:S(2)}) async-start(), calls=%async_computation.12 | async-start | bytes 1310720 | tf_op jit(solution)/shard_map/reduce_scatter | solution.py:1310
  416.3 10.4 %collective-permute-start.9 = (bf16[128,2048]{1,0:T(8,128)(2,1)}, bf16[128,2048]{1,0:T(8,128)(2,1)S(1)}, u32[]{:S(2)}, u32[]{:S(2)}) collective-permute-start(bf16[128,2048]{1,0:T(8,128)(2,1)} %collective-permute-done.8), channel_id=1, source_target_pairs={{0,1},{1,0},{2,3},{3,2},{4,5},{5,4},{6,7},{7,6},{8,9},{9,8},{10,11... | collective-permute-start | bytes 1572872 | tf_op jit(solution)/shard_map/ppermute | solution.py:1094
  431.7 47.4 %collective-permute-start.10 = (bf16[4,64,2048]{2,1,0:T(8,128)(2,1)}, bf16[4,64,2048]{2,1,0:T(8,128)(2,1)}, u32[]{:S(2)}, u32[]{:S(2)}) collective-permute-start(bf16[4,64,2048]{2,1,0:T(8,128)(2,1)} %dynamic-slice_bitcast_fusion), channel_id=1, source_target_pairs={{0,4},{4,0},{8,12},{12,8},{16,20},{20,16},{24,28},{28,24},{1,5},{5... | collective-permute-start | bytes 3145736 | tf_op jit(solution)/shard_map/ppermute | solution.py:1108
  433.7 53.4 %collective-permute-start.4 = (bf16[256,2048]{1,0:T(8,128)(2,1)}, bf16[256,2048]{1,0:T(8,128)(2,1)S(1)}, u32[]{:S(2)}, u32[]{:S(2)}) collective-permute-start(bf16[256,2048]{1,0:T(8,128)(2,1)} %reduce-scatter.4.cloned.1.call-done), channel_id=1, source_target_pairs={{0,0},{1,8},{2,16},{3,24},{4,4},{5,12},{6,20},{7,28},{8,1},{9,9},{... | collective-permute-start | bytes 3145736 | tf_op jit(solution)/shard_map/ppermute | solution.py:1313
  490.4 149.1 %reduce-scatter.8.cloned.1.call-start = ((), (), s32[]{:S(2)}) async-start(), calls=%async_computation.13 | async-start | bytes 5242880 | tf_op jit(solution)/shard_map/reduce_scatter | solution.py:1310
  493.5 11.0 %collective-permute-start.11 = (bf16[2,8,64,1408]{3,2,1,0:T(8,128)(2,1)S(1)}, bf16[2,8,64,1408]{3,2,1,0:T(8,128)(2,1)S(1)}, u32[]{:S(2)}, u32[]{:S(2)}) collective-permute-start(bf16[2,8,64,1408]{3,2,1,0:T(8,128)(2,1)S(1)} %pad_maximum_fusion), channel_id=1, source_target_pairs={{0,1},{1,0},{2,3},{3,2},{4,5},{5,4},{6,7},{7,6},{8,9},{9,8},{10,11... | collective-permute-start | bytes 8650760 | tf_op jit(solution)/shard_map/ppermute | solution.py:1094
  505.5 67.1 %collective-permute-start.12 = (bf16[8,64,1408]{2,1,0:T(8,128)(2,1)S(1)}, bf16[8,64,1408]{2,1,0:T(8,128)(2,1)S(1)}, u32[]{:S(2)}, u32[]{:S(2)}) collective-permute-start(bf16[8,64,1408]{2,1,0:T(8,128)(2,1)S(1)} %fusion.31), channel_id=1, source_target_pairs={{0,2},{1,3},{2,0},{3,1},{4,6},{5,7},{6,4},{7,5},{8,10},{9,11},{10,... | collective-permute-start | bytes 4325384 | tf_op jit(solution)/shard_map/ppermute | solution.py:1094
  574.2 120.6 %all-to-all-start.6 = ((bf16[8,64,1408]{2,1,0:T(8,128)(2,1)}), bf16[8,64,1408]{2,1,0:T(8,128)(2,1)S(1)}, u32[]{:S(2)}, u32[]{:S(2)}) async-start(bf16[8,64,1408]{2,1,0:T(8,128)(2,1)} %fusion.17), calls=%async_computation.8 | async-start | bytes 2883584 | tf_op jit(solution)/shard_map/all_to_all | solution.py:1089
  584.8 2.8 collective-permute-start.13
  639.5 51.6 %collective-permute-start.15 = (bf16[256,2048]{1,0:T(8,128)(2,1)}, bf16[256,2048]{1,0:T(8,128)(2,1)}, u32[]{:S(2)}, u32[]{:S(2)}) collective-permute-start(bf16[256,2048]{1,0:T(8,128)(2,1)} %reduce-scatter.8.cloned.1.call-done), channel_id=1, source_target_pairs={{0,0},{1,8},{2,16},{3,24},{4,4},{5,12},{6,20},{7,28},{8,1},{9,9},{... | collective-permute-start | bytes 3145736 | tf_op jit(solution)/shard_map/ppermute | solution.py:1313
  645.0 10.3 %collective-permute-start.14 = (bf16[64,640]{1,0:T(8,128)(2,1)S(1)}, bf16[64,640]{1,0:T(8,128)(2,1)S(1)}, u32[]{:S(2)}, u32[]{:S(2)}) collective-permute-start(bf16[64,640]{1,0:T(8,128)(2,1)S(1)} %fusion.62), channel_id=1, source_target_pairs={{0,2},{1,3},{2,0},{3,1},{4,6},{5,7},{6,4},{7,5},{8,10},{9,11},{10,... | collective-permute-start | bytes 245768 | tf_op jit(solution)/shard_map/ppermute | solution.py:1094
  655.2 38.7 %copy-start.36 = (bf16[64,2048]{1,0:T(8,128)(2,1)S(1)}, bf16[64,2048]{1,0:T(8,128)(2,1)}, u32[]{:S(2)}) copy-start(bf16[64,2048]{1,0:T(8,128)(2,1)} %reduce-scatter.6.cloned.1.call-done) | copy-start | bytes 786436
  (44 other events, 234.7 us)
Sparse Core Ops, SparseCore 0:
  88.5 58.3 all-gather.1
  340.0 75.8 reduce-scatter.3
  490.5 25.6 reduce-scatter.5
  518.4 121.0 reduce-scatter.7

commit v6 on v5

--- a/solution.py
+++ b/solution.py
@@ -780,7 +780,7 @@
     given = ((seqs, own), (seqs, tail), (parts, weight))
     return pl.pallas_call(
         gather_kernel,
-        in_specs=[pl.BlockSpec(memory_space=pl.ANY)] * 3,
+        in_specs=[pl.BlockSpec(memory_space=pltpu.VMEM)] * 3,
         out_specs=[pl.BlockSpec(memory_space=pl.ANY)] * 3,
         out_shape=[jax.ShapeDtypeStruct((n,) + x.shape, x.dtype) for n, x in given],
         scratch_shapes=[dma((3,))] + [dma((3, 2))] * 4 + [dma((4, 2))] * 2 + [dma((2,))] * 2 + [dma] * 2,
@@ -1342,7 +1342,7 @@
         out_half = (out_mine + out_other.astype(F32)).astype(BF16).reshape(-1, width)
         out_half, sums = lax.optimization_barrier((out_half, sums))
         grad_out = along(out_half)
-        grad_ffn_value, grad_ffn_key = value_turned.astype(F32), turn(key_sum).astype(F32)
+        grad_ffn_value = value_turned.astype(F32)
     else:
         moved, scaled_grad, sums, wide = lax.optimization_barrier((moved, scaled_grad, sums, wide))
     output = dot(arrange, moved[:, : rows // seqs].reshape(rows, width), TN).astype(BF16)
@@ -1360,7 +1360,9 @@
     else:
         wide_part = block_sum(wide)
     grad_tokens = reduce_seq(grad_given).astype(BF16)
-    wide_part, grad_tokens, grad_out = lax.optimization_barrier((wide_part, grad_tokens, grad_out))
+    if paired:
+        wide_part, grad_tokens, grad_out, key_sum = lax.optimization_barrier((wide_part, grad_tokens, grad_out, key_sum))
+        grad_ffn_key = turn(key_sum).astype(F32)
     wide_all = exchange(wide_part.astype(BF16), "seq").astype(F32)
 
     def square(at):

time: 716 us -> 748 us (1.045)
  waiting for transfers between devices: 115 us -> 165 us
  Pallas kernels: 368 us -> 342 us
  other arithmetic: 35.4 us -> 46.4 us
  starting transfers between devices: 68.6 us -> 60.9 us
    ppermute x2, waiting for transfers between devices: 42.2 us -> 142 us  [turn(): return lax.ppermute(part, ('seq', 'wsh'), turned)]
    reduce_scatter x3, waiting for transfers between devices: 51.9 us -> 0.01 us  [along(): lax.psum_scatter(part, 'seq', scatter_dimension=0, tiled=True, axis_index...]
    pallas_call x1, Pallas kernels: 70 us -> 54.4 us  [gather_first(): pl.pallas_call(gather_kernel, in_specs=[pl.BlockSpec(memory_space=pltpu.V...]
    pallas_call x1, Pallas kernels: 66.1 us -> 54.8 us  [reduce_seq(): pl.pallas_call(functools.partial(reduce_kernel, splits), in_specs=[pl.Blo...]
    unnamed x112 -> x102, local copies, waits for them, and re-layouts: 22 us -> 20 us
  transfers between devices with their start and end apart: 27 -> 27, of which waited for: 9 -> 9; matrix products, arithmetic and copies ran while one was open for 12% -> 14% of each run, Pallas kernels for 30% -> 27%
where the time goes in v6:
time: 748 us; the launch traced here: 739 us
  Pallas kernels  342 us (46%)
  waiting for transfers between devices  165 us (22%)
  matrix products  63.6 us (9%)
  starting transfers between devices  60.9 us (8%)
  other arithmetic  46.4 us (6%)
  local copies, waits for them, and re-layouts  45.4 us (6%)
  between operations  16.1 us (2%)
    ppermute x2, waiting for transfers between devices, turn(): return lax.ppermute(part, ('seq', 'wsh'), turned)  142 us
    pallas_call x2, Pallas kernels, channel_stage(): pl.pallas_call(body, in_specs=[pl.BlockSpec(memory_space=pltpu.VMEM)] + [...  89.3 us
    dot_general x17, matrix products, dot(): return lax.dot_general(a, b, dims, preferred_element_type=F32)  63.6 us
    pallas_call x1, Pallas kernels, reduce_seq(): pl.pallas_call(functools.partial(reduce_kernel, splits), in_specs=[pl.Blo...  54.8 us
    pallas_call x1, Pallas kernels, gather_first(): pl.pallas_call(gather_kernel, in_specs=[pl.BlockSpec(memory_space=pltpu.V...  54.4 us
    pallas_call x1, Pallas kernels, run_backward(): pl.pallas_call(functools.partial(backward_kernel, count), grid=(rows // s...  47.4 us
    pallas_call x1, Pallas kernels, run_unproject(): pl.pallas_call(functools.partial(unproject_kernel, own_width, parts, piec...  40.3 us
    all_to_all x7, starting transfers between devices, exchange(): return lax.all_to_all(x, axis, split_axis=0, concat_axis=0, tiled=True)  37.2 us
  transfers between devices with their start and end apart: 27, of which 9 were waited for; matrix products, arithmetic and copies ran while one was open for 14% of the time, Pallas kernels for 27%

profile of v6, /device:TPU:4, one launch (start us, length us, event | category | flops | bytes accessed | tf_op | source)
XLA Modules:
  0.0 738.8 jit_solution(2751746542450398134)
XLA Ops:
  18.3 54.4 %gather_first.1 = (bf16[8,128,2048]{2,1,0:T(8,128)(2,1)}, bf16[8,128,128]{2,1,0:T(8,128)(2,1)}, bf16[4,512,1664]{2,1,0:T(8,128)(2,1)}) custom-call(bf16[128,2048]{1,0:T(8,128)(2,1)} %own_ref.1, bf16[128,128]{1,0:T(8,128)(2,1)} %pad.30.tail_ref, bf16[512,1664]{1,0:T(8,128)(2,1)} %copy-done.26), custom_call_target="tpu_custom_call" | custom-call | bytes 104857600 | tf_op jit(solution)/shard_map/gather_first/pallas_call | solution.py:781
  74.3 7.0 convert_reduce_fusion
  96.2 19.4 %mix_project.1 = (f32[1024,256]{1,0:T(8,128)}, f32[1024,256]{1,0:T(8,128)}, f32[1024,256]{1,0:T(8,128)}, f32[1024,640]{1,0:T(8,128)}, bf16[1024,640]{1,0:T(8,128)(2,1)}) custom-call(bf16[1024,2048]{1,0:T(8,128)(2,1)} %copy-done.17, f32[1024,4]{1,0:T(8,128)} %copy.132.stats_ref, f32[8,2048]{1,0:T(8,128)} %slice_bitcast_fusion.3.vec_ref, ...), custom_call_target="tpu_custom_call" | custom-call | flops 134217728 | bytes 62914560 | tf_op jit(solution)/shard_map/mix_project/pallas_call | solution.py:569
  117.2 6.3 all-to-all-start.1
  124.5 36.2 %mix_forward.1 = (bf16[1024,256]{1,0:T(8,128)(2,1)S(1)}, bf16[1024,256]{1,0:T(8,128)(2,1)S(1)}, f32[1024,256]{1,0:T(8,128)S(1)}, f32[1024,256]{1,0:T(8,128)S(1)}, f32[1024,256]{1,0:T(8,128)S(1)}) custom-call(f32[1024,256]{1,0:T(8,128)S(1)} %copy-done.4, f32[1024,256]{1,0:T(8,128)} %get-tuple-element.92.keys_ref, f32[1024,256]{1,0:T(8,128)} %get-tuple-element.93.values_ref, ...), custom_call_target="tpu_custom_call" | custom-call | flops 134217728 | bytes 115343360 | tf_op jit(solution)/shard_map/mix_forward/pallas_call | solution.py:385
  164.7 6.0 all-to-all-start.2
  177.5 7.8 %all-to-all-done.2 = bf16[8,128,256]{1,2,0:T(8,128)(2,1)S(1)} async-done(((bf16[8,128,256]{1,2,0:T(8,128)(2,1)}), bf16[8,128,256]{1,2,0:T(8,128)(2,1)S(1)}, u32[]{:S(2)}, u32[]{:S(2)}) %all-to-all-start.2) | async-done | bytes 524320 | tf_op jit(solution)/shard_map/all_to_all | solution.py:1089
  185.2 5.0 fusion.85
  196.9 37.3 %channel_forward.1 = (f32[128,2048]{1,0:T(8,128)}, bf16[512,2048]{1,0:T(8,128)(2,1)}, bf16[512,1024]{1,0:T(8,128)(2,1)}, bf16[512,1024]{1,0:T(8,128)(2,1)}, f32[512,2048]{1,0:T(8,128)}) custom-call(bf16[128,2048]{1,0:T(8,128)(2,1)} %add_convert_fusion.2.refs_0_, bf16[2048,2048]{1,0:T(8,128)(2,1)} %refs_2_.3, bf16[2048,2048]{1,0:T(8,128)(2,1)} %refs_1_.3), custom_call_target="tpu_custom_call" | custom-call | bytes 104857600 | tf_op jit(solution)/shard_map/channel_forward/pallas_call | solution.py:1061
  237.4 51.9 %channel_backward.1 = (f32[128,2048]{1,0:T(8,128)}, bf16[512,2048]{1,0:T(8,128)(2,1)}, bf16[512,1024]{1,0:T(8,128)(2,1)}, bf16[512,2048]{1,0:T(8,128)(2,1)}, bf16[512,1024]{1,0:T(8,128)(2,1)}) custom-call(bf16[128,2048]{1,0:T(8,128)(2,1)} %get-tuple-element.270.refs_0_, bf16[2048,2048]{1,0:T(8,128)(2,1)} %refs_1_.3, bf16[2048,2048]{1,0:T(8,128)(2,1)} %refs_2_.3, ...), custom_call_target="tpu_custom_call" | custom-call | bytes 104857600 | tf_op jit(solution)/shard_map/channel_backward/pallas_call | solution.py:1061
  293.6 4.1 collective-permute-done.3
  299.9 6.5 convolution_convert_fusion.1
  307.2 3.8 all-to-all-start.3
  311.3 4.5 fusion.91
  315.8 4.7 add_convert_fusion.1
  320.5 4.0 all-to-all-done.3
  328.4 6.1 all-to-all-start.5
  334.5 7.7 %fusion.92 = f32[1024,2048]{1,0:T(8,128)} fusion(bf16[512,1024]{1,0:T(8,128)(2,1)} %get-tuple-element.121, bf16[512,2048]{1,0:T(8,128)(2,1)} %get-tuple-element.116), kind=kOutput, calls=%fused_computation.216 | convolution fusion | flops 2147483648 | bytes 11534336 | tf_op jit(solution)/shard_map/dot_general | solution.py:28
  342.2 47.4 %mix_backward.1 = (bf16[1024,256]{1,0:T(8,128)(2,1)S(1)}, bf16[1024,256]{1,0:T(8,128)(2,1)S(1)}, bf16[1024,256]{1,0:T(8,128)(2,1)S(1)}, bf16[4,1024,256]{2,1,0:T...) custom-call(bf16[1024,256]{1,0:T(8,128)(2,1)S(1)} %bitcast.129, f32[1024,256]{1,0:T(8,128)S(1)} %copy-done.4, ...), custom_call_target="tpu_custom_call" | custom-call | flops 134217728 | bytes 157286400 | tf_op jit(solution)/shard_map/mix_backward/pallas_call | solution.py:413
  394.7 8.8 %add_convert_fusion = bf16[1024,2048]{1,0:T(8,128)(2,1)} fusion(f32[1024,2048]{1,0:T(8,128)} %fusion.92, bf16[512,1024]{1,0:T(8,128)(2,1)} %collective-permute-done.6, bf16[512,2048]{1,0:T(8,128)(2,1)} %collective-permute-done.5), kind=kOutput, calls=%fused_computation.8 | convolution fusion | flops 2151677952 | bytes 15728640 | tf_op jit(solution)/shard_map/dot_general | solution.py:28
  403.5 3.8 convolution_convert_fusion
  412.5 4.6 all-to-all-start.4
  426.1 40.3 %mix_unproject.1 = (f32[1024,2048]{1,0:T(8,128)}, f32[1024,2]{1,0:T(8,128)}, bf16[4,8,64,1408]{3,2,1,0:T(8,128)(2,1)}, bf16[256,640]{1,0:T(8,128)(2,1)}) custom-call(bf16[1024,2048]{1,0:T(8,128)(2,1)} %copy-done.17, f32[1024,4]{1,0:T(8,128)} %copy.132.stats_ref, f32[8,2048]{1,0:T(8,128)} %slice_bitcast_fusion.3.vec_ref, bf16[2048,1664]{1,0:T(8,128)(2,1)} %bitcast.135, ...), custom_call_target="tpu_custom_call" | custom-call | flops 134217728 | bytes 125829120 | tf_op jit(solution)/shard_map/mix_unproject/pallas_call | solution.py:592
  468.3 82.9 %collective-permute-done.4 = bf16[256,2048]{1,0:T(8,128)(2,1)S(1)} collective-permute-done((bf16[256,2048]{1,0:T(8,128)(2,1)}, bf16[256,2048]{1,0:T(8,128)(2,1)S(1)}, u32[]{:S(2)}, u32[]{:S(2)}) %collective-permute-start.4) | collective-permute-done | bytes 1048608 | tf_op jit(solution)/shard_map/ppermute | solution.py:1313
  559.1 5.9 fusion.5
  565.3 6.3 fusion.12
  574.0 3.8 fusion.31
  580.0 54.8 %reduce_seq.1 = f32[128,2048]{1,0:T(8,128)S(1)} custom-call(bf16[8,128,2048]{2,1,0:T(8,128)(2,1)S(1)} %bitcast.128), custom_call_target="tpu_custom_call" | custom-call | bytes 1048576 | tf_op jit(solution)/shard_map/reduce_seq/pallas_call | solution.py:903
  638.6 6.7 all-to-all-start.6
  646.9 4.8 collective-permute-start.15
  652.6 5.3 collective-permute-start.14
  665.5 58.9 %collective-permute-done.15 = bf16[256,2048]{1,0:T(8,128)(2,1)} collective-permute-done((bf16[256,2048]{1,0:T(8,128)(2,1)}, bf16[256,2048]{1,0:T(8,128)(2,1)}, u32[]{:S(2)}, u32[]{:S(2)}) %collective-permute-start.15) | collective-permute-done | bytes 1048608 | tf_op jit(solution)/shard_map/ppermute | solution.py:1313
  (283 shorter events, 115.8 us)
Async XLA Ops:
  7.2 109.0 %copy-start = (bf16[128,2048]{1,0:T(8,128)(2,1)S(1)}, bf16[128,2048]{1,0:T(8,128)(2,1)}, u32[]{:S(2)}) copy-start(bf16[128,2048]{1,0:T(8,128)(2,1)} %param.17) | copy-start | bytes 1572868
  7.2 178.0 %all-gather.2.cloned.1.call-start = ((), (), s32[]{:S(2)}) async-start(), calls=%async_computation.10 | async-start | bytes 10485760 | tf_op jit(solution)/shard_map/all_gather | solution.py:1213
  15.6 57.2 %copy-start.43 = (s32[1,4]{1,0:T(1,128)S(1)}, s32[1,4]{1,0:T(1,128)}, u32[]{:S(2)}) copy-start(s32[1,4]{1,0:T(1,128)} %param.20) | copy-start | bytes 52
  85.9 30.0 %all-to-all-start = ((bf16[8,128,256]{1,2,0:T(8,128)(2,1)}), bf16[8,128,256]{1,2,0:T(8,128)(2,1)S(1)}, u32[]{:S(2)}, u32[]{:S(2)}) async-start(bf16[8,128,256]{1,2,0:T(8,128)(2,1)} %bitcast.15), calls=%async_computation | async-start | bytes 1048576 | tf_op jit(solution)/shard_map/all_to_all | solution.py:1089
  90.8 80.4 %collective-permute-start.1 = (f32[8,128]{1,0:T(8,128)S(1)}, f32[8,128]{1,0:T(8,128)S(1)}, u32[]{:S(2)}, u32[]{:S(2)}) collective-permute-start(f32[8,128]{1,0:T(8,128)S(1)} %broadcast_in_dim.4), channel_id=1, source_target_pairs={{0,1},{1,0},{2,3},{3,2},{4,5},{5,4},{6,7},{7,6},{8,9},{9,8},{10,11... | collective-permute-start | bytes 12296 | tf_op jit(solution)/shard_map/ppermute | solution.py:1094
  96.2 19.6 %copy-start.40 = (pred[128]{0:T(512)(128)(4,1)S(1)}, pred[128]{0:T(512)(128)(4,1)}, u32[]{:S(2)}) copy-start(pred[128]{0:T(512)(128)(4,1)} %constant.191.clone.1) | copy-start | bytes 388
  117.2 46.4 %all-to-all-start.1 = ((bf16[8,16,2048]{2,1,0:T(8,128)(2,1)}), bf16[8,16,2048]{2,1,0:T(8,128)(2,1)}, u32[]{:S(2)}, u32[]{:S(2)}) async-start(bf16[8,16,2048]{2,1,0:T(8,128)(2,1)} %bitcast.17), calls=%async_computation.1 | async-start | bytes 1048576 | tf_op jit(solution)/shard_map/all_to_all | solution.py:1089
  123.7 218.5 %copy-start.2 = (bf16[640,256]{1,0:T(8,128)(2,1)}, bf16[640,256]{1,0:T(8,128)(2,1)S(1)}, u32[]{:S(2)}) copy-start(bf16[640,256]{1,0:T(8,128)(2,1)S(1)} %fusion.50.up_ref) | copy-start | bytes 983044
  164.7 20.6 %all-to-all-start.2 = ((bf16[8,128,256]{1,2,0:T(8,128)(2,1)}), bf16[8,128,256]{1,2,0:T(8,128)(2,1)S(1)}, u32[]{:S(2)}, u32[]{:S(2)}) async-start(bf16[8,128,256]{1,2,0:T(8,128)(2,1)} %copy.140), calls=%async_computation.2 | async-start | bytes 1048576 | tf_op jit(solution)/shard_map/all_to_all | solution.py:1089
  171.9 3.7 collective-permute-start.2
  190.8 4.7 collective-permute-start
  292.2 5.5 collective-permute-start.3
  307.2 17.2 %all-to-all-start.3 = ((bf16[8,128,256]{2,1,0:T(8,128)(2,1)}), bf16[8,128,256]{2,1,0:T(8,128)(2,1)S(1)}, u32[]{:S(2)}, u32[]{:S(2)}) async-start(bf16[8,128,256]{2,1,0:T(8,128)(2,1)} %bitcast.144), calls=%async_computation.3 | async-start | bytes 1048576 | tf_op jit(solution)/shard_map/all_to_all | solution.py:1089
  311.0 110.5 %reduce-scatter.4.cloned.1.call-start = ((), (), s32[]{:S(2)}) async-start(), calls=%async_computation.11 | async-start | bytes 5242880 | tf_op jit(solution)/shard_map/reduce_scatter | solution.py:1310
  324.4 68.4 %collective-permute-start.5 = (bf16[512,2048]{1,0:T(8,128)(2,1)}, bf16[512,2048]{1,0:T(8,128)(2,1)}, u32[]{:S(2)}, u32[]{:S(2)}) collective-permute-start(bf16[512,2048]{1,0:T(8,128)(2,1)} %get-tuple-element.116), channel_id=1, source_target_pairs={{0,4},{4,0},{8,12},{12,8},{16,20},{20,16},{24,28},{28,24},{1,5},{5... | collective-permute-start | bytes 6291464 | tf_op jit(solution)/shard_map/ppermute | solution.py:1108
  326.0 66.8 %collective-permute-start.6 = (bf16[512,1024]{1,0:T(8,128)(2,1)}, bf16[512,1024]{1,0:T(8,128)(2,1)}, u32[]{:S(2)}, u32[]{:S(2)}) collective-permute-start(bf16[512,1024]{1,0:T(8,128)(2,1)} %get-tuple-element.117), channel_id=1, source_target_pairs={{0,4},{4,0},{8,12},{12,8},{16,20},{20,16},{24,28},{28,24},{1,5},{5... | collective-permute-start | bytes 3145736 | tf_op jit(solution)/shard_map/ppermute | solution.py:1108
  326.5 66.3 %collective-permute-start.7 = (bf16[128,2048]{1,0:T(8,128)(2,1)}, bf16[128,2048]{1,0:T(8,128)(2,1)}, u32[]{:S(2)}, u32[]{:S(2)}) collective-permute-start(bf16[128,2048]{1,0:T(8,128)(2,1)} %copy-done.27), channel_id=1, source_target_pairs={{0,1},{1,0},{2,3},{3,2},{4,5},{5,4},{6,7},{7,6},{8,9},{9,8},{10,11... | collective-permute-start | bytes 1572872 | tf_op jit(solution)/shard_map/ppermute | solution.py:1094
  326.5 66.3 %collective-permute-start.8 = (bf16[128,2048]{1,0:T(8,128)(2,1)}, bf16[128,2048]{1,0:T(8,128)(2,1)}, u32[]{:S(2)}, u32[]{:S(2)}) collective-permute-start(bf16[128,2048]{1,0:T(8,128)(2,1)} %copy-done.27), channel_id=1, source_target_pairs={{0,2},{1,3},{2,0},{3,1},{4,6},{5,7},{6,4},{7,5},{8,10},{9,11},{10,... | collective-permute-start | bytes 1572872 | tf_op jit(solution)/shard_map/ppermute | solution.py:1094
  328.4 64.4 %all-to-all-start.5 = ((bf16[4,128,8,64]{1,3,2,0:T(8,128)(2,1)}), bf16[4,128,8,64]{1,3,2,0:T(8,128)(2,1)}, u32[]{:S(2)}, u32[]{:S(2)}) async-start(bf16[4,128,8,64]{1,3,2,0:T(8,128)(2,1)} %copy.142), calls=%async_computation.6 | async-start | bytes 1048576 | tf_op jit(solution)/shard_map/all_to_all | solution.py:1089
  334.5 304.1 %reduce-scatter.8.cloned.1.call-start = ((), (), s32[]{:S(2)}) async-start(), calls=%async_computation.13 | async-start | bytes 5242880 | tf_op jit(solution)/shard_map/reduce_scatter | solution.py:1310
  392.8 10.6 %collective-permute-start.9 = (bf16[128,2048]{1,0:T(8,128)(2,1)}, bf16[128,2048]{1,0:T(8,128)(2,1)S(1)}, u32[]{:S(2)}, u32[]{:S(2)}) collective-permute-start(bf16[128,2048]{1,0:T(8,128)(2,1)} %collective-permute-done.8), channel_id=1, source_target_pairs={{0,1},{1,0},{2,3},{3,2},{4,5},{5,4},{6,7},{7,6},{8,9},{9,8},{10,11... | collective-permute-start | bytes 1572872 | tf_op jit(solution)/shard_map/ppermute | solution.py:1094
  412.5 55.8 %all-to-all-start.4 = ((bf16[8,32,2048]{2,1,0:T(8,128)(2,1)}), bf16[8,32,2048]{2,1,0:T(8,128)(2,1)S(1)}, u32[]{:S(2)}, u32[]{:S(2)}) async-start(bf16[8,32,2048]{2,1,0:T(8,128)(2,1)} %pad_maximum_fusion.1), calls=%async_computation.4 | async-start | bytes 2097152 | tf_op jit(solution)/shard_map/all_to_all | solution.py:1089
  417.1 221.5 %reduce-scatter.6.cloned.1.call-start = ((), (), s32[]{:S(2)}) async-start(), calls=%async_computation.12 | async-start | bytes 1310720 | tf_op jit(solution)/shard_map/reduce_scatter | solution.py:1310
  419.5 48.8 %collective-permute-start.10 = (bf16[4,64,2048]{2,1,0:T(8,128)(2,1)}, bf16[4,64,2048]{2,1,0:T(8,128)(2,1)}, u32[]{:S(2)}, u32[]{:S(2)}) collective-permute-start(bf16[4,64,2048]{2,1,0:T(8,128)(2,1)} %dynamic-slice_bitcast_fusion), channel_id=1, source_target_pairs={{0,4},{4,0},{8,12},{12,8},{16,20},{20,16},{24,28},{28,24},{1,5},{5... | collective-permute-start | bytes 3145736 | tf_op jit(solution)/shard_map/ppermute | solution.py:1108
  421.5 129.8 %collective-permute-start.4 = (bf16[256,2048]{1,0:T(8,128)(2,1)}, bf16[256,2048]{1,0:T(8,128)(2,1)S(1)}, u32[]{:S(2)}, u32[]{:S(2)}) collective-permute-start(bf16[256,2048]{1,0:T(8,128)(2,1)} %reduce-scatter.4.cloned.1.call-done), channel_id=1, source_target_pairs={{0,0},{1,8},{2,16},{3,24},{4,4},{5,12},{6,20},{7,28},{8,1},{9,9},{... | collective-permute-start | bytes 3145736 | tf_op jit(solution)/shard_map/ppermute | solution.py:1313
  555.6 15.9 %collective-permute-start.11 = (bf16[2,8,64,1408]{3,2,1,0:T(8,128)(2,1)}, bf16[2,8,64,1408]{3,2,1,0:T(8,128)(2,1)}, u32[]{:S(2)}, u32[]{:S(2)}) collective-permute-start(bf16[2,8,64,1408]{3,2,1,0:T(8,128)(2,1)} %pad_maximum_fusion), channel_id=1, source_target_pairs={{0,1},{1,0},{2,3},{3,2},{4,5},{5,4},{6,7},{7,6},{8,9},{9,8},{10,11... | collective-permute-start | bytes 8650760 | tf_op jit(solution)/shard_map/ppermute | solution.py:1094
  577.8 57.8 %collective-permute-start.12 = (bf16[8,64,1408]{2,1,0:T(8,128)(2,1)}, bf16[8,64,1408]{2,1,0:T(8,128)(2,1)S(1)}, u32[]{:S(2)}, u32[]{:S(2)}) collective-permute-start(bf16[8,64,1408]{2,1,0:T(8,128)(2,1)} %fusion.31), channel_id=1, source_target_pairs={{0,2},{1,3},{2,0},{3,1},{4,6},{5,7},{6,4},{7,5},{8,10},{9,11},{10,... | collective-permute-start | bytes 4325384 | tf_op jit(solution)/shard_map/ppermute | solution.py:1094
  580.0 55.6 %copy-start.19 = (f32[2,8,64,1408]{3,2,1,0:T(8,128)S(1)}, f32[2,8,64,1408]{3,2,1,0:T(8,128)}, u32[]{:S(2)}) copy-start(f32[2,8,64,1408]{3,2,1,0:T(8,128)} %copy-done.18) | copy-start | bytes 17301508
  638.6 88.6 %all-to-all-start.6 = ((bf16[8,64,1408]{2,1,0:T(8,128)(2,1)}), bf16[8,64,1408]{2,1,0:T(8,128)(2,1)S(1)}, u32[]{:S(2)}, u32[]{:S(2)}) async-start(bf16[8,64,1408]{2,1,0:T(8,128)(2,1)} %fusion.17), calls=%async_computation.9 | async-start | bytes 2883584 | tf_op jit(solution)/shard_map/all_to_all | solution.py:1089
  645.4 1.5 collective-permute-start.13
  646.9 77.5 %collective-permute-start.15 = (bf16[256,2048]{1,0:T(8,128)(2,1)}, bf16[256,2048]{1,0:T(8,128)(2,1)}, u32[]{:S(2)}, u32[]{:S(2)}) collective-permute-start(bf16[256,2048]{1,0:T(8,128)(2,1)} %reduce-scatter.8.cloned.1.call-done), channel_id=1, source_target_pairs={{0,0},{1,8},{2,16},{3,24},{4,4},{5,12},{6,20},{7,28},{8,1},{9,9},{... | collective-permute-start | bytes 3145736 | tf_op jit(solution)/shard_map/ppermute | solution.py:1313
  652.6 10.3 %collective-permute-start.14 = (bf16[64,640]{1,0:T(8,128)(2,1)S(1)}, bf16[64,640]{1,0:T(8,128)(2,1)S(1)}, u32[]{:S(2)}, u32[]{:S(2)}) collective-permute-start(bf16[64,640]{1,0:T(8,128)(2,1)S(1)} %fusion.62), channel_id=1, source_target_pairs={{0,2},{1,3},{2,0},{3,1},{4,6},{5,7},{6,4},{7,5},{8,10},{9,11},{10,... | collective-permute-start | bytes 245768 | tf_op jit(solution)/shard_map/ppermute | solution.py:1094
  (39 other events, 165.3 us)
Sparse Core Ops, SparseCore 0:
  72.9 56.2 all-gather.1
  324.6 75.8 reduce-scatter.3
  407.4 122.3 reduce-scatter.7
  578.0 39.3 reduce-scatter.5

commit v7 on v6

--- a/solution.py
+++ b/solution.py
@@ -1256,6 +1256,7 @@
     cotangent = (result - target) * (own_valid * (total_tokens / total_valid))[:, None]
     cot_low = cotangent.astype(BF16)
 
+    result_back = exchange(dot(settle, result.astype(BF16), TN).astype(BF16).reshape(seqs, rows // seqs, width), "seq")
     if paired:
         grad_channel, cot, pre_mine, cot_other, pre_spare = channel_stage(
             cot_low, channel_value_weight, channel_key_weight, active
@@ -1265,6 +1266,8 @@
         cot = gather_near(cot_low)
         grad_pre = (dot(cot, channel_value_weight, NT) * 2.0 * active).astype(BF16)
         grad_channel = near_sum(dot(grad_pre, channel_key_weight))
+    result_back, grad_channel = lax.optimization_barrier((result_back, grad_channel))
+    output = dot(arrange, result_back.reshape(rows, width), TN).astype(BF16)
     grad_vec_mix_two = jnp.sum(grad_channel * delta_two, 0)
     shifted = grad_channel * vectors[:, 18] * own_flowing
     behind = from_behind(shifted[:1], "seq", -1)
@@ -1296,9 +1299,7 @@
         lefts = jnp.stack([lax.dynamic_index_in_dim(lefts, lax.axis_index("wsh") ^ k, 0, keepdims=False) for k in range(4)])
     out_part = dot(lefts.reshape(rows * parts, -1), near_grad, TN).astype(BF16)
 
-    result_back = dot(settle, result.astype(BF16), TN).astype(BF16).reshape(seqs, rows // seqs, width)
-    first_back = dot(permute, grad_first, TN).astype(BF16).reshape(seqs, rows // seqs, width)
-    moved = exchange(jnp.concatenate([result_back, first_back], 1), "seq")
+    moved = exchange(dot(permute, grad_first, TN).astype(BF16).reshape(seqs, rows, own_width), "seq")
     recept_low, key_part, out_part = lax.optimization_barrier((recept_low, key_part, out_part))
     if paired:
         lines = [[0, 2, 4, 6], [1, 3, 5, 7]]
@@ -1316,7 +1317,7 @@
         x_side = me % 2
         out_mine = lax.dynamic_index_in_dim(halves_out, x_side, 1, keepdims=False).astype(F32)
         out_other = beside(lax.dynamic_index_in_dim(halves_out, 1 - x_side, 1, keepdims=False))
-        value_turned, key_sum = turn(along(value_part)), along(key_part)
+        value_sum, key_sum = along(value_part), along(key_part)
     else:
         moves = [(s * parts + w, w * seqs + s) for s in range(seqs) for w in range(parts)]
 
@@ -1336,17 +1337,16 @@
         balanced, stats, mix_vec, weights, others, (recept_low, keys_low, values_low), ups_low, hidden, downs, up, parts
     )
     if paired:
-        moved, value_turned, out_other, scaled_grad, sums, wide, up_grad = lax.optimization_barrier(
-            (moved, value_turned, out_other, scaled_grad, sums, wide, up_grad)
+        moved, value_sum, out_other, scaled_grad, sums, wide, up_grad = lax.optimization_barrier(
+            (moved, value_sum, out_other, scaled_grad, sums, wide, up_grad)
         )
         out_half = (out_mine + out_other.astype(F32)).astype(BF16).reshape(-1, width)
         out_half, sums = lax.optimization_barrier((out_half, sums))
         grad_out = along(out_half)
-        grad_ffn_value = value_turned.astype(F32)
+        grad_ffn_value = turn(value_sum).astype(F32)
     else:
         moved, scaled_grad, sums, wide = lax.optimization_barrier((moved, scaled_grad, sums, wide))
-    output = dot(arrange, moved[:, : rows // seqs].reshape(rows, width), TN).astype(BF16)
-    grad_first_rows = moved[:, rows // seqs :].reshape(seqs, rows, own_width).transpose(1, 0, 2).reshape(rows, width)
+    grad_first_rows = moved.transpose(1, 0, 2).reshape(rows, width)
 
     standard = (balanced.astype(F32) - mean) * scale_one
     grad_balanced = scale_one * (scaled_grad - sums[:, :1] * (1.0 / width) - standard * (sums[:, 1:] * (1.0 / width)))

time: 748 us -> 722 us (0.965)
  waiting for transfers between devices: 165 us -> 127 us
    ppermute x2, waiting for transfers between devices: 142 us -> 105 us  [turn(): return lax.ppermute(part, ('seq', 'wsh'), turned)]
    all_to_all x7 -> x8, starting transfers between devices: 37.2 us -> 43 us  [exchange(): return lax.all_to_all(x, axis, split_axis=0, concat_axis=0, tiled=True)]
    unnamed x102 -> x143, local copies, waits for them, and re-layouts: 20 us -> 17 us
  transfers between devices with their start and end apart: 27 -> 28, of which waited for: 9 -> 10; matrix products, arithmetic and copies ran while one was open for 14% -> 16% of each run, Pallas kernels for 27% -> 36%
where the time goes in v7:
time: 722 us; the launch traced here: 712 us
  Pallas kernels  346 us (48%)
  waiting for transfers between devices  127 us (18%)
  matrix products  69.3 us (10%)
  starting transfers between devices  61.3 us (8%)
  other arithmetic  48.8 us (7%)
  local copies, waits for them, and re-layouts  43.7 us (6%)
  between operations  16 us (2%)
    ppermute x2, waiting for transfers between devices, turn(): return lax.ppermute(part, ('seq', 'wsh'), turned)  105 us
    pallas_call x2, Pallas kernels, channel_stage(): pl.pallas_call(body, in_specs=[pl.BlockSpec(memory_space=pltpu.VMEM)] + [...  88.4 us
    dot_general x17, matrix products, dot(): return lax.dot_general(a, b, dims, preferred_element_type=F32)  69.3 us
    pallas_call x1, Pallas kernels, reduce_seq(): pl.pallas_call(functools.partial(reduce_kernel, splits), in_specs=[pl.Blo...  59.9 us
    pallas_call x1, Pallas kernels, gather_first(): pl.pallas_call(gather_kernel, in_specs=[pl.BlockSpec(memory_space=pltpu.V...  54.4 us
    pallas_call x1, Pallas kernels, run_backward(): pl.pallas_call(functools.partial(backward_kernel, count), grid=(rows // s...  47.4 us
    all_to_all x8, starting transfers between devices, exchange(): return lax.all_to_all(x, axis, split_axis=0, concat_axis=0, tiled=True)  43 us
    pallas_call x1, Pallas kernels, run_unproject(): pl.pallas_call(functools.partial(unproject_kernel, own_width, parts, piec...  40.4 us
  transfers between devices with their start and end apart: 28, of which 10 were waited for; matrix products, arithmetic and copies ran while one was open for 16% of the time, Pallas kernels for 36%

profile of v7, /device:TPU:4, one launch (start us, length us, event | category | flops | bytes accessed | tf_op | source)
XLA Modules:
  0.0 712.5 jit_solution(6835024346010614628)
XLA Ops:
  18.3 54.4 %gather_first.1 = (bf16[8,128,2048]{2,1,0:T(8,128)(2,1)}, bf16[8,128,128]{2,1,0:T(8,128)(2,1)}, bf16[4,512,1664]{2,1,0:T(8,128)(2,1)}) custom-call(bf16[128,2048]{1,0:T(8,128)(2,1)} %own_ref.1, bf16[128,128]{1,0:T(8,128)(2,1)} %pad.30.tail_ref, bf16[512,1664]{1,0:T(8,128)(2,1)} %copy-done.20), custom_call_target="tpu_custom_call" | custom-call | bytes 104857600 | tf_op jit(solution)/shard_map/gather_first/pallas_call | solution.py:781
  74.8 8.3 %convert_reduce_fusion = (f32[1024]{0:T(1024)S(1)}, bf16[1024,2048]{1,0:T(8,128)(2,1)}) fusion(bf16[1024,2048]{1,0:T(8,128)(2,1)} %bitcast.184, s32[1024]{0:T(1024)S(1)} %bitcast.177), kind=kOutput, calls=%fused_computation.1 | convolution fusion | flops 4302306304 | bytes 8396800 | tf_op jit(solution)/shard_map/dot_general | solution.py:28
  83.2 4.1 fusion.2
  88.3 4.3 all-to-all-start
  98.7 19.5 %mix_project.1 = (f32[1024,256]{1,0:T(8,128)}, f32[1024,256]{1,0:T(8,128)}, f32[1024,256]{1,0:T(8,128)}, f32[1024,640]{1,0:T(8,128)}, bf16[1024,640]{1,0:T(8,128)(2,1)}) custom-call(bf16[1024,2048]{1,0:T(8,128)(2,1)} %get-tuple-element.269.block_ref, f32[1024,4]{1,0:T(8,128)} %copy.132.stats_ref, f32[8,2048]{1,0:T(8,128)} %slice_bitcast_fusion.3.vec_ref, ...), custom_call_target="tpu_custom_call" | custom-call | flops 134217728 | bytes 62914560 | tf_op jit(solution)/shard_map/mix_project/pallas_call | solution.py:569
  120.0 6.5 all-to-all-start.1
  129.2 36.1 %mix_forward.1 = (bf16[1024,256]{1,0:T(8,128)(2,1)S(1)}, bf16[1024,256]{1,0:T(8,128)(2,1)S(1)}, f32[1024,256]{1,0:T(8,128)S(1)}, f32[1024,256]{1,0:T(8,128)S(1)}, f32[1024,256]{1,0:T(8,128)S(1)}) custom-call(f32[1024,256]{1,0:T(8,128)S(1)} %copy-done.4, f32[1024,256]{1,0:T(8,128)} %get-tuple-element.94.keys_ref, f32[1024,256]{1,0:T(8,128)} %get-tuple-element.95.values_ref, ...), custom_call_target="tpu_custom_call" | custom-call | flops 134217728 | bytes 115343360 | tf_op jit(solution)/shard_map/mix_forward/pallas_call | solution.py:385
  169.3 6.0 all-to-all-start.2
  178.9 7.5 %all-to-all-done.2 = bf16[8,128,256]{1,2,0:T(8,128)(2,1)S(1)} async-done(((bf16[8,128,256]{1,2,0:T(8,128)(2,1)}), bf16[8,128,256]{1,2,0:T(8,128)(2,1)S(1)}, u32[]{:S(2)}, u32[]{:S(2)}) %all-to-all-start.2) | async-done | bytes 524320 | tf_op jit(solution)/shard_map/all_to_all | solution.py:1089
  186.3 4.8 fusion.84
  191.7 3.9 collective-permute-start
  197.9 37.3 %channel_forward.1 = (f32[128,2048]{1,0:T(8,128)}, bf16[512,2048]{1,0:T(8,128)(2,1)}, bf16[512,1024]{1,0:T(8,128)(2,1)}, bf16[512,1024]{1,0:T(8,128)(2,1)}, f32[512,2048]{1,0:T(8,128)}) custom-call(bf16[128,2048]{1,0:T(8,128)(2,1)} %add_convert_fusion.2.refs_0_, bf16[2048,2048]{1,0:T(8,128)(2,1)} %refs_2_.3, bf16[2048,2048]{1,0:T(8,128)(2,1)} %refs_1_.3), custom_call_target="tpu_custom_call" | custom-call | bytes 104857600 | tf_op jit(solution)/shard_map/channel_forward/pallas_call | solution.py:1061
  237.9 4.9 all-to-all-start.3
  256.6 51.1 %channel_backward.1 = (f32[128,2048]{1,0:T(8,128)}, bf16[512,2048]{1,0:T(8,128)(2,1)}, bf16[512,1024]{1,0:T(8,128)(2,1)}, bf16[512,2048]{1,0:T(8,128)(2,1)}, bf16[512,1024]{1,0:T(8,128)(2,1)}) custom-call(bf16[128,2048]{1,0:T(8,128)(2,1)} %get-tuple-element.272.refs_0_, bf16[2048,2048]{1,0:T(8,128)(2,1)} %refs_1_.3, bf16[2048,2048]{1,0:T(8,128)(2,1)} %refs_2_.3, ...), custom_call_target="tpu_custom_call" | custom-call | bytes 104857600 | tf_op jit(solution)/shard_map/channel_backward/pallas_call | solution.py:1061
  312.8 3.9 collective-permute-done.3
  319.4 6.4 convolution_convert_fusion.1
  326.7 4.3 all-to-all-start.4
  331.1 4.5 fusion.90
  335.6 4.6 add_convert_fusion.1
  346.8 6.1 all-to-all-start.6
  352.9 7.7 %fusion.91 = f32[1024,2048]{1,0:T(8,128)} fusion(bf16[512,1024]{1,0:T(8,128)(2,1)} %get-tuple-element.125, bf16[512,2048]{1,0:T(8,128)(2,1)} %get-tuple-element.120), kind=kOutput, calls=%fused_computation.214 | convolution fusion | flops 2147483648 | bytes 11534336 | tf_op jit(solution)/shard_map/dot_general | solution.py:28
  360.6 47.4 %mix_backward.1 = (bf16[1024,256]{1,0:T(8,128)(2,1)S(1)}, bf16[1024,256]{1,0:T(8,128)(2,1)S(1)}, bf16[1024,256]{1,0:T(8,128)(2,1)S(1)}, bf16[4,1024,256]{2,1,0:T...) custom-call(bf16[1024,256]{1,0:T(8,128)(2,1)S(1)} %bitcast.129, f32[1024,256]{1,0:T(8,128)S(1)} %copy-done.4, ...), custom_call_target="tpu_custom_call" | custom-call | flops 134217728 | bytes 157286400 | tf_op jit(solution)/shard_map/mix_backward/pallas_call | solution.py:413
  413.2 8.9 %add_convert_fusion = bf16[1024,2048]{1,0:T(8,128)(2,1)} fusion(f32[1024,2048]{1,0:T(8,128)} %fusion.91, bf16[512,1024]{1,0:T(8,128)(2,1)} %collective-permute-done.5, bf16[512,2048]{1,0:T(8,128)(2,1)} %collective-permute-done.4), kind=kOutput, calls=%fused_computation.8 | convolution fusion | flops 2151677952 | bytes 15728640 | tf_op jit(solution)/shard_map/dot_general | solution.py:28
  431.1 5.1 all-to-all-start.5
  437.8 40.4 %mix_unproject.1 = (f32[1024,2048]{1,0:T(8,128)}, f32[1024,2]{1,0:T(8,128)}, bf16[4,8,64,1408]{3,2,1,0:T(8,128)(2,1)}, bf16[256,640]{1,0:T(8,128)(2,1)}) custom-call(bf16[1024,2048]{1,0:T(8,128)(2,1)} %get-tuple-element.269.block_ref, f32[1024,4]{1,0:T(8,128)} %copy.132.stats_ref, f32[8,2048]{1,0:T(8,128)} %slice_bitcast_fusion.3.vec_ref, ...), custom_call_target="tpu_custom_call" | custom-call | flops 134217728 | bytes 125829120 | tf_op jit(solution)/shard_map/mix_unproject/pallas_call | solution.py:592
  486.2 6.0 fusion.5
  492.4 6.3 fusion.12
  506.2 59.9 %reduce_seq.1 = f32[128,2048]{1,0:T(8,128)S(1)} custom-call(bf16[8,128,2048]{2,1,0:T(8,128)(2,1)S(1)} %bitcast.128), custom_call_target="tpu_custom_call" | custom-call | bytes 1048576 | tf_op jit(solution)/shard_map/reduce_seq/pallas_call | solution.py:903
  569.9 5.8 all-to-all-start.7
  575.8 6.4 collective-permute-start.15
  592.2 87.9 %collective-permute-done.15 = bf16[256,2048]{1,0:T(8,128)(2,1)S(1)} collective-permute-done((bf16[256,2048]{1,0:T(8,128)(2,1)}, bf16[256,2048]{1,0:T(8,128)(2,1)S(1)}, u32[]{:S(2)}, u32[]{:S(2)}) %collective-permute-start.15) | collective-permute-done | bytes 1048608 | tf_op jit(solution)/shard_map/ppermute | solution.py:1314
  682.5 17.2 %collective-permute-done.14 = bf16[256,2048]{1,0:T(8,128)(2,1)S(1)} collective-permute-done((bf16[256,2048]{1,0:T(8,128)(2,1)}, bf16[256,2048]{1,0:T(8,128)(2,1)S(1)}, u32[]{:S(2)}, u32[]{:S(2)}) %collective-permute-start.14) | collective-permute-done | bytes 1048608 | tf_op jit(solution)/shard_map/ppermute | solution.py:1314
  (323 shorter events, 119.2 us)
Async XLA Ops:
  7.2 111.7 %copy-start = (bf16[128,2048]{1,0:T(8,128)(2,1)S(1)}, bf16[128,2048]{1,0:T(8,128)(2,1)}, u32[]{:S(2)}) copy-start(bf16[128,2048]{1,0:T(8,128)(2,1)} %param.17) | copy-start | bytes 1572868
  7.2 179.1 %all-gather.2.cloned.1.call-start = ((), (), s32[]{:S(2)}) async-start(), calls=%async_computation.11 | async-start | bytes 10485760 | tf_op jit(solution)/shard_map/all_gather | solution.py:1213
  74.8 101.2 %copy-start.50 = (s32[1024,1]{0,1:T(1,128)}, s32[1024,1]{0,1:T(1,128)S(1)}, u32[]{:S(2)}) copy-start(s32[1024,1]{0,1:T(1,128)S(1)} %get-tuple-element.242) | copy-start | bytes 12292
  88.3 30.2 %all-to-all-start = ((bf16[8,128,256]{1,2,0:T(8,128)(2,1)}), bf16[8,128,256]{1,2,0:T(8,128)(2,1)S(1)}, u32[]{:S(2)}, u32[]{:S(2)}) async-start(bf16[8,128,256]{1,2,0:T(8,128)(2,1)} %bitcast.15), calls=%async_computation | async-start | bytes 1048576 | tf_op jit(solution)/shard_map/all_to_all | solution.py:1089
  120.0 48.3 %all-to-all-start.1 = ((bf16[8,16,2048]{2,1,0:T(8,128)(2,1)}), bf16[8,16,2048]{2,1,0:T(8,128)(2,1)S(1)}, u32[]{:S(2)}, u32[]{:S(2)}) async-start(bf16[8,16,2048]{2,1,0:T(8,128)(2,1)} %bitcast.17), calls=%async_computation.1 | async-start | bytes 1048576 | tf_op jit(solution)/shard_map/all_to_all | solution.py:1089
  128.3 232.3 %copy-start.2 = (bf16[640,256]{1,0:T(8,128)(2,1)}, bf16[640,256]{1,0:T(8,128)(2,1)S(1)}, u32[]{:S(2)}) copy-start(bf16[640,256]{1,0:T(8,128)(2,1)S(1)} %fusion.50.up_ref) | copy-start | bytes 983044
  169.3 17.0 %all-to-all-start.2 = ((bf16[8,128,256]{1,2,0:T(8,128)(2,1)}), bf16[8,128,256]{1,2,0:T(8,128)(2,1)S(1)}, u32[]{:S(2)}, u32[]{:S(2)}) async-start(bf16[8,128,256]{1,2,0:T(8,128)(2,1)} %copy.140), calls=%async_computation.2 | async-start | bytes 1048576 | tf_op jit(solution)/shard_map/all_to_all | solution.py:1089
  191.7 4.7 collective-permute-start
  237.9 69.8 %all-to-all-start.3 = ((bf16[8,16,2048]{2,1,0:T(8,128)(2,1)}), bf16[8,16,2048]{2,1,0:T(8,128)(2,1)}, u32[]{:S(2)}, u32[]{:S(2)}) async-start(bf16[8,16,2048]{2,1,0:T(8,128)(2,1)} %bitcast.147), calls=%async_computation.3 | async-start | bytes 1048576 | tf_op jit(solution)/shard_map/all_to_all | solution.py:1089
  244.8 1.2 collective-permute-start.1
  246.7 3.7 collective-permute-start.2
  311.2 5.5 collective-permute-start.3
  326.7 17.2 %all-to-all-start.4 = ((bf16[8,128,256]{2,1,0:T(8,128)(2,1)}), bf16[8,128,256]{2,1,0:T(8,128)(2,1)S(1)}, u32[]{:S(2)}, u32[]{:S(2)}) async-start(bf16[8,128,256]{2,1,0:T(8,128)(2,1)} %bitcast.146), calls=%async_computation.4 | async-start | bytes 1048576 | tf_op jit(solution)/shard_map/all_to_all | solution.py:1089
  331.0 147.2 %reduce-scatter.4.cloned.1.call-start = ((), (), s32[]{:S(2)}) async-start(), calls=%async_computation.12 | async-start | bytes 5242880 | tf_op jit(solution)/shard_map/reduce_scatter | solution.py:1311
  343.9 66.8 %collective-permute-start.4 = (bf16[512,2048]{1,0:T(8,128)(2,1)}, bf16[512,2048]{1,0:T(8,128)(2,1)}, u32[]{:S(2)}, u32[]{:S(2)}) collective-permute-start(bf16[512,2048]{1,0:T(8,128)(2,1)} %get-tuple-element.120), channel_id=1, source_target_pairs={{0,4},{4,0},{8,12},{12,8},{16,20},{20,16},{24,28},{28,24},{1,5},{5... | collective-permute-start | bytes 6291464 | tf_op jit(solution)/shard_map/ppermute | solution.py:1108
  345.4 65.2 %collective-permute-start.5 = (bf16[512,1024]{1,0:T(8,128)(2,1)}, bf16[512,1024]{1,0:T(8,128)(2,1)}, u32[]{:S(2)}, u32[]{:S(2)}) collective-permute-start(bf16[512,1024]{1,0:T(8,128)(2,1)} %get-tuple-element.121), channel_id=1, source_target_pairs={{0,4},{4,0},{8,12},{12,8},{16,20},{20,16},{24,28},{28,24},{1,5},{5... | collective-permute-start | bytes 3145736 | tf_op jit(solution)/shard_map/ppermute | solution.py:1108
  346.0 64.7 %collective-permute-start.6 = (bf16[128,2048]{1,0:T(8,128)(2,1)}, bf16[128,2048]{1,0:T(8,128)(2,1)}, u32[]{:S(2)}, u32[]{:S(2)}) collective-permute-start(bf16[128,2048]{1,0:T(8,128)(2,1)} %copy-done.21), channel_id=1, source_target_pairs={{0,1},{1,0},{2,3},{3,2},{4,5},{5,4},{6,7},{7,6},{8,9},{9,8},{10,11... | collective-permute-start | bytes 1572872 | tf_op jit(solution)/shard_map/ppermute | solution.py:1094
  346.0 64.7 %collective-permute-start.7 = (bf16[128,2048]{1,0:T(8,128)(2,1)}, bf16[128,2048]{1,0:T(8,128)(2,1)}, u32[]{:S(2)}, u32[]{:S(2)}) collective-permute-start(bf16[128,2048]{1,0:T(8,128)(2,1)} %copy-done.21), channel_id=1, source_target_pairs={{0,2},{1,3},{2,0},{3,1},{4,6},{5,7},{6,4},{7,5},{8,10},{9,11},{10,... | collective-permute-start | bytes 1572872 | tf_op jit(solution)/shard_map/ppermute | solution.py:1094
  346.8 63.8 %all-to-all-start.6 = ((bf16[4,128,8,64]{1,3,2,0:T(8,128)(2,1)}), bf16[4,128,8,64]{1,3,2,0:T(8,128)(2,1)}, u32[]{:S(2)}, u32[]{:S(2)}) async-start(bf16[4,128,8,64]{1,3,2,0:T(8,128)(2,1)} %copy.142), calls=%async_computation.7 | async-start | bytes 1048576 | tf_op jit(solution)/shard_map/all_to_all | solution.py:1089
  352.9 217.0 %reduce-scatter.8.cloned.1.call-start = ((), (), s32[]{:S(2)}) async-start(), calls=%async_computation.14 | async-start | bytes 5242880 | tf_op jit(solution)/shard_map/reduce_scatter | solution.py:1311
  410.6 11.4 %collective-permute-start.8 = (bf16[128,2048]{1,0:T(8,128)(2,1)}, bf16[128,2048]{1,0:T(8,128)(2,1)S(1)}, u32[]{:S(2)}, u32[]{:S(2)}) collective-permute-start(bf16[128,2048]{1,0:T(8,128)(2,1)} %collective-permute-done.7), channel_id=1, source_target_pairs={{0,1},{1,0},{2,3},{3,2},{4,5},{5,4},{6,7},{7,6},{8,9},{9,8},{10,11... | collective-permute-start | bytes 1572872 | tf_op jit(solution)/shard_map/ppermute | solution.py:1094
  427.3 50.9 %collective-permute-start.9 = (bf16[4,64,2048]{2,1,0:T(8,128)(2,1)}, bf16[4,64,2048]{2,1,0:T(8,128)(2,1)}, u32[]{:S(2)}, u32[]{:S(2)}) collective-permute-start(bf16[4,64,2048]{2,1,0:T(8,128)(2,1)} %dynamic-slice_bitcast_fusion), channel_id=1, source_target_pairs={{0,4},{4,0},{8,12},{12,8},{16,20},{20,16},{24,28},{28,24},{1,5},{5... | collective-permute-start | bytes 3145736 | tf_op jit(solution)/shard_map/ppermute | solution.py:1108
  431.1 47.0 %all-to-all-start.5 = ((bf16[8,128,256]{2,1,0:T(8,128)(2,1)}), bf16[8,128,256]{2,1,0:T(8,128)(2,1)S(1)}, u32[]{:S(2)}, u32[]{:S(2)}) async-start(bf16[8,128,256]{2,1,0:T(8,128)(2,1)} %bitcast.37), calls=%async_computation.5 | async-start | bytes 1048576 | tf_op jit(solution)/shard_map/all_to_all | solution.py:1089
  436.3 133.7 %reduce-scatter.6.cloned.1.call-start = ((), (), s32[]{:S(2)}) async-start(), calls=%async_computation.13 | async-start | bytes 1310720 | tf_op jit(solution)/shard_map/reduce_scatter | solution.py:1311
  480.6 18.1 %collective-permute-start.10 = (bf16[2,8,64,1408]{3,2,1,0:T(8,128)(2,1)S(1)}, bf16[2,8,64,1408]{3,2,1,0:T(8,128)(2,1)}, u32[]{:S(2)}, u32[]{:S(2)}) collective-permute-start(bf16[2,8,64,1408]{3,2,1,0:T(8,128)(2,1)S(1)} %pad_maximum_fusion), channel_id=1, source_target_pairs={{0,1},{1,0},{2,3},{3,2},{4,5},{5,4},{6,7},{7,6},{8,9},{9,8},{10,11... | collective-permute-start | bytes 8650760 | tf_op jit(solution)/shard_map/ppermute | solution.py:1094
  503.9 63.0 %collective-permute-start.11 = (bf16[8,64,1408]{2,1,0:T(8,128)(2,1)S(1)}, bf16[8,64,1408]{2,1,0:T(8,128)(2,1)S(1)}, u32[]{:S(2)}, u32[]{:S(2)}) collective-permute-start(bf16[8,64,1408]{2,1,0:T(8,128)(2,1)S(1)} %fusion.31), channel_id=1, source_target_pairs={{0,2},{1,3},{2,0},{3,1},{4,6},{5,7},{6,4},{7,5},{8,10},{9,11},{10,... | collective-permute-start | bytes 4325384 | tf_op jit(solution)/shard_map/ppermute | solution.py:1094
  569.9 131.3 %all-to-all-start.7 = ((bf16[8,64,1408]{2,1,0:T(8,128)(2,1)}), bf16[8,64,1408]{2,1,0:T(8,128)(2,1)S(1)}, u32[]{:S(2)}, u32[]{:S(2)}) async-start(bf16[8,64,1408]{2,1,0:T(8,128)(2,1)} %fusion.17), calls=%async_computation.10 | async-start | bytes 2883584 | tf_op jit(solution)/shard_map/all_to_all | solution.py:1089
  575.8 6.5 collective-permute-start.12
  575.8 104.3 %collective-permute-start.15 = (bf16[256,2048]{1,0:T(8,128)(2,1)}, bf16[256,2048]{1,0:T(8,128)(2,1)S(1)}, u32[]{:S(2)}, u32[]{:S(2)}) collective-permute-start(bf16[256,2048]{1,0:T(8,128)(2,1)} %reduce-scatter.4.cloned.1.call-done), channel_id=1, source_target_pairs={{0,0},{1,8},{2,16},{3,24},{4,4},{5,12},{6,20},{7,28},{8,1},{9,9},{... | collective-permute-start | bytes 3145736 | tf_op jit(solution)/shard_map/ppermute | solution.py:1314
  582.3 117.4 %collective-permute-start.14 = (bf16[256,2048]{1,0:T(8,128)(2,1)}, bf16[256,2048]{1,0:T(8,128)(2,1)S(1)}, u32[]{:S(2)}, u32[]{:S(2)}) collective-permute-start(bf16[256,2048]{1,0:T(8,128)(2,1)} %reduce-scatter.8.cloned.1.call-done), channel_id=1, source_target_pairs={{0,0},{1,8},{2,16},{3,24},{4,4},{5,12},{6,20},{7,28},{8,1},{9,9},{... | collective-permute-start | bytes 3145736 | tf_op jit(solution)/shard_map/ppermute | solution.py:1314
  585.1 5.3 collective-permute-start.13
  587.4 94.3 %copy-start.30 = (bf16[64,2048]{1,0:T(8,128)(2,1)S(1)}, bf16[64,2048]{1,0:T(8,128)(2,1)}, u32[]{:S(2)}) copy-start(bf16[64,2048]{1,0:T(8,128)(2,1)} %reduce-scatter.6.cloned.1.call-done) | copy-start | bytes 786436
  (61 other events, 758.7 us)
Sparse Core Ops, SparseCore 0:
  72.9 56.2 all-gather.1
  344.0 75.8 reduce-scatter.3
  425.8 86.9 reduce-scatter.7
  515.6 44.5 reduce-scatter.5

commit v8 on v7

--- a/solution.py
+++ b/solution.py
@@ -790,15 +790,50 @@
     )(own, tail, weight)
 
 
+def turning(x_ref, out_ref, send_sem, recv_sem):
+    s, w, side, z, _, _, _ = places()
+    home = z == w
+    greetings = tuple(((source != z) | (z != w), (source * 2 + side, z)) for source in range(4))
+
+    def copy(j):
+        piece = (z + j) % 4
+        return send(x_ref.at[piece], out_ref.at[z], send_sem.at[j], recv_sem.at[j], (w * 2 + side, piece))
+
+    def start():
+        for j in (3, 2, 1):
+            copy(j).start()
+
+        @pl.when(jnp.logical_not(home))
+        def _():
+            copy(0).start()
+
+        @pl.when(home)
+        def _():
+            out_ref[z] = x_ref[z]
+
+    def end():
+        for j in range(1, 4):
+            copy(j).wait_recv()
+            copy(j).wait_send()
+
+        @pl.when(jnp.logical_not(home))
+        def _():
+            copy(0).wait_recv()
+            copy(0).wait_send()
+
+    return greetings, jnp.where(home, 3, 4), start, end
+
+
 def reduce_kernel(
-    splits, x_ref, out_ref, x_buf, right_buf, left_buf, right_out, left_out,
-    x_send, x_recv, right_send, right_recv, left_send, left_recv,
+    splits, x_ref, turn_ref, out_ref, turn_out, x_buf, right_buf, left_buf, right_out, left_out,
+    x_send, x_recv, right_send, right_recv, left_send, left_recv, turn_send, turn_recv,
 ):
     s, w, side, z, x_device, _, _ = places()
     up, down = (s + 2, w), (s - 2, w)
     size = x_ref.shape[2] // splits
     columns = [slice(c * size, (c + 1) * size) for c in range(splits)]
-    greet(((None, x_device), (z < 3, up), (z > 0, down)), 1 + line_ends(z))
+    greetings, number, start_turn, end_turn = turning(turn_ref, turn_out, turn_send, turn_recv)
+    greet(((None, x_device), (z < 3, up), (z > 0, down)) + greetings, 1 + line_ends(z) + number)
 
     def to_x(target, c):
         return send(
@@ -837,6 +872,7 @@
             start_x(z - k)
 
     start_x(z)
+    start_turn()
     for k in (3, 2, 1):
         for c in range(splits):
 
@@ -894,25 +930,60 @@
             def _(k=k, c=c):
                 to_left(k, c).wait_send()
 
-
-def reduce_seq(x):
+    end_turn()
+
+
+def reduce_seq(x, turned):
     seqs, rows, width = x.shape
-    if seqs != 8 or lax.axis_size("wsh") != 4:
-        return jnp.sum(exchange(x, "seq").astype(F32), 0)
     splits = 2
+    vmem = pl.BlockSpec(memory_space=pltpu.VMEM)
+    dma = pltpu.SemaphoreType.DMA
     return pl.pallas_call(
         functools.partial(reduce_kernel, splits),
-        in_specs=[pl.BlockSpec(memory_space=pltpu.VMEM)],
-        out_specs=pl.BlockSpec(memory_space=pltpu.VMEM),
-        out_shape=jax.ShapeDtypeStruct((rows, width), F32),
+        in_specs=[vmem] * 2,
+        out_specs=[vmem] * 2,
+        out_shape=[jax.ShapeDtypeStruct((rows, width), F32), jax.ShapeDtypeStruct(turned.shape, turned.dtype)],
         scratch_shapes=[pltpu.VMEM((4, rows, width), BF16)]
         + [pltpu.VMEM((3, rows, width), BF16)] * 4
-        + [pltpu.SemaphoreType.DMA((4, splits))] * 2
-        + [pltpu.SemaphoreType.DMA((3, splits))] * 4,
+        + [dma((4, splits))] * 2 + [dma((3, splits))] * 4 + [dma((4,))] * 2,
         compiler_params=pltpu.CompilerParams(collective_id=2, has_side_effects=True, vmem_limit_bytes=40 << 20),
         cost_estimate=pl.CostEstimate(flops=0, bytes_accessed=1 << 20, transcendentals=0),
         name="reduce_seq",
-    )(x)
+    )(x, turned)
+
+
+def finish_kernel(wide_ref, key_ref, wide_out, key_out, wide_send, wide_recv, key_send, key_recv):
+    s, w, _, _, _, _, _ = places()
+    greetings, number, start_turn, end_turn = turning(key_ref, key_out, key_send, key_recv)
+    greet(tuple((None, ((s + d) % 8, w)) for d in range(1, 8)) + greetings, 7 + number)
+
+    def wide(d):
+        target = (s + d) % 8
+        return send(wide_ref.at[target], wide_out.at[s], wide_send.at[d - 1], wide_recv.at[d - 1], (target, w))
+
+    for d in (4, 3, 5, 2, 6, 1, 7):
+        wide(d).start()
+    start_turn()
+    wide_out[s] = wide_ref[s]
+    for d in range(1, 8):
+        wide(d).wait_recv()
+        wide(d).wait_send()
+    end_turn()
+
+
+def finish(wide, key):
+    vmem = pl.BlockSpec(memory_space=pltpu.VMEM)
+    dma = pltpu.SemaphoreType.DMA
+    return pl.pallas_call(
+        finish_kernel,
+        in_specs=[vmem] * 2,
+        out_specs=[vmem] * 2,
+        out_shape=[jax.ShapeDtypeStruct(x.shape, x.dtype) for x in (wide, key)],
+        scratch_shapes=[dma((7,)), dma((7,)), dma((4,)), dma((4,))],
+        compiler_params=pltpu.CompilerParams(collective_id=5, has_side_effects=True, vmem_limit_bytes=24 << 20),
+        cost_estimate=pl.CostEstimate(flops=0, bytes_accessed=100 << 20, transcendentals=0),
+        name="finish",
+    )(wide, key)
 
 
 def channel_kernel(
@@ -1108,6 +1179,11 @@
     return lax.ppermute(x, "seq", [(i, i ^ 1) for i in range(lax.axis_size("seq"))])
 
 
+def quartered(x):
+    rows, columns = x.shape
+    return x.reshape(rows, 4, 4, columns // 16).transpose(0, 2, 1, 3).reshape(rows, columns)
+
+
 def scalar_sum(x):
     if lax.axis_size("wsh") != 4:
         return jnp.sum(lax.all_gather(x.reshape(1), "wsh", axis=0, tiled=True))
@@ -1227,7 +1303,7 @@
     teacher_rows = exchange(dot(arrange, teacher_late).astype(BF16).reshape(seqs, rows // seqs, width), "seq")
     inputs = (recept, keys, values, hidden, first, up, vec, segments)
     mixed_out, *saved = run_forward(*inputs)
-    teacher_rows, mixed_out = lax.optimization_barrier((teacher_rows, mixed_out))
+    teacher_rows, mixed_out, total_valid = lax.optimization_barrier((teacher_rows, mixed_out, total_valid))
     target = dot(settle, teacher_rows.reshape(rows, width))
 
     mixed_rows = exchange(mixed_out.reshape(seqs, rows, own_width), "seq").transpose(1, 0, 2).reshape(rows, width)
@@ -1278,7 +1354,9 @@
     grad_posted = dot(grad_low, w_out, NT).astype(BF16)
     if paired:
         hidden_mine, grad_posted = lax.optimization_barrier((hidden_mine, grad_posted))
-        value_part = (dot(hidden_mine, cot, TN) + dot(hidden_other, cot_other, TN)).astype(BF16)
+        value_part = (
+            dot(quartered(hidden_mine), cot, TN) + dot(quartered(hidden_other), cot_other, TN)
+        ).astype(BF16)
     else:
         value_part = dot(hidden_rows, cot, TN).astype(BF16)
     grad_heads = exchange(grad_posted.reshape(rows, seqs, own_width).transpose(1, 0, 2), "seq").reshape(group, own_width)
@@ -1290,7 +1368,9 @@
         channel_other, pre_other, lefts, near_grad, recept_low = lax.optimization_barrier(
             (channel_other, pre_other, lefts, near_grad, recept_low)
         )
-        key_part = (dot(pre_mine, channel, TN) + dot(pre_other, channel_other, TN)).astype(BF16)
+        key_part = (
+            dot(quartered(pre_mine), channel, TN) + dot(quartered(pre_other), channel_other, TN)
+        ).astype(BF16)
     else:
         lefts, near_grad, recept_low = lax.optimization_barrier((lefts, near_grad, recept_low))
         key_part = dot(grad_pre, channel, TN).astype(BF16)
@@ -1303,15 +1383,8 @@
     recept_low, key_part, out_part = lax.optimization_barrier((recept_low, key_part, out_part))
     if paired:
         lines = [[0, 2, 4, 6], [1, 3, 5, 7]]
-        turned = [
-            ((z * 2 + x) * 4 + w, (w * 2 + x) * 4 + z) for z in range(4) for x in range(2) for w in range(4)
-        ]
-
         def along(part):
             return lax.psum_scatter(part, "seq", scatter_dimension=0, tiled=True, axis_index_groups=lines)
-
-        def turn(part):
-            return lax.ppermute(part, ("seq", "wsh"), turned)
 
         halves_out = out_part.reshape(seqs // 2, 2, piece, width)
         x_side = me % 2
@@ -1343,7 +1416,6 @@
         out_half = (out_mine + out_other.astype(F32)).astype(BF16).reshape(-1, width)
         out_half, sums = lax.optimization_barrier((out_half, sums))
         grad_out = along(out_half)
-        grad_ffn_value = turn(value_sum).astype(F32)
     else:
         moved, scaled_grad, sums, wide = lax.optimization_barrier((moved, scaled_grad, sums, wide))
     grad_first_rows = moved.transpose(1, 0, 2).reshape(rows, width)
@@ -1359,11 +1431,15 @@
         wide_part = kept_part + swap(far, 2).astype(F32)
     else:
         wide_part = block_sum(wide)
-    grad_tokens = reduce_seq(grad_given).astype(BF16)
     if paired:
+        grad_tokens, value_all = reduce_seq(grad_given, value_sum.reshape(4, -1, width))
         wide_part, grad_tokens, grad_out, key_sum = lax.optimization_barrier((wide_part, grad_tokens, grad_out, key_sum))
-        grad_ffn_key = turn(key_sum).astype(F32)
-    wide_all = exchange(wide_part.astype(BF16), "seq").astype(F32)
+        wide_all, key_all = finish(wide_part.astype(BF16), key_sum.reshape(4, -1, width))
+        wide_all = wide_all.astype(F32)
+        grad_ffn_key, grad_ffn_value = [x.reshape(-1, width).astype(F32) for x in (key_all, value_all)]
+    else:
+        grad_tokens = jnp.sum(exchange(grad_given, "seq").astype(F32), 0)
+        wide_all = exchange(wide_part.astype(BF16), "seq").astype(F32)
 
     def square(at):
         taken = wide_all[:, :, at * own_width : (at + 1) * own_width]
@@ -1375,7 +1451,7 @@
     up_part = unpad_ranks(block_sum(up_grad.reshape(parts, piece, WIDE)))
 
     return (
-        output, grad_tokens, grad_first_rows,
+        output, grad_tokens.astype(BF16), grad_first_rows,
         square(0), square(1), square(2),
         grad_out.astype(F32), grad_down, up_part,
         grad_ffn_key, grad_ffn_value, grad_vectors,

time: 722 us -> 736 us (1.019)
  Pallas kernels: 346 us -> 439 us
  waiting for transfers between devices: 127 us -> 46.4 us
  local copies, waits for them, and re-layouts: 43.7 us -> 61.4 us
  starting transfers between devices: 61.3 us -> 50.3 us
    ppermute x2 -> x0, waiting for transfers between devices: 105 us -> none  [turn(): return lax.ppermute(part, ('seq', 'wsh'), turned)]
    pallas_call x1 -> x2, Pallas kernels: 59.9 us -> 153 us  [the longest x1 92.4 us: finish(): pl.pallas_call(finish_kernel, in_specs=[vmem] * 2, out_specs=[vmem] * 2,...]
    ppermute x9, waiting for transfers between devices: 6.75 us -> 33.8 us  [swap(): return lax.ppermute(x, 'wsh', [(i, i ^ by) for i in range(size)])]
    ppermute x2 -> x0, starting transfers between devices: 8.29 us -> none  [turn(): return lax.ppermute(part, ('seq', 'wsh'), turned)]
    all_to_all x8 -> x7, starting transfers between devices: 43 us -> 37.5 us  [exchange(): return lax.all_to_all(x, axis, split_axis=0, concat_axis=0, tiled=True)]
    unnamed x143 -> x139, local copies, waits for them, and re-layouts: 17 us -> 17.4 us
  transfers between devices with their start and end apart: 28 -> 25, of which waited for: 10 -> 5; matrix products, arithmetic and copies ran while one was open for 16% -> 17% of each run, Pallas kernels for 36% -> 35%
where the time goes in v8:
time: 736 us; the launch traced here: 727 us
  Pallas kernels  439 us (60%)
  matrix products  66.6 us (9%)
  local copies, waits for them, and re-layouts  61.4 us (8%)
  starting transfers between devices  50.3 us (7%)
  other arithmetic  47.3 us (6%)
  waiting for transfers between devices  46.4 us (6%)
  between operations  16 us (2%)
    pallas_call x1, Pallas kernels, finish(): pl.pallas_call(finish_kernel, in_specs=[vmem] * 2, out_specs=[vmem] * 2,...  92.4 us
    pallas_call x2, Pallas kernels, channel_stage(): pl.pallas_call(body, in_specs=[pl.BlockSpec(memory_space=pltpu.VMEM)] + [...  88.8 us
    dot_general x17, matrix products, dot(): return lax.dot_general(a, b, dims, preferred_element_type=F32)  66.6 us
    pallas_call x1, Pallas kernels, reduce_seq(): pl.pallas_call(functools.partial(reduce_kernel, splits), in_specs=[vmem]...  60.3 us
    pallas_call x1, Pallas kernels, gather_first(): pl.pallas_call(gather_kernel, in_specs=[pl.BlockSpec(memory_space=pltpu.V...  54.4 us
    pallas_call x1, Pallas kernels, run_backward(): pl.pallas_call(functools.partial(backward_kernel, count), grid=(rows // s...  47.2 us
    pallas_call x1, Pallas kernels, run_unproject(): pl.pallas_call(functools.partial(unproject_kernel, own_width, parts, piec...  40 us
    all_to_all x7, starting transfers between devices, exchange(): return lax.all_to_all(x, axis, split_axis=0, concat_axis=0, tiled=True)  37.5 us
  transfers between devices with their start and end apart: 25, of which 5 were waited for; matrix products, arithmetic and copies ran while one was open for 17% of the time, Pallas kernels for 35%

profile of v8, /device:TPU:4, one launch (start us, length us, event | category | flops | bytes accessed | tf_op | source)
XLA Modules:
  0.0 726.6 jit_solution(14554215692698668202)
XLA Ops:
  18.3 54.4 %gather_first.1 = (bf16[8,128,2048]{2,1,0:T(8,128)(2,1)}, bf16[8,128,128]{2,1,0:T(8,128)(2,1)}, bf16[4,512,1664]{2,1,0:T(8,128)(2,1)}) custom-call(bf16[128,2048]{1,0:T(8,128)(2,1)} %own_ref.1, bf16[128,128]{1,0:T(8,128)(2,1)} %pad.30.tail_ref, bf16[512,1664]{1,0:T(8,128)(2,1)} %copy-done.21), custom_call_target="tpu_custom_call" | custom-call | bytes 104857600 | tf_op jit(solution)/shard_map/gather_first/pallas_call | solution.py:781
  74.8 8.3 %convert_reduce_fusion = (f32[1024]{0:T(1024)S(1)}, bf16[1024,2048]{1,0:T(8,128)(2,1)}) fusion(bf16[1024,2048]{1,0:T(8,128)(2,1)} %bitcast.219, s32[1024]{0:T(1024)S(1)} %bitcast.212), kind=kOutput, calls=%fused_computation.1 | convolution fusion | flops 4302306304 | bytes 8396800 | tf_op jit(solution)/shard_map/dot_general | solution.py:28
  83.1 4.1 fusion.2
  88.3 4.3 all-to-all-start
  100.0 19.5 %mix_project.1 = (f32[1024,256]{1,0:T(8,128)}, f32[1024,256]{1,0:T(8,128)}, f32[1024,256]{1,0:T(8,128)}, f32[1024,640]{1,0:T(8,128)}, bf16[1024,640]{1,0:T(8,128)(2,1)}) custom-call(bf16[1024,2048]{1,0:T(8,128)(2,1)} %get-tuple-element.279.block_ref, f32[1024,4]{1,0:T(8,128)} %copy.164.stats_ref, f32[8,2048]{1,0:T(8,128)} %slice_bitcast_fusion.3.vec_ref, ...), custom_call_target="tpu_custom_call" | custom-call | flops 134217728 | bytes 62914560 | tf_op jit(solution)/shard_map/mix_project/pallas_call | solution.py:569
  121.2 6.3 all-to-all-start.1
  134.9 36.1 %mix_forward.1 = (bf16[1024,256]{1,0:T(8,128)(2,1)S(1)}, bf16[1024,256]{1,0:T(8,128)(2,1)S(1)}, f32[1024,256]{1,0:T(8,128)S(1)}, f32[1024,256]{1,0:T(8,128)S(1)}, f32[1024,256]{1,0:T(8,128)S(1)}) custom-call(f32[1024,256]{1,0:T(8,128)S(1)} %copy-done.4, f32[1024,256]{1,0:T(8,128)} %get-tuple-element.99.keys_ref, f32[1024,256]{1,0:T(8,128)} %get-tuple-element.100.values_ref, ...), custom_call_target="tpu_custom_call" | custom-call | flops 134217728 | bytes 115343360 | tf_op jit(solution)/shard_map/mix_forward/pallas_call | solution.py:385
  175.0 6.0 all-to-all-start.2
  184.0 10.7 %all-to-all-done.2 = bf16[8,128,256]{1,2,0:T(8,128)(2,1)S(1)} async-done(((bf16[8,128,256]{1,2,0:T(8,128)(2,1)}), bf16[8,128,256]{1,2,0:T(8,128)(2,1)S(1)}, u32[]{:S(2)}, u32[]{:S(2)}) %all-to-all-start.2) | async-done | bytes 524320 | tf_op jit(solution)/shard_map/all_to_all | solution.py:1160
  194.7 4.8 fusion.84
  200.1 3.8 collective-permute-start.2
  206.8 37.3 %channel_forward.1 = (f32[128,2048]{1,0:T(8,128)}, bf16[512,2048]{1,0:T(8,128)(2,1)}, bf16[512,1024]{1,0:T(8,128)(2,1)}, bf16[512,1024]{1,0:T(8,128)(2,1)}, f32[512,2048]{1,0:T(8,128)}) custom-call(bf16[128,2048]{1,0:T(8,128)(2,1)} %add_convert_fusion.2.refs_0_, bf16[2048,2048]{1,0:T(8,128)(2,1)} %refs_2_.3, bf16[2048,2048]{1,0:T(8,128)(2,1)} %refs_1_.3), custom_call_target="tpu_custom_call" | custom-call | bytes 104857600 | tf_op jit(solution)/shard_map/channel_forward/pallas_call | solution.py:1132
  246.4 4.9 all-to-all-start.3
  253.2 3.2 fusion.85
  256.5 51.5 %channel_backward.1 = (f32[128,2048]{1,0:T(8,128)}, bf16[512,2048]{1,0:T(8,128)(2,1)}, bf16[512,1024]{1,0:T(8,128)(2,1)}, bf16[512,2048]{1,0:T(8,128)(2,1)}, bf16[512,1024]{1,0:T(8,128)(2,1)}) custom-call(bf16[128,2048]{1,0:T(8,128)(2,1)} %get-tuple-element.282.refs_0_, bf16[2048,2048]{1,0:T(8,128)(2,1)} %refs_1_.3, bf16[2048,2048]{1,0:T(8,128)(2,1)} %refs_2_.3, ...), custom_call_target="tpu_custom_call" | custom-call | bytes 104857600 | tf_op jit(solution)/shard_map/channel_backward/pallas_call | solution.py:1132
  308.0 3.5 multiply_reduce_fusion
  324.8 6.5 convolution_convert_fusion.1
  332.2 6.4 all-to-all-start.4
  342.2 4.1 fusion.86
  346.4 4.4 add_convert_fusion.1
  359.9 6.1 all-to-all-start.6
  366.3 7.7 %fusion.87 = f32[1024,2048]{1,0:T(8,128)} fusion(bf16[512,1024]{0,1:T(8,128)(2,1)} %bitcast.181, bf16[512,2048]{1,0:T(8,128)(2,1)} %get-tuple-element.126), kind=kOutput, calls=%fused_computation.216 | convolution fusion | flops 2147483648 | bytes 11534336 | tf_op jit(solution)/shard_map/dot_general | solution.py:28
  374.0 47.2 %mix_backward.1 = (bf16[1024,256]{1,0:T(8,128)(2,1)S(1)}, bf16[1024,256]{1,0:T(8,128)(2,1)S(1)}, bf16[1024,256]{1,0:T(8,128)(2,1)S(1)}, bf16[4,1024,256]{2,1,0:T...) custom-call(bf16[1024,256]{1,0:T(8,128)(2,1)S(1)} %bitcast.153, f32[1024,256]{1,0:T(8,128)S(1)} %copy-done.4, ...), custom_call_target="tpu_custom_call" | custom-call | flops 134217728 | bytes 157286400 | tf_op jit(solution)/shard_map/mix_backward/pallas_call | solution.py:413
  427.8 8.5 %add_convert_fusion = bf16[1024,2048]{1,0:T(8,128)(2,1)} fusion(f32[1024,2048]{1,0:T(8,128)} %fusion.87, bf16[512,1024]{0,1:T(8,128)(2,1)S(1)} %bitcast.180, bf16[512,2048]{1,0:T(8,128)(2,1)} %collective-permute-done.4), kind=kOutput, calls=%fused_computation.8 | convolution fusion | flops 2151677952 | bytes 15728640 | tf_op jit(solution)/shard_map/dot_general | solution.py:28
  437.1 2.8 convolution_convert_fusion
  445.0 3.5 all-to-all-start.5
  450.4 40.0 %mix_unproject.1 = (f32[1024,2048]{1,0:T(8,128)}, f32[1024,2]{1,0:T(8,128)}, bf16[4,8,64,1408]{3,2,1,0:T(8,128)(2,1)}, bf16[256,640]{1,0:T(8,128)(2,1)}) custom-call(bf16[1024,2048]{1,0:T(8,128)(2,1)} %get-tuple-element.279.block_ref, f32[1024,4]{1,0:T(8,128)} %copy.164.stats_ref, f32[8,2048]{1,0:T(8,128)} %slice_bitcast_fusion.3.vec_ref, ...), custom_call_target="tpu_custom_call" | custom-call | flops 134217728 | bytes 125829120 | tf_op jit(solution)/shard_map/mix_unproject/pallas_call | solution.py:592
  500.1 5.9 fusion.5
  506.3 6.4 fusion.12
  522.2 31.6 %collective-permute-done.13 = bf16[64,640]{1,0:T(8,128)(2,1)S(1)} collective-permute-done((bf16[64,640]{1,0:T(8,128)(2,1)S(1)}, bf16[64,640]{1,0:T(8,128)(2,1)S(1)}, u32[]{:S(2)}, u32[]{:S(2)}) %collective-permute-start.13) | collective-permute-done | bytes 81952 | tf_op jit(solution)/shard_map/ppermute | solution.py:1165
  554.6 60.3 %reduce_seq.1 = (f32[128,2048]{1,0:T(8,128)S(1)}, bf16[4,64,2048]{2,1,0:T(8,128)(2,1)S(1)}) custom-call(bf16[8,128,2048]{2,1,0:T(8,128)(2,1)S(1)} %bitcast.152, bf16[4,64,2048]{2,1,0:T(8,128)(2,1)S(1)} %bitcast.154), custom_call_target="tpu_custom_call" | custom-call | bytes 1048576 | tf_op jit(solution)/shard_map/reduce_seq/pallas_call | solution.py:941
  619.6 92.4 %finish.1 = (bf16[8,64,1408]{2,1,0:T(8,128)(2,1)S(1)}, bf16[4,64,2048]{2,1,0:T(8,128)(2,1)S(1)}) custom-call(bf16[8,64,1408]{2,1,0:T(8,128)(2,1)S(1)} %fusion.17.wide_ref, bf16[4,64,2048]{2,1,0:T(8,128)(2,1)S(1)} %bitcast.155), custom_call_target="tpu_custom_call" | custom-call | bytes 104857600 | tf_op jit(solution)/shard_map/finish/pallas_call | solution.py:977
  (324 shorter events, 118.1 us)
Async XLA Ops:
  7.2 112.9 %copy-start = (bf16[128,2048]{1,0:T(8,128)(2,1)S(1)}, bf16[128,2048]{1,0:T(8,128)(2,1)}, u32[]{:S(2)}) copy-start(bf16[128,2048]{1,0:T(8,128)(2,1)} %param.17) | copy-start | bytes 1572868
  7.2 187.5 %all-gather.2.cloned.1.call-start = ((), (), s32[]{:S(2)}) async-start(), calls=%async_computation.10 | async-start | bytes 10485760 | tf_op jit(solution)/shard_map/all_gather | solution.py:1289
  15.6 58.3 %copy-start.61 = (s32[1,4]{1,0:T(1,128)S(1)}, s32[1,4]{1,0:T(1,128)}, u32[]{:S(2)}) copy-start(s32[1,4]{1,0:T(1,128)} %param.20) | copy-start | bytes 52
  74.8 106.9 %copy-start.51 = (s32[1024,1]{0,1:T(1,128)}, s32[1024,1]{0,1:T(1,128)S(1)}, u32[]{:S(2)}) copy-start(s32[1024,1]{0,1:T(1,128)S(1)} %get-tuple-element.252) | copy-start | bytes 12292
  88.3 31.5 %all-to-all-start = ((bf16[8,128,256]{1,2,0:T(8,128)(2,1)}), bf16[8,128,256]{1,2,0:T(8,128)(2,1)S(1)}, u32[]{:S(2)}, u32[]{:S(2)}) async-start(bf16[8,128,256]{1,2,0:T(8,128)(2,1)} %bitcast.15), calls=%async_computation | async-start | bytes 1048576 | tf_op jit(solution)/shard_map/all_to_all | solution.py:1160
  93.8 34.7 %collective-permute-start = (f32[8,128]{1,0:T(8,128)S(1)}, f32[8,128]{1,0:T(8,128)S(1)}, u32[]{:S(2)}, u32[]{:S(2)}) collective-permute-start(f32[8,128]{1,0:T(8,128)S(1)} %broadcast_in_dim.4), channel_id=1, source_target_pairs={{0,1},{1,0},{2,3},{3,2},{4,5},{5,4},{6,7},{7,6},{8,9},{9,8},{10,11... | collective-permute-start | bytes 12296 | tf_op jit(solution)/shard_map/ppermute | solution.py:1165
  119.7 254.3 %copy-start.2 = (bf16[640,256]{1,0:T(8,128)(2,1)}, bf16[640,256]{1,0:T(8,128)(2,1)S(1)}, u32[]{:S(2)}) copy-start(bf16[640,256]{1,0:T(8,128)(2,1)S(1)} %fusion.50.up_ref) | copy-start | bytes 983044
  121.2 52.8 %all-to-all-start.1 = ((bf16[8,16,2048]{2,1,0:T(8,128)(2,1)}), bf16[8,16,2048]{2,1,0:T(8,128)(2,1)S(1)}, u32[]{:S(2)}, u32[]{:S(2)}) async-start(bf16[8,16,2048]{2,1,0:T(8,128)(2,1)} %bitcast.17), calls=%async_computation.1 | async-start | bytes 1048576 | tf_op jit(solution)/shard_map/all_to_all | solution.py:1160
  129.2 3.7 collective-permute-start.1
  175.0 19.7 %all-to-all-start.2 = ((bf16[8,128,256]{1,2,0:T(8,128)(2,1)}), bf16[8,128,256]{1,2,0:T(8,128)(2,1)S(1)}, u32[]{:S(2)}, u32[]{:S(2)}) async-start(bf16[8,128,256]{1,2,0:T(8,128)(2,1)} %copy.172), calls=%async_computation.2 | async-start | bytes 1048576 | tf_op jit(solution)/shard_map/all_to_all | solution.py:1160
  182.9 61.1 %copy-start.38 = (bf16[128,128]{1,0:T(8,128)(2,1)}, bf16[128,128]{1,0:T(8,128)(2,1)S(1)}, u32[]{:S(2)}) copy-start(bf16[128,128]{1,0:T(8,128)(2,1)S(1)} %convolution_convert_fusion.5) | copy-start | bytes 98308
  199.5 44.5 %copy-start.14 = (f32[128,2048]{1,0:T(8,128)}, f32[128,2048]{1,0:T(8,128)S(1)}, u32[]{:S(2)}) copy-start(f32[128,2048]{1,0:T(8,128)S(1)} %get-tuple-element.281) | copy-start | bytes 3145732
  200.1 4.7 collective-permute-start.2
  246.4 61.6 %all-to-all-start.3 = ((bf16[8,16,2048]{2,1,0:T(8,128)(2,1)}), bf16[8,16,2048]{2,1,0:T(8,128)(2,1)S(1)}, u32[]{:S(2)}, u32[]{:S(2)}) async-start(bf16[8,16,2048]{2,1,0:T(8,128)(2,1)} %bitcast.178), calls=%async_computation.3 | async-start | bytes 1048576 | tf_op jit(solution)/shard_map/all_to_all | solution.py:1160
  313.2 8.2 %collective-permute-start.3 = (f32[1,2048]{1,0:T(1,128)}, f32[1,2048]{1,0:T(1,128)}, u32[]{:S(2)}, u32[]{:S(2)}) collective-permute-start(f32[1,2048]{1,0:T(1,128)} %slice.229), channel_id=1, source_target_pairs={{4,0},{8,4},{12,8},{16,12},{20,16},{24,20},{28,24},{5,1},{9,5},{13... | collective-permute-start | bytes 24584 | tf_op jit(solution)/shard_map/ppermute | solution.py:1156
  332.2 20.3 %all-to-all-start.4 = ((bf16[8,128,256]{2,1,0:T(8,128)(2,1)}), bf16[8,128,256]{2,1,0:T(8,128)(2,1)S(1)}, u32[]{:S(2)}, u32[]{:S(2)}) async-start(bf16[8,128,256]{2,1,0:T(8,128)(2,1)} %bitcast.177), calls=%async_computation.4 | async-start | bytes 1048576 | tf_op jit(solution)/shard_map/all_to_all | solution.py:1160
  338.6 151.9 %reduce-scatter.4.cloned.1.call-start = ((), (), s32[]{:S(2)}) async-start(), calls=%async_computation.11 | async-start | bytes 5242880 | tf_op jit(solution)/shard_map/reduce_scatter | solution.py:1387
  352.4 71.1 %collective-permute-start.4 = (bf16[512,2048]{1,0:T(8,128)(2,1)}, bf16[512,2048]{1,0:T(8,128)(2,1)}, u32[]{:S(2)}, u32[]{:S(2)}) collective-permute-start(bf16[512,2048]{1,0:T(8,128)(2,1)} %get-tuple-element.126), channel_id=1, source_target_pairs={{0,4},{4,0},{8,12},{12,8},{16,20},{20,16},{24,28},{28,24},{1,5},{5... | collective-permute-start | bytes 6291464 | tf_op jit(solution)/shard_map/ppermute | solution.py:1179
  353.9 69.6 %collective-permute-start.5 = (bf16[512,1024]{1,0:T(8,128)(2,1)}, bf16[512,1024]{1,0:T(8,128)(2,1)}, u32[]{:S(2)}, u32[]{:S(2)}) collective-permute-start(bf16[512,1024]{1,0:T(8,128)(2,1)} %get-tuple-element.127), channel_id=1, source_target_pairs={{0,4},{4,0},{8,12},{12,8},{16,20},{20,16},{24,28},{28,24},{1,5},{5... | collective-permute-start | bytes 3145736 | tf_op jit(solution)/shard_map/ppermute | solution.py:1179
  359.1 64.4 %collective-permute-start.6 = (bf16[128,2048]{1,0:T(8,128)(2,1)}, bf16[128,2048]{1,0:T(8,128)(2,1)}, u32[]{:S(2)}, u32[]{:S(2)}) collective-permute-start(bf16[128,2048]{1,0:T(8,128)(2,1)} %copy-done.22), channel_id=1, source_target_pairs={{0,1},{1,0},{2,3},{3,2},{4,5},{5,4},{6,7},{7,6},{8,9},{9,8},{10,11... | collective-permute-start | bytes 1572872 | tf_op jit(solution)/shard_map/ppermute | solution.py:1165
  359.1 64.4 %collective-permute-start.7 = (bf16[128,2048]{1,0:T(8,128)(2,1)}, bf16[128,2048]{1,0:T(8,128)(2,1)}, u32[]{:S(2)}, u32[]{:S(2)}) collective-permute-start(bf16[128,2048]{1,0:T(8,128)(2,1)} %copy-done.22), channel_id=1, source_target_pairs={{0,2},{1,3},{2,0},{3,1},{4,6},{5,7},{6,4},{7,5},{8,10},{9,11},{10,... | collective-permute-start | bytes 1572872 | tf_op jit(solution)/shard_map/ppermute | solution.py:1165
  359.9 63.6 %all-to-all-start.6 = ((bf16[4,128,8,64]{1,3,2,0:T(8,128)(2,1)}), bf16[4,128,8,64]{1,3,2,0:T(8,128)(2,1)}, u32[]{:S(2)}, u32[]{:S(2)}) async-start(bf16[4,128,8,64]{1,3,2,0:T(8,128)(2,1)} %copy.178), calls=%async_computation.7 | async-start | bytes 1048576 | tf_op jit(solution)/shard_map/all_to_all | solution.py:1160
  366.0 252.3 %reduce-scatter.8.cloned.1.call-start = ((), (), s32[]{:S(2)}) async-start(), calls=%async_computation.13 | async-start | bytes 5242880 | tf_op jit(solution)/shard_map/reduce_scatter | solution.py:1387
  425.1 11.1 %collective-permute-start.8 = (bf16[128,2048]{1,0:T(8,128)(2,1)}, bf16[128,2048]{1,0:T(8,128)(2,1)S(1)}, u32[]{:S(2)}, u32[]{:S(2)}) collective-permute-start(bf16[128,2048]{1,0:T(8,128)(2,1)} %collective-permute-done.7), channel_id=1, source_target_pairs={{0,1},{1,0},{2,3},{3,2},{4,5},{5,4},{6,7},{7,6},{8,9},{9,8},{10,11... | collective-permute-start | bytes 1572872 | tf_op jit(solution)/shard_map/ppermute | solution.py:1165
  441.5 48.9 %collective-permute-start.9 = (bf16[4,64,2048]{2,1,0:T(8,128)(2,1)}, bf16[4,64,2048]{2,1,0:T(8,128)(2,1)}, u32[]{:S(2)}, u32[]{:S(2)}) collective-permute-start(bf16[4,64,2048]{2,1,0:T(8,128)(2,1)} %dynamic-slice_bitcast_fusion), channel_id=1, source_target_pairs={{0,4},{4,0},{8,12},{12,8},{16,20},{20,16},{24,28},{28,24},{1,5},{5... | collective-permute-start | bytes 3145736 | tf_op jit(solution)/shard_map/ppermute | solution.py:1179
  445.0 45.4 %all-to-all-start.5 = ((bf16[8,128,256]{2,1,0:T(8,128)(2,1)}), bf16[8,128,256]{2,1,0:T(8,128)(2,1)S(1)}, u32[]{:S(2)}, u32[]{:S(2)}) async-start(bf16[8,128,256]{2,1,0:T(8,128)(2,1)} %bitcast.43), calls=%async_computation.5 | async-start | bytes 1048576 | tf_op jit(solution)/shard_map/all_to_all | solution.py:1160
  448.5 169.9 %reduce-scatter.6.cloned.1.call-start = ((), (), s32[]{:S(2)}) async-start(), calls=%async_computation.12 | async-start | bytes 1310720 | tf_op jit(solution)/shard_map/reduce_scatter | solution.py:1387
  492.8 20.9 %collective-permute-start.10 = (bf16[2,8,64,1408]{3,2,1,0:T(8,128)(2,1)S(1)}, bf16[2,8,64,1408]{3,2,1,0:T(8,128)(2,1)}, u32[]{:S(2)}, u32[]{:S(2)}) collective-permute-start(bf16[2,8,64,1408]{3,2,1,0:T(8,128)(2,1)S(1)} %pad_maximum_fusion), channel_id=1, source_target_pairs={{0,1},{1,0},{2,3},{3,2},{4,5},{5,4},{6,7},{7,6},{8,9},{9,8},{10,11... | collective-permute-start | bytes 8650760 | tf_op jit(solution)/shard_map/ppermute | solution.py:1165
  498.3 14.4 %collective-permute-start.12 = (bf16[2,64,640]{2,1,0:T(8,128)(2,1)}, bf16[2,64,640]{2,1,0:T(8,128)(2,1)}, u32[]{:S(2)}, u32[]{:S(2)}) collective-permute-start(bf16[2,64,640]{2,1,0:T(8,128)(2,1)} %pad_maximum_fusion.3), channel_id=1, source_target_pairs={{0,1},{1,0},{2,3},{3,2},{4,5},{5,4},{6,7},{7,6},{8,9},{9,8},{10,11... | collective-permute-start | bytes 491528 | tf_op jit(solution)/shard_map/ppermute | solution.py:1165
  516.2 38.4 %copy-start.3 = (bf16[1024,2048]{1,0:T(8,128)(2,1)S(1)}, bf16[1024,2048]{1,0:T(8,128)(2,1)}, u32[]{:S(2)}) copy-start(bf16[1024,2048]{1,0:T(8,128)(2,1)} %fusion.12) | copy-start | bytes 12582916
  518.0 98.5 %collective-permute-start.11 = (bf16[8,64,1408]{2,1,0:T(8,128)(2,1)S(1)}, bf16[8,64,1408]{2,1,0:T(8,128)(2,1)S(1)}, u32[]{:S(2)}, u32[]{:S(2)}) collective-permute-start(bf16[8,64,1408]{2,1,0:T(8,128)(2,1)S(1)} %fusion.31), channel_id=1, source_target_pairs={{0,2},{1,3},{2,0},{3,1},{4,6},{5,7},{6,4},{7,5},{8,10},{9,11},{10,... | collective-permute-start | bytes 4325384 | tf_op jit(solution)/shard_map/ppermute | solution.py:1165
  518.4 35.3 %collective-permute-start.13 = (bf16[64,640]{1,0:T(8,128)(2,1)S(1)}, bf16[64,640]{1,0:T(8,128)(2,1)S(1)}, u32[]{:S(2)}, u32[]{:S(2)}) collective-permute-start(bf16[64,640]{1,0:T(8,128)(2,1)S(1)} %fusion.62), channel_id=1, source_target_pairs={{0,2},{1,3},{2,0},{3,1},{4,6},{5,7},{6,4},{7,5},{8,10},{9,11},{10,... | collective-permute-start | bytes 245768 | tf_op jit(solution)/shard_map/ppermute | solution.py:1165
  (58 other events, 332.0 us)
Sparse Core Ops, SparseCore 0:
  72.9 56.2 all-gather.1
  352.6 76.4 reduce-scatter.3
  440.0 84.9 reduce-scatter.7
  527.7 28.9 reduce-scatter.5

commit v9 on v8

--- a/solution.py
+++ b/solution.py
@@ -986,6 +986,60 @@
     )(wide, key)
 
 
+def deal_kernel(to_heads, x_ref, out_ref, send_sem, recv_sem):
+    s, w, _, _, _, _, _ = places()
+    tall, thin = (out_ref, x_ref) if to_heads else (x_ref, out_ref)
+    columns, rows = tall.shape[1], thin.shape[0]
+
+    def column(number):
+        return pl.ds(pl.multiple_of(number * columns, columns), columns)
+
+    def row(number):
+        return pl.ds(pl.multiple_of(number * rows, rows), rows)
+
+    greet(tuple((None, ((s + d) % 8, w)) for d in range(1, 8)), 7)
+
+    def copy(d):
+        target = (s + d) % 8
+        if to_heads:
+            source, goal = x_ref.at[:, column(target)], out_ref.at[row(s)]
+        else:
+            source, goal = x_ref.at[row(target)], out_ref.at[:, column(s)]
+        return send(source, goal, send_sem.at[d - 1], recv_sem.at[d - 1], (target, w))
+
+    for d in (4, 3, 5, 2, 6, 1, 7):
+        copy(d).start()
+    if to_heads:
+        out_ref[row(s), :] = x_ref[:, column(s)]
+    else:
+        out_ref[:, column(s)] = x_ref[row(s), :]
+    for d in range(1, 8):
+        copy(d).wait_recv()
+        copy(d).wait_send()
+
+
+def deal(x, to_heads):
+    seqs = lax.axis_size("seq")
+    if seqs != 8 or lax.axis_size("wsh") != 4:
+        if to_heads:
+            split = x.reshape(x.shape[0], seqs, -1).transpose(1, 0, 2)
+            return exchange(split, "seq").reshape(x.shape[0] * seqs, -1)
+        moved = exchange(x.reshape(seqs, x.shape[0] // seqs, -1), "seq")
+        return moved.transpose(1, 0, 2).reshape(x.shape[0] // seqs, -1)
+    shape = (x.shape[0] * seqs, x.shape[1] // seqs) if to_heads else (x.shape[0] // seqs, x.shape[1] * seqs)
+    vmem, dma = pl.BlockSpec(memory_space=pltpu.VMEM), pltpu.SemaphoreType.DMA
+    return pl.pallas_call(
+        functools.partial(deal_kernel, to_heads),
+        in_specs=[vmem],
+        out_specs=vmem,
+        out_shape=jax.ShapeDtypeStruct(shape, x.dtype),
+        scratch_shapes=[dma((7,)), dma((7,))],
+        compiler_params=pltpu.CompilerParams(collective_id=6 if to_heads else 7, has_side_effects=True),
+        cost_estimate=pl.CostEstimate(flops=0, bytes_accessed=60 << 20, transcendentals=0),
+        name="deal_heads" if to_heads else "deal_rows",
+    )(x)
+
+
 def channel_kernel(
     forward, x_ref, first_hbm, second_hbm, active_hbm,
     sum_ref, all_hbm, mine_hbm, other_hbm, extra_hbm,
@@ -1306,7 +1360,7 @@
     teacher_rows, mixed_out, total_valid = lax.optimization_barrier((teacher_rows, mixed_out, total_valid))
     target = dot(settle, teacher_rows.reshape(rows, width))
 
-    mixed_rows = exchange(mixed_out.reshape(seqs, rows, own_width), "seq").transpose(1, 0, 2).reshape(rows, width)
+    mixed_rows = deal(mixed_out, False)
     own = lax.dynamic_slice_in_dim(balanced, me * rows, rows, 0).astype(F32)
     own_starts = lax.dynamic_slice_in_dim(starts, me * rows, rows, 0)
     own_flowing = (1.0 - own_starts)[:, None]
@@ -1342,7 +1396,13 @@
         cot = gather_near(cot_low)
         grad_pre = (dot(cot, channel_value_weight, NT) * 2.0 * active).astype(BF16)
         grad_channel = near_sum(dot(grad_pre, channel_key_weight))
-    result_back, grad_channel = lax.optimization_barrier((result_back, grad_channel))
+    if paired:
+        value_part = (
+            dot(quartered(hidden_mine), cot, TN) + dot(quartered(hidden_other), cot_other, TN)
+        ).astype(BF16)
+    else:
+        value_part = dot(hidden_rows, cot, TN).astype(BF16)
+    result_back, grad_channel, value_part = lax.optimization_barrier((result_back, grad_channel, value_part))
     output = dot(arrange, result_back.reshape(rows, width), TN).astype(BF16)
     grad_vec_mix_two = jnp.sum(grad_channel * delta_two, 0)
     shifted = grad_channel * vectors[:, 18] * own_flowing
@@ -1352,21 +1412,14 @@
     grad_low = grad_residual.astype(BF16)
 
     grad_posted = dot(grad_low, w_out, NT).astype(BF16)
-    if paired:
-        hidden_mine, grad_posted = lax.optimization_barrier((hidden_mine, grad_posted))
-        value_part = (
-            dot(quartered(hidden_mine), cot, TN) + dot(quartered(hidden_other), cot_other, TN)
-        ).astype(BF16)
-    else:
-        value_part = dot(hidden_rows, cot, TN).astype(BF16)
-    grad_heads = exchange(grad_posted.reshape(rows, seqs, own_width).transpose(1, 0, 2), "seq").reshape(group, own_width)
-    grad_heads, value_part, mixed_late = lax.optimization_barrier((grad_heads, value_part, mixed_rows))
+    grad_heads = deal(grad_posted, True)
+    grad_heads, mixed_late = lax.optimization_barrier((grad_heads, mixed_rows))
     lefts = exchange(mixed_late.reshape(rows, seqs, parts, piece).transpose(2, 0, 1, 3), "wsh")
     near_grad = (swap(grad_low, 1), swap(grad_low, 2)) if near else gather_near(grad_low)
     recept_low, keys_low, values_low, ups_low, grad_first, grad_vec_heads = run_backward(grad_heads, *inputs, saved)
     if paired:
-        channel_other, pre_other, lefts, near_grad, recept_low = lax.optimization_barrier(
-            (channel_other, pre_other, lefts, near_grad, recept_low)
+        channel_other, pre_mine, pre_other, lefts, near_grad, recept_low = lax.optimization_barrier(
+            (channel_other, pre_mine, pre_other, lefts, near_grad, recept_low)
         )
         key_part = (
             dot(quartered(pre_mine), channel, TN) + dot(quartered(pre_other), channel_other, TN)
@@ -1427,13 +1480,16 @@
     grad_given = dot(permute, grad_balanced.astype(BF16), TN).astype(BF16).reshape(seqs, rows, width)
     if near:
         kept_part, far = block_halves(wide)
-        grad_given, far = lax.optimization_barrier((grad_given, far))
-        wide_part = kept_part + swap(far, 2).astype(F32)
+        kept_up, far_up = block_halves(up_grad.reshape(parts, piece, WIDE))
+        grad_given, far, far_up = lax.optimization_barrier((grad_given, far, far_up))
+        wide_part, across_up = kept_part + swap(far, 2).astype(F32), swap(far_up, 2)
     else:
         wide_part = block_sum(wide)
     if paired:
         grad_tokens, value_all = reduce_seq(grad_given, value_sum.reshape(4, -1, width))
-        wide_part, grad_tokens, grad_out, key_sum = lax.optimization_barrier((wide_part, grad_tokens, grad_out, key_sum))
+        wide_part, grad_tokens, grad_out, key_sum, across_up = lax.optimization_barrier(
+            (wide_part, grad_tokens, grad_out, key_sum, across_up)
+        )
         wide_all, key_all = finish(wide_part.astype(BF16), key_sum.reshape(4, -1, width))
         wide_all = wide_all.astype(F32)
         grad_ffn_key, grad_ffn_value = [x.reshape(-1, width).astype(F32) for x in (key_all, value_all)]
@@ -1448,7 +1504,7 @@
     narrow = jnp.sum(wide_all[:, :, 3 * own_width :], 0)
     grad_down = unpad_ranks(narrow)
     grad_vectors = narrow[:, RANKS[0] : RANKS[0] + vectors.shape[1]]
-    up_part = unpad_ranks(block_sum(up_grad.reshape(parts, piece, WIDE)))
+    up_part = unpad_ranks(kept_up + across_up.astype(F32) if near else block_sum(up_grad.reshape(parts, piece, WIDE)))
 
     return (
         output, grad_tokens.astype(BF16), grad_first_rows,

time: 736 us -> 777 us (1.056)
  Pallas kernels: 439 us -> 538 us
  waiting for transfers between devices: 46.4 us -> 3.54 us
  starting transfers between devices: 50.3 us -> 37.4 us
    pallas_call x0 -> x2, Pallas kernels: none -> 82.3 us  [deal(): pl.pallas_call(functools.partial(deal_kernel, to_heads), in_specs=[vmem],...]
    ppermute x9, waiting for transfers between devices: 33.8 us -> 2.21 us  [swap(): return lax.ppermute(x, 'wsh', [(i, i ^ by) for i in range(size)])]
    pallas_call x1, Pallas kernels: 60.3 us -> 77.1 us  [reduce_seq(): pl.pallas_call(functools.partial(reduce_kernel, splits), in_specs=[vmem]...]
    all_to_all x7 -> x5, starting transfers between devices: 37.5 us -> 24.9 us  [exchange(): return lax.all_to_all(x, axis, split_axis=0, concat_axis=0, tiled=True)]
    all_to_all x7 -> x5, waiting for transfers between devices: 12.4 us -> 0.01 us  [exchange(): return lax.all_to_all(x, axis, split_axis=0, concat_axis=0, tiled=True)]
    unnamed x139 -> x167, local copies, waits for them, and re-layouts: 17.4 us -> 22.4 us
  transfers between devices with their start and end apart: 25 -> 23, of which waited for: 5 -> 2; matrix products, arithmetic and copies ran while one was open for 17% -> 16% of each run, Pallas kernels for 35% -> 46%
where the time goes in v9:
time: 777 us; the launch traced here: 767 us
  Pallas kernels  538 us (69%)
  matrix products  64.4 us (8%)
  local copies, waits for them, and re-layouts  59.9 us (8%)
  other arithmetic  47.2 us (6%)
  starting transfers between devices  37.4 us (5%)
  between operations  16.5 us (2%)
    pallas_call x1, Pallas kernels, finish(): pl.pallas_call(finish_kernel, in_specs=[vmem] * 2, out_specs=[vmem] * 2,...  92.2 us
    pallas_call x2, Pallas kernels, channel_stage(): pl.pallas_call(body, in_specs=[pl.BlockSpec(memory_space=pltpu.VMEM)] + [...  89.1 us
    pallas_call x2, Pallas kernels, deal(): pl.pallas_call(functools.partial(deal_kernel, to_heads), in_specs=[vmem],...  82.3 us
    pallas_call x1, Pallas kernels, reduce_seq(): pl.pallas_call(functools.partial(reduce_kernel, splits), in_specs=[vmem]...  77.1 us
    dot_general x17, matrix products, dot(): return lax.dot_general(a, b, dims, preferred_element_type=F32)  64.4 us
    pallas_call x1, Pallas kernels, gather_first(): pl.pallas_call(gather_kernel, in_specs=[pl.BlockSpec(memory_space=pltpu.V...  54.4 us
    pallas_call x1, Pallas kernels, run_backward(): pl.pallas_call(functools.partial(backward_kernel, count), grid=(rows // s...  47.1 us
    pallas_call x1, Pallas kernels, run_unproject(): pl.pallas_call(functools.partial(unproject_kernel, own_width, parts, piec...  40.3 us
  transfers between devices with their start and end apart: 23, of which 2 were waited for; matrix products, arithmetic and copies ran while one was open for 16% of the time, Pallas kernels for 46%

profile of v9, /device:TPU:4, one launch (start us, length us, event | category | flops | bytes accessed | tf_op | source)
XLA Modules:
  0.0 767.1 jit_solution(4386837677566648256)
XLA Ops:
  18.3 54.4 %gather_first.1 = (bf16[8,128,2048]{2,1,0:T(8,128)(2,1)}, bf16[8,128,128]{2,1,0:T(8,128)(2,1)}, bf16[4,512,1664]{2,1,0:T(8,128)(2,1)}) custom-call(bf16[128,2048]{1,0:T(8,128)(2,1)} %own_ref.1, bf16[128,128]{1,0:T(8,128)(2,1)} %pad.30.tail_ref, bf16[512,1664]{1,0:T(8,128)(2,1)} %copy-done.28), custom_call_target="tpu_custom_call" | custom-call | bytes 104857600 | tf_op jit(solution)/shard_map/gather_first/pallas_call | solution.py:781
  74.3 8.3 %convert_reduce_fusion = (f32[1024]{0:T(1024)S(1)}, bf16[1024,2048]{1,0:T(8,128)(2,1)}) fusion(bf16[1024,2048]{1,0:T(8,128)(2,1)} %bitcast.203, s32[1024]{0:T(1024)S(1)} %bitcast.196), kind=kOutput, calls=%fused_computation.1 | convolution fusion | flops 4302306304 | bytes 8396800 | tf_op jit(solution)/shard_map/dot_general | solution.py:28
  82.5 4.5 fusion.2
  88.2 3.5 all-to-all-start
  98.5 19.4 %mix_project.1 = (f32[1024,256]{1,0:T(8,128)}, f32[1024,256]{1,0:T(8,128)}, f32[1024,256]{1,0:T(8,128)}, f32[1024,640]{1,0:T(8,128)}, bf16[1024,640]{1,0:T(8,128)(2,1)}) custom-call(bf16[1024,2048]{1,0:T(8,128)(2,1)} %get-tuple-element.281.block_ref, f32[1024,4]{1,0:T(8,128)} %copy.159.stats_ref, f32[8,2048]{1,0:T(8,128)} %slice_bitcast_fusion.3.vec_ref, ...), custom_call_target="tpu_custom_call" | custom-call | flops 134217728 | bytes 62914560 | tf_op jit(solution)/shard_map/mix_project/pallas_call | solution.py:569
  121.1 6.2 all-to-all-start.1
  133.8 36.1 %mix_forward.1 = (bf16[1024,256]{1,0:T(8,128)(2,1)S(1)}, bf16[1024,256]{1,0:T(8,128)(2,1)S(1)}, f32[1024,256]{1,0:T(8,128)S(1)}, f32[1024,256]{1,0:T(8,128)S(1)}, f32[1024,256]{1,0:T(8,128)S(1)}) custom-call(f32[1024,256]{1,0:T(8,128)S(1)} %copy-done.4, f32[1024,256]{1,0:T(8,128)} %get-tuple-element.100.keys_ref, f32[1024,256]{1,0:T(8,128)} %get-tuple-element.101.values_ref, ...), custom_call_target="tpu_custom_call" | custom-call | flops 134217728 | bytes 115343360 | tf_op jit(solution)/shard_map/mix_forward/pallas_call | solution.py:385
  173.5 16.3 %deal_rows.1 = bf16[128,2048]{1,0:T(8,128)(2,1)} custom-call(bf16[1024,256]{1,0:T(8,128)(2,1)} %copy-done.15), custom_call_target="tpu_custom_call" | custom-call | bytes 62914560 | tf_op jit(solution)/shard_map/deal_rows/pallas_call | solution.py:1031
  190.5 5.0 fusion.84
  196.1 3.5 collective-permute-start.2
  202.5 38.1 %channel_forward.1 = (f32[128,2048]{1,0:T(8,128)}, bf16[512,2048]{1,0:T(8,128)(2,1)}, bf16[512,1024]{1,0:T(8,128)(2,1)}, bf16[512,1024]{1,0:T(8,128)(2,1)}, f32[512,2048]{1,0:T(8,128)}) custom-call(bf16[128,2048]{1,0:T(8,128)(2,1)} %add_convert_fusion.2.refs_0_, bf16[2048,2048]{1,0:T(8,128)(2,1)} %refs_2_.3, bf16[2048,2048]{1,0:T(8,128)(2,1)} %refs_1_.3), custom_call_target="tpu_custom_call" | custom-call | bytes 104857600 | tf_op jit(solution)/shard_map/channel_forward/pallas_call | solution.py:1186
  243.1 7.4 all-to-all-start.2
  255.1 2.7 fusion.85
  257.8 51.0 %channel_backward.1 = (f32[128,2048]{1,0:T(8,128)}, bf16[512,2048]{1,0:T(8,128)(2,1)}, bf16[512,1024]{1,0:T(8,128)(2,1)}, bf16[512,2048]{1,0:T(8,128)(2,1)}, bf16[512,1024]{1,0:T(8,128)(2,1)}) custom-call(bf16[128,2048]{1,0:T(8,128)(2,1)} %get-tuple-element.284.refs_0_, bf16[2048,2048]{1,0:T(8,128)(2,1)} %refs_1_.3, bf16[2048,2048]{1,0:T(8,128)(2,1)} %refs_2_.3, ...), custom_call_target="tpu_custom_call" | custom-call | bytes 104857600 | tf_op jit(solution)/shard_map/channel_backward/pallas_call | solution.py:1186
  308.8 7.2 fusion.86
  319.7 8.3 %add_convert_fusion.1 = bf16[1024,2048]{1,0:T(8,128)(2,1)} fusion(f32[1024,2048]{1,0:T(8,128)} %fusion.86, bf16[512,1024]{0,1:T(8,128)(2,1)S(1)} %bitcast.166, bf16[512,2048]{1,0:T(8,128)(2,1)} %get-tuple-element.115), kind=kOutput, calls=%fused_computation.9 | convolution fusion | flops 2151677952 | bytes 15728640 | tf_op jit(solution)/shard_map/dot_general | solution.py:28
  328.7 3.1 multiply_reduce_fusion
  333.3 2.7 collective-permute-start.4
  340.2 4.7 convolution_convert_fusion.1.x_ref
  345.0 66.0 %deal_heads.1.grad_ref = bf16[1024,256]{1,0:T(8,128)(2,1)} custom-call(bf16[128,2048]{1,0:T(8,128)(2,1)} %convolution_convert_fusion.1.x_ref), custom_call_target="tpu_custom_call" | custom-call | bytes 62914560 | tf_op jit(solution)/shard_map/deal_heads/pallas_call | solution.py:1031
  414.9 4.1 all-to-all-start.4
  420.2 47.1 %mix_backward.1 = (bf16[1024,256]{1,0:T(8,128)(2,1)S(1)}, bf16[1024,256]{1,0:T(8,128)(2,1)S(1)}, bf16[1024,256]{1,0:T(8,128)(2,1)S(1)}, bf16[4,1024,256]{2,1,0:T...) custom-call(bf16[1024,256]{1,0:T(8,128)(2,1)S(1)} %copy-done.6, f32[1024,256]{1,0:T(8,128)S(1)} %copy-done.4, ...), custom_call_target="tpu_custom_call" | custom-call | flops 134217728 | bytes 157286400 | tf_op jit(solution)/shard_map/mix_backward/pallas_call | solution.py:413
  478.2 5.9 add_convert_fusion
  484.9 2.8 convolution_convert_fusion
  493.2 3.6 all-to-all-start.3
  498.2 40.3 %mix_unproject.1 = (f32[1024,2048]{1,0:T(8,128)}, f32[1024,2]{1,0:T(8,128)}, bf16[4,8,64,1408]{3,2,1,0:T(8,128)(2,1)}, bf16[256,640]{1,0:T(8,128)(2,1)}) custom-call(bf16[1024,2048]{1,0:T(8,128)(2,1)} %get-tuple-element.281.block_ref, f32[1024,4]{1,0:T(8,128)} %copy.159.stats_ref, f32[8,2048]{1,0:T(8,128)} %slice_bitcast_fusion.3.vec_ref, ...), custom_call_target="tpu_custom_call" | custom-call | flops 134217728 | bytes 125829120 | tf_op jit(solution)/shard_map/mix_unproject/pallas_call | solution.py:592
  542.2 2.6 fusion.26
  547.8 6.0 fusion.5
  554.0 6.5 fusion.12
  564.1 3.8 fusion.31
  575.2 77.1 %reduce_seq.1 = (f32[128,2048]{1,0:T(8,128)S(1)}, bf16[4,64,2048]{2,1,0:T(8,128)(2,1)S(1)}) custom-call(bf16[8,128,2048]{2,1,0:T(8,128)(2,1)S(1)} %bitcast.140, bf16[4,64,2048]{2,1,0:T(8,128)(2,1)S(1)} %bitcast.141), custom_call_target="tpu_custom_call" | custom-call | bytes 1048576 | tf_op jit(solution)/shard_map/reduce_seq/pallas_call | solution.py:941
  657.5 92.2 %finish.1 = (bf16[8,64,1408]{2,1,0:T(8,128)(2,1)S(1)}, bf16[4,64,2048]{2,1,0:T(8,128)(2,1)S(1)}) custom-call(bf16[8,64,1408]{2,1,0:T(8,128)(2,1)S(1)} %fusion.17.wide_ref, bf16[4,64,2048]{2,1,0:T(8,128)(2,1)S(1)} %bitcast.142), custom_call_target="tpu_custom_call" | custom-call | bytes 104857600 | tf_op jit(solution)/shard_map/finish/pallas_call | solution.py:977
  (352 shorter events, 110.0 us)
Async XLA Ops:
  7.2 112.8 %copy-start = (bf16[128,2048]{1,0:T(8,128)(2,1)S(1)}, bf16[128,2048]{1,0:T(8,128)(2,1)}, u32[]{:S(2)}) copy-start(bf16[128,2048]{1,0:T(8,128)(2,1)} %param.17) | copy-start | bytes 1572868
  7.2 183.2 %all-gather.2.cloned.1.call-start = ((), (), s32[]{:S(2)}) async-start(), calls=%async_computation.8 | async-start | bytes 10485760 | tf_op jit(solution)/shard_map/all_gather | solution.py:1343
  15.6 58.3 %copy-start.72 = (s32[1,4]{1,0:T(1,128)S(1)}, s32[1,4]{1,0:T(1,128)}, u32[]{:S(2)}) copy-start(s32[1,4]{1,0:T(1,128)} %param.20) | copy-start | bytes 52
  74.2 58.7 %copy-start.60 = (s32[1024,1]{0,1:T(1,128)}, s32[1024,1]{0,1:T(1,128)S(1)}, u32[]{:S(2)}) copy-start(s32[1024,1]{0,1:T(1,128)S(1)} %get-tuple-element.254) | copy-start | bytes 12292
  88.2 31.6 %all-to-all-start = ((bf16[8,128,256]{1,2,0:T(8,128)(2,1)}), bf16[8,128,256]{1,2,0:T(8,128)(2,1)S(1)}, u32[]{:S(2)}, u32[]{:S(2)}) async-start(bf16[8,128,256]{1,2,0:T(8,128)(2,1)} %bitcast.15), calls=%async_computation | async-start | bytes 1048576 | tf_op jit(solution)/shard_map/all_to_all | solution.py:1214
  92.9 34.5 %collective-permute-start = (f32[8,128]{1,0:T(8,128)S(1)}, f32[8,128]{1,0:T(8,128)S(1)}, u32[]{:S(2)}, u32[]{:S(2)}) collective-permute-start(f32[8,128]{1,0:T(8,128)S(1)} %broadcast_in_dim.4), channel_id=1, source_target_pairs={{0,1},{1,0},{2,3},{3,2},{4,5},{5,4},{6,7},{7,6},{8,9},{9,8},{10,11... | collective-permute-start | bytes 12296 | tf_op jit(solution)/shard_map/ppermute | solution.py:1219
  96.6 322.5 %copy-start.2 = (bf16[640,256]{1,0:T(8,128)(2,1)}, bf16[640,256]{1,0:T(8,128)(2,1)S(1)}, u32[]{:S(2)}) copy-start(bf16[640,256]{1,0:T(8,128)(2,1)S(1)} %fusion.50.up_ref) | copy-start | bytes 983044
  121.1 52.4 %all-to-all-start.1 = ((bf16[8,16,2048]{2,1,0:T(8,128)(2,1)}), bf16[8,16,2048]{2,1,0:T(8,128)(2,1)S(1)}, u32[]{:S(2)}, u32[]{:S(2)}) async-start(bf16[8,16,2048]{2,1,0:T(8,128)(2,1)} %bitcast.17), calls=%async_computation.1 | async-start | bytes 1048576 | tf_op jit(solution)/shard_map/all_to_all | solution.py:1214
  128.0 3.7 collective-permute-start.1
  195.5 45.2 %copy-start.20 = (f32[128,2048]{1,0:T(8,128)}, f32[128,2048]{1,0:T(8,128)S(1)}, u32[]{:S(2)}) copy-start(f32[128,2048]{1,0:T(8,128)S(1)} %get-tuple-element.283) | copy-start | bytes 3145732
  195.8 44.9 %copy-start.63 = (f32[128]{0:T(128)}, f32[128]{0:T(128)S(1)}, u32[]{:S(2)}) copy-start(f32[128]{0:T(128)S(1)} %add_rsqrt_fusion.1) | copy-start | bytes 1540
  196.1 4.4 collective-permute-start.2
  243.1 84.9 %all-to-all-start.2 = ((bf16[8,16,2048]{2,1,0:T(8,128)(2,1)}), bf16[8,16,2048]{2,1,0:T(8,128)(2,1)}, u32[]{:S(2)}, u32[]{:S(2)}) async-start(bf16[8,16,2048]{2,1,0:T(8,128)(2,1)} %bitcast.162), calls=%async_computation.2 | async-start | bytes 1048576 | tf_op jit(solution)/shard_map/all_to_all | solution.py:1214
  250.5 288.1 %reduce-scatter.4.cloned.1.call-start = ((), (), s32[]{:S(2)}) async-start(), calls=%async_computation.9 | async-start | bytes 5242880 | tf_op jit(solution)/shard_map/reduce_scatter | solution.py:1440
  257.8 51.0 %copy-start.35 = (bf16[512,4,4,64]{0,3,2,1:T(8,128)(2,1)S(1)}, bf16[512,4,4,64]{0,3,2,1:T(8,128)(2,1)}, u32[]{:S(2)}) copy-start(bf16[512,4,4,64]{0,3,2,1:T(8,128)(2,1)} %copy.168) | copy-start | bytes 3145732
  331.9 5.6 collective-permute-start.3
  333.3 137.2 %collective-permute-start.4 = (bf16[512,2048]{1,0:T(8,128)(2,1)}, bf16[512,2048]{1,0:T(8,128)(2,1)}, u32[]{:S(2)}, u32[]{:S(2)}) collective-permute-start(bf16[512,2048]{1,0:T(8,128)(2,1)} %get-tuple-element.125), channel_id=1, source_target_pairs={{0,4},{4,0},{8,12},{12,8},{16,20},{20,16},{24,28},{28,24},{1,5},{5... | collective-permute-start | bytes 6291464 | tf_op jit(solution)/shard_map/ppermute | solution.py:1233
  336.1 134.5 %collective-permute-start.5 = (bf16[512,1024]{1,0:T(8,128)(2,1)}, bf16[512,1024]{1,0:T(8,128)(2,1)}, u32[]{:S(2)}, u32[]{:S(2)}) collective-permute-start(bf16[512,1024]{1,0:T(8,128)(2,1)} %get-tuple-element.127), channel_id=1, source_target_pairs={{0,4},{4,0},{8,12},{12,8},{16,20},{20,16},{24,28},{28,24},{1,5},{5... | collective-permute-start | bytes 3145736 | tf_op jit(solution)/shard_map/ppermute | solution.py:1233
  340.2 130.4 %collective-permute-start.6 = (bf16[128,2048]{1,0:T(8,128)(2,1)}, bf16[128,2048]{1,0:T(8,128)(2,1)}, u32[]{:S(2)}, u32[]{:S(2)}) collective-permute-start(bf16[128,2048]{1,0:T(8,128)(2,1)} %get-tuple-element.250), channel_id=1, source_target_pairs={{0,1},{1,0},{2,3},{3,2},{4,5},{5,4},{6,7},{7,6},{8,9},{9,8},{10,11... | collective-permute-start | bytes 1572872 | tf_op jit(solution)/shard_map/ppermute | solution.py:1219
  340.2 130.4 %collective-permute-start.7 = (bf16[128,2048]{1,0:T(8,128)(2,1)}, bf16[128,2048]{1,0:T(8,128)(2,1)}, u32[]{:S(2)}, u32[]{:S(2)}) collective-permute-start(bf16[128,2048]{1,0:T(8,128)(2,1)} %get-tuple-element.250), channel_id=1, source_target_pairs={{0,2},{1,3},{2,0},{3,1},{4,6},{5,7},{6,4},{7,5},{8,10},{9,11},{10,... | collective-permute-start | bytes 1572872 | tf_op jit(solution)/shard_map/ppermute | solution.py:1219
  345.0 74.2 %copy-start.5 = (f32[1024,256]{1,0:T(8,128)S(1)}, f32[1024,256]{1,0:T(8,128)}, u32[]{:S(2)}) copy-start(f32[1024,256]{1,0:T(8,128)} %get-tuple-element.100.keys_ref) | copy-start | bytes 3145732
  414.9 55.6 %all-to-all-start.4 = ((bf16[4,128,8,64]{1,3,2,0:T(8,128)(2,1)}), bf16[4,128,8,64]{1,3,2,0:T(8,128)(2,1)}, u32[]{:S(2)}, u32[]{:S(2)}) async-start(bf16[4,128,8,64]{1,3,2,0:T(8,128)(2,1)} %copy.172), calls=%async_computation.5 | async-start | bytes 1048576 | tf_op jit(solution)/shard_map/all_to_all | solution.py:1214
  419.1 237.2 %reduce-scatter.8.cloned.1.call-start = ((), (), s32[]{:S(2)}) async-start(), calls=%async_computation.11 | async-start | bytes 5242880 | tf_op jit(solution)/shard_map/reduce_scatter | solution.py:1440
  474.0 10.1 %collective-permute-start.8 = (bf16[128,2048]{1,0:T(8,128)(2,1)}, bf16[128,2048]{1,0:T(8,128)(2,1)S(1)}, u32[]{:S(2)}, u32[]{:S(2)}) collective-permute-start(bf16[128,2048]{1,0:T(8,128)(2,1)} %collective-permute-done.7), channel_id=1, source_target_pairs={{0,1},{1,0},{2,3},{3,2},{4,5},{5,4},{6,7},{7,6},{8,9},{9,8},{10,11... | collective-permute-start | bytes 1572872 | tf_op jit(solution)/shard_map/ppermute | solution.py:1219
  489.4 49.2 %collective-permute-start.9 = (bf16[4,64,2048]{2,1,0:T(8,128)(2,1)}, bf16[4,64,2048]{2,1,0:T(8,128)(2,1)}, u32[]{:S(2)}, u32[]{:S(2)}) collective-permute-start(bf16[4,64,2048]{2,1,0:T(8,128)(2,1)} %dynamic-slice_bitcast_fusion), channel_id=1, source_target_pairs={{0,4},{4,0},{8,12},{12,8},{16,20},{20,16},{24,28},{28,24},{1,5},{5... | collective-permute-start | bytes 3145736 | tf_op jit(solution)/shard_map/ppermute | solution.py:1233
  493.2 45.3 %all-to-all-start.3 = ((bf16[8,128,256]{2,1,0:T(8,128)(2,1)}), bf16[8,128,256]{2,1,0:T(8,128)(2,1)S(1)}, u32[]{:S(2)}, u32[]{:S(2)}) async-start(bf16[8,128,256]{2,1,0:T(8,128)(2,1)} %bitcast.37), calls=%async_computation.3 | async-start | bytes 1048576 | tf_op jit(solution)/shard_map/all_to_all | solution.py:1214
  496.8 159.5 %reduce-scatter.6.cloned.1.call-start = ((), (), s32[]{:S(2)}) async-start(), calls=%async_computation.10 | async-start | bytes 1310720 | tf_op jit(solution)/shard_map/reduce_scatter | solution.py:1440
  540.9 20.6 %collective-permute-start.10 = (bf16[2,8,64,1408]{3,2,1,0:T(8,128)(2,1)S(1)}, bf16[2,8,64,1408]{3,2,1,0:T(8,128)(2,1)}, u32[]{:S(2)}, u32[]{:S(2)}) collective-permute-start(bf16[2,8,64,1408]{3,2,1,0:T(8,128)(2,1)S(1)} %pad_maximum_fusion), channel_id=1, source_target_pairs={{0,1},{1,0},{2,3},{3,2},{4,5},{5,4},{6,7},{7,6},{8,9},{9,8},{10,11... | collective-permute-start | bytes 8650760 | tf_op jit(solution)/shard_map/ppermute | solution.py:1219
  545.8 14.7 %collective-permute-start.11 = (bf16[2,64,640]{2,1,0:T(8,128)(2,1)S(1)}, bf16[2,64,640]{2,1,0:T(8,128)(2,1)S(1)}, u32[]{:S(2)}, u32[]{:S(2)}) collective-permute-start(bf16[2,64,640]{2,1,0:T(8,128)(2,1)S(1)} %pad_maximum_fusion.3), channel_id=1, source_target_pairs={{0,1},{1,0},{2,3},{3,2},{4,5},{5,4},{6,7},{7,6},{8,9},{9,8},{10,11... | collective-permute-start | bytes 491528 | tf_op jit(solution)/shard_map/ppermute | solution.py:1219
  567.9 86.1 %collective-permute-start.12 = (bf16[8,64,1408]{2,1,0:T(8,128)(2,1)}, bf16[8,64,1408]{2,1,0:T(8,128)(2,1)}, u32[]{:S(2)}, u32[]{:S(2)}) collective-permute-start(bf16[8,64,1408]{2,1,0:T(8,128)(2,1)} %fusion.31), channel_id=1, source_target_pairs={{0,2},{1,3},{2,0},{3,1},{4,6},{5,7},{6,4},{7,5},{8,10},{9,11},{10,... | collective-permute-start | bytes 4325384 | tf_op jit(solution)/shard_map/ppermute | solution.py:1219
  571.1 85.2 %collective-permute-start.13 = (bf16[64,640]{1,0:T(8,128)(2,1)S(1)}, bf16[64,640]{1,0:T(8,128)(2,1)S(1)}, u32[]{:S(2)}, u32[]{:S(2)}) collective-permute-start(bf16[64,640]{1,0:T(8,128)(2,1)S(1)} %fusion.62), channel_id=1, source_target_pairs={{0,2},{1,3},{2,0},{3,1},{4,6},{5,7},{6,4},{7,5},{8,10},{9,11},{10,... | collective-permute-start | bytes 245768 | tf_op jit(solution)/shard_map/ppermute | solution.py:1219
  575.2 78.8 %copy-start.23 = (f32[2,8,64,1408]{3,2,1,0:T(8,128)S(1)}, f32[2,8,64,1408]{3,2,1,0:T(8,128)}, u32[]{:S(2)}) copy-start(f32[2,8,64,1408]{3,2,1,0:T(8,128)} %copy-done.22) | copy-start | bytes 17301508
  (72 other events, 443.3 us)
Sparse Core Ops, SparseCore 0:
  72.9 56.2 all-gather.1
  328.2 85.0 reduce-scatter.3
  487.9 85.3 reduce-scatter.7
  575.4 50.4 reduce-scatter.5

commit v10 on v9

--- a/solution.py
+++ b/solution.py
@@ -1054,10 +1054,17 @@
         pltpu.make_async_copy(first_hbm, first, load_sem.at[0]),
         pltpu.make_async_copy(second_hbm, second, load_sem.at[1]),
     ]
+    size = units // 32
+    for number, (source, target) in enumerate(((first_hbm, first), (second_hbm, second))):
+        for at in range(32):
+            h, k, q = at // 16, at // 4 % 4, at % 4
+            to = (h * 4 + q) * 4 + k
+            pltpu.make_async_copy(
+                source.at[pl.ds(at * size, size)], target.at[pl.ds(to * size, size)], load_sem.at[number]
+            ).start()
     if not forward:
         loads.append(pltpu.make_async_copy(active_hbm, active, load_sem.at[2]))
-    for load in loads:
-        load.start()
+        loads[2].start()
     rows_all[0:rows] = x_ref[...]
     greet(((None, x_device), (None, core_device), (None, y_device)), 3)
 
@@ -1233,11 +1240,6 @@
     return lax.ppermute(x, "seq", [(i, i ^ 1) for i in range(lax.axis_size("seq"))])
 
 
-def quartered(x):
-    rows, columns = x.shape
-    return x.reshape(rows, 4, 4, columns // 16).transpose(0, 2, 1, 3).reshape(rows, columns)
-
-
 def scalar_sum(x):
     if lax.axis_size("wsh") != 4:
         return jnp.sum(lax.all_gather(x.reshape(1), "wsh", axis=0, tiled=True))
@@ -1391,15 +1393,12 @@
         grad_channel, cot, pre_mine, cot_other, pre_spare = channel_stage(
             cot_low, channel_value_weight, channel_key_weight, active
         )
-        channel_other, pre_other = beside(channel), beside(pre_spare)
     else:
         cot = gather_near(cot_low)
         grad_pre = (dot(cot, channel_value_weight, NT) * 2.0 * active).astype(BF16)
         grad_channel = near_sum(dot(grad_pre, channel_key_weight))
     if paired:
-        value_part = (
-            dot(quartered(hidden_mine), cot, TN) + dot(quartered(hidden_other), cot_other, TN)
-        ).astype(BF16)
+        value_part = (dot(hidden_mine, cot, TN) + dot(hidden_other, cot_other, TN)).astype(BF16)
     else:
         value_part = dot(hidden_rows, cot, TN).astype(BF16)
     result_back, grad_channel, value_part = lax.optimization_barrier((result_back, grad_channel, value_part))
@@ -1413,7 +1412,13 @@
 
     grad_posted = dot(grad_low, w_out, NT).astype(BF16)
     grad_heads = deal(grad_posted, True)
-    grad_heads, mixed_late = lax.optimization_barrier((grad_heads, mixed_rows))
+    if paired:
+        grad_heads, value_part, mixed_late, channel, pre_spare = lax.optimization_barrier(
+            (grad_heads, value_part, mixed_rows, channel, pre_spare)
+        )
+        channel_other, pre_other = beside(channel), beside(pre_spare)
+    else:
+        grad_heads, mixed_late = lax.optimization_barrier((grad_heads, mixed_rows))
     lefts = exchange(mixed_late.reshape(rows, seqs, parts, piece).transpose(2, 0, 1, 3), "wsh")
     near_grad = (swap(grad_low, 1), swap(grad_low, 2)) if near else gather_near(grad_low)
     recept_low, keys_low, values_low, ups_low, grad_first, grad_vec_heads = run_backward(grad_heads, *inputs, saved)
@@ -1421,9 +1426,7 @@
         channel_other, pre_mine, pre_other, lefts, near_grad, recept_low = lax.optimization_barrier(
             (channel_other, pre_mine, pre_other, lefts, near_grad, recept_low)
         )
-        key_part = (
-            dot(quartered(pre_mine), channel, TN) + dot(quartered(pre_other), channel_other, TN)
-        ).astype(BF16)
+        key_part = (dot(pre_mine, channel, TN) + dot(pre_other, channel_other, TN)).astype(BF16)
     else:
         lefts, near_grad, recept_low = lax.optimization_barrier((lefts, near_grad, recept_low))
         key_part = dot(grad_pre, channel, TN).astype(BF16)
@@ -1481,14 +1484,15 @@
     if near:
         kept_part, far = block_halves(wide)
         kept_up, far_up = block_halves(up_grad.reshape(parts, piece, WIDE))
-        grad_given, far, far_up = lax.optimization_barrier((grad_given, far, far_up))
+        if paired:
+            grad_given, far, far_up, key_sum = lax.optimization_barrier((grad_given, far, far_up, key_sum))
         wide_part, across_up = kept_part + swap(far, 2).astype(F32), swap(far_up, 2)
     else:
         wide_part = block_sum(wide)
     if paired:
         grad_tokens, value_all = reduce_seq(grad_given, value_sum.reshape(4, -1, width))
-        wide_part, grad_tokens, grad_out, key_sum, across_up = lax.optimization_barrier(
-            (wide_part, grad_tokens, grad_out, key_sum, across_up)
+        wide_part, grad_tokens, grad_out, across_up = lax.optimization_barrier(
+            (wide_part, grad_tokens, grad_out, across_up)
         )
         wide_all, key_all = finish(wide_part.astype(BF16), key_sum.reshape(4, -1, width))
         wide_all = wide_all.astype(F32)

time: 777 us -> 722 us (0.929)
  Pallas kernels: 538 us -> 491 us
  local copies, waits for them, and re-layouts: 59.9 us -> 48.7 us
  waiting for transfers between devices: 3.54 us -> 12.6 us
  matrix products: 64.4 us -> 56.6 us
    pallas_call x2, Pallas kernels: 82.3 us -> 31 us  [deal(): pl.pallas_call(functools.partial(deal_kernel, to_heads), in_specs=[vmem],...]
    unnamed x167 -> x173, local copies, waits for them, and re-layouts: 22.4 us -> 23 us
  transfers between devices with their start and end apart: 23 -> 23, of which waited for: 2 -> 4; matrix products, arithmetic and copies ran while one was open for 16% -> 13% of each run, Pallas kernels for 46% -> 41%
where the time goes in v10:
time: 722 us; the launch traced here: 713 us
  Pallas kernels  491 us (68%)
  matrix products  56.6 us (8%)
  local copies, waits for them, and re-layouts  48.7 us (7%)
  other arithmetic  46.7 us (6%)
  starting transfers between devices  41.3 us (6%)
  between operations  16.5 us (2%)
  waiting for transfers between devices  12.6 us (2%)
    pallas_call x1, Pallas kernels, finish(): pl.pallas_call(finish_kernel, in_specs=[vmem] * 2, out_specs=[vmem] * 2,...  94 us
    pallas_call x2, Pallas kernels, channel_stage(): pl.pallas_call(body, in_specs=[pl.BlockSpec(memory_space=pltpu.VMEM)] + [...  90.8 us
    pallas_call x1, Pallas kernels, reduce_seq(): pl.pallas_call(functools.partial(reduce_kernel, splits), in_specs=[vmem]...  77.2 us
    dot_general x17, matrix products, dot(): return lax.dot_general(a, b, dims, preferred_element_type=F32)  56.6 us
    pallas_call x1, Pallas kernels, gather_first(): pl.pallas_call(gather_kernel, in_specs=[pl.BlockSpec(memory_space=pltpu.V...  54.4 us
    pallas_call x1, Pallas kernels, run_backward(): pl.pallas_call(functools.partial(backward_kernel, count), grid=(rows // s...  47.3 us
    pallas_call x1, Pallas kernels, run_unproject(): pl.pallas_call(functools.partial(unproject_kernel, own_width, parts, piec...  40.3 us
    pallas_call x1, Pallas kernels, run_forward(): pl.pallas_call(functools.partial(forward_kernel, count), grid=(rows // st...  36.1 us
  transfers between devices with their start and end apart: 23, of which 4 were waited for; matrix products, arithmetic and copies ran while one was open for 13% of the time, Pallas kernels for 41%

profile of v10, /device:TPU:4, one launch (start us, length us, event | category | flops | bytes accessed | tf_op | source)
XLA Modules:
  0.0 713.1 jit_solution(13243370831679182437)
XLA Ops:
  18.3 54.4 %gather_first.1 = (bf16[8,128,2048]{2,1,0:T(8,128)(2,1)}, bf16[8,128,128]{2,1,0:T(8,128)(2,1)}, bf16[4,512,1664]{2,1,0:T(8,128)(2,1)}) custom-call(bf16[128,2048]{1,0:T(8,128)(2,1)} %own_ref.1, bf16[128,128]{1,0:T(8,128)(2,1)} %pad.30.tail_ref, bf16[512,1664]{1,0:T(8,128)(2,1)} %copy-done.29), custom_call_target="tpu_custom_call" | custom-call | bytes 104857600 | tf_op jit(solution)/shard_map/gather_first/pallas_call | solution.py:781
  74.3 8.3 %convert_reduce_fusion = (f32[1024]{0:T(1024)S(1)}, bf16[1024,2048]{1,0:T(8,128)(2,1)}) fusion(bf16[1024,2048]{1,0:T(8,128)(2,1)} %bitcast.180, s32[1024]{0:T(1024)S(1)} %bitcast.173), kind=kOutput, calls=%fused_computation.1 | convolution fusion | flops 4302306304 | bytes 8396800 | tf_op jit(solution)/shard_map/dot_general | solution.py:28
  82.6 4.5 fusion.2
  88.2 3.6 all-to-all-start
  98.6 19.5 %mix_project.1 = (f32[1024,256]{1,0:T(8,128)}, f32[1024,256]{1,0:T(8,128)}, f32[1024,256]{1,0:T(8,128)}, f32[1024,640]{1,0:T(8,128)}, bf16[1024,640]{1,0:T(8,128)(2,1)}) custom-call(bf16[1024,2048]{1,0:T(8,128)(2,1)} %get-tuple-element.287.block_ref, f32[1024,4]{1,0:T(8,128)} %copy.127.stats_ref, f32[8,2048]{1,0:T(8,128)} %slice_bitcast_fusion.3.vec_ref, ...), custom_call_target="tpu_custom_call" | custom-call | flops 134217728 | bytes 62914560 | tf_op jit(solution)/shard_map/mix_project/pallas_call | solution.py:569
  121.2 6.2 all-to-all-start.1
  133.8 36.1 %mix_forward.1 = (bf16[1024,256]{1,0:T(8,128)(2,1)S(1)}, bf16[1024,256]{1,0:T(8,128)(2,1)S(1)}, f32[1024,256]{1,0:T(8,128)S(1)}, f32[1024,256]{1,0:T(8,128)S(1)}, f32[1024,256]{1,0:T(8,128)S(1)}) custom-call(f32[1024,256]{1,0:T(8,128)S(1)} %copy-done.4, f32[1024,256]{1,0:T(8,128)} %get-tuple-element.103.keys_ref, f32[1024,256]{1,0:T(8,128)} %get-tuple-element.104.values_ref, ...), custom_call_target="tpu_custom_call" | custom-call | flops 134217728 | bytes 115343360 | tf_op jit(solution)/shard_map/mix_forward/pallas_call | solution.py:385
  173.5 16.3 %deal_rows.1 = bf16[128,2048]{1,0:T(8,128)(2,1)} custom-call(bf16[1024,256]{1,0:T(8,128)(2,1)} %copy-done.15), custom_call_target="tpu_custom_call" | custom-call | bytes 62914560 | tf_op jit(solution)/shard_map/deal_rows/pallas_call | solution.py:1031
  190.5 5.1 fusion.84
  196.2 3.4 collective-permute-start.2
  202.5 38.2 %channel_forward.1 = (f32[128,2048]{1,0:T(8,128)}, bf16[512,2048]{1,0:T(8,128)(2,1)}, bf16[512,1024]{1,0:T(8,128)(2,1)}, bf16[512,1024]{1,0:T(8,128)(2,1)}, f32[512,2048]{1,0:T(8,128)}) custom-call(bf16[128,2048]{1,0:T(8,128)(2,1)} %add_convert_fusion.2.refs_0_, bf16[2048,2048]{1,0:T(8,128)(2,1)} %refs_2_.3, bf16[2048,2048]{1,0:T(8,128)(2,1)} %refs_1_.3), custom_call_target="tpu_custom_call" | custom-call | bytes 104857600 | tf_op jit(solution)/shard_map/channel_forward/pallas_call | solution.py:1193
  243.2 7.6 %all-to-all-start.2 = ((bf16[8,16,2048]{2,1,0:T(8,128)(2,1)}), bf16[8,16,2048]{2,1,0:T(8,128)(2,1)S(1)}, u32[]{:S(2)}, u32[]{:S(2)}) async-start(bf16[8,16,2048]{2,1,0:T(8,128)(2,1)} %bitcast.143), calls=%async_computation.2 | async-start | bytes 1048576 | tf_op jit(solution)/shard_map/all_to_all | solution.py:1221
  250.9 2.8 fusion.85
  253.7 52.6 %channel_backward.1 = (f32[128,2048]{1,0:T(8,128)}, bf16[512,2048]{1,0:T(8,128)(2,1)}, bf16[512,1024]{1,0:T(8,128)(2,1)}, bf16[512,2048]{1,0:T(8,128)(2,1)}, bf16[512,1024]{1,0:T(8,128)(2,1)}) custom-call(bf16[128,2048]{1,0:T(8,128)(2,1)} %get-tuple-element.290.refs_0_, bf16[2048,2048]{1,0:T(8,128)(2,1)} %refs_1_.3, bf16[2048,2048]{1,0:T(8,128)(2,1)} %refs_2_.3, ...), custom_call_target="tpu_custom_call" | custom-call | bytes 104857600 | tf_op jit(solution)/shard_map/channel_backward/pallas_call | solution.py:1193
  306.4 4.2 fusion.86
  310.6 4.7 add_convert_fusion.1
  315.3 3.2 multiply_reduce_fusion
  320.2 3.9 collective-permute-done.3
  327.6 3.7 convolution_convert_fusion.1.x_ref
  331.2 14.8 %deal_heads.1.grad_ref = bf16[1024,256]{1,0:T(8,128)(2,1)} custom-call(bf16[128,2048]{1,0:T(8,128)(2,1)} %convolution_convert_fusion.1.x_ref), custom_call_target="tpu_custom_call" | custom-call | bytes 62914560 | tf_op jit(solution)/shard_map/deal_heads/pallas_call | solution.py:1031
  352.1 6.3 all-to-all-start.4
  359.4 47.3 %mix_backward.1 = (bf16[1024,256]{1,0:T(8,128)(2,1)S(1)}, bf16[1024,256]{1,0:T(8,128)(2,1)S(1)}, bf16[1024,256]{1,0:T(8,128)(2,1)S(1)}, bf16[4,1024,256]{2,1,0:T...) custom-call(bf16[1024,256]{1,0:T(8,128)(2,1)S(1)} %copy-done.6, f32[1024,256]{1,0:T(8,128)S(1)} %copy-done.4, ...), custom_call_target="tpu_custom_call" | custom-call | flops 134217728 | bytes 157286400 | tf_op jit(solution)/shard_map/mix_backward/pallas_call | solution.py:413
  409.9 3.7 collective-permute-done.5
  415.3 4.5 fusion.87
  419.8 4.6 add_convert_fusion
  431.1 7.4 %all-to-all-start.3 = ((bf16[8,128,256]{2,1,0:T(8,128)(2,1)}), bf16[8,128,256]{2,1,0:T(8,128)(2,1)S(1)}, u32[]{:S(2)}, u32[]{:S(2)}) async-start(bf16[8,128,256]{2,1,0:T(8,128)(2,1)} %bitcast.31), calls=%async_computation.3 | async-start | bytes 1048576 | tf_op jit(solution)/shard_map/all_to_all | solution.py:1221
  439.9 40.3 %mix_unproject.1 = (f32[1024,2048]{1,0:T(8,128)}, f32[1024,2]{1,0:T(8,128)}, bf16[4,8,64,1408]{3,2,1,0:T(8,128)(2,1)}, bf16[256,640]{1,0:T(8,128)(2,1)}) custom-call(bf16[1024,2048]{1,0:T(8,128)(2,1)} %get-tuple-element.287.block_ref, f32[1024,4]{1,0:T(8,128)} %copy.127.stats_ref, f32[8,2048]{1,0:T(8,128)} %slice_bitcast_fusion.3.vec_ref, ...), custom_call_target="tpu_custom_call" | custom-call | flops 134217728 | bytes 125829120 | tf_op jit(solution)/shard_map/mix_unproject/pallas_call | solution.py:592
  489.3 5.9 fusion.5
  495.5 6.5 fusion.12
  508.6 2.8 fusion.31
  520.4 77.2 %reduce_seq.1 = (f32[128,2048]{1,0:T(8,128)S(1)}, bf16[4,64,2048]{2,1,0:T(8,128)(2,1)S(1)}) custom-call(bf16[8,128,2048]{2,1,0:T(8,128)(2,1)S(1)} %bitcast.124, bf16[4,64,2048]{2,1,0:T(8,128)(2,1)S(1)} %bitcast.125), custom_call_target="tpu_custom_call" | custom-call | bytes 1048576 | tf_op jit(solution)/shard_map/reduce_seq/pallas_call | solution.py:941
  601.7 94.0 %finish.1 = (bf16[8,64,1408]{2,1,0:T(8,128)(2,1)S(1)}, bf16[4,64,2048]{2,1,0:T(8,128)(2,1)S(1)}) custom-call(bf16[8,64,1408]{2,1,0:T(8,128)(2,1)S(1)} %fusion.17.wide_ref, bf16[4,64,2048]{2,1,0:T(8,128)(2,1)S(1)} %bitcast.126), custom_call_target="tpu_custom_call" | custom-call | bytes 104857600 | tf_op jit(solution)/shard_map/finish/pallas_call | solution.py:977
  (350 shorter events, 103.0 us)
Async XLA Ops:
  7.2 112.9 %copy-start = (bf16[128,2048]{1,0:T(8,128)(2,1)S(1)}, bf16[128,2048]{1,0:T(8,128)(2,1)}, u32[]{:S(2)}) copy-start(bf16[128,2048]{1,0:T(8,128)(2,1)} %param.17) | copy-start | bytes 1572868
  7.2 183.3 %all-gather.2.cloned.1.call-start = ((), (), s32[]{:S(2)}) async-start(), calls=%async_computation.8 | async-start | bytes 10485760 | tf_op jit(solution)/shard_map/all_gather | solution.py:1345
  15.6 58.3 %copy-start.75 = (s32[1,4]{1,0:T(1,128)S(1)}, s32[1,4]{1,0:T(1,128)}, u32[]{:S(2)}) copy-start(s32[1,4]{1,0:T(1,128)} %param.20) | copy-start | bytes 52
  74.2 58.7 %copy-start.61 = (s32[1024,1]{0,1:T(1,128)}, s32[1024,1]{0,1:T(1,128)S(1)}, u32[]{:S(2)}) copy-start(s32[1024,1]{0,1:T(1,128)S(1)} %get-tuple-element.260) | copy-start | bytes 12292
  88.2 31.7 %all-to-all-start = ((bf16[8,128,256]{1,2,0:T(8,128)(2,1)}), bf16[8,128,256]{1,2,0:T(8,128)(2,1)S(1)}, u32[]{:S(2)}, u32[]{:S(2)}) async-start(bf16[8,128,256]{1,2,0:T(8,128)(2,1)} %bitcast.15), calls=%async_computation | async-start | bytes 1048576 | tf_op jit(solution)/shard_map/all_to_all | solution.py:1221
  93.0 34.5 %collective-permute-start = (f32[8,128]{1,0:T(8,128)S(1)}, f32[8,128]{1,0:T(8,128)S(1)}, u32[]{:S(2)}, u32[]{:S(2)}) collective-permute-start(f32[8,128]{1,0:T(8,128)S(1)} %broadcast_in_dim.4), channel_id=1, source_target_pairs={{0,1},{1,0},{2,3},{3,2},{4,5},{5,4},{6,7},{7,6},{8,9},{9,8},{10,11... | collective-permute-start | bytes 12296 | tf_op jit(solution)/shard_map/ppermute | solution.py:1226
  96.7 261.6 %copy-start.2 = (bf16[640,256]{1,0:T(8,128)(2,1)}, bf16[640,256]{1,0:T(8,128)(2,1)S(1)}, u32[]{:S(2)}) copy-start(bf16[640,256]{1,0:T(8,128)(2,1)S(1)} %fusion.50.up_ref) | copy-start | bytes 983044
  121.2 52.3 %all-to-all-start.1 = ((bf16[8,16,2048]{2,1,0:T(8,128)(2,1)}), bf16[8,16,2048]{2,1,0:T(8,128)(2,1)S(1)}, u32[]{:S(2)}, u32[]{:S(2)}) async-start(bf16[8,16,2048]{2,1,0:T(8,128)(2,1)} %bitcast.17), calls=%async_computation.1 | async-start | bytes 1048576 | tf_op jit(solution)/shard_map/all_to_all | solution.py:1221
  128.1 3.7 collective-permute-start.1
  195.6 45.1 %copy-start.20 = (f32[128,2048]{1,0:T(8,128)}, f32[128,2048]{1,0:T(8,128)S(1)}, u32[]{:S(2)}) copy-start(f32[128,2048]{1,0:T(8,128)S(1)} %get-tuple-element.289) | copy-start | bytes 3145732
  195.9 44.8 %copy-start.64 = (f32[128]{0:T(128)}, f32[128]{0:T(128)S(1)}, u32[]{:S(2)}) copy-start(f32[128]{0:T(128)S(1)} %add_rsqrt_fusion.1) | copy-start | bytes 1540
  196.2 44.5 %copy-start.24 = (f32[128,2048]{1,0:T(8,128)}, f32[128,2048]{1,0:T(8,128)S(1)}, u32[]{:S(2)}) copy-start(f32[128,2048]{1,0:T(8,128)S(1)} %multiply_add_fusion.1) | copy-start | bytes 3145732
  196.2 4.3 collective-permute-start.2
  243.2 72.1 %all-to-all-start.2 = ((bf16[8,16,2048]{2,1,0:T(8,128)(2,1)}), bf16[8,16,2048]{2,1,0:T(8,128)(2,1)S(1)}, u32[]{:S(2)}, u32[]{:S(2)}) async-start(bf16[8,16,2048]{2,1,0:T(8,128)(2,1)} %bitcast.143), calls=%async_computation.2 | async-start | bytes 1048576 | tf_op jit(solution)/shard_map/all_to_all | solution.py:1221
  250.8 229.4 %reduce-scatter.4.cloned.1.call-start = ((), (), s32[]{:S(2)}) async-start(), calls=%async_computation.9 | async-start | bytes 5242880 | tf_op jit(solution)/shard_map/reduce_scatter | solution.py:1443
  253.7 52.6 %copy-start.74 = (bf16[512,1024]{1,0:T(8,128)(2,1)S(1)}, bf16[512,1024]{1,0:T(8,128)(2,1)}, u32[]{:S(2)}) copy-start(bf16[512,1024]{1,0:T(8,128)(2,1)} %get-tuple-element.115) | copy-start | bytes 3145732
  318.6 5.5 collective-permute-start.3
  346.1 67.6 %collective-permute-start.4 = (bf16[512,2048]{1,0:T(8,128)(2,1)}, bf16[512,2048]{1,0:T(8,128)(2,1)}, u32[]{:S(2)}, u32[]{:S(2)}) collective-permute-start(bf16[512,2048]{1,0:T(8,128)(2,1)} %get-tuple-element.131), channel_id=1, source_target_pairs={{0,4},{4,0},{8,12},{12,8},{16,20},{20,16},{24,28},{28,24},{1,5},{5... | collective-permute-start | bytes 6291464 | tf_op jit(solution)/shard_map/ppermute | solution.py:1240
  347.1 66.6 %collective-permute-start.5 = (bf16[512,1024]{1,0:T(8,128)(2,1)}, bf16[512,1024]{1,0:T(8,128)(2,1)}, u32[]{:S(2)}, u32[]{:S(2)}) collective-permute-start(bf16[512,1024]{1,0:T(8,128)(2,1)} %get-tuple-element.133), channel_id=1, source_target_pairs={{0,4},{4,0},{8,12},{12,8},{16,20},{20,16},{24,28},{28,24},{1,5},{5... | collective-permute-start | bytes 3145736 | tf_op jit(solution)/shard_map/ppermute | solution.py:1240
  348.2 61.8 %collective-permute-start.6 = (bf16[128,2048]{1,0:T(8,128)(2,1)}, bf16[128,2048]{1,0:T(8,128)(2,1)}, u32[]{:S(2)}, u32[]{:S(2)}) collective-permute-start(bf16[128,2048]{1,0:T(8,128)(2,1)} %copy-done.30), channel_id=1, source_target_pairs={{0,1},{1,0},{2,3},{3,2},{4,5},{5,4},{6,7},{7,6},{8,9},{9,8},{10,11... | collective-permute-start | bytes 1572872 | tf_op jit(solution)/shard_map/ppermute | solution.py:1226
  348.2 61.8 %collective-permute-start.7 = (bf16[128,2048]{1,0:T(8,128)(2,1)}, bf16[128,2048]{1,0:T(8,128)(2,1)}, u32[]{:S(2)}, u32[]{:S(2)}) collective-permute-start(bf16[128,2048]{1,0:T(8,128)(2,1)} %copy-done.30), channel_id=1, source_target_pairs={{0,2},{1,3},{2,0},{3,1},{4,6},{5,7},{6,4},{7,5},{8,10},{9,11},{10,... | collective-permute-start | bytes 1572872 | tf_op jit(solution)/shard_map/ppermute | solution.py:1226
  352.1 57.8 %all-to-all-start.4 = ((bf16[4,128,8,64]{1,3,2,0:T(8,128)(2,1)}), bf16[4,128,8,64]{1,3,2,0:T(8,128)(2,1)}, u32[]{:S(2)}, u32[]{:S(2)}) async-start(bf16[4,128,8,64]{1,3,2,0:T(8,128)(2,1)} %copy.136), calls=%async_computation.5 | async-start | bytes 1048576 | tf_op jit(solution)/shard_map/all_to_all | solution.py:1221
  358.3 155.8 %reduce-scatter.6.cloned.1.call-start = ((), (), s32[]{:S(2)}) async-start(), calls=%async_computation.10 | async-start | bytes 5242880 | tf_op jit(solution)/shard_map/reduce_scatter | solution.py:1443
  413.7 10.7 %collective-permute-start.8 = (bf16[128,2048]{1,0:T(8,128)(2,1)}, bf16[128,2048]{1,0:T(8,128)(2,1)}, u32[]{:S(2)}, u32[]{:S(2)}) collective-permute-start(bf16[128,2048]{1,0:T(8,128)(2,1)} %collective-permute-done.7), channel_id=1, source_target_pairs={{0,1},{1,0},{2,3},{3,2},{4,5},{5,4},{6,7},{7,6},{8,9},{9,8},{10,11... | collective-permute-start | bytes 1572872 | tf_op jit(solution)/shard_map/ppermute | solution.py:1226
  428.7 51.5 %collective-permute-start.9 = (bf16[4,64,2048]{2,1,0:T(8,128)(2,1)}, bf16[4,64,2048]{2,1,0:T(8,128)(2,1)}, u32[]{:S(2)}, u32[]{:S(2)}) collective-permute-start(bf16[4,64,2048]{2,1,0:T(8,128)(2,1)} %dynamic-slice_bitcast_fusion), channel_id=1, source_target_pairs={{0,4},{4,0},{8,12},{12,8},{16,20},{20,16},{24,28},{28,24},{1,5},{5... | collective-permute-start | bytes 3145736 | tf_op jit(solution)/shard_map/ppermute | solution.py:1240
  431.1 49.1 %all-to-all-start.3 = ((bf16[8,128,256]{2,1,0:T(8,128)(2,1)}), bf16[8,128,256]{2,1,0:T(8,128)(2,1)S(1)}, u32[]{:S(2)}, u32[]{:S(2)}) async-start(bf16[8,128,256]{2,1,0:T(8,128)(2,1)} %bitcast.31), calls=%async_computation.3 | async-start | bytes 1048576 | tf_op jit(solution)/shard_map/all_to_all | solution.py:1221
  438.4 163.2 %reduce-scatter.8.cloned.1.call-start = ((), (), s32[]{:S(2)}) async-start(), calls=%async_computation.11 | async-start | bytes 1310720 | tf_op jit(solution)/shard_map/reduce_scatter | solution.py:1443
  482.6 21.1 %collective-permute-start.10 = (bf16[2,8,64,1408]{3,2,1,0:T(8,128)(2,1)S(1)}, bf16[2,8,64,1408]{3,2,1,0:T(8,128)(2,1)}, u32[]{:S(2)}, u32[]{:S(2)}) collective-permute-start(bf16[2,8,64,1408]{3,2,1,0:T(8,128)(2,1)S(1)} %pad_maximum_fusion), channel_id=1, source_target_pairs={{0,1},{1,0},{2,3},{3,2},{4,5},{5,4},{6,7},{7,6},{8,9},{9,8},{10,11... | collective-permute-start | bytes 8650760 | tf_op jit(solution)/shard_map/ppermute | solution.py:1226
  487.5 14.5 %collective-permute-start.11 = (bf16[2,64,640]{2,1,0:T(8,128)(2,1)S(1)}, bf16[2,64,640]{2,1,0:T(8,128)(2,1)S(1)}, u32[]{:S(2)}, u32[]{:S(2)}) collective-permute-start(bf16[2,64,640]{2,1,0:T(8,128)(2,1)S(1)} %pad_maximum_fusion.3), channel_id=1, source_target_pairs={{0,1},{1,0},{2,3},{3,2},{4,5},{5,4},{6,7},{7,6},{8,9},{9,8},{10,11... | collective-permute-start | bytes 491528 | tf_op jit(solution)/shard_map/ppermute | solution.py:1226
  514.1 85.1 %collective-permute-start.12 = (bf16[8,64,1408]{2,1,0:T(8,128)(2,1)}, bf16[8,64,1408]{2,1,0:T(8,128)(2,1)}, u32[]{:S(2)}, u32[]{:S(2)}) collective-permute-start(bf16[8,64,1408]{2,1,0:T(8,128)(2,1)} %fusion.31), channel_id=1, source_target_pairs={{0,2},{1,3},{2,0},{3,1},{4,6},{5,7},{6,4},{7,5},{8,10},{9,11},{10,... | collective-permute-start | bytes 4325384 | tf_op jit(solution)/shard_map/ppermute | solution.py:1226
  516.7 84.9 %collective-permute-start.13 = (bf16[64,640]{1,0:T(8,128)(2,1)}, bf16[64,640]{1,0:T(8,128)(2,1)}, u32[]{:S(2)}, u32[]{:S(2)}) collective-permute-start(bf16[64,640]{1,0:T(8,128)(2,1)} %fusion.62), channel_id=1, source_target_pairs={{0,2},{1,3},{2,0},{3,1},{4,6},{5,7},{6,4},{7,5},{8,10},{9,11},{10,... | collective-permute-start | bytes 245768 | tf_op jit(solution)/shard_map/ppermute | solution.py:1226
  520.4 78.9 %copy-start.23 = (f32[2,8,64,1408]{3,2,1,0:T(8,128)S(1)}, f32[2,8,64,1408]{3,2,1,0:T(8,128)}, u32[]{:S(2)}) copy-start(f32[2,8,64,1408]{3,2,1,0:T(8,128)} %copy-done.22) | copy-start | bytes 17301508
  (75 other events, 469.5 us)
Sparse Core Ops, SparseCore 0:
  72.9 56.2 all-gather.1
  346.2 76.9 reduce-scatter.3
  427.2 86.8 reduce-scatter.5
  516.3 54.4 reduce-scatter.7

commit v11 on v10

--- a/solution.py
+++ b/solution.py
@@ -790,50 +790,15 @@
     )(own, tail, weight)
 
 
-def turning(x_ref, out_ref, send_sem, recv_sem):
-    s, w, side, z, _, _, _ = places()
-    home = z == w
-    greetings = tuple(((source != z) | (z != w), (source * 2 + side, z)) for source in range(4))
-
-    def copy(j):
-        piece = (z + j) % 4
-        return send(x_ref.at[piece], out_ref.at[z], send_sem.at[j], recv_sem.at[j], (w * 2 + side, piece))
-
-    def start():
-        for j in (3, 2, 1):
-            copy(j).start()
-
-        @pl.when(jnp.logical_not(home))
-        def _():
-            copy(0).start()
-
-        @pl.when(home)
-        def _():
-            out_ref[z] = x_ref[z]
-
-    def end():
-        for j in range(1, 4):
-            copy(j).wait_recv()
-            copy(j).wait_send()
-
-        @pl.when(jnp.logical_not(home))
-        def _():
-            copy(0).wait_recv()
-            copy(0).wait_send()
-
-    return greetings, jnp.where(home, 3, 4), start, end
-
-
 def reduce_kernel(
-    splits, x_ref, turn_ref, out_ref, turn_out, x_buf, right_buf, left_buf, right_out, left_out,
-    x_send, x_recv, right_send, right_recv, left_send, left_recv, turn_send, turn_recv,
+    splits, x_ref, out_ref, x_buf, right_buf, left_buf, right_out, left_out,
+    x_send, x_recv, right_send, right_recv, left_send, left_recv,
 ):
     s, w, side, z, x_device, _, _ = places()
     up, down = (s + 2, w), (s - 2, w)
     size = x_ref.shape[2] // splits
     columns = [slice(c * size, (c + 1) * size) for c in range(splits)]
-    greetings, number, start_turn, end_turn = turning(turn_ref, turn_out, turn_send, turn_recv)
-    greet(((None, x_device), (z < 3, up), (z > 0, down)) + greetings, 1 + line_ends(z) + number)
+    greet(((None, x_device), (z < 3, up), (z > 0, down)), 1 + line_ends(z))
 
     def to_x(target, c):
         return send(
@@ -872,7 +837,6 @@
             start_x(z - k)
 
     start_x(z)
-    start_turn()
     for k in (3, 2, 1):
         for c in range(splits):
 
@@ -930,60 +894,24 @@
             def _(k=k, c=c):
                 to_left(k, c).wait_send()
 
-    end_turn()
-
-
-def reduce_seq(x, turned):
+
+def reduce_seq(x):
     seqs, rows, width = x.shape
     splits = 2
     vmem = pl.BlockSpec(memory_space=pltpu.VMEM)
     dma = pltpu.SemaphoreType.DMA
     return pl.pallas_call(
         functools.partial(reduce_kernel, splits),
-        in_specs=[vmem] * 2,
-        out_specs=[vmem] * 2,
-        out_shape=[jax.ShapeDtypeStruct((rows, width), F32), jax.ShapeDtypeStruct(turned.shape, turned.dtype)],
+        in_specs=[vmem],
+        out_specs=vmem,
+        out_shape=jax.ShapeDtypeStruct((rows, width), F32),
         scratch_shapes=[pltpu.VMEM((4, rows, width), BF16)]
         + [pltpu.VMEM((3, rows, width), BF16)] * 4
-        + [dma((4, splits))] * 2 + [dma((3, splits))] * 4 + [dma((4,))] * 2,
+        + [dma((4, splits))] * 2 + [dma((3, splits))] * 4,
         compiler_params=pltpu.CompilerParams(collective_id=2, has_side_effects=True, vmem_limit_bytes=40 << 20),
         cost_estimate=pl.CostEstimate(flops=0, bytes_accessed=1 << 20, transcendentals=0),
         name="reduce_seq",
-    )(x, turned)
-
-
-def finish_kernel(wide_ref, key_ref, wide_out, key_out, wide_send, wide_recv, key_send, key_recv):
-    s, w, _, _, _, _, _ = places()
-    greetings, number, start_turn, end_turn = turning(key_ref, key_out, key_send, key_recv)
-    greet(tuple((None, ((s + d) % 8, w)) for d in range(1, 8)) + greetings, 7 + number)
-
-    def wide(d):
-        target = (s + d) % 8
-        return send(wide_ref.at[target], wide_out.at[s], wide_send.at[d - 1], wide_recv.at[d - 1], (target, w))
-
-    for d in (4, 3, 5, 2, 6, 1, 7):
-        wide(d).start()
-    start_turn()
-    wide_out[s] = wide_ref[s]
-    for d in range(1, 8):
-        wide(d).wait_recv()
-        wide(d).wait_send()
-    end_turn()
-
-
-def finish(wide, key):
-    vmem = pl.BlockSpec(memory_space=pltpu.VMEM)
-    dma = pltpu.SemaphoreType.DMA
-    return pl.pallas_call(
-        finish_kernel,
-        in_specs=[vmem] * 2,
-        out_specs=[vmem] * 2,
-        out_shape=[jax.ShapeDtypeStruct(x.shape, x.dtype) for x in (wide, key)],
-        scratch_shapes=[dma((7,)), dma((7,)), dma((4,)), dma((4,))],
-        compiler_params=pltpu.CompilerParams(collective_id=5, has_side_effects=True, vmem_limit_bytes=24 << 20),
-        cost_estimate=pl.CostEstimate(flops=0, bytes_accessed=100 << 20, transcendentals=0),
-        name="finish",
-    )(wide, key)
+    )(x)
 
 
 def deal_kernel(to_heads, x_ref, out_ref, send_sem, recv_sem):
@@ -1054,14 +982,8 @@
         pltpu.make_async_copy(first_hbm, first, load_sem.at[0]),
         pltpu.make_async_copy(second_hbm, second, load_sem.at[1]),
     ]
-    size = units // 32
-    for number, (source, target) in enumerate(((first_hbm, first), (second_hbm, second))):
-        for at in range(32):
-            h, k, q = at // 16, at // 4 % 4, at % 4
-            to = (h * 4 + q) * 4 + k
-            pltpu.make_async_copy(
-                source.at[pl.ds(at * size, size)], target.at[pl.ds(to * size, size)], load_sem.at[number]
-            ).start()
+    for load in loads:
+        load.start()
     if not forward:
         loads.append(pltpu.make_async_copy(active_hbm, active, load_sem.at[2]))
         loads[2].start()
@@ -1490,16 +1412,19 @@
     else:
         wide_part = block_sum(wide)
     if paired:
-        grad_tokens, value_all = reduce_seq(grad_given, value_sum.reshape(4, -1, width))
-        wide_part, grad_tokens, grad_out, across_up = lax.optimization_barrier(
-            (wide_part, grad_tokens, grad_out, across_up)
-        )
-        wide_all, key_all = finish(wide_part.astype(BF16), key_sum.reshape(4, -1, width))
-        wide_all = wide_all.astype(F32)
-        grad_ffn_key, grad_ffn_value = [x.reshape(-1, width).astype(F32) for x in (key_all, value_all)]
+        grad_tokens = reduce_seq(grad_given)
+        turned = [
+            ((z * 2 + x) * 4 + w, (w * 2 + x) * 4 + z) for z in range(4) for x in range(2) for w in range(4)
+        ]
+        value_turned = lax.ppermute(value_sum, ("seq", "wsh"), turned)
+        wide_part, grad_tokens, grad_out, value_turned, across_up, key_sum = lax.optimization_barrier(
+            (wide_part, grad_tokens, grad_out, value_turned, across_up, key_sum)
+        )
+        grad_ffn_key = lax.ppermute(key_sum, ("seq", "wsh"), turned).astype(F32)
+        grad_ffn_value = value_turned.astype(F32)
     else:
         grad_tokens = jnp.sum(exchange(grad_given, "seq").astype(F32), 0)
-        wide_all = exchange(wide_part.astype(BF16), "seq").astype(F32)
+    wide_all = exchange(wide_part.astype(BF16), "seq").astype(F32)
 
     def square(at):
         taken = wide_all[:, :, at * own_width : (at + 1) * own_width]

time: 722 us -> 716 us (level)
  Pallas kernels: 491 us -> 390 us
  waiting for transfers between devices: 12.6 us -> 77.6 us
  starting transfers between devices: 41.3 us -> 69 us
    pallas_call x2 -> x1, Pallas kernels: 171 us -> 70.5 us  [reduce_seq(): pl.pallas_call(functools.partial(reduce_kernel, splits), in_specs=[vmem],...]
    ppermute x0 -> x2, waiting for transfers between devices: none -> 64.6 us  [the longest x1 64.6 us: local(): grad_ffn_key = lax.ppermute(key_sum, ('seq', 'wsh'), turned).astype(F32)]
    ppermute x0 -> x2, starting transfers between devices: none -> 12.8 us  [the longest x1 7.11 us: local(): value_turned = lax.ppermute(value_sum, ('seq', 'wsh'), turned)]
    ppermute x9, starting transfers between devices: 2.92 us -> 10.6 us  [swap(): return lax.ppermute(x, 'wsh', [(i, i ^ by) for i in range(size)])]
    all_to_all x5 -> x6, starting transfers between devices: 31.1 us -> 38.4 us  [exchange(): return lax.all_to_all(x, axis, split_axis=0, concat_axis=0, tiled=True)]
    unnamed x173 -> x161, local copies, waits for them, and re-layouts: 23 us -> 22.3 us
  transfers between devices with their start and end apart: 23 -> 26, of which waited for: 4 -> 5; matrix products, arithmetic and copies ran while one was open for 13% -> 15% of each run, Pallas kernels for 41% -> 40%
where the time goes in v11:
time: 716 us; the launch traced here: 706 us
  Pallas kernels  390 us (54%)
  waiting for transfers between devices  77.6 us (11%)
  starting transfers between devices  69 us (10%)
  matrix products  56.3 us (8%)
  other arithmetic  49.2 us (7%)
  local copies, waits for them, and re-layouts  48.1 us (7%)
  between operations  16.5 us (2%)
    pallas_call x2, Pallas kernels, channel_stage(): pl.pallas_call(body, in_specs=[pl.BlockSpec(memory_space=pltpu.VMEM)] + [...  90.6 us
    pallas_call x1, Pallas kernels, reduce_seq(): pl.pallas_call(functools.partial(reduce_kernel, splits), in_specs=[vmem],...  70.5 us
    ppermute x1, waiting for transfers between devices, local(): grad_ffn_key = lax.ppermute(key_sum, ('seq', 'wsh'), turned).astype(F32)  64.6 us
    dot_general x17, matrix products, dot(): return lax.dot_general(a, b, dims, preferred_element_type=F32)  56.3 us
    pallas_call x1, Pallas kernels, gather_first(): pl.pallas_call(gather_kernel, in_specs=[pl.BlockSpec(memory_space=pltpu.V...  54.4 us
    pallas_call x1, Pallas kernels, run_backward(): pl.pallas_call(functools.partial(backward_kernel, count), grid=(rows // s...  47.3 us
    pallas_call x1, Pallas kernels, run_unproject(): pl.pallas_call(functools.partial(unproject_kernel, own_width, parts, piec...  40.3 us
    all_to_all x6, starting transfers between devices, exchange(): return lax.all_to_all(x, axis, split_axis=0, concat_axis=0, tiled=True)  38.4 us
  transfers between devices with their start and end apart: 26, of which 5 were waited for; matrix products, arithmetic and copies ran while one was open for 15% of the time, Pallas kernels for 40%

profile of v11, /device:TPU:4, one launch (start us, length us, event | category | flops | bytes accessed | tf_op | source)
XLA Modules:
  0.0 706.4 jit_solution(15508643817583114605)
XLA Ops:
  18.3 54.4 %gather_first.1 = (bf16[8,128,2048]{2,1,0:T(8,128)(2,1)}, bf16[8,128,128]{2,1,0:T(8,128)(2,1)}, bf16[4,512,1664]{2,1,0:T(8,128)(2,1)}) custom-call(bf16[128,2048]{1,0:T(8,128)(2,1)} %own_ref.1, bf16[128,128]{1,0:T(8,128)(2,1)} %pad.30.tail_ref, bf16[512,1664]{1,0:T(8,128)(2,1)} %copy-done.26), custom_call_target="tpu_custom_call" | custom-call | bytes 104857600 | tf_op jit(solution)/shard_map/gather_first/pallas_call | solution.py:781
  74.3 8.3 %convert_reduce_fusion = (f32[1024]{0:T(1024)S(1)}, bf16[1024,2048]{1,0:T(8,128)(2,1)}) fusion(bf16[1024,2048]{1,0:T(8,128)(2,1)} %bitcast.170, s32[1024]{0:T(1024)S(1)} %bitcast.163), kind=kOutput, calls=%fused_computation.1 | convolution fusion | flops 4302306304 | bytes 8396800 | tf_op jit(solution)/shard_map/dot_general | solution.py:28
  82.6 4.5 fusion.2
  98.5 19.4 %mix_project.1 = (f32[1024,256]{1,0:T(8,128)}, f32[1024,256]{1,0:T(8,128)}, f32[1024,256]{1,0:T(8,128)}, f32[1024,640]{1,0:T(8,128)}, bf16[1024,640]{1,0:T(8,128)(2,1)}) custom-call(bf16[1024,2048]{1,0:T(8,128)(2,1)} %get-tuple-element.283.block_ref, f32[1024,4]{1,0:T(8,128)} %copy.127.stats_ref, f32[8,2048]{1,0:T(8,128)} %slice_bitcast_fusion.3.vec_ref, ...), custom_call_target="tpu_custom_call" | custom-call | flops 134217728 | bytes 62914560 | tf_op jit(solution)/shard_map/mix_project/pallas_call | solution.py:569
  121.2 6.2 all-to-all-start.1
  133.8 36.1 %mix_forward.1 = (bf16[1024,256]{1,0:T(8,128)(2,1)S(1)}, bf16[1024,256]{1,0:T(8,128)(2,1)S(1)}, f32[1024,256]{1,0:T(8,128)S(1)}, f32[1024,256]{1,0:T(8,128)S(1)}, f32[1024,256]{1,0:T(8,128)S(1)}) custom-call(f32[1024,256]{1,0:T(8,128)S(1)} %copy-done.4, f32[1024,256]{1,0:T(8,128)} %get-tuple-element.101.keys_ref, f32[1024,256]{1,0:T(8,128)} %get-tuple-element.102.values_ref, ...), custom_call_target="tpu_custom_call" | custom-call | flops 134217728 | bytes 115343360 | tf_op jit(solution)/shard_map/mix_forward/pallas_call | solution.py:385
  173.5 16.3 %deal_rows.1 = bf16[128,2048]{1,0:T(8,128)(2,1)} custom-call(bf16[1024,256]{1,0:T(8,128)(2,1)} %copy-done.13), custom_call_target="tpu_custom_call" | custom-call | bytes 62914560 | tf_op jit(solution)/shard_map/deal_rows/pallas_call | solution.py:959
  190.5 5.1 fusion.84
  202.5 38.1 %channel_forward.1 = (f32[128,2048]{1,0:T(8,128)}, bf16[512,2048]{1,0:T(8,128)(2,1)}, bf16[512,1024]{1,0:T(8,128)(2,1)}, bf16[512,1024]{1,0:T(8,128)(2,1)}, f32[512,2048]{1,0:T(8,128)}) custom-call(bf16[128,2048]{1,0:T(8,128)(2,1)} %add_convert_fusion.2.refs_0_, bf16[2048,2048]{1,0:T(8,128)(2,1)} %refs_2_.3, bf16[2048,2048]{1,0:T(8,128)(2,1)} %refs_1_.3), custom_call_target="tpu_custom_call" | custom-call | bytes 104857600 | tf_op jit(solution)/shard_map/channel_forward/pallas_call | solution.py:1115
  243.1 7.6 %all-to-all-start.2 = ((bf16[8,16,2048]{2,1,0:T(8,128)(2,1)}), bf16[8,16,2048]{2,1,0:T(8,128)(2,1)S(1)}, u32[]{:S(2)}, u32[]{:S(2)}) async-start(bf16[8,16,2048]{2,1,0:T(8,128)(2,1)} %bitcast.133), calls=%async_computation.2 | async-start | bytes 1048576 | tf_op jit(solution)/shard_map/all_to_all | solution.py:1143
  253.6 52.6 %channel_backward.1 = (f32[128,2048]{1,0:T(8,128)}, bf16[512,2048]{1,0:T(8,128)(2,1)}, bf16[512,1024]{1,0:T(8,128)(2,1)}, bf16[512,2048]{1,0:T(8,128)(2,1)}, bf16[512,1024]{1,0:T(8,128)(2,1)}) custom-call(bf16[128,2048]{1,0:T(8,128)(2,1)} %get-tuple-element.286.refs_0_, bf16[2048,2048]{1,0:T(8,128)(2,1)} %refs_1_.3, bf16[2048,2048]{1,0:T(8,128)(2,1)} %refs_2_.3, ...), custom_call_target="tpu_custom_call" | custom-call | bytes 104857600 | tf_op jit(solution)/shard_map/channel_backward/pallas_call | solution.py:1115
  306.2 4.2 fusion.86
  310.4 4.7 add_convert_fusion.1
  320.0 3.9 collective-permute-done.3
  327.4 3.7 convolution_convert_fusion.1.x_ref
  331.0 14.8 %deal_heads.1.grad_ref = bf16[1024,256]{1,0:T(8,128)(2,1)} custom-call(bf16[128,2048]{1,0:T(8,128)(2,1)} %convolution_convert_fusion.1.x_ref), custom_call_target="tpu_custom_call" | custom-call | bytes 62914560 | tf_op jit(solution)/shard_map/deal_heads/pallas_call | solution.py:959
  351.9 6.3 all-to-all-start.4
  359.2 47.3 %mix_backward.1 = (bf16[1024,256]{1,0:T(8,128)(2,1)S(1)}, bf16[1024,256]{1,0:T(8,128)(2,1)S(1)}, bf16[1024,256]{1,0:T(8,128)(2,1)S(1)}, bf16[4,1024,256]{2,1,0:T...) custom-call(bf16[1024,256]{1,0:T(8,128)(2,1)S(1)} %copy-done.6, f32[1024,256]{1,0:T(8,128)S(1)} %copy-done.4, ...), custom_call_target="tpu_custom_call" | custom-call | flops 134217728 | bytes 157286400 | tf_op jit(solution)/shard_map/mix_backward/pallas_call | solution.py:413
  409.7 3.7 collective-permute-done.5
  415.1 4.5 fusion.87
  419.7 4.6 add_convert_fusion
  430.9 7.4 %all-to-all-start.3 = ((bf16[8,128,256]{2,1,0:T(8,128)(2,1)}), bf16[8,128,256]{2,1,0:T(8,128)(2,1)S(1)}, u32[]{:S(2)}, u32[]{:S(2)}) async-start(bf16[8,128,256]{2,1,0:T(8,128)(2,1)} %bitcast.31), calls=%async_computation.3 | async-start | bytes 1048576 | tf_op jit(solution)/shard_map/all_to_all | solution.py:1143
  439.8 40.3 %mix_unproject.1 = (f32[1024,2048]{1,0:T(8,128)}, f32[1024,2]{1,0:T(8,128)}, bf16[4,8,64,1408]{3,2,1,0:T(8,128)(2,1)}, bf16[256,640]{1,0:T(8,128)(2,1)}) custom-call(bf16[1024,2048]{1,0:T(8,128)(2,1)} %get-tuple-element.283.block_ref, f32[1024,4]{1,0:T(8,128)} %copy.127.stats_ref, f32[8,2048]{1,0:T(8,128)} %slice_bitcast_fusion.3.vec_ref, ...), custom_call_target="tpu_custom_call" | custom-call | flops 134217728 | bytes 125829120 | tf_op jit(solution)/shard_map/mix_unproject/pallas_call | solution.py:592
  489.1 5.9 fusion.5
  495.2 6.3 fusion.12
  514.5 7.1 %collective-permute-start.13 = (bf16[256,2048]{1,0:T(8,128)(2,1)}, bf16[256,2048]{1,0:T(8,128)(2,1)}, u32[]{:S(2)}, u32[]{:S(2)}) collective-permute-start(bf16[256,2048]{1,0:T(8,128)(2,1)} %reduce-scatter.4.cloned.1.call-done), channel_id=1, source_target_pairs={{0,0},{1,8},{2,16},{3,24},{4,4},{5,12},{6,20},{7,28},{8,1},{9,9},{... | collective-permute-start | bytes 3145736 | tf_op jit(solution)/shard_map/ppermute | solution.py:1419
  523.9 70.5 %reduce_seq.1 = f32[128,2048]{1,0:T(8,128)S(1)} custom-call(bf16[8,128,2048]{2,1,0:T(8,128)(2,1)S(1)} %bitcast.116), custom_call_target="tpu_custom_call" | custom-call | bytes 1048576 | tf_op jit(solution)/shard_map/reduce_seq/pallas_call | solution.py:903
  594.4 9.1 %collective-permute-start.14 = (bf16[64,640]{1,0:T(8,128)(2,1)}, bf16[64,640]{1,0:T(8,128)(2,1)}, u32[]{:S(2)}, u32[]{:S(2)}) collective-permute-start(bf16[64,640]{1,0:T(8,128)(2,1)} %fusion.62), channel_id=1, source_target_pairs={{0,2},{1,3},{2,0},{3,1},{4,6},{5,7},{6,4},{7,5},{8,10},{9,11},{10,... | collective-permute-start | bytes 245768 | tf_op jit(solution)/shard_map/ppermute | solution.py:1148
  603.5 3.8 fusion.17
  607.4 7.3 %all-to-all-start.5 = ((bf16[8,64,1408]{2,1,0:T(8,128)(2,1)}), bf16[8,64,1408]{2,1,0:T(8,128)(2,1)S(1)}, u32[]{:S(2)}, u32[]{:S(2)}) async-start(bf16[8,64,1408]{2,1,0:T(8,128)(2,1)} %fusion.17), calls=%async_computation.8 | async-start | bytes 2883584 | tf_op jit(solution)/shard_map/all_to_all | solution.py:1143
  614.7 5.7 collective-permute-start.15
  628.7 64.6 %collective-permute-done.15 = bf16[256,2048]{1,0:T(8,128)(2,1)S(1)} collective-permute-done((bf16[256,2048]{1,0:T(8,128)(2,1)}, bf16[256,2048]{1,0:T(8,128)(2,1)S(1)}, u32[]{:S(2)}, u32[]{:S(2)}) %collective-permute-start.15) | collective-permute-done | bytes 1048608 | tf_op jit(solution)/shard_map/ppermute | solution.py:1423
  (339 shorter events, 115.8 us)
Async XLA Ops:
  7.2 112.9 %copy-start = (bf16[128,2048]{1,0:T(8,128)(2,1)S(1)}, bf16[128,2048]{1,0:T(8,128)(2,1)}, u32[]{:S(2)}) copy-start(bf16[128,2048]{1,0:T(8,128)(2,1)} %param.17) | copy-start | bytes 1572868
  7.2 183.3 %all-gather.2.cloned.1.call-start = ((), (), s32[]{:S(2)}) async-start(), calls=%async_computation.9 | async-start | bytes 10485760 | tf_op jit(solution)/shard_map/all_gather | solution.py:1267
  15.6 58.3 %copy-start.69 = (s32[1,4]{1,0:T(1,128)S(1)}, s32[1,4]{1,0:T(1,128)}, u32[]{:S(2)}) copy-start(s32[1,4]{1,0:T(1,128)} %param.20) | copy-start | bytes 52
  74.2 58.7 %copy-start.55 = (s32[1024,1]{0,1:T(1,128)}, s32[1024,1]{0,1:T(1,128)S(1)}, u32[]{:S(2)}) copy-start(s32[1024,1]{0,1:T(1,128)S(1)} %get-tuple-element.256) | copy-start | bytes 12292
  88.2 31.7 %all-to-all-start = ((bf16[8,128,256]{1,2,0:T(8,128)(2,1)}), bf16[8,128,256]{1,2,0:T(8,128)(2,1)S(1)}, u32[]{:S(2)}, u32[]{:S(2)}) async-start(bf16[8,128,256]{1,2,0:T(8,128)(2,1)} %bitcast.15), calls=%async_computation | async-start | bytes 1048576 | tf_op jit(solution)/shard_map/all_to_all | solution.py:1143
  93.0 34.5 %collective-permute-start = (f32[8,128]{1,0:T(8,128)S(1)}, f32[8,128]{1,0:T(8,128)S(1)}, u32[]{:S(2)}, u32[]{:S(2)}) collective-permute-start(f32[8,128]{1,0:T(8,128)S(1)} %broadcast_in_dim.4), channel_id=1, source_target_pairs={{0,1},{1,0},{2,3},{3,2},{4,5},{5,4},{6,7},{7,6},{8,9},{9,8},{10,11... | collective-permute-start | bytes 12296 | tf_op jit(solution)/shard_map/ppermute | solution.py:1148
  96.7 261.5 %copy-start.2 = (bf16[640,256]{1,0:T(8,128)(2,1)}, bf16[640,256]{1,0:T(8,128)(2,1)S(1)}, u32[]{:S(2)}) copy-start(bf16[640,256]{1,0:T(8,128)(2,1)S(1)} %fusion.50.up_ref) | copy-start | bytes 983044
  121.2 52.3 %all-to-all-start.1 = ((bf16[8,16,2048]{2,1,0:T(8,128)(2,1)}), bf16[8,16,2048]{2,1,0:T(8,128)(2,1)S(1)}, u32[]{:S(2)}, u32[]{:S(2)}) async-start(bf16[8,16,2048]{2,1,0:T(8,128)(2,1)} %bitcast.17), calls=%async_computation.1 | async-start | bytes 1048576 | tf_op jit(solution)/shard_map/all_to_all | solution.py:1143
  128.1 3.7 collective-permute-start.1
  195.6 45.0 %copy-start.18 = (f32[128,2048]{1,0:T(8,128)}, f32[128,2048]{1,0:T(8,128)S(1)}, u32[]{:S(2)}) copy-start(f32[128,2048]{1,0:T(8,128)S(1)} %get-tuple-element.285) | copy-start | bytes 3145732
  196.2 4.3 collective-permute-start.2
  243.1 72.0 %all-to-all-start.2 = ((bf16[8,16,2048]{2,1,0:T(8,128)(2,1)}), bf16[8,16,2048]{2,1,0:T(8,128)(2,1)S(1)}, u32[]{:S(2)}, u32[]{:S(2)}) async-start(bf16[8,16,2048]{2,1,0:T(8,128)(2,1)} %bitcast.133), calls=%async_computation.2 | async-start | bytes 1048576 | tf_op jit(solution)/shard_map/all_to_all | solution.py:1143
  250.7 229.4 %reduce-scatter.4.cloned.1.call-start = ((), (), s32[]{:S(2)}) async-start(), calls=%async_computation.10 | async-start | bytes 5242880 | tf_op jit(solution)/shard_map/reduce_scatter | solution.py:1365
  253.6 52.6 %copy-start.68 = (bf16[512,1024]{1,0:T(8,128)(2,1)S(1)}, bf16[512,1024]{1,0:T(8,128)(2,1)}, u32[]{:S(2)}) copy-start(bf16[512,1024]{1,0:T(8,128)(2,1)} %get-tuple-element.113) | copy-start | bytes 3145732
  318.4 5.5 collective-permute-start.3
  345.9 67.6 %collective-permute-start.4 = (bf16[512,2048]{1,0:T(8,128)(2,1)}, bf16[512,2048]{1,0:T(8,128)(2,1)}, u32[]{:S(2)}, u32[]{:S(2)}) collective-permute-start(bf16[512,2048]{1,0:T(8,128)(2,1)} %get-tuple-element.129), channel_id=1, source_target_pairs={{0,4},{4,0},{8,12},{12,8},{16,20},{20,16},{24,28},{28,24},{1,5},{5... | collective-permute-start | bytes 6291464 | tf_op jit(solution)/shard_map/ppermute | solution.py:1162
  346.9 66.6 %collective-permute-start.5 = (bf16[512,1024]{1,0:T(8,128)(2,1)}, bf16[512,1024]{1,0:T(8,128)(2,1)}, u32[]{:S(2)}, u32[]{:S(2)}) collective-permute-start(bf16[512,1024]{1,0:T(8,128)(2,1)} %get-tuple-element.131), channel_id=1, source_target_pairs={{0,4},{4,0},{8,12},{12,8},{16,20},{20,16},{24,28},{28,24},{1,5},{5... | collective-permute-start | bytes 3145736 | tf_op jit(solution)/shard_map/ppermute | solution.py:1162
  348.0 61.8 %collective-permute-start.6 = (bf16[128,2048]{1,0:T(8,128)(2,1)}, bf16[128,2048]{1,0:T(8,128)(2,1)}, u32[]{:S(2)}, u32[]{:S(2)}) collective-permute-start(bf16[128,2048]{1,0:T(8,128)(2,1)} %copy-done.27), channel_id=1, source_target_pairs={{0,1},{1,0},{2,3},{3,2},{4,5},{5,4},{6,7},{7,6},{8,9},{9,8},{10,11... | collective-permute-start | bytes 1572872 | tf_op jit(solution)/shard_map/ppermute | solution.py:1148
  348.0 61.8 %collective-permute-start.7 = (bf16[128,2048]{1,0:T(8,128)(2,1)}, bf16[128,2048]{1,0:T(8,128)(2,1)}, u32[]{:S(2)}, u32[]{:S(2)}) collective-permute-start(bf16[128,2048]{1,0:T(8,128)(2,1)} %copy-done.27), channel_id=1, source_target_pairs={{0,2},{1,3},{2,0},{3,1},{4,6},{5,7},{6,4},{7,5},{8,10},{9,11},{10,... | collective-permute-start | bytes 1572872 | tf_op jit(solution)/shard_map/ppermute | solution.py:1148
  351.9 57.9 %all-to-all-start.4 = ((bf16[4,128,8,64]{1,3,2,0:T(8,128)(2,1)}), bf16[4,128,8,64]{1,3,2,0:T(8,128)(2,1)}, u32[]{:S(2)}, u32[]{:S(2)}) async-start(bf16[4,128,8,64]{1,3,2,0:T(8,128)(2,1)} %copy.136), calls=%async_computation.5 | async-start | bytes 1048576 | tf_op jit(solution)/shard_map/all_to_all | solution.py:1143
  358.2 155.8 %reduce-scatter.6.cloned.1.call-start = ((), (), s32[]{:S(2)}) async-start(), calls=%async_computation.11 | async-start | bytes 5242880 | tf_op jit(solution)/shard_map/reduce_scatter | solution.py:1365
  413.5 10.8 %collective-permute-start.8 = (bf16[128,2048]{1,0:T(8,128)(2,1)}, bf16[128,2048]{1,0:T(8,128)(2,1)}, u32[]{:S(2)}, u32[]{:S(2)}) collective-permute-start(bf16[128,2048]{1,0:T(8,128)(2,1)} %collective-permute-done.7), channel_id=1, source_target_pairs={{0,1},{1,0},{2,3},{3,2},{4,5},{5,4},{6,7},{7,6},{8,9},{9,8},{10,11... | collective-permute-start | bytes 1572872 | tf_op jit(solution)/shard_map/ppermute | solution.py:1148
  428.5 51.5 %collective-permute-start.9 = (bf16[4,64,2048]{2,1,0:T(8,128)(2,1)}, bf16[4,64,2048]{2,1,0:T(8,128)(2,1)}, u32[]{:S(2)}, u32[]{:S(2)}) collective-permute-start(bf16[4,64,2048]{2,1,0:T(8,128)(2,1)} %dynamic-slice_bitcast_fusion), channel_id=1, source_target_pairs={{0,4},{4,0},{8,12},{12,8},{16,20},{20,16},{24,28},{28,24},{1,5},{5... | collective-permute-start | bytes 3145736 | tf_op jit(solution)/shard_map/ppermute | solution.py:1162
  430.9 49.1 %all-to-all-start.3 = ((bf16[8,128,256]{2,1,0:T(8,128)(2,1)}), bf16[8,128,256]{2,1,0:T(8,128)(2,1)S(1)}, u32[]{:S(2)}, u32[]{:S(2)}) async-start(bf16[8,128,256]{2,1,0:T(8,128)(2,1)} %bitcast.31), calls=%async_computation.3 | async-start | bytes 1048576 | tf_op jit(solution)/shard_map/all_to_all | solution.py:1143
  438.2 169.1 %reduce-scatter.8.cloned.1.call-start = ((), (), s32[]{:S(2)}) async-start(), calls=%async_computation.12 | async-start | bytes 1310720 | tf_op jit(solution)/shard_map/reduce_scatter | solution.py:1365
  482.4 20.8 %collective-permute-start.10 = (bf16[2,8,64,1408]{3,2,1,0:T(8,128)(2,1)S(1)}, bf16[2,8,64,1408]{3,2,1,0:T(8,128)(2,1)}, u32[]{:S(2)}, u32[]{:S(2)}) collective-permute-start(bf16[2,8,64,1408]{3,2,1,0:T(8,128)(2,1)S(1)} %pad_maximum_fusion), channel_id=1, source_target_pairs={{0,1},{1,0},{2,3},{3,2},{4,5},{5,4},{6,7},{7,6},{8,9},{9,8},{10,11... | collective-permute-start | bytes 8650760 | tf_op jit(solution)/shard_map/ppermute | solution.py:1148
  487.3 14.3 %collective-permute-start.11 = (bf16[2,64,640]{2,1,0:T(8,128)(2,1)S(1)}, bf16[2,64,640]{2,1,0:T(8,128)(2,1)S(1)}, u32[]{:S(2)}, u32[]{:S(2)}) collective-permute-start(bf16[2,64,640]{2,1,0:T(8,128)(2,1)S(1)} %pad_maximum_fusion.3), channel_id=1, source_target_pairs={{0,1},{1,0},{2,3},{3,2},{4,5},{5,4},{6,7},{7,6},{8,9},{9,8},{10,11... | collective-permute-start | bytes 491528 | tf_op jit(solution)/shard_map/ppermute | solution.py:1148
  514.0 89.5 %collective-permute-start.12 = (bf16[8,64,1408]{2,1,0:T(8,128)(2,1)}, bf16[8,64,1408]{2,1,0:T(8,128)(2,1)S(1)}, u32[]{:S(2)}, u32[]{:S(2)}) collective-permute-start(bf16[8,64,1408]{2,1,0:T(8,128)(2,1)} %fusion.31), channel_id=1, source_target_pairs={{0,2},{1,3},{2,0},{3,1},{4,6},{5,7},{6,4},{7,5},{8,10},{9,11},{10,... | collective-permute-start | bytes 4325384 | tf_op jit(solution)/shard_map/ppermute | solution.py:1148
  514.5 92.8 %collective-permute-start.13 = (bf16[256,2048]{1,0:T(8,128)(2,1)}, bf16[256,2048]{1,0:T(8,128)(2,1)}, u32[]{:S(2)}, u32[]{:S(2)}) collective-permute-start(bf16[256,2048]{1,0:T(8,128)(2,1)} %reduce-scatter.4.cloned.1.call-done), channel_id=1, source_target_pairs={{0,0},{1,8},{2,16},{3,24},{4,4},{5,12},{6,20},{7,28},{8,1},{9,9},{... | collective-permute-start | bytes 3145736 | tf_op jit(solution)/shard_map/ppermute | solution.py:1419
  594.4 13.0 %collective-permute-start.14 = (bf16[64,640]{1,0:T(8,128)(2,1)}, bf16[64,640]{1,0:T(8,128)(2,1)}, u32[]{:S(2)}, u32[]{:S(2)}) collective-permute-start(bf16[64,640]{1,0:T(8,128)(2,1)} %fusion.62), channel_id=1, source_target_pairs={{0,2},{1,3},{2,0},{3,1},{4,6},{5,7},{6,4},{7,5},{8,10},{9,11},{10,... | collective-permute-start | bytes 245768 | tf_op jit(solution)/shard_map/ppermute | solution.py:1148
  607.4 87.5 %all-to-all-start.5 = ((bf16[8,64,1408]{2,1,0:T(8,128)(2,1)}), bf16[8,64,1408]{2,1,0:T(8,128)(2,1)S(1)}, u32[]{:S(2)}, u32[]{:S(2)}) async-start(bf16[8,64,1408]{2,1,0:T(8,128)(2,1)} %fusion.17), calls=%async_computation.8 | async-start | bytes 2883584 | tf_op jit(solution)/shard_map/all_to_all | solution.py:1143
  614.7 78.6 %collective-permute-start.15 = (bf16[256,2048]{1,0:T(8,128)(2,1)}, bf16[256,2048]{1,0:T(8,128)(2,1)S(1)}, u32[]{:S(2)}, u32[]{:S(2)}) collective-permute-start(bf16[256,2048]{1,0:T(8,128)(2,1)} %reduce-scatter.6.cloned.1.call-done), channel_id=1, source_target_pairs={{0,0},{1,8},{2,16},{3,24},{4,4},{5,12},{6,20},{7,28},{8,1},{9,9},{... | collective-permute-start | bytes 3145736 | tf_op jit(solution)/shard_map/ppermute | solution.py:1423
  (68 other events, 544.0 us)
Sparse Core Ops, SparseCore 0:
  72.9 56.2 all-gather.1
  346.0 76.9 reduce-scatter.3
  427.0 86.8 reduce-scatter.5
  516.7 50.5 reduce-scatter.7

commit v12 on v5

--- a/solution.py
+++ b/solution.py
@@ -780,7 +780,7 @@
     given = ((seqs, own), (seqs, tail), (parts, weight))
     return pl.pallas_call(
         gather_kernel,
-        in_specs=[pl.BlockSpec(memory_space=pl.ANY)] * 3,
+        in_specs=[pl.BlockSpec(memory_space=pltpu.VMEM)] * 3,
         out_specs=[pl.BlockSpec(memory_space=pl.ANY)] * 3,
         out_shape=[jax.ShapeDtypeStruct((n,) + x.shape, x.dtype) for n, x in given],
         scratch_shapes=[dma((3,))] + [dma((3, 2))] * 4 + [dma((4, 2))] * 2 + [dma((2,))] * 2 + [dma] * 2,

time: 716 us -> 698 us (0.975)
  Pallas kernels: 368 us -> 353 us
    pallas_call x1, Pallas kernels: 70 us -> 54.4 us  [gather_first(): pl.pallas_call(gather_kernel, in_specs=[pl.BlockSpec(memory_space=pltpu.V...]
where the time goes in v12:
time: 698 us; the launch traced here: 689 us
  Pallas kernels  353 us (51%)
  waiting for transfers between devices  115 us (16%)
  starting transfers between devices  66.5 us (10%)
  matrix products  57.8 us (8%)
  local copies, waits for them, and re-layouts  45 us (6%)
  other arithmetic  35.4 us (5%)
  between operations  16.3 us (2%)
    pallas_call x2, Pallas kernels, channel_stage(): pl.pallas_call(body, in_specs=[pl.BlockSpec(memory_space=pltpu.VMEM)] + [...  89.3 us
    pallas_call x1, Pallas kernels, reduce_seq(): pl.pallas_call(functools.partial(reduce_kernel, splits), in_specs=[pl.Blo...  66.1 us
    dot_general x17, matrix products, dot(): return lax.dot_general(a, b, dims, preferred_element_type=F32)  57.8 us
    pallas_call x1, Pallas kernels, gather_first(): pl.pallas_call(gather_kernel, in_specs=[pl.BlockSpec(memory_space=pltpu.V...  54.4 us
    reduce_scatter x3, waiting for transfers between devices, along(): lax.psum_scatter(part, 'seq', scatter_dimension=0, tiled=True, axis_index...  51.9 us
    pallas_call x1, Pallas kernels, run_backward(): pl.pallas_call(functools.partial(backward_kernel, count), grid=(rows // s...  47.3 us
    ppermute x2, waiting for transfers between devices, turn(): return lax.ppermute(part, ('seq', 'wsh'), turned)  42.2 us
    all_to_all x7, starting transfers between devices, exchange(): return lax.all_to_all(x, axis, split_axis=0, concat_axis=0, tiled=True)  40.5 us
  transfers between devices with their start and end apart: 27, of which 9 were waited for; matrix products, arithmetic and copies ran while one was open for 12% of the time, Pallas kernels for 30%

profile of v12, /device:TPU:4, one launch (start us, length us, event | category | flops | bytes accessed | tf_op | source)
XLA Modules:
  0.0 688.7 jit_solution(12813973757329898420)
XLA Ops:
  18.3 54.4 %gather_first.1 = (bf16[8,128,2048]{2,1,0:T(8,128)(2,1)}, bf16[8,128,128]{2,1,0:T(8,128)(2,1)}, bf16[4,512,1664]{2,1,0:T(8,128)(2,1)}) custom-call(bf16[128,2048]{1,0:T(8,128)(2,1)} %own_ref.1, bf16[128,128]{1,0:T(8,128)(2,1)} %pad.30.tail_ref, bf16[512,1664]{1,0:T(8,128)(2,1)} %copy-done.28), custom_call_target="tpu_custom_call" | custom-call | bytes 104857600 | tf_op jit(solution)/shard_map/gather_first/pallas_call | solution.py:781
  74.3 7.0 %convert_reduce_fusion = (f32[1024]{0:T(1024)S(1)}, bf16[1024,2048]{1,0:T(8,128)(2,1)S(1)}) fusion(bf16[1024,2048]{1,0:T(8,128)(2,1)} %bitcast.188, s32[1024]{0:T(1024)S(1)} %bitcast.181), kind=kOutput, calls=%fused_computation.1 | convolution fusion | flops 4302306304 | bytes 8396800 | tf_op jit(solution)/shard_map/dot_general | solution.py:28
  96.2 19.4 %mix_project.1 = (f32[1024,256]{1,0:T(8,128)}, f32[1024,256]{1,0:T(8,128)}, f32[1024,256]{1,0:T(8,128)}, f32[1024,640]{1,0:T(8,128)}, bf16[1024,640]{1,0:T(8,128)(2,1)}) custom-call(bf16[1024,2048]{1,0:T(8,128)(2,1)} %copy-done.18, f32[1024,4]{1,0:T(8,128)} %copy.132.stats_ref, f32[8,2048]{1,0:T(8,128)} %slice_bitcast_fusion.3.vec_ref, ...), custom_call_target="tpu_custom_call" | custom-call | flops 134217728 | bytes 62914560 | tf_op jit(solution)/shard_map/mix_project/pallas_call | solution.py:569
  117.2 6.3 all-to-all-start.1
  124.5 36.2 %mix_forward.1 = (bf16[1024,256]{1,0:T(8,128)(2,1)S(1)}, bf16[1024,256]{1,0:T(8,128)(2,1)S(1)}, f32[1024,256]{1,0:T(8,128)S(1)}, f32[1024,256]{1,0:T(8,128)S(1)}, f32[1024,256]{1,0:T(8,128)S(1)}) custom-call(f32[1024,256]{1,0:T(8,128)S(1)} %copy-done.3, f32[1024,256]{1,0:T(8,128)} %get-tuple-element.91.keys_ref, f32[1024,256]{1,0:T(8,128)} %get-tuple-element.92.values_ref, ...), custom_call_target="tpu_custom_call" | custom-call | flops 134217728 | bytes 115343360 | tf_op jit(solution)/shard_map/mix_forward/pallas_call | solution.py:385
  165.5 6.0 all-to-all-start.2
  178.3 7.7 %all-to-all-done.2 = bf16[8,128,256]{1,2,0:T(8,128)(2,1)S(1)} async-done(((bf16[8,128,256]{1,2,0:T(8,128)(2,1)}), bf16[8,128,256]{1,2,0:T(8,128)(2,1)S(1)}, u32[]{:S(2)}, u32[]{:S(2)}) %all-to-all-start.2) | async-done | bytes 524320 | tf_op jit(solution)/shard_map/all_to_all | solution.py:1089
  186.1 5.0 fusion.85
  191.7 3.8 collective-permute-start
  197.8 37.4 %channel_forward.1 = (f32[128,2048]{1,0:T(8,128)}, bf16[512,2048]{1,0:T(8,128)(2,1)}, bf16[512,1024]{1,0:T(8,128)(2,1)}, bf16[512,1024]{1,0:T(8,128)(2,1)}, f32[512,2048]{1,0:T(8,128)}) custom-call(bf16[128,2048]{1,0:T(8,128)(2,1)} %add_convert_fusion.2.refs_0_, bf16[2048,2048]{1,0:T(8,128)(2,1)} %refs_2_.3, bf16[2048,2048]{1,0:T(8,128)(2,1)} %refs_1_.3), custom_call_target="tpu_custom_call" | custom-call | bytes 104857600 | tf_op jit(solution)/shard_map/channel_forward/pallas_call | solution.py:1061
  237.9 51.9 %channel_backward.1 = (f32[128,2048]{1,0:T(8,128)}, bf16[512,2048]{1,0:T(8,128)(2,1)}, bf16[512,1024]{1,0:T(8,128)(2,1)}, bf16[512,2048]{1,0:T(8,128)(2,1)}, bf16[512,1024]{1,0:T(8,128)(2,1)}) custom-call(bf16[128,2048]{1,0:T(8,128)(2,1)} %get-tuple-element.268.refs_0_, bf16[2048,2048]{1,0:T(8,128)(2,1)} %refs_1_.3, bf16[2048,2048]{1,0:T(8,128)(2,1)} %refs_2_.3, ...), custom_call_target="tpu_custom_call" | custom-call | bytes 104857600 | tf_op jit(solution)/shard_map/channel_backward/pallas_call | solution.py:1061
  293.8 4.1 collective-permute-done.3
  300.2 3.9 convolution_convert_fusion.1
  305.0 3.8 all-to-all-start.3
  309.1 4.5 fusion.91
  313.6 4.7 add_convert_fusion.1
  318.3 3.9 all-to-all-done.3
  324.4 7.5 %fusion.92 = f32[1024,2048]{1,0:T(8,128)} fusion(bf16[512,1024]{1,0:T(8,128)(2,1)S(1)} %copy-done.42, bf16[512,2048]{1,0:T(8,128)(2,1)} %get-tuple-element.115), kind=kOutput, calls=%fused_computation.216 | convolution fusion | flops 2147483648 | bytes 11534336 | tf_op jit(solution)/shard_map/dot_general | solution.py:28
  333.9 6.3 all-to-all-start.5
  342.3 47.3 %mix_backward.1 = (bf16[1024,256]{1,0:T(8,128)(2,1)S(1)}, bf16[1024,256]{1,0:T(8,128)(2,1)S(1)}, bf16[1024,256]{1,0:T(8,128)(2,1)S(1)}, bf16[4,1024,256]{2,1,0:T...) custom-call(bf16[1024,256]{1,0:T(8,128)(2,1)S(1)} %bitcast.129, f32[1024,256]{1,0:T(8,128)S(1)} %copy-done.3, ...), custom_call_target="tpu_custom_call" | custom-call | flops 134217728 | bytes 157286400 | tf_op jit(solution)/shard_map/mix_backward/pallas_call | solution.py:413
  394.6 4.0 all-to-all-start.4
  398.7 8.7 %add_convert_fusion = bf16[1024,2048]{1,0:T(8,128)(2,1)} fusion(f32[1024,2048]{1,0:T(8,128)} %fusion.92, bf16[512,1024]{1,0:T(8,128)(2,1)} %collective-permute-done.6, bf16[512,2048]{1,0:T(8,128)(2,1)} %collective-permute-done.5), kind=kOutput, calls=%fused_computation.8 | convolution fusion | flops 2151677952 | bytes 15728640 | tf_op jit(solution)/shard_map/dot_general | solution.py:28
  416.0 4.0 collective-permute-start.4
  421.4 40.0 %mix_unproject.1 = (f32[1024,2048]{1,0:T(8,128)}, f32[1024,2]{1,0:T(8,128)}, bf16[4,8,64,1408]{3,2,1,0:T(8,128)(2,1)}, bf16[256,640]{1,0:T(8,128)(2,1)}) custom-call(bf16[1024,2048]{1,0:T(8,128)(2,1)} %copy-done.18, f32[1024,4]{1,0:T(8,128)} %copy.132.stats_ref, f32[8,2048]{1,0:T(8,128)} %slice_bitcast_fusion.3.vec_ref, bf16[2048,1664]{1,0:T(8,128)(2,1)} %bitcast.137, ...), custom_call_target="tpu_custom_call" | custom-call | flops 134217728 | bytes 125829120 | tf_op jit(solution)/shard_map/mix_unproject/pallas_call | solution.py:592
  461.5 8.0 %collective-permute-done.4 = bf16[256,2048]{1,0:T(8,128)(2,1)S(1)} collective-permute-done((bf16[256,2048]{1,0:T(8,128)(2,1)}, bf16[256,2048]{1,0:T(8,128)(2,1)S(1)}, u32[]{:S(2)}, u32[]{:S(2)}) %collective-permute-start.4) | collective-permute-done | bytes 1048608 | tf_op jit(solution)/shard_map/ppermute | solution.py:1313
  482.0 4.9 fusion.12
  487.9 66.1 %reduce_seq.1 = f32[128,2048]{1,0:T(8,128)S(1)} custom-call(bf16[8,128,2048]{2,1,0:T(8,128)(2,1)S(1)} %bitcast.128), custom_call_target="tpu_custom_call" | custom-call | bytes 1048576 | tf_op jit(solution)/shard_map/reduce_seq/pallas_call | solution.py:903
  556.6 10.5 %all-to-all-start.6 = ((bf16[8,64,1408]{2,1,0:T(8,128)(2,1)}), bf16[8,64,1408]{2,1,0:T(8,128)(2,1)S(1)}, u32[]{:S(2)}, u32[]{:S(2)}) async-start(bf16[8,64,1408]{2,1,0:T(8,128)(2,1)} %fusion.17), calls=%async_computation.8 | async-start | bytes 2883584 | tf_op jit(solution)/shard_map/all_to_all | solution.py:1089
  570.0 51.9 %reduce-scatter.8.cloned.1.call-done = bf16[256,2048]{1,0:T(8,128)(2,1)} async-done(((bf16[1024,2048]{1,0:T(8,128)(2,1)}), bf16[256,2048]{1,0:T(8,128)(2,1)}) %reduce-scatter.8.cloned.1.call-update) | async-done | bytes 1048592 | tf_op jit(solution)/shard_map/reduce_scatter | solution.py:1310
  621.9 4.5 collective-permute-start.15
  627.3 5.2 collective-permute-start.14
  639.4 34.2 %collective-permute-done.15 = bf16[256,2048]{1,0:T(8,128)(2,1)} collective-permute-done((bf16[256,2048]{1,0:T(8,128)(2,1)}, bf16[256,2048]{1,0:T(8,128)(2,1)}, u32[]{:S(2)}, u32[]{:S(2)}) %collective-permute-start.15) | collective-permute-done | bytes 1048608 | tf_op jit(solution)/shard_map/ppermute | solution.py:1313
  (295 shorter events, 109.3 us)
Async XLA Ops:
  7.2 109.0 %copy-start = (bf16[128,2048]{1,0:T(8,128)(2,1)S(1)}, bf16[128,2048]{1,0:T(8,128)(2,1)}, u32[]{:S(2)}) copy-start(bf16[128,2048]{1,0:T(8,128)(2,1)} %param.17) | copy-start | bytes 1572868
  7.2 178.8 %all-gather.2.cloned.1.call-start = ((), (), s32[]{:S(2)}) async-start(), calls=%async_computation.10 | async-start | bytes 10485760 | tf_op jit(solution)/shard_map/all_gather | solution.py:1213
  15.6 57.2 %copy-start.44 = (s32[1,4]{1,0:T(1,128)S(1)}, s32[1,4]{1,0:T(1,128)}, u32[]{:S(2)}) copy-start(s32[1,4]{1,0:T(1,128)} %param.20) | copy-start | bytes 52
  85.9 30.0 %all-to-all-start = ((bf16[8,128,256]{1,2,0:T(8,128)(2,1)}), bf16[8,128,256]{1,2,0:T(8,128)(2,1)S(1)}, u32[]{:S(2)}, u32[]{:S(2)}) async-start(bf16[8,128,256]{1,2,0:T(8,128)(2,1)} %bitcast.15), calls=%async_computation | async-start | bytes 1048576 | tf_op jit(solution)/shard_map/all_to_all | solution.py:1089
  90.8 81.3 %collective-permute-start.1 = (f32[8,128]{1,0:T(8,128)S(1)}, f32[8,128]{1,0:T(8,128)S(1)}, u32[]{:S(2)}, u32[]{:S(2)}) collective-permute-start(f32[8,128]{1,0:T(8,128)S(1)} %broadcast_in_dim.4), channel_id=1, source_target_pairs={{0,1},{1,0},{2,3},{3,2},{4,5},{5,4},{6,7},{7,6},{8,9},{9,8},{10,11... | collective-permute-start | bytes 12296 | tf_op jit(solution)/shard_map/ppermute | solution.py:1094
  117.2 47.2 %all-to-all-start.1 = ((bf16[8,16,2048]{2,1,0:T(8,128)(2,1)}), bf16[8,16,2048]{2,1,0:T(8,128)(2,1)S(1)}, u32[]{:S(2)}, u32[]{:S(2)}) async-start(bf16[8,16,2048]{2,1,0:T(8,128)(2,1)} %bitcast.17), calls=%async_computation.1 | async-start | bytes 1048576 | tf_op jit(solution)/shard_map/all_to_all | solution.py:1089
  123.7 216.6 %copy-start.2 = (bf16[640,256]{1,0:T(8,128)(2,1)}, bf16[640,256]{1,0:T(8,128)(2,1)S(1)}, u32[]{:S(2)}) copy-start(bf16[640,256]{1,0:T(8,128)(2,1)S(1)} %fusion.50.up_ref) | copy-start | bytes 983044
  165.5 20.6 %all-to-all-start.2 = ((bf16[8,128,256]{1,2,0:T(8,128)(2,1)}), bf16[8,128,256]{1,2,0:T(8,128)(2,1)S(1)}, u32[]{:S(2)}, u32[]{:S(2)}) async-start(bf16[8,128,256]{1,2,0:T(8,128)(2,1)} %copy.140), calls=%async_computation.2 | async-start | bytes 1048576 | tf_op jit(solution)/shard_map/all_to_all | solution.py:1089
  172.8 3.7 collective-permute-start.2
  191.7 4.7 collective-permute-start
  197.8 37.4 %copy-start.16 = (f32[128,2048]{1,0:T(8,128)S(1)}, f32[128,2048]{1,0:T(8,128)}, u32[]{:S(2)}) copy-start(f32[128,2048]{1,0:T(8,128)} %copy-done.15) | copy-start | bytes 3145732
  292.4 5.5 collective-permute-start.3
  305.0 17.2 %all-to-all-start.3 = ((bf16[8,128,256]{2,1,0:T(8,128)(2,1)}), bf16[8,128,256]{2,1,0:T(8,128)(2,1)S(1)}, u32[]{:S(2)}, u32[]{:S(2)}) async-start(bf16[8,128,256]{2,1,0:T(8,128)(2,1)} %bitcast.125), calls=%async_computation.3 | async-start | bytes 1048576 | tf_op jit(solution)/shard_map/all_to_all | solution.py:1089
  308.8 107.2 %reduce-scatter.4.cloned.1.call-start = ((), (), s32[]{:S(2)}) async-start(), calls=%async_computation.11 | async-start | bytes 5242880 | tf_op jit(solution)/shard_map/reduce_scatter | solution.py:1310
  322.3 76.4 %collective-permute-start.5 = (bf16[512,2048]{1,0:T(8,128)(2,1)}, bf16[512,2048]{1,0:T(8,128)(2,1)}, u32[]{:S(2)}, u32[]{:S(2)}) collective-permute-start(bf16[512,2048]{1,0:T(8,128)(2,1)} %get-tuple-element.115), channel_id=1, source_target_pairs={{0,4},{4,0},{8,12},{12,8},{16,20},{20,16},{24,28},{28,24},{1,5},{5... | collective-permute-start | bytes 6291464 | tf_op jit(solution)/shard_map/ppermute | solution.py:1108
  323.8 74.8 %collective-permute-start.6 = (bf16[512,1024]{1,0:T(8,128)(2,1)}, bf16[512,1024]{1,0:T(8,128)(2,1)}, u32[]{:S(2)}, u32[]{:S(2)}) collective-permute-start(bf16[512,1024]{1,0:T(8,128)(2,1)} %get-tuple-element.116), channel_id=1, source_target_pairs={{0,4},{4,0},{8,12},{12,8},{16,20},{20,16},{24,28},{28,24},{1,5},{5... | collective-permute-start | bytes 3145736 | tf_op jit(solution)/shard_map/ppermute | solution.py:1108
  331.8 66.8 %collective-permute-start.7 = (bf16[128,2048]{1,0:T(8,128)(2,1)}, bf16[128,2048]{1,0:T(8,128)(2,1)}, u32[]{:S(2)}, u32[]{:S(2)}) collective-permute-start(bf16[128,2048]{1,0:T(8,128)(2,1)} %get-tuple-element.232), channel_id=1, source_target_pairs={{0,1},{1,0},{2,3},{3,2},{4,5},{5,4},{6,7},{7,6},{8,9},{9,8},{10,11... | collective-permute-start | bytes 1572872 | tf_op jit(solution)/shard_map/ppermute | solution.py:1094
  331.8 66.8 %collective-permute-start.8 = (bf16[128,2048]{1,0:T(8,128)(2,1)}, bf16[128,2048]{1,0:T(8,128)(2,1)}, u32[]{:S(2)}, u32[]{:S(2)}) collective-permute-start(bf16[128,2048]{1,0:T(8,128)(2,1)} %get-tuple-element.232), channel_id=1, source_target_pairs={{0,2},{1,3},{2,0},{3,1},{4,6},{5,7},{6,4},{7,5},{8,10},{9,11},{10,... | collective-permute-start | bytes 1572872 | tf_op jit(solution)/shard_map/ppermute | solution.py:1094
  333.9 60.7 %all-to-all-start.5 = ((bf16[4,128,8,64]{1,3,2,0:T(8,128)(2,1)}), bf16[4,128,8,64]{1,3,2,0:T(8,128)(2,1)}, u32[]{:S(2)}, u32[]{:S(2)}) async-start(bf16[4,128,8,64]{1,3,2,0:T(8,128)(2,1)} %copy.142), calls=%async_computation.6 | async-start | bytes 1048576 | tf_op jit(solution)/shard_map/all_to_all | solution.py:1089
  394.6 66.8 %all-to-all-start.4 = ((bf16[8,32,2048]{2,1,0:T(8,128)(2,1)}), bf16[8,32,2048]{2,1,0:T(8,128)(2,1)S(1)}, u32[]{:S(2)}, u32[]{:S(2)}) async-start(bf16[8,32,2048]{2,1,0:T(8,128)(2,1)} %pad_maximum_fusion.1), calls=%async_computation.4 | async-start | bytes 2097152 | tf_op jit(solution)/shard_map/all_to_all | solution.py:1089
  398.6 158.0 %reduce-scatter.6.cloned.1.call-start = ((), (), s32[]{:S(2)}) async-start(), calls=%async_computation.12 | async-start | bytes 1310720 | tf_op jit(solution)/shard_map/reduce_scatter | solution.py:1310
  398.6 10.4 %collective-permute-start.9 = (bf16[128,2048]{1,0:T(8,128)(2,1)}, bf16[128,2048]{1,0:T(8,128)(2,1)S(1)}, u32[]{:S(2)}, u32[]{:S(2)}) collective-permute-start(bf16[128,2048]{1,0:T(8,128)(2,1)} %collective-permute-done.8), channel_id=1, source_target_pairs={{0,1},{1,0},{2,3},{3,2},{4,5},{5,4},{6,7},{7,6},{8,9},{9,8},{10,11... | collective-permute-start | bytes 1572872 | tf_op jit(solution)/shard_map/ppermute | solution.py:1094
  414.1 47.4 %collective-permute-start.10 = (bf16[4,64,2048]{2,1,0:T(8,128)(2,1)}, bf16[4,64,2048]{2,1,0:T(8,128)(2,1)}, u32[]{:S(2)}, u32[]{:S(2)}) collective-permute-start(bf16[4,64,2048]{2,1,0:T(8,128)(2,1)} %dynamic-slice_bitcast_fusion), channel_id=1, source_target_pairs={{0,4},{4,0},{8,12},{12,8},{16,20},{20,16},{24,28},{28,24},{1,5},{5... | collective-permute-start | bytes 3145736 | tf_op jit(solution)/shard_map/ppermute | solution.py:1108
  416.0 53.4 %collective-permute-start.4 = (bf16[256,2048]{1,0:T(8,128)(2,1)}, bf16[256,2048]{1,0:T(8,128)(2,1)S(1)}, u32[]{:S(2)}, u32[]{:S(2)}) collective-permute-start(bf16[256,2048]{1,0:T(8,128)(2,1)} %reduce-scatter.4.cloned.1.call-done), channel_id=1, source_target_pairs={{0,0},{1,8},{2,16},{3,24},{4,4},{5,12},{6,20},{7,28},{8,1},{9,9},{... | collective-permute-start | bytes 3145736 | tf_op jit(solution)/shard_map/ppermute | solution.py:1313
  472.8 149.1 %reduce-scatter.8.cloned.1.call-start = ((), (), s32[]{:S(2)}) async-start(), calls=%async_computation.13 | async-start | bytes 5242880 | tf_op jit(solution)/shard_map/reduce_scatter | solution.py:1310
  475.9 11.0 %collective-permute-start.11 = (bf16[2,8,64,1408]{3,2,1,0:T(8,128)(2,1)S(1)}, bf16[2,8,64,1408]{3,2,1,0:T(8,128)(2,1)S(1)}, u32[]{:S(2)}, u32[]{:S(2)}) collective-permute-start(bf16[2,8,64,1408]{3,2,1,0:T(8,128)(2,1)S(1)} %pad_maximum_fusion), channel_id=1, source_target_pairs={{0,1},{1,0},{2,3},{3,2},{4,5},{5,4},{6,7},{7,6},{8,9},{9,8},{10,11... | collective-permute-start | bytes 8650760 | tf_op jit(solution)/shard_map/ppermute | solution.py:1094
  487.9 67.1 %collective-permute-start.12 = (bf16[8,64,1408]{2,1,0:T(8,128)(2,1)S(1)}, bf16[8,64,1408]{2,1,0:T(8,128)(2,1)S(1)}, u32[]{:S(2)}, u32[]{:S(2)}) collective-permute-start(bf16[8,64,1408]{2,1,0:T(8,128)(2,1)S(1)} %fusion.31), channel_id=1, source_target_pairs={{0,2},{1,3},{2,0},{3,1},{4,6},{5,7},{6,4},{7,5},{8,10},{9,11},{10,... | collective-permute-start | bytes 4325384 | tf_op jit(solution)/shard_map/ppermute | solution.py:1094
  556.6 120.6 %all-to-all-start.6 = ((bf16[8,64,1408]{2,1,0:T(8,128)(2,1)}), bf16[8,64,1408]{2,1,0:T(8,128)(2,1)S(1)}, u32[]{:S(2)}, u32[]{:S(2)}) async-start(bf16[8,64,1408]{2,1,0:T(8,128)(2,1)} %fusion.17), calls=%async_computation.8 | async-start | bytes 2883584 | tf_op jit(solution)/shard_map/all_to_all | solution.py:1089
  567.1 2.8 collective-permute-start.13
  621.9 51.6 %collective-permute-start.15 = (bf16[256,2048]{1,0:T(8,128)(2,1)}, bf16[256,2048]{1,0:T(8,128)(2,1)}, u32[]{:S(2)}, u32[]{:S(2)}) collective-permute-start(bf16[256,2048]{1,0:T(8,128)(2,1)} %reduce-scatter.8.cloned.1.call-done), channel_id=1, source_target_pairs={{0,0},{1,8},{2,16},{3,24},{4,4},{5,12},{6,20},{7,28},{8,1},{9,9},{... | collective-permute-start | bytes 3145736 | tf_op jit(solution)/shard_map/ppermute | solution.py:1313
  627.3 10.3 %collective-permute-start.14 = (bf16[64,640]{1,0:T(8,128)(2,1)S(1)}, bf16[64,640]{1,0:T(8,128)(2,1)S(1)}, u32[]{:S(2)}, u32[]{:S(2)}) collective-permute-start(bf16[64,640]{1,0:T(8,128)(2,1)S(1)} %fusion.62), channel_id=1, source_target_pairs={{0,2},{1,3},{2,0},{3,1},{4,6},{5,7},{6,4},{7,5},{8,10},{9,11},{10,... | collective-permute-start | bytes 245768 | tf_op jit(solution)/shard_map/ppermute | solution.py:1094
  637.6 38.7 %copy-start.36 = (bf16[64,2048]{1,0:T(8,128)(2,1)S(1)}, bf16[64,2048]{1,0:T(8,128)(2,1)}, u32[]{:S(2)}) copy-start(bf16[64,2048]{1,0:T(8,128)(2,1)} %reduce-scatter.6.cloned.1.call-done) | copy-start | bytes 786436
  (44 other events, 232.9 us)
Sparse Core Ops, SparseCore 0:
  72.9 56.2 all-gather.1
  322.4 75.8 reduce-scatter.3
  472.9 25.6 reduce-scatter.5
  500.8 121.0 reduce-scatter.7
